TPU v7x, 128 devices: a whole 4x4x4 slice. The times are simulated.
128 devices in a mesh: ctx: 32 (over y, x, core), head: 4 (over z).
Axes of the slice: x: 4, y: 4, z: 4, core: 2. Of those that a mesh axis runs over, the one named last changes fastest.
Arguments:
- prompt_values: bfloat16 [16384, 8192], P('ctx', 'head'), may hold values from -6 to 6
- prompt_gate: bfloat16 [16384, 8192], P('ctx', 'head'), may hold values from -6 to 6
- prompt_inject: bfloat16 [16384, 4, 256], P('ctx', 'head'), may hold values from -6 to 6
- prompt_read: bfloat16 [16384, 4, 256], P('ctx', 'head'), may hold values from -0.375 to 0.375
- prompt_step: float32 [128, 16384], P('head', 'ctx'), may hold values from -8 to 256
- decay_log: float32 [128], P('head'), may hold values from -10 to 0
- skip_gain: float32 [128], P('head'), may hold values from 0.5 to 1.5
- norm_weight: float32 [8192], P('head'), may hold values from 0.1 to 1.9
- out_weight: bfloat16 [8192, 4096], P('head'), may hold values from -0.0625 to 0.0625
- sample_values: bfloat16 [64, 16, 8192], P('ctx', None, 'head'), may hold values from -6 to 6
- sample_gate: bfloat16 [64, 16, 8192], P('ctx', None, 'head'), may hold values from -6 to 6
- sample_inject: bfloat16 [64, 16, 4, 256], P('ctx', None, 'head'), may hold values from -6 to 6
- sample_read: bfloat16 [64, 16, 4, 256], P('ctx', None, 'head'), may hold values from -0.375 to 0.375
- sample_step: float32 [128, 64, 16], P('head', 'ctx'), may hold values from -8 to 256
- sample_length: int32 [64], P('ctx'), may hold values from 1 to 16
Outputs:
- prompt_mixed: bfloat16 [4096, 16384], P('head', 'ctx')
- sample_mixed: bfloat16 [4096, 64], P('head', 'ctx')
All inputs are finite; a program needn't handle non-finite values.
Results may differ from a plain program's by a relative error of at most 0.02.
Values may be sent and summed in bfloat16 or wider, within the bound.
No kernel may reach another device: no remote copies, remote signals or barrier semaphores. Data moves between devices by JAX's collectives and lax.ppermute only.
A program may use at most 192 MiB of HBM per device.

v0:
```python
import jax
import jax.numpy as jnp
from jax import lax
from jax.sharding import Mesh
from jax.sharding import PartitionSpec as P

HEAD_DIM = 64
STATE = 256
BLOCK = 128
SLEN = 16
CTX = ("ctx_0", "ctx_1", "ctx_2")


def nothing_yet(shard, identity):
    return jax.tree.map(
        lambda a, e: jnp.broadcast_to(jnp.asarray(e, a.dtype), a.shape), shard, identity
    )


def prefix_by_axis(shard, axes, combine, identity):
    before = start = nothing_yet(shard, identity)
    so_far = shard
    for axis in reversed(axes):
        peers, place = (lax.axis_size(axis), lax.axis_index(axis))
        pieces = jax.tree.map(
            lambda part, kind: lax.all_gather(part.astype(kind), axis),
            so_far,
            (jnp.bfloat16, jnp.bfloat16),
        )
        inside, so_far = (start, start)
        for k in range(peers):
            passed = k < place
            so_far = combine(
                so_far, jax.tree.map(lambda part, own: part[k].astype(own.dtype), pieces, shard)
            )
            inside = jax.tree.map(lambda new, old: jnp.where(passed, new, old), so_far, inside)
        before = combine(inside, before)
    return before


def copy_for_each(shard, axis):
    copies = jnp.broadcast_to(shard, (lax.axis_size(axis), *shard.shape))
    return lax.all_to_all(copies, axis, split_axis=0, concat_axis=0, tiled=True)


def joined_by_halves(pieces, combine):
    while len(jax.tree.leaves(pieces)[0]) > 1:
        pieces = jax.vmap(combine)(*(pieces[side::2] for side in (0, 1)))
    return pieces[0]


def carried_in(shard, axis, combine, identity):
    peers, place = (lax.axis_size(axis), lax.axis_index(axis))
    passed = jnp.arange(peers) > place

    def kept(part, zero, own):
        part = jnp.where(
            passed.reshape(-1, *(1 for _ in own.shape)), part, jnp.asarray(zero, own.dtype)
        )
        return part[::-1]

    pieces = copy_for_each(shard, axis)
    return joined_by_halves(kept(pieces, identity, shard), combine)


def laid_out(blocks, dim):
    blocks = jnp.moveaxis(blocks, 0, dim)
    shape = blocks.shape
    return blocks.reshape(*shape[:dim], shape[dim] * shape[dim + 1], *shape[dim + 2 :])


def gather_directly(shard, axis, dim):
    blocks = copy_for_each(shard, axis)
    return laid_out(blocks, dim)


def cut_along(shard, dim, peers):
    shape = shard.shape
    blocks = shard.reshape(*shape[:dim], peers, shape[dim] // peers, *shape[dim + 1 :])
    return jnp.moveaxis(blocks, dim, 0)


def sent_and_summed(shard, axis, dim):
    blocks = cut_along(shard, dim, lax.axis_size(axis))
    arrived = lax.all_to_all(blocks, axis, split_axis=0, concat_axis=0, tiled=True)
    return arrived.astype(jnp.float32).sum(axis=0)


def block_terms(values, inject, readout, steps, decay_rate):
    length = values.shape[0]
    log_decay = steps * decay_rate[:, None]
    running = jnp.cumsum(log_decay, axis=1)
    scores = jnp.dot(readout.astype(jnp.float32), inject.astype(jnp.float32).T)
    causal = jnp.arange(length)[:, None] >= jnp.arange(length)[None, :]
    gap_logs = jnp.where(causal[None], running[:, :, None] - running[:, None, :], 0.0)
    mixing = jnp.where(
        causal[None], scores[None] * jnp.exp(gap_logs) * steps[:, None, :], 0.0
    ).astype(jnp.bfloat16)
    local_out = jnp.einsum("hts,shp->thp", mixing.astype(jnp.float32), values.astype(jnp.float32))
    to_end = jnp.exp(running[:, -1:] - running) * steps
    weighted = (to_end[:, :, None] * inject.astype(jnp.float32)[None]).astype(jnp.bfloat16)
    local_state = jnp.einsum(
        "shp,hsn->hpn", values.astype(jnp.float32), weighted.astype(jnp.float32)
    )
    return (local_out, local_state, running)


def group_block(values, inject, readout, steps, decay_rate, carry_state):
    local_out, local_state, running = block_terms(values, inject, readout, steps, decay_rate)
    carried = jnp.einsum("tn,hpn->thp", readout.astype(jnp.float32), carry_state)
    carried = carried * jnp.exp(running).T[:, :, None]
    next_state = jnp.exp(running[:, -1])[:, None, None] * carry_state + local_state
    return (local_out + carried, next_state, running)


def finish(outputs, values, gate, skip_gain, norm_weight, groups):
    row_count = values.shape[0]
    with_skip = outputs + skip_gain[None, :, None] * values.reshape(
        row_count, skip_gain.shape[0], -1
    ).astype(jnp.float32)
    gated_out = with_skip.reshape(row_count, -1) * jax.nn.silu(gate.astype(jnp.float32))
    grouped = gated_out.reshape(row_count, groups, -1)
    inverse_rms = lax.rsqrt(jnp.mean(grouped * grouped, axis=2, keepdims=True) + 1e-05)
    return ((grouped * inverse_rms).reshape(row_count, -1) * norm_weight[None]).astype(jnp.bfloat16)


def chain_pair(before_pair, after_pair):
    return (
        before_pair[0] + after_pair[0],
        jnp.exp(after_pair[0])[:, :, None, None] * before_pair[1] + after_pair[1],
    )


def add_logs(before_logs, after_logs):
    return before_logs + after_logs


def projector(out_weight, row_matrix):
    return lax.dot_general(
        out_weight.astype(jnp.float32), row_matrix.astype(jnp.float32), (((0,), (1,)), ((), ()))
    )


def per_device(
    prompt_values,
    prompt_gate,
    prompt_inject,
    prompt_read,
    prompt_step,
    decay_log,
    skip_gain,
    norm_weight,
    out_weight,
    sample_values,
    sample_gate,
    sample_inject,
    sample_read,
    sample_step,
    sample_length,
):
    tokens = prompt_values.shape[0]
    local_groups = prompt_inject.shape[1]
    local_heads = prompt_step.shape[0]
    per_group = local_heads // local_groups
    blocks = tokens // BLOCK
    samples = sample_values.shape[0]
    decay_rate = (-jnp.exp(decay_log)).reshape(local_groups, per_group)
    steps = (
        jax.nn.softplus(prompt_step)
        .reshape(local_groups, per_group, blocks, BLOCK)
        .transpose(2, 0, 1, 3)
    )
    values = prompt_values.reshape(blocks, BLOCK, local_groups, per_group, HEAD_DIM)
    inject = prompt_inject.reshape(blocks, BLOCK, local_groups, STATE)
    readout = prompt_read.reshape(blocks, BLOCK, local_groups, STATE)
    grouped_block = jax.vmap(group_block, in_axes=(1, 1, 1, 0, 0, 0), out_axes=(1, 0, 0))

    def advance(carried_pair, block_data):
        carry_state, offset = carried_pair
        block_values, block_inject, block_readout, block_steps = block_data
        block_out, next_state, running = grouped_block(
            block_values, block_inject, block_readout, block_steps, decay_rate, carry_state
        )
        return ((next_state, offset + running[:, :, -1]), (block_out, running + offset[:, :, None]))

    zero_state = jnp.zeros((local_groups, per_group, HEAD_DIM, STATE), jnp.float32)
    zero_log = jnp.zeros((local_groups, per_group), jnp.float32)
    (end_state, total_log), (outputs, prefix_log) = lax.scan(
        advance, (zero_state, zero_log), (values, inject, readout, steps)
    )
    incoming_log, incoming_state = prefix_by_axis(
        (total_log, end_state), CTX, chain_pair, (zero_log, zero_state)
    )
    arrival = jnp.einsum("tgn,ghpn->tghp", prompt_read.astype(jnp.float32), incoming_state)
    decay_in = jnp.exp(prefix_log).transpose(0, 3, 1, 2).reshape(tokens, local_groups, per_group)
    outputs = (
        outputs.reshape(tokens, local_groups, per_group, HEAD_DIM)
        + arrival * decay_in[:, :, :, None]
    )
    normed = finish(
        outputs.reshape(tokens, local_heads, HEAD_DIM),
        prompt_values,
        prompt_gate,
        skip_gain,
        norm_weight,
        local_groups,
    )
    sample_steps = (
        jax.nn.softplus(sample_step)
        .reshape(local_groups, per_group, samples, SLEN)
        .transpose(2, 0, 1, 3)
    )
    sample_vals = sample_values.reshape(samples, SLEN, local_groups, per_group, HEAD_DIM)
    per_sample = jax.vmap(grouped_block, in_axes=(0, 0, 0, 0, None, None), out_axes=(0, 0, 0))
    onehot = (jnp.arange(SLEN)[None, :] == (sample_length - 1)[:, None]).astype(jnp.float32)
    tail_log = carried_in(total_log, CTX, add_logs, zero_log)
    decayed = jnp.exp(tail_log)[:, :, None, None] * end_state
    last_read = jnp.einsum("sl,slgn->sgn", onehot, sample_read.astype(jnp.float32)).astype(
        jnp.bfloat16
    )
    all_read = gather_directly(last_read, CTX, 0)
    readings = jnp.einsum("sgn,ghpn->sghp", all_read.astype(jnp.float32), decayed)
    arriving = sent_and_summed(readings.astype(jnp.bfloat16), CTX, 0)
    local_out, unused_state, sample_running = per_sample(
        sample_vals, sample_inject, sample_read, sample_steps, decay_rate, zero_state
    )
    local_pick = jnp.einsum("sl,slghp->sghp", onehot, local_out)
    running_pick = jnp.einsum("sl,sghl->sgh", onehot, sample_running)
    joined_out = local_pick + arriving * jnp.exp(running_pick)[:, :, :, None]
    picked_vals = jnp.einsum("sl,slc->sc", onehot, sample_values.astype(jnp.float32)).astype(
        jnp.bfloat16
    )
    picked_gate = jnp.einsum("sl,slc->sc", onehot, sample_gate.astype(jnp.float32)).astype(
        jnp.bfloat16
    )
    picked = finish(
        joined_out.reshape(samples, local_heads, HEAD_DIM),
        picked_vals,
        picked_gate,
        skip_gain,
        norm_weight,
        local_groups,
    )
    joined = jnp.concatenate([normed, picked], axis=0)
    combined = lax.psum_scatter(
        projector(out_weight, joined).astype(jnp.bfloat16), "head", scatter_dimension=0, tiled=True
    ).astype(jnp.float32)
    prompt_mixed = combined[:, :tokens].astype(jnp.bfloat16)
    sample_mixed = combined[:, tokens:].astype(jnp.bfloat16)
    return (prompt_mixed, sample_mixed)


def solution(mesh):
    split = Mesh(
        mesh.devices.reshape(4, 4, 2, mesh.shape["head"]), ("ctx_0", "ctx_1", "ctx_2", "head")
    )
    return jax.shard_map(
        per_device,
        mesh=split,
        in_specs=(
            P(CTX, "head"),
            P(CTX, "head"),
            P(CTX, "head", None),
            P(CTX, "head", None),
            P("head", CTX),
            P("head"),
            P("head"),
            P("head"),
            P("head", None),
            P(CTX, None, "head"),
            P(CTX, None, "head"),
            P(CTX, None, "head", None),
            P(CTX, None, "head", None),
            P("head", CTX, None),
            P(CTX),
        ),
        out_specs=(P("head", CTX), P("head", CTX)),
        check_vma=False,
    )
```

profile of v0, /device:TPU:1, one launch (start us, length us, event | category | flops | bytes accessed | tf_op | source)
XLA Modules:
  0.0 371.1 jit_solution(15669944872590820928)
XLA Ops:
  8.8 7.1 %reshape.789 = bf16[4,128,1,32,64]{4,3,1,0,2:T(8,128)(2,1)} reshape(bf16[512,2048]{1,0:T(8,128)(2,1)} %param.17) | data formatting | bytes 4194304 | tf_op jit(solution)/shard_map/reshape | solution.py:173
  15.9 6.5 %copy.38 = bf16[4,128,1,32,64]{1,4,3,2,0:T(8,128)(2,1)} copy(bf16[4,128,1,32,64]{4,3,1,0,2:T(8,128)(2,1)} %reshape.789) | data formatting | bytes 4194304
  22.4 130.6 %while.20 = (s32[]{:T(128)}, f32[1,32,64,256]{3,2,1,0:T(8,128)S(1)}, f32[1,32]{1,0:T(1,128)S(1)}, f32[4,128,1,32,64]{1,0,4,3,2:T(4,128)}, f32[4,1,32,128]{3,2,1,...) while((s32[]{:T(128)}, ...), condition=%wide.region_2.3_spmd.clone, body=%wide.region_0.2_spmd.clone.sunk | while | flops 352383040 | bytes 21958092 | solution.py:188
  28.6 26.4 %dynamic_update_slice.14 = f32[4,128,1,32,64]{1,0,4,3,2:T(4,128)} dynamic-update-slice(f32[4,128,1,32,64]{1,0,4,3,2:T(4,128)} %get-tuple-element.246, f32[1,128,1,32,64]{1,0,4,3,2:T(1,128)S(1)} %bitcast.278, s32[]{:T(128)S(6)} %copy.98, s32[]{:T(128)} %constant.33.clone.1..sunk, s32[]{:T(128)} %constant.33.clone.1..sunk, s32[]{:T(128)} %constant.33.clone.1..sunk, s32[]{:T(128)} %constant.33.clone.1..sunk) | dynamic-update-slice | bytes 2097156 | tf_op jit(solution)/shard_map/while/body/jit(dynamic_update_index_in_dim)/dynamic_update_slice | solution.py:188
  61.2 26.4 %dynamic_update_slice.14 = f32[4,128,1,32,64]{1,0,4,3,2:T(4,128)} dynamic-update-slice(f32[4,128,1,32,64]{1,0,4,3,2:T(4,128)} %get-tuple-element.246, f32[1,128,1,32,64]{1,0,4,3,2:T(1,128)S(1)} %bitcast.278, s32[]{:T(128)S(6)} %copy.98, s32[]{:T(128)} %constant.33.clone.1..sunk, s32[]{:T(128)} %constant.33.clone.1..sunk, s32[]{:T(128)} %constant.33.clone.1..sunk, s32[]{:T(128)} %constant.33.clone.1..sunk) | dynamic-update-slice | bytes 2097156 | tf_op jit(solution)/shard_map/while/body/jit(dynamic_update_index_in_dim)/dynamic_update_slice | solution.py:188
  93.8 26.4 %dynamic_update_slice.14 = f32[4,128,1,32,64]{1,0,4,3,2:T(4,128)} dynamic-update-slice(f32[4,128,1,32,64]{1,0,4,3,2:T(4,128)} %get-tuple-element.246, f32[1,128,1,32,64]{1,0,4,3,2:T(1,128)S(1)} %bitcast.278, s32[]{:T(128)S(6)} %copy.98, s32[]{:T(128)} %constant.33.clone.1..sunk, s32[]{:T(128)} %constant.33.clone.1..sunk, s32[]{:T(128)} %constant.33.clone.1..sunk, s32[]{:T(128)} %constant.33.clone.1..sunk) | dynamic-update-slice | bytes 2097156 | tf_op jit(solution)/shard_map/while/body/jit(dynamic_update_index_in_dim)/dynamic_update_slice | solution.py:188
  126.5 26.4 %dynamic_update_slice.14 = f32[4,128,1,32,64]{1,0,4,3,2:T(4,128)} dynamic-update-slice(f32[4,128,1,32,64]{1,0,4,3,2:T(4,128)} %get-tuple-element.246, f32[1,128,1,32,64]{1,0,4,3,2:T(1,128)S(1)} %bitcast.278, s32[]{:T(128)S(6)} %copy.98, s32[]{:T(128)} %constant.33.clone.1..sunk, s32[]{:T(128)} %constant.33.clone.1..sunk, s32[]{:T(128)} %constant.33.clone.1..sunk, s32[]{:T(128)} %constant.33.clone.1..sunk) | dynamic-update-slice | bytes 2097156 | tf_op jit(solution)/shard_map/while/body/jit(dynamic_update_index_in_dim)/dynamic_update_slice | solution.py:188
  157.1 14.1 %all-gather.11.cloned.1.call-done = bf16[2,32,64,256]{3,2,1,0:T(8,128)(2,1)} async-done(((bf16[1,32,64,256]{3,2,1,0:T(8,128)(2,1)}), bf16[2,32,64,256]{3,2,1,0:T(8,128)(2,1)}) %all-gather.11.cloned.1.call-update) | async-done | bytes 2097168 | tf_op jit(solution)/shard_map/all_gather | solution.py:26
  171.2 3.0 fusion.81
  174.8 7.2 %all-to-all-start = ((f32[32,1,32]{2,1,0:T(1,128)}), f32[32,1,32]{2,1,0:T(1,128)S(1)}, u32[]{:S(2)}, u32[]{:S(2)}) async-start(f32[32,1,32]{2,1,0:T(1,128)} %broadcast_in_dim.131), calls=%async_computation | async-start | bytes 32768 | tf_op jit(solution)/shard_map/all_to_all | solution.py:43
  182.0 7.8 %all_gather.30 = bf16[4,1,32]{2,1,0:T(2,128)(2,1)S(1)} all-gather(bf16[1,1,32]{2,1,0:T(2,128)(2,1)S(1)} %get-tuple-element.161), channel_id=1, replica_groups=mesh['ctx_0'=4,'ctx_1'=4,'ctx_2'=2,'head'=4] {'ctx_1'}, dimensions={0}, use_global_device_ids=true | all-gather | bytes 320 | tf_op jit(solution)/shard_map/all_gather | solution.py:26
  189.8 33.6 %all-gather.7.cloned.1.call-done = bf16[4,1,32,64,256]{4,3,2,1,0:T(8,128)(2,1)} async-done(((bf16[1,1,32,64,256]{4,3,2,1,0:T(8,128)(2,1)}), bf16[4,1,32,64,256]{4,3,2,1,0:T(8,128)(2,1)}) %all-gather.7.cloned.1.call-update) | async-done | bytes 4194320 | tf_op jit(solution)/shard_map/all_gather | solution.py:26
  223.5 4.1 %fusion.80 = bf16[1,1,32,64,256]{4,3,2,1,0:T(8,128)(2,1)} fusion(f32[32]{0:T(128)S(1)} %multiply_bitcast_fusion.1, f32[32]{0:T(128)S(1)} %get-tuple-element.156, f32[32]{0:T(128)S(1)} %get-tuple-element.155, f32[32]{0:T(128)S(1)} %get-tuple-element.159, bf16[4,1,32,64,256]{4,3,2,1,0:T(8,128)(2,1)} %all-gather.7.cloned.1.call-done), kind=kLoop, calls=%fused_computation.98 | loop fusion | flops 6291456 | bytes 5243392 | tf_op jit(solution)/shard_map/convert_element_type | solution.py:26
  228.1 7.6 %all_gather.31 = bf16[4,1,32]{2,1,0:T(2,128)(2,1)S(1)} all-gather(bf16[1,1,32]{2,1,0:T(2,128)(2,1)S(1)} %get-tuple-element.154), channel_id=1, replica_groups=mesh['ctx_0'=4,'ctx_1'=4,'ctx_2'=2,'head'=4] {'ctx_0'}, dimensions={0}, use_global_device_ids=true | all-gather | bytes 320 | tf_op jit(solution)/shard_map/all_gather | solution.py:26
  238.3 6.5 %all-to-all-start.1 = ((bf16[32,2,1,256]{3,1,2,0:T(2,128)(2,1)}), bf16[32,2,1,256]{3,1,2,0:T(2,128)(2,1)S(1)}, u32[]{:S(2)}, u32[]{:S(2)}) async-start(bf16[32,2,1,256]{3,1,2,0:T(2,128)(2,1)} %broadcast_in_dim.133), calls=%async_computation.1 | async-start | bytes 65536 | tf_op jit(solution)/shard_map/all_to_all | solution.py:43
  244.9 7.0 %all-to-all-done.1 = bf16[32,2,1,256]{3,1,2,0:T(2,128)(2,1)S(1)} async-done(((bf16[32,2,1,256]{3,1,2,0:T(2,128)(2,1)}), bf16[32,2,1,256]{3,1,2,0:T(2,128)(2,1)S(1)}, u32[]{:S(2)}, u32[]{:S(2)}) %all-to-all-start.1) | async-done | bytes 32800 | tf_op jit(solution)/shard_map/all_to_all | solution.py:43
  254.4 3.9 %all-to-all-start.2 = ((bf16[32,2,2048]{2,1,0:T(2,128)(2,1)}), bf16[32,2,2048]{2,1,0:T(2,128)(2,1)S(1)}, u32[]{:S(2)}, u32[]{:S(2)}) async-start(bf16[32,2,2048]{2,1,0:T(2,128)(2,1)} %reshape.793), calls=%async_computation.2 | async-start | bytes 524288 | tf_op jit(solution)/shard_map/all_to_all | solution.py:85
  259.1 5.5 %reshape.709 = f32[512,1,32,64]{0,3,2,1:T(8,128)} reshape(f32[4,128,1,32,64]{1,0,4,3,2:T(4,128)} %get-tuple-element.57) | data formatting | bytes 8388608 | tf_op jit(solution)/shard_map/reshape | solution.py:197
  268.3 11.3 %all-gather.9.cloned.1.call-done = bf16[4,1,32,64,256]{4,3,2,1,0:T(8,128)(2,1)} async-done(((bf16[1,1,32,64,256]{4,3,2,1,0:T(8,128)(2,1)}), bf16[4,1,32,64,256]{4,3,2,1,0:T(8,128)(2,1)}) %all-gather.9.cloned.1.call-update) | async-done | bytes 4194320 | tf_op jit(solution)/shard_map/all_gather | solution.py:26
  279.6 8.9 %fusion.45 = f32[512,1,32,64]{0,3,2,1:T(8,128)} fusion(f32[512,1,32,64]{0,3,2,1:T(8,128)} %reshape.709, f32[512,32]{0,1:T(8,128)S(1)} %bitcast.288, bf16[4,1,32,64,256]{4,3,2,1,0:T(8,128)(2,1)} %all-gather.9.cloned.1.call-done, f32[32]{0:T(128)S(1)} %exponential_bitcast_fusion.5, f32[32]{0:T(128)S(1)} %get-tuple-element.162, f32[32]{0:T(128)S(1)} %get-tuple-element.160, ...), kind=kOutput, calls=%fused_computation.59 | convolution fusion | flops 560463872 | bytes 19203594 | tf_op jit(solution)/shard_map/tgn,ghpn->tghp/dot_general | solution.py:194
  288.4 5.6 %copy.41 = f32[512,2048]{1,0:T(8,128)} copy(f32[512,2048]{0,1:T(8,128)} %bitcast.280) | data formatting | bytes 8388608 | tf_op jit(solution)/shard_map/reshape | solution.py:201
  294.0 4.5 %multiply_reduce_fusion = (f32[512]{0:T(512)S(1)}, f32[512,2048]{1,0:T(8,128)S(1)}) fusion(bf16[512,2048]{1,0:T(8,128)(2,1)} %param.18, f32[512,2048]{1,0:T(8,128)} %copy.41, bf16[512,2048]{1,0:T(8,128)(2,1)S(1)} %copy-done.3, f32[2048]{0:T(1024)S(1)} %mul.432), kind=kLoop, calls=%fused_computation.61 | loop fusion | flops 11533824 | bytes 12593152 | tf_op jit(solution)/shard_map/reduce_sum | solution.py:123
  299.0 13.9 %fusion.40 = bf16[4096,514]{0,1:T(8,128)(2,1)} fusion(bf16[2048,4096]{1,0:T(8,128)(2,1)} %param.25, bf16[2,2048]{1,0:T(2,128)(2,1)S(1)} %multiply_convert_fusion.5, bf16[512,2048]{1,0:T(8,128)(2,1)S(1)} %multiply_convert_fusion.4), kind=kOutput, calls=%fused_computation.51 | convolution fusion | flops 8629805056 | bytes 23093248 | tf_op jit(solution)/shard_map/dot_general | solution.py:139
  313.0 48.1 %reduce-scatter.2.cloned.1.call-done = bf16[1024,514]{0,1:T(8,128)(2,1)} async-done(((bf16[4096,514]{0,1:T(8,128)(2,1)}), bf16[1024,514]{0,1:T(8,128)(2,1)}) %reduce-scatter.2.cloned.1.call-update) | async-done | bytes 1052688 | tf_op jit(solution)/shard_map/reduce_scatter | solution.py:245
  (168 shorter events, 44.7 us)
Async XLA Ops:
  7.2 230.1 %copy-start = (bf16[2,16,2048]{2,1,0:T(8,128)(2,1)S(1)}, bf16[2,16,2048]{2,1,0:T(8,128)(2,1)}, u32[]{:S(2)}) copy-start(bf16[2,16,2048]{2,1,0:T(8,128)(2,1)} %param.27) | copy-start | bytes 393220
  7.2 164.0 %all-gather.11.cloned.1.call-start = ((), (), s32[]{:S(2)}) async-start(), calls=%async_computation.7 | async-start | bytes 3145728 | tf_op jit(solution)/shard_map/all_gather | solution.py:26
  22.8 2.6 copy-start.2
  55.4 2.6 copy-start.2
  88.1 2.6 copy-start.2
  120.7 2.6 copy-start.2
  154.1 69.4 %all-gather.7.cloned.1.call-start = ((), (), s32[]{:S(2)}) async-start(), calls=%async_computation.4 | async-start | bytes 5242880 | tf_op jit(solution)/shard_map/all_gather | solution.py:26
  174.8 62.8 %all-to-all-start = ((f32[32,1,32]{2,1,0:T(1,128)}), f32[32,1,32]{2,1,0:T(1,128)S(1)}, u32[]{:S(2)}, u32[]{:S(2)}) async-start(f32[32,1,32]{2,1,0:T(1,128)} %broadcast_in_dim.131), calls=%async_computation | async-start | bytes 32768 | tf_op jit(solution)/shard_map/all_to_all | solution.py:43
  182.0 97.6 %all-gather.9.cloned.1.call-start = ((), (), s32[]{:S(2)}) async-start(), calls=%async_computation.5 | async-start | bytes 5242880 | tf_op jit(solution)/shard_map/all_gather | solution.py:26
  223.5 4.2 %copy-start.8 = (f32[32,2,16]{0,2,1:T(8,128)S(1)}, f32[32,2,16]{0,2,1:T(8,128)}, u32[]{:S(2)}) copy-start(f32[32,2,16]{0,2,1:T(8,128)} %param.30) | copy-start | bytes 12292
  223.5 12.3 %copy-start.7 = (bf16[2,16,1,256]{3,1,2,0:T(8,128)(2,1)S(1)}, bf16[2,16,1,256]{3,1,2,0:T(8,128)(2,1)}, u32[]{:S(2)}) copy-start(bf16[2,16,1,256]{3,1,2,0:T(8,128)(2,1)} %param.29) | copy-start | bytes 49156
  223.5 13.3 %copy-start.12 = (s32[2]{0:T(128)S(1)}, s32[2]{0:T(128)}, u32[]{:S(2)}) copy-start(s32[2]{0:T(128)} %param.31) | copy-start | bytes 28
  223.5 13.7 %copy-start.10 = (bf16[2,16,1,256]{3,1,2,0:T(8,128)(2,1)S(1)}, bf16[2,16,1,256]{3,1,2,0:T(8,128)(2,1)}, u32[]{:S(2)}) copy-start(bf16[2,16,1,256]{3,1,2,0:T(8,128)(2,1)} %param.28) | copy-start | bytes 49156
  227.6 9.8 %copy-start.6 = (bf16[2,16,2048]{2,1,0:T(8,128)(2,1)S(1)}, bf16[2,16,2048]{2,1,0:T(8,128)(2,1)}, u32[]{:S(2)}) copy-start(bf16[2,16,2048]{2,1,0:T(8,128)(2,1)} %param.26) | copy-start | bytes 393220
  238.3 13.7 %all-to-all-start.1 = ((bf16[32,2,1,256]{3,1,2,0:T(2,128)(2,1)}), bf16[32,2,1,256]{3,1,2,0:T(2,128)(2,1)S(1)}, u32[]{:S(2)}, u32[]{:S(2)}) async-start(bf16[32,2,1,256]{3,1,2,0:T(2,128)(2,1)} %broadcast_in_dim.133), calls=%async_computation.1 | async-start | bytes 65536 | tf_op jit(solution)/shard_map/all_to_all | solution.py:43
  252.0 6.9 %copy-start.11 = (f32[32]{0:T(128)S(1)}, f32[32]{0:T(128)}, u32[]{:S(2)}) copy-start(f32[32]{0:T(128)} %param.23) | copy-start | bytes 388
  254.4 13.0 %all-to-all-start.2 = ((bf16[32,2,2048]{2,1,0:T(2,128)(2,1)}), bf16[32,2,2048]{2,1,0:T(2,128)(2,1)S(1)}, u32[]{:S(2)}, u32[]{:S(2)}) async-start(bf16[32,2,2048]{2,1,0:T(2,128)(2,1)} %reshape.793), calls=%async_computation.2 | async-start | bytes 524288 | tf_op jit(solution)/shard_map/all_to_all | solution.py:85
  258.3 102.8 %reduce-scatter.2.cloned.1.call-start = ((), (), s32[]{:S(2)}) async-start(), calls=%async_computation.6 | async-start | bytes 5324800 | tf_op jit(solution)/shard_map/reduce_scatter | solution.py:245
  264.5 3.6 copy-start.9
  264.5 15.0 %copy-start.5 = (bf16[2,32,64,256]{3,2,1,0:T(8,128)(2,1)S(1)}, bf16[2,32,64,256]{3,2,1,0:T(8,128)(2,1)}, u32[]{:S(2)}) copy-start(bf16[2,32,64,256]{3,2,1,0:T(8,128)(2,1)} %all-gather.11.cloned.1.call-done) | copy-start | bytes 6291460
  288.4 5.6 %copy-start.3 = (bf16[512,2048]{1,0:T(8,128)(2,1)S(1)}, bf16[512,2048]{1,0:T(8,128)(2,1)}, u32[]{:S(2)}) copy-start(bf16[512,2048]{1,0:T(8,128)(2,1)} %param.17) | copy-start | bytes 6291460
  313.0 51.6 %copy-start.1 = (bf16[2,16,2048]{2,1,0:T(8,128)(2,1)S(1)}, bf16[2,16,2048]{2,1,0:T(8,128)(2,1)}, u32[]{:S(2)}) copy-start(bf16[2,16,2048]{2,1,0:T(8,128)(2,1)} %param.27) | copy-start | bytes 393220
  361.1 1.5 slice-start
  361.1 2.9 copy-start.4
Sparse Core Ops, SparseCore 0:
  154.2 16.9 all-gather.10
  174.3 49.1 all-gather.6
  227.8 51.7 all-gather.8
  313.1 47.9 reduce-scatter.1
where the time goes:
time: 375 us; the launch traced here: 371 us
  local copies, waits for them, and re-layouts  139 us (37%)
  waiting for transfers between devices  115 us (31%)
  matrix products  44.7 us (12%)
  other arithmetic  21.5 us (6%)
  blocking collectives  18.3 us (5%)
  starting transfers between devices  17.9 us (5%)
  between operations  14.1 us (4%)
    dynamic_update_slice x4, local copies, waits for them, and re-layouts, per_device(): lax.scan(advance, (zero_state, zero_log), (values, inject, readout, steps))  106 us
    all_gather x3, waiting for transfers between devices, prefix_by_axis(): lax.all_gather(part.astype(kind), axis)  59.1 us
    reduce_scatter x1, waiting for transfers between devices, per_device(): lax.psum_scatter(projector(out_weight, joined).astype(jnp.bfloat16), 'hea...  48.1 us
    all_gather x3, blocking collectives, prefix_by_axis(): lax.all_gather(part.astype(kind), axis)  18.3 us
    dot_general x1, matrix products, projector(): lax.dot_general(out_weight.astype(jnp.float32), row_matrix.astype(jnp.flo...  13.9 us
    all_to_all x2, starting transfers between devices, copy_for_each(): return lax.all_to_all(copies, axis, split_axis=0, concat_axis=0, tiled=True)  13.6 us
    unnamed x29, local copies, waits for them, and re-layouts  9.34 us
    dot_general x1, matrix products, per_device(): jnp.einsum('tgn,ghpn->tghp', prompt_read.astype(jnp.float32), incoming_st...  8.86 us
  transfers between devices with their start and end apart: 7, of which 6 were waited for; matrix products, arithmetic and copies ran while one was open for 5% of the time, Pallas kernels for 0%

commit v1 on v0

v1 whole, which is shorter than its diff:
```python
import jax
import jax.numpy as jnp
from jax import lax
from jax.experimental import pallas as pl
from jax.experimental.pallas import tpu as pltpu
from jax.sharding import Mesh
from jax.sharding import PartitionSpec as P

HEADS = 32
HEAD_DIM = 64
STATE = 256
BLOCK = 128
SLEN = 16
TOK = 512
CH = HEADS * HEAD_DIM
COLS = 4096
PIECE = 512
ROWS = 144
CTX = ("y", "x", "core")
F32 = jnp.float32
BF16 = jnp.bfloat16
EXACT = lax.Precision.HIGHEST
CHUNK = 256
MB = 1 << 20


def softplus(v):
    return jnp.maximum(v, 0.0) + jnp.log1p(jnp.exp(-jnp.abs(v)))


def iota(shape, dim):
    return lax.broadcasted_iota(jnp.int32, shape, dim)


def column(row):
    n = row.shape[1]
    square = jnp.broadcast_to(row, (n, n))
    return jnp.sum(jnp.where(iota((n, n), 0) == iota((n, n), 1), square, 0.0), axis=1, keepdims=True)


def tokens_first(x):
    pad = jnp.zeros((128 - x.shape[0], x.shape[1]), F32)
    return jnp.transpose(jnp.concatenate([x, pad], axis=0))


def per_pair(columns, pair, shape, low):
    first = jnp.broadcast_to(columns[:, 2 * pair : 2 * pair + 1], shape)
    second = jnp.broadcast_to(columns[:, 2 * pair + 1 : 2 * pair + 2], shape)
    return jnp.where(low, first, second)


def three_parts(x):
    hi = x.astype(BF16).astype(F32)
    mid = (x - hi).astype(BF16).astype(F32)
    lo = (x - hi - mid).astype(BF16).astype(F32)
    return hi, mid, lo


def decay_of(tail):
    return tail[8:9] + tail[9:10] + tail[10:11]


def with_decay(tail, decay):
    row = iota((16, 128), 0)
    hi, mid, lo = three_parts(decay)
    tail = jnp.where(row == 8, hi, tail)
    tail = jnp.where(row == 9, mid, tail)
    return jnp.where(row == 10, lo, tail)


def end_state_kernel(meta, step_ref, decay_ref, values_ref, inject_ref, read_ref, keep_ref, send_ref, scaled):
    core = meta[0]
    step = softplus(step_ref[...])
    logs = step * -jnp.exp(column(decay_ref[...]))
    later = (iota((BLOCK, BLOCK), 0) > iota((BLOCK, BLOCK), 1)).astype(F32)
    after = jnp.zeros((HEADS, 1), F32)
    parts = []
    for b in reversed(range(TOK // BLOCK)):
        here = logs[:, b * BLOCK : (b + 1) * BLOCK]
        parts.append(jnp.dot(here, later, precision=EXACT, preferred_element_type=F32) + after)
        after = after + jnp.sum(here, axis=1, keepdims=True)
    weight = tokens_first(jnp.exp(jnp.concatenate(parts[::-1], axis=1)) * step)
    total = tokens_first(jnp.broadcast_to(jnp.exp(after), (HEADS, 128)))[0:8]
    inject_t = jnp.transpose(inject_ref[...].astype(F32)).astype(BF16)
    low = iota((TOK, 128), 1) < HEAD_DIM
    low_row = iota((8, 128), 1) < HEAD_DIM
    row = iota((16, 128), 0)
    tails = []
    for half in range(2):
        lanes = slice(half * 128, (half + 1) * 128)
        tail = jnp.zeros((16, 128), F32)
        for s in range(2):
            last = iota((SLEN, 128), 0) == meta[1 + s] - 1
            picked = jnp.sum(jnp.where(last, read_ref[s, :, lanes].astype(F32), 0.0), axis=0, keepdims=True)
            tail = jnp.where(row == 2 * core + s, picked, tail)
        tails.append(tail)
    for half in range(2):
        for q in range(8):
            pair = half * 8 + q
            lanes = slice(pair * 128, (pair + 1) * 128)
            w = per_pair(weight, pair, (TOK, 128), low)
            scaled[:, q * 128 : (q + 1) * 128] = (values_ref[:, lanes].astype(F32) * w).astype(BF16)
        state = jnp.dot(inject_t, scaled[...], preferred_element_type=F32).astype(BF16)

        def put(out_ref, half=half, state=state):
            for q in range(8):
                decay = per_pair(total, half * 8 + q, (8, 128), low_row)[0:1]
                for n in range(2):
                    out_ref[2 * q + n, 0:128, :] = state[n * 128 : (n + 1) * 128, q * 128 : (q + 1) * 128]
                    out_ref[2 * q + n, 128:ROWS, :] = with_decay(tails[n], decay).astype(BF16)

        @pl.when(core == half)
        def _(put=put):
            put(keep_ref)

        @pl.when(core != half)
        def _(put=put):
            put(send_ref)


def join_cores_kernel(meta, own_ref, sib_ref, out_ref):
    first = meta[0] == 0
    row = iota((16, 128), 0)
    for k in range(16):
        own_tail = own_ref[k, 128:ROWS, :].astype(F32)
        sib_tail = sib_ref[k, 128:ROWS, :].astype(F32)
        own_decay, sib_decay = decay_of(own_tail), decay_of(sib_tail)
        own_weight = jnp.where(first, sib_decay, 1.0)
        sib_weight = jnp.where(first, 1.0, own_decay)
        out_ref[k, 0:128, :] = (
            own_ref[k, 0:128, :].astype(F32) * own_weight + sib_ref[k, 0:128, :].astype(F32) * sib_weight
        ).astype(BF16)
        tail = jnp.where(row < 8, own_tail + sib_tail, 0.0)
        out_ref[k, 128:ROWS, :] = with_decay(tail, own_decay * sib_decay).astype(BF16)


def prefix_kernel(in_ref, out_ref):
    state = jnp.zeros((128, 128), F32)
    for i in range(16):
        out_ref[i, 0:128, :] = state.astype(BF16)
        decay = decay_of(in_ref[i, 128:ROWS, :].astype(F32))
        state = state * decay + in_ref[i, 0:128, :].astype(F32)
    final = state.astype(BF16)
    for i in range(16):
        out_ref[i, 128:ROWS, :] = jnp.dot(
            in_ref[i, 128:ROWS, :], final, preferred_element_type=F32
        ).astype(BF16)


def split_cores_kernel(meta, back_ref, own_ref, sib_ref, mine_ref, send_ref):
    first = meta[0] == 0
    for k in range(16):
        q, n = k // 2, k % 2
        arrived = back_ref[k, 0:128, :].astype(F32)
        own_decay = decay_of(own_ref[k, 128:ROWS, :].astype(F32))
        sib_decay = decay_of(sib_ref[k, 128:ROWS, :].astype(F32))
        decay = jnp.where(first, own_decay, sib_decay)
        state = jnp.where(first, own_ref[k, 0:128, :].astype(F32), sib_ref[k, 0:128, :].astype(F32))
        second = arrived * decay + state
        mine_ref[n * 128 : (n + 1) * 128, q * 128 : (q + 1) * 128] = jnp.where(first, arrived, second).astype(BF16)
        send_ref[k, 0:128, :] = jnp.where(first, second, arrived).astype(BF16)
        send_ref[k, 128:ROWS, :] = back_ref[k, 128:ROWS, :]
    for q in range(8):
        mine_ref[256:272, q * 128 : (q + 1) * 128] = (
            back_ref[2 * q, 128:ROWS, :].astype(F32) + back_ref[2 * q + 1, 128:ROWS, :].astype(F32)
        ).astype(BF16)


def local_kernel(
    step_ref, decay_ref, skip_ref, values_ref, gate_ref, inject_ref, read_ref,
    scaled_ref, gain_ref, state, before, ends, weighted, carried,
):
    first = pl.program_id(0) == 0

    @pl.when(first)
    def _():
        state[...] = jnp.zeros_like(state)
        before[...] = jnp.ones_like(before)

    step = softplus(step_ref[...])
    logs = step * -jnp.exp(column(decay_ref[...]))
    upto = (iota((BLOCK, BLOCK), 0) <= iota((BLOCK, BLOCK), 1)).astype(F32)
    running = jnp.dot(logs, upto, precision=EXACT, preferred_element_type=F32)
    running_t = tokens_first(running)
    step_t = tokens_first(step)
    read = read_ref[...]
    inject = inject_ref[...]
    inject_t = jnp.transpose(inject.astype(F32)).astype(BF16)
    scores = jnp.dot(read, inject_t, preferred_element_type=F32)
    carried[...] = jnp.dot(read, state[...].astype(BF16), preferred_element_type=F32)
    causal = iota((BLOCK, BLOCK), 0) >= iota((BLOCK, BLOCK), 1)
    low = iota((BLOCK, 128), 1) < HEAD_DIM
    for pair in range(16):
        lanes = slice(pair * 128, (pair + 1) * 128)
        mixing = []
        spread = []
        for h in (2 * pair, 2 * pair + 1):
            mine = jnp.broadcast_to(running_t[:, h : h + 1], (BLOCK, BLOCK))
            gap = jnp.where(causal, mine - running[h : h + 1, :], -1e30)
            mixing.append((scores * jnp.exp(gap)).astype(BF16))
            spread.append(mine)
        now = jnp.where(low, spread[0], spread[1])
        grown = jnp.exp(now)
        values = values_ref[:, lanes].astype(F32)
        stepped = values * per_pair(step_t, pair, (BLOCK, 128), low)
        diagonal = jnp.concatenate([jnp.where(low, stepped, 0.0), jnp.where(low, 0.0, stepped)], axis=0)
        local = jnp.dot(
            jnp.concatenate(mixing, axis=1), diagonal.astype(BF16), preferred_element_type=F32
        )
        out = local + carried[:, lanes] * grown + skip_ref[:, lanes] * values
        gate = gate_ref[:, lanes].astype(F32)
        gate = gate / (1.0 + jnp.exp(-gate))
        scaled_ref[:, lanes] = (out * gate).astype(BF16)
        gain_ref[:, lanes] = (gate * grown * before[0:1, lanes]).astype(BF16)
        end = now[BLOCK - 1 : BLOCK, :]
        weighted[:, lanes] = (stepped * jnp.exp(end - now)).astype(BF16)
        ends[0:1, lanes] = jnp.exp(end)
    state[...] = state[...] * ends[0:1, :] + jnp.dot(inject_t, weighted[...], preferred_element_type=F32)
    before[0:1, :] = before[0:1, :] * ends[0:1, :]


def sample_kernel(
    meta, step_ref, decay_ref, skip_ref, values_ref, gate_ref, inject_ref, read_ref, local_ref, grown_ref, gate_out_ref
):
    rate = -jnp.exp(column(decay_ref[...]))
    row = iota((16, CH), 0)
    spread = (iota((128, CH), 1) // HEAD_DIM == iota((128, CH), 0)).astype(F32)
    local_all = jnp.zeros((16, CH), F32)
    grown_all = jnp.zeros((16, CH), F32)
    gate_all = jnp.zeros((16, CH), F32)
    for s in range(2):
        last = meta[1 + s] - 1
        step = softplus(step_ref[s])
        logs = step * rate
        pad = jnp.zeros((HEADS, 128 - SLEN), F32)
        step_t = tokens_first(jnp.concatenate([step, pad], axis=1))[0:SLEN]
        logs_t = tokens_first(jnp.concatenate([logs, pad], axis=1))[0:SLEN]
        place = iota((SLEN, 128), 0)
        logs_t = jnp.where(place <= last, logs_t, 0.0)
        gap = jnp.zeros((SLEN, 128), F32)
        for k in range(SLEN):
            gap = gap + jnp.where(place < k, logs_t[k : k + 1], 0.0)
        whole = jnp.sum(logs_t, axis=0, keepdims=True)
        place_wide = iota((SLEN, STATE), 0)
        read = jnp.sum(jnp.where(place_wide == last, read_ref[s].astype(F32), 0.0), axis=0, keepdims=True)
        scores = jnp.sum(inject_ref[s].astype(F32) * read, axis=1, keepdims=True)
        weight = jnp.where(place <= last, scores * jnp.exp(gap) * step_t, 0.0)
        both = jnp.concatenate([weight, jnp.broadcast_to(jnp.exp(whole), (8, 128))], axis=0)
        wide = jnp.dot(both, spread, precision=EXACT, preferred_element_type=F32)
        values = values_ref[s].astype(F32)
        at_last = iota((SLEN, CH), 0) == last
        picked = jnp.sum(jnp.where(at_last, values, 0.0), axis=0, keepdims=True)
        gate = jnp.sum(jnp.where(at_last, gate_ref[s].astype(F32), 0.0), axis=0, keepdims=True)
        local = jnp.sum(wide[0:SLEN] * values, axis=0, keepdims=True) + skip_ref[...] * picked
        local_all = jnp.where(row == s, local, local_all)
        grown_all = jnp.where(row == s, wide[SLEN : SLEN + 1], grown_all)
        gate_all = jnp.where(row == s, gate / (1.0 + jnp.exp(-gate)), gate_all)
    local_ref[...] = local_all
    grown_ref[...] = grown_all
    gate_out_ref[...] = gate_all


def normalize(gated, weight):
    mean = jnp.sum(gated * gated, axis=1, keepdims=True) * (1.0 / CH)
    return (gated * lax.rsqrt(mean + 1e-05) * weight).astype(BF16)


def project(j, normed, weight_ref, first_ref, second_ref):
    out = jnp.dot(normed, weight_ref[...], preferred_element_type=F32).astype(BF16)

    @pl.when(j < 2)
    def _():
        first_ref[0] = out

    @pl.when(j >= 2)
    def _():
        second_ref[0] = out


def chunk_one_kernel(
    meta, mine_ref, theirs_ref, read_ref, scaled_ref, gain_ref, norm_ref, weight_ref,
    first_ref, second_ref, normed_ref, state_ref,
):
    j = pl.program_id(0)

    @pl.when(j == 0)
    def _():
        core = meta[0]
        own = pl.multiple_of(core * 1024, 1024)
        state_ref[:, pl.ds(own, 1024)] = mine_ref[...]
        for q in range(8):
            at = pl.multiple_of((1 - core) * 1024 + q * 128, 128)
            for n in range(2):
                state_ref[n * 128 : (n + 1) * 128, pl.ds(at, 128)] = theirs_ref[2 * q + n, 0:128, :]
            state_ref[256:272, pl.ds(at, 128)] = (
                theirs_ref[2 * q, 128:ROWS, :].astype(F32) + theirs_ref[2 * q + 1, 128:ROWS, :].astype(F32)
            ).astype(BF16)
        arrived = jnp.dot(read_ref[...], state_ref[0:256, :], preferred_element_type=F32)
        gated = scaled_ref[...].astype(F32) + arrived * gain_ref[...].astype(F32)
        normed_ref[...] = normalize(gated, norm_ref[...])

    project(j, normed_ref[...], weight_ref, first_ref, second_ref)


def chunk_two_kernel(
    meta, state_ref, read_ref, scaled_ref, gain_ref, norm_ref, local_ref, grown_ref, gate_ref, weight_ref,
    first_ref, second_ref, normed_ref,
):
    j = pl.program_id(0)

    @pl.when(j == 0)
    def _():
        arrived = jnp.dot(read_ref[...], state_ref[0:256, :], preferred_element_type=F32)
        gated = scaled_ref[...].astype(F32) + arrived * gain_ref[...].astype(F32)
        normed_ref[0:CHUNK, :] = normalize(gated, norm_ref[...])
        readings = state_ref[256:272, :].astype(F32)
        moved = jnp.concatenate([readings[2:16], readings[0:2]], axis=0)
        readings = jnp.where(meta[0] == 0, readings, moved)
        sampled = (local_ref[...] + readings * grown_ref[...]) * gate_ref[...]
        normed_ref[CHUNK : CHUNK + 16, :] = normalize(sampled, norm_ref[...])

    project(j, normed_ref[...], weight_ref, first_ref, second_ref)


def rest_kernel(meta, normed_ref, weight_ref, out_ref):
    out_ref[0] = jnp.dot(normed_ref[...], weight_ref[...], preferred_element_type=F32).astype(BF16)


def finish_kernel(*refs):
    ins, out_ref, sample_ref = refs[:-2], refs[-2], refs[-1]
    for c in range(2):
        rest, ra, rb, sa, sb = ins[5 * c : 5 * c + 5]
        for half, (own, near, far) in enumerate(((0, ra, sa), (2, rb, sb))):
            total = rest[own].astype(F32) + near[0].astype(F32) + far[...].astype(F32)
            rows = slice(half * PIECE, (half + 1) * PIECE)
            out_ref[rows, c * CHUNK : (c + 1) * CHUNK] = jnp.transpose(total[0:CHUNK]).astype(BF16)
            if c == 1:
                extra = jnp.concatenate([total[CHUNK : CHUNK + 16], jnp.zeros((112, PIECE), F32)], axis=0)
                sample_ref[rows, :] = jnp.transpose(extra)[:, 0:2].astype(BF16)


def params(limit=56):
    return pltpu.CompilerParams(vmem_limit_bytes=limit * MB)


SMEM = pl.BlockSpec(memory_space=pltpu.SMEM)
VMEM = pl.BlockSpec(memory_space=pltpu.VMEM)


def shape(dims, dtype=BF16):
    return jax.ShapeDtypeStruct(dims, dtype)


def swap(x, step):
    return lax.ppermute(x, "head", [(i, i ^ step) for i in range(4)])


def per_device(
    prompt_values, prompt_gate, prompt_inject, prompt_read, prompt_step, decay_log, skip_gain, norm_weight, out_weight,
    sample_values, sample_gate, sample_inject, sample_read, sample_step, sample_length,
):
    core = lax.axis_index("core")
    z = lax.axis_index("head")
    flip = [(z ^ k) * 2 for k in range(4)]
    order = [flip[1], flip[2], flip[3] + 1, flip[2] + 1, flip[0], flip[3], flip[0] + 1, flip[1] + 1]
    meta = jnp.concatenate([core[None], sample_length, jnp.stack(order)]).astype(jnp.int32)
    inject = prompt_inject.reshape(TOK, STATE)
    read = prompt_read.reshape(TOK, STATE)
    decay = decay_log.reshape(1, HEADS)
    skip = jnp.repeat(skip_gain, HEAD_DIM).reshape(1, CH)
    norm = norm_weight.reshape(1, CH)
    s_read = sample_read.reshape(2, SLEN, STATE)
    s_inject = sample_inject.reshape(2, SLEN, STATE)

    keep, send = pl.pallas_call(
        end_state_kernel,
        out_shape=(shape((16, ROWS, 128)),) * 2,
        in_specs=[SMEM] + [VMEM] * 5,
        out_specs=(VMEM, VMEM),
        scratch_shapes=[pltpu.VMEM((TOK, 1024), BF16)],
        compiler_params=params(),
        name="end_state",
    )(meta, prompt_step, decay, prompt_values, inject, s_read)
    sibling = lax.ppermute(send, "core", [(0, 1), (1, 0)])
    joined = pl.pallas_call(
        join_cores_kernel,
        out_shape=shape((16, ROWS, 128)),
        in_specs=[SMEM, VMEM, VMEM],
        out_specs=VMEM,
        compiler_params=params(16),
        name="join_cores",
    )(meta, keep, sibling)
    joined, step_b = lax.optimization_barrier((joined, prompt_step))
    slices = lax.all_to_all(joined, ("y", "x"), 0, 0, tiled=True)

    row = lambda width: pl.BlockSpec((1, width), lambda b: (0, 0))
    tokens = lambda width: pl.BlockSpec((BLOCK, width), lambda b: (b, 0))
    scaled, gain = pl.pallas_call(
        local_kernel,
        grid=(TOK // BLOCK,),
        out_shape=(shape((TOK, CH)),) * 2,
        in_specs=[
            pl.BlockSpec((HEADS, BLOCK), lambda b: (0, b)), row(HEADS), row(CH),
            tokens(CH), tokens(CH), tokens(STATE), tokens(STATE),
        ],
        out_specs=(tokens(CH), tokens(CH)),
        scratch_shapes=[
            pltpu.VMEM((STATE, CH), F32), pltpu.VMEM((8, CH), F32), pltpu.VMEM((8, CH), F32),
            pltpu.VMEM((BLOCK, CH), BF16), pltpu.VMEM((BLOCK, CH), F32),
        ],
        compiler_params=params(),
        name="local_outputs",
    )(step_b, decay, skip, prompt_values, prompt_gate, inject, read)
    s_local, s_grown, s_gate = pl.pallas_call(
        sample_kernel,
        out_shape=(shape((16, CH), F32),) * 3,
        in_specs=[SMEM] + [VMEM] * 7,
        out_specs=(VMEM,) * 3,
        compiler_params=params(16),
        name="sample_outputs",
    )(meta, sample_step.transpose(1, 0, 2), decay, skip, sample_values, sample_gate, s_inject, s_read)

    prefix = pl.pallas_call(
        prefix_kernel,
        out_shape=shape((16, ROWS, 128)),
        in_specs=[VMEM],
        out_specs=VMEM,
        compiler_params=params(16),
        name="prefix",
    )(slices)
    back = lax.all_to_all(prefix, ("y", "x"), 0, 0, tiled=True)
    mine, send = pl.pallas_call(
        split_cores_kernel,
        out_shape=(shape((272, 1024)), shape((16, ROWS, 128))),
        in_specs=[SMEM] + [VMEM] * 3,
        out_specs=(VMEM, VMEM),
        compiler_params=params(16),
        name="split_cores",
    )(meta, back, keep, sibling)
    theirs = lax.ppermute(send, "core", [(0, 1), (1, 0)])

    def whole(*dims):
        return pl.BlockSpec(dims, lambda j, m: (0,) * len(dims))

    def chunk(width, c):
        return pl.BlockSpec((CHUNK, width), lambda j, m: (c, 0))

    def weight(base):
        return pl.BlockSpec((CH, PIECE), lambda j, m: (0, m[3 + base + j]))

    def sent(rows):
        return (
            pl.BlockSpec((1, rows, PIECE), lambda j, m: (jnp.minimum(j, 1), 0, 0)),
            pl.BlockSpec((1, rows, PIECE), lambda j, m: (jnp.maximum(j - 2, 0), 0, 0)),
        )

    first_1, second_1, normed_1, state = pl.pallas_call(
        chunk_one_kernel,
        grid_spec=pltpu.PrefetchScalarGridSpec(
            num_scalar_prefetch=1,
            grid=(4,),
            in_specs=[
                whole(272, 1024), whole(16, ROWS, 128), chunk(STATE, 0), chunk(CH, 0), chunk(CH, 0), whole(1, CH), weight(0),
            ],
            out_specs=(*sent(CHUNK), whole(CHUNK, CH), whole(272, CH)),
        ),
        out_shape=(
            shape((2, CHUNK, PIECE)), shape((2, CHUNK, PIECE)), shape((CHUNK, CH)), shape((272, CH)),
        ),
        compiler_params=params(),
        name="chunk_one",
    )(meta, mine, theirs, read, scaled, gain, norm, out_weight)
    near_1 = lax.optimization_barrier((swap(first_1, 1), swap(second_1, 3)))

    def rest(normed, name):
        rows = normed.shape[0]
        return pl.pallas_call(
            rest_kernel,
            grid_spec=pltpu.PrefetchScalarGridSpec(
                num_scalar_prefetch=1,
                grid=(4,),
                in_specs=[whole(rows, CH), weight(4)],
                out_specs=pl.BlockSpec((1, rows, PIECE), lambda j, m: (j, 0, 0)),
            ),
            out_shape=shape((4, rows, PIECE)),
            compiler_params=params(),
            name=name,
        )(meta, normed, out_weight)

    rows = CHUNK + 16
    first_2, second_2, normed_2 = pl.pallas_call(
        chunk_two_kernel,
        grid_spec=pltpu.PrefetchScalarGridSpec(
            num_scalar_prefetch=1,
            grid=(4,),
            in_specs=[
                whole(272, CH), chunk(STATE, 1), chunk(CH, 1), chunk(CH, 1), whole(1, CH),
                whole(16, CH), whole(16, CH), whole(16, CH), weight(0),
            ],
            out_specs=(*sent(rows), whole(rows, CH)),
        ),
        out_shape=(shape((2, rows, PIECE)), shape((2, rows, PIECE)), shape((rows, CH))),
        compiler_params=params(),
        name="chunk_two",
    )(meta, state, read, scaled, gain, norm, s_local, s_grown, s_gate, out_weight)
    near_2 = lax.optimization_barrier((swap(first_2, 1), swap(second_2, 3)))
    rest_1 = rest(normed_1, "rest_one")
    rest_2 = rest(normed_2, "rest_two")

    def onward(rest, near):
        a = (rest[1].astype(F32) + near[0][1].astype(F32)).astype(BF16)
        b = (rest[3].astype(F32) + near[1][1].astype(F32)).astype(BF16)
        a, b = lax.optimization_barrier((a, b))
        return lax.optimization_barrier((swap(a, 3), swap(b, 1)))

    far_1 = onward(rest_1, near_1)
    far_2 = onward(rest_2, near_2)
    return pl.pallas_call(
        finish_kernel,
        out_shape=(shape((1024, TOK)), shape((1024, 2))),
        in_specs=[VMEM] * 10,
        out_specs=(VMEM, VMEM),
        compiler_params=params(),
        name="finish",
    )(rest_1, *near_1, *far_1, rest_2, *near_2, *far_2)


def solution(mesh):
    split = Mesh(mesh.devices.reshape(4, 4, 2, mesh.shape["head"]), ("y", "x", "core", "head"))
    return jax.shard_map(
        per_device,
        mesh=split,
        in_specs=(
            P(CTX, "head"), P(CTX, "head"), P(CTX, "head", None), P(CTX, "head", None), P("head", CTX),
            P("head"), P("head"), P("head"), P("head", None),
            P(CTX, None, "head"), P(CTX, None, "head"), P(CTX, None, "head", None), P(CTX, None, "head", None),
            P("head", CTX, None), P(CTX),
        ),
        out_specs=(P("head", CTX), P("head", CTX)),
        check_vma=False,
    )
```

time: 375 us -> 139 us (0.37)
  local copies, waits for them, and re-layouts: 139 us -> 9.29 us
  waiting for transfers between devices: 115 us -> 19.7 us
  Pallas kernels: 0 us -> 60.5 us
  matrix products: 44.7 us -> 0 us
  other arithmetic: 21.5 us -> 1.31 us
  blocking collectives: 18.3 us -> 32 us
  between operations: 14.1 us -> 0.88 us
  starting transfers between devices: 17.9 us -> 13.6 us
    dynamic_update_slice x4 -> x0, local copies, waits for them, and re-layouts: 106 us -> none  [per_device(): lax.scan(advance, (zero_state, zero_log), (values, inject, readout, steps))]
    pallas_call x0 -> x11, Pallas kernels: none -> 60.5 us  [the longest x2 14.8 us: rest(): pl.pallas_call(rest_kernel, grid_spec=pltpu.PrefetchScalarGridSpec(num_sc...]
    all_gather x3 -> x0, waiting for transfers between devices: 59.1 us -> none  [prefix_by_axis(): lax.all_gather(part.astype(kind), axis)]
    reduce_scatter x1 -> x0, waiting for transfers between devices: 48.1 us -> none  [per_device(): lax.psum_scatter(projector(out_weight, joined).astype(jnp.bfloat16), 'hea...]
    dot_general x26 -> x0, matrix products: 44.7 us -> none  [the longest x1 13.9 us: projector(): lax.dot_general(out_weight.astype(jnp.float32), row_matrix.astype(jnp.flo...]
    all_to_all x0 -> x2, blocking collectives: none -> 32 us  [the longest x1 18.2 us: per_device(): slices = lax.all_to_all(joined, ('y', 'x'), 0, 0, tiled=True)]
    ppermute x0 -> x10, waiting for transfers between devices: none -> 19.7 us  [the longest x8 17.8 us: swap(): return lax.ppermute(x, 'head', [(i, i ^ step) for i in range(4)])]
    all_gather x3 -> x0, blocking collectives: 18.3 us -> none  [prefix_by_axis(): lax.all_gather(part.astype(kind), axis)]
  transfers between devices with their start and end apart: 7 -> 10, of which waited for: 6 -> 5; matrix products, arithmetic and copies ran while one was open for 5% -> 1% of each run, Pallas kernels for 0% -> 20%
where the time goes in v1:
time: 139 us; the launch traced here: 137 us
  Pallas kernels  60.5 us (44%)
  blocking collectives  32 us (23%)
  waiting for transfers between devices  19.7 us (14%)
  starting transfers between devices  13.6 us (10%)
  local copies, waits for them, and re-layouts  9.29 us (7%)
    all_to_all x1, blocking collectives, per_device(): slices = lax.all_to_all(joined, ('y', 'x'), 0, 0, tiled=True)  18.2 us
    ppermute x8, waiting for transfers between devices, swap(): return lax.ppermute(x, 'head', [(i, i ^ step) for i in range(4)])  17.8 us
    pallas_call x2, Pallas kernels, rest(): pl.pallas_call(rest_kernel, grid_spec=pltpu.PrefetchScalarGridSpec(num_sc...  14.8 us
    all_to_all x1, blocking collectives, per_device(): back = lax.all_to_all(prefix, ('y', 'x'), 0, 0, tiled=True)  13.8 us
    pallas_call x1, Pallas kernels, per_device(): pl.pallas_call(local_kernel, grid=(TOK // BLOCK,), out_shape=(shape((TOK,...  11.9 us
    pallas_call x1, Pallas kernels, per_device(): pl.pallas_call(chunk_one_kernel, grid_spec=pltpu.PrefetchScalarGridSpec(n...  9.89 us
    pallas_call x1, Pallas kernels, per_device(): pl.pallas_call(chunk_two_kernel, grid_spec=pltpu.PrefetchScalarGridSpec(n...  9.72 us
    ppermute x8, starting transfers between devices, swap(): return lax.ppermute(x, 'head', [(i, i ^ step) for i in range(4)])  9.46 us
  transfers between devices with their start and end apart: 10, of which 5 were waited for; matrix products, arithmetic and copies ran while one was open for 1% of the time, Pallas kernels for 20%

profile of v1, /device:TPU:1, one launch (start us, length us, event | category | flops | bytes accessed | tf_op | source)
XLA Modules:
  0.0 137.2 jit_solution(6676660067394579920)
XLA Ops:
  0.6 1.2 concatenate.3.meta
  1.9 6.7 %end_state.1 = (bf16[16,144,128]{2,1,0:T(8,128)(2,1)}, bf16[16,144,128]{2,1,0:T(8,128)(2,1)}) custom-call(s32[11]{0:T(128)} %concatenate.3.meta, f32[32,512]{1,0:T(8,128)} %step_ref.2, f32[1,32]{1,0:T(1,128)} %bitcast.28, bf16[512,2048]{1,0:T(8,128)(2,1)} %values_ref.4, bf16[512,256]{1,0:T(8,128)(2,1)} %bitcast.34, bf16[2,16,256]{2,1,0:T(8,128)(2,1)} %bitcast.25), custom_call_target="tpu_custom_call" | custom-call | tf_op jit(solution)/shard_map/end_state/pallas_call | solution.py:375
  8.6 1.4 %collective-permute-start = (bf16[16,144,128]{2,1,0:T(8,128)(2,1)}, bf16[16,144,128]{2,1,0:T(8,128)(2,1)S(1)}, u32[]{:S(2)}, u32[]{:S(2)}) collective-permute-start(bf16[16,144,128]{2,1,0:T(8,128)(2,1)} %get-tuple-element.33), channel_id=1, source_target_pairs={{0,4},{4,0},{1,5},{5,1},{2,6},{6,2},{3,7},{7,3},{8,12},{12,8},{9,1... | collective-permute-start | bytes 1769480 | tf_op jit(solution)/shard_map/ppermute | solution.py:384
  10.0 1.8 %collective-permute-done.sib_ref = bf16[16,144,128]{2,1,0:T(8,128)(2,1)S(1)} collective-permute-done((bf16[16,144,128]{2,1,0:T(8,128)(2,1)}, bf16[16,144,128]{2,1,0:T(8,128)(2,1)S(1)}, u32[]{:S(2)}, u32[]{:S(2)}) %collective-permute-start) | collective-permute-done | bytes 589856 | tf_op jit(solution)/shard_map/ppermute | solution.py:384
  11.9 1.1 copy-done
  13.7 18.2 %all_to_all.10.in_ref = bf16[16,144,128]{2,1,0:T(8,128)(2,1)S(1)} all-to-all(bf16[16,144,128]{2,1,0:T(8,128)(2,1)S(1)} %join_cores.1), channel_id=1, replica_groups=mesh['y'=4,'x'=4,'core'=2,'head'=4] {'y','x'}, dimensions={0} | all-to-all | bytes 1179648 | tf_op jit(solution)/shard_map/all_to_all | solution.py:394
  32.3 13.8 %all_to_all.11.back_ref = bf16[16,144,128]{2,1,0:T(8,128)(2,1)S(1)} all-to-all(bf16[16,144,128]{2,1,0:T(8,128)(2,1)S(1)} %prefix.1), channel_id=1, replica_groups=mesh['y'=4,'x'=4,'core'=2,'head'=4] {'y','x'}, dimensions={0} | all-to-all | bytes 1179648 | tf_op jit(solution)/shard_map/all_to_all | solution.py:431
  47.8 2.7 %collective-permute-start.1 = (bf16[16,144,128]{2,1,0:T(8,128)(2,1)S(1)}, bf16[16,144,128]{2,1,0:T(8,128)(2,1)S(1)}, u32[]{:S(2)}, u32[]{:S(2)}) collective-permute-start(bf16[16,144,128]{2,1,0:T(8,128)(2,1)S(1)} %get-tuple-element.36), channel_id=1, source_target_pairs={{0,4},{4,0},{1,5},{5,1},{2,6},{6,2},{3,7},{7,3},{8,12},{12,8},{9,1... | collective-permute-start | bytes 1769480 | tf_op jit(solution)/shard_map/ppermute | solution.py:440
  50.8 1.3 sample_outputs.1
  54.1 11.9 %local_outputs.1 = (bf16[512,2048]{1,0:T(8,128)(2,1)}, bf16[512,2048]{1,0:T(8,128)(2,1)}) custom-call(f32[32,512]{1,0:T(8,128)} %step_ref.2, f32[1,32]{1,0:T(1,128)} %bitcast.29, f32[1,2048]{1,0:T(1,128)} %copy-done.8, bf16[512,2048]{1,0:T(8,128)(2,1)} %values_ref.4, bf16[512,2048]{1,0:T(8,128)(2,1)} %gate_ref.2, bf16[512,256]{1,0:T(8,128)(2,1)} %bitcast.35, ...), custom_call_target="tpu_custom_call" | custom-call | tf_op jit(solution)/shard_map/local_outputs/pallas_call | solution.py:398
  66.8 9.9 %chunk_one.1 = (bf16[2,256,512]{2,1,0:T(8,128)(2,1)}, bf16[2,256,512]{2,1,0:T(8,128)(2,1)}, bf16[256,2048]{1,0:T(8,128)(2,1)}, bf16[272,2048]{1,0:T(8,128)(2,1)}) custom-call(s32[11]{0:T(128)} %concatenate.3.meta, bf16[272,1024]{1,0:T(8,128)(2,1)} %copy-done.2, bf16[16,144,128]{2,1,0:T(8,128)(2,1)} %copy-done.18, bf16[512,256]{1,0:T(8,128)(2,1)} %bitcast.32, ...), custom_call_target="tpu_custom_call" | custom-call | tf_op jit(solution)/shard_map/chunk_one/pallas_call | solution.py:457
  76.7 9.7 %chunk_two.1 = (bf16[2,272,512]{2,1,0:T(8,128)(2,1)}, bf16[2,272,512]{2,1,0:T(8,128)(2,1)}, bf16[272,2048]{1,0:T(8,128)(2,1)}) custom-call(s32[11]{0:T(128)} %concatenate.3.meta, bf16[272,2048]{1,0:T(8,128)(2,1)} %get-tuple-element.49.state_ref, bf16[512,256]{1,0:T(8,128)(2,1)} %bitcast.33, bf16[512,2048]{1,0:T(8,128)(2,1)} %get-tuple-element.38.scaled_ref, ...), custom_call_target="tpu_custom_call" | custom-call | tf_op jit(solution)/shard_map/chunk_two/pallas_call | solution.py:491
  86.4 1.9 %collective-permute-start.6 = (bf16[2,272,512]{2,1,0:T(8,128)(2,1)}, bf16[2,272,512]{2,1,0:T(8,128)(2,1)S(1)}, u32[]{:S(2)}, u32[]{:S(2)}) collective-permute-start(bf16[2,272,512]{2,1,0:T(8,128)(2,1)} %get-tuple-element.54), channel_id=1, source_target_pairs={{0,1},{1,0},{2,3},{3,2},{4,5},{5,4},{6,7},{7,6},{8,9},{9,8},{10,11... | collective-permute-start | bytes 1671176 | tf_op jit(solution)/shard_map/ppermute | solution.py:355
  88.3 2.2 %collective-permute-start.7 = (bf16[2,272,512]{2,1,0:T(8,128)(2,1)}, bf16[2,272,512]{2,1,0:T(8,128)(2,1)S(1)}, u32[]{:S(2)}, u32[]{:S(2)}) collective-permute-start(bf16[2,272,512]{2,1,0:T(8,128)(2,1)} %get-tuple-element.55), channel_id=1, source_target_pairs={{0,3},{1,2},{2,1},{3,0},{4,7},{5,6},{6,5},{7,4},{8,11},{9,10},{10,... | collective-permute-start | bytes 1671176 | tf_op jit(solution)/shard_map/ppermute | solution.py:355
  91.9 7.4 %rest_two.1.refs_5_ = bf16[4,272,512]{2,1,0:T(8,128)(2,1)} custom-call(s32[11]{0:T(128)} %concatenate.3.meta, bf16[272,2048]{1,0:T(8,128)(2,1)} %get-tuple-element.53.normed_ref, bf16[2048,4096]{1,0:T(8,128)(2,1)} %weight_ref.7), custom_call_target="tpu_custom_call" | custom-call | tf_op jit(solution)/shard_map/rest_two/pallas_call | solution.py:477
  99.3 7.4 %rest_one.1.refs_0_ = bf16[4,256,512]{2,1,0:T(8,128)(2,1)} custom-call(s32[11]{0:T(128)} %concatenate.3.meta, bf16[256,2048]{1,0:T(8,128)(2,1)} %get-tuple-element.40.normed_ref, bf16[2048,4096]{1,0:T(8,128)(2,1)} %weight_ref.7), custom_call_target="tpu_custom_call" | custom-call | tf_op jit(solution)/shard_map/rest_one/pallas_call | solution.py:477
  106.7 5.9 %collective-permute-done.2.refs_1_ = bf16[2,256,512]{2,1,0:T(8,128)(2,1)S(1)} collective-permute-done((bf16[2,256,512]{2,1,0:T(8,128)(2,1)S(1)}, bf16[2,256,512]{2,1,0:T(8,128)(2,1)S(1)}, u32[]{:S(2)}, u32[]{:S(2)}) %collective-permute-start.2) | collective-permute-done | bytes 524320 | tf_op jit(solution)/shard_map/ppermute | solution.py:355
  112.7 2.3 %collective-permute-done.3.refs_2_ = bf16[2,256,512]{2,1,0:T(8,128)(2,1)S(1)} collective-permute-done((bf16[2,256,512]{2,1,0:T(8,128)(2,1)S(1)}, bf16[2,256,512]{2,1,0:T(8,128)(2,1)S(1)}, u32[]{:S(2)}, u32[]{:S(2)}) %collective-permute-start.3) | collective-permute-done | bytes 524320 | tf_op jit(solution)/shard_map/ppermute | solution.py:355
  115.1 2.3 %collective-permute-start.8 = (bf16[272,512]{1,0:T(8,128)(2,1)S(1)}, bf16[272,512]{1,0:T(8,128)(2,1)S(1)}, u32[]{:S(2)}, u32[]{:S(2)}) collective-permute-start(bf16[272,512]{1,0:T(8,128)(2,1)S(1)} %get-tuple-element.58), channel_id=1, source_target_pairs={{0,3},{1,2},{2,1},{3,0},{4,7},{5,6},{6,5},{7,4},{8,11},{9,10},{10,... | collective-permute-start | bytes 835592 | tf_op jit(solution)/shard_map/ppermute | solution.py:355
  117.5 1.2 fusion.3
  119.2 1.1 collective-permute-start.5
  120.3 8.8 %collective-permute-done.4.refs_3_ = bf16[256,512]{1,0:T(8,128)(2,1)S(1)} collective-permute-done((bf16[256,512]{1,0:T(8,128)(2,1)S(1)}, bf16[256,512]{1,0:T(8,128)(2,1)S(1)}, u32[]{:S(2)}, u32[]{:S(2)}) %collective-permute-start.4) | collective-permute-done | bytes 262176 | tf_op jit(solution)/shard_map/ppermute | solution.py:355
  131.4 4.1 %finish.1 = (bf16[1024,512]{1,0:T(8,128)(2,1)}, bf16[1024,2]{1,0:T(8,128)(2,1)}) custom-call(bf16[4,256,512]{2,1,0:T(8,128)(2,1)} %rest_one.1.refs_0_, bf16[2,256,512]{2,1,0:T(8,128)(2,1)} %copy-done.16, bf16[2,256,512]{2,1,0:T(8,128)(2,1)} %copy-done.17, bf16[256,512]{1,0:T(8,128)(2,1)} %copy-done.21, bf16[256,512]{1,0:T(8,128)(2,1)} %copy-done.22, ...), custom_call_target="tpu_custom_call" | custom-call | tf_op jit(solution)/shard_map/finish/pallas_call | solution.py:518
  135.5 1.7 %copy.18 = bf16[1024,2]{0,1:T(2,128)(2,1)} copy(bf16[1024,2]{1,0:T(8,128)(2,1)} %get-tuple-element.63) | data formatting | bytes 8192 | tf_op jit(solution)/shard_map/finish/pallas_call | solution.py:518
  (70 shorter events, 10.2 us)
Async XLA Ops:
  8.6 3.3 %collective-permute-start = (bf16[16,144,128]{2,1,0:T(8,128)(2,1)}, bf16[16,144,128]{2,1,0:T(8,128)(2,1)S(1)}, u32[]{:S(2)}, u32[]{:S(2)}) collective-permute-start(bf16[16,144,128]{2,1,0:T(8,128)(2,1)} %get-tuple-element.33), channel_id=1, source_target_pairs={{0,4},{4,0},{1,5},{5,1},{2,6},{6,2},{3,7},{7,3},{8,12},{12,8},{9,1... | collective-permute-start | bytes 1769480 | tf_op jit(solution)/shard_map/ppermute | solution.py:384
  13.7 32.4 %copy-start.1 = (bf16[16,144,128]{2,1,0:T(8,128)(2,1)S(1)}, bf16[16,144,128]{2,1,0:T(8,128)(2,1)}, u32[]{:S(2)}) copy-start(bf16[16,144,128]{2,1,0:T(8,128)(2,1)} %get-tuple-element.32.own_ref) | copy-start | bytes 1769476
  31.9 18.6 %copy-start.24 = (f32[32]{0:T(128)S(1)}, f32[32]{0:T(128)}, u32[]{:S(2)}) copy-start(f32[32]{0:T(128)} %param.21) | copy-start | bytes 388
  31.9 18.8 %copy-start.23 = (f32[32,2,16]{0,2,1:T(8,128)S(1)}, f32[32,2,16]{0,2,1:T(8,128)}, u32[]{:S(2)}) copy-start(f32[32,2,16]{0,2,1:T(8,128)} %param.28) | copy-start | bytes 12292
  31.9 18.9 %copy-start.6 = (bf16[2,16,2048]{2,1,0:T(8,128)(2,1)S(1)}, bf16[2,16,2048]{2,1,0:T(8,128)(2,1)}, u32[]{:S(2)}) copy-start(bf16[2,16,2048]{2,1,0:T(8,128)(2,1)} %values_ref.5) | copy-start | bytes 393220
  31.9 18.9 %copy-start.7 = (bf16[2,16,2048]{2,1,0:T(8,128)(2,1)S(1)}, bf16[2,16,2048]{2,1,0:T(8,128)(2,1)}, u32[]{:S(2)}) copy-start(bf16[2,16,2048]{2,1,0:T(8,128)(2,1)} %gate_ref.3) | copy-start | bytes 393220
  31.9 18.9 %copy-start.9 = (bf16[2,16,1,256]{3,1,2,0:T(8,128)(2,1)S(1)}, bf16[2,16,1,256]{3,1,2,0:T(8,128)(2,1)}, u32[]{:S(2)}) copy-start(bf16[2,16,1,256]{3,1,2,0:T(8,128)(2,1)} %param.27) | copy-start | bytes 49156
  32.0 18.9 %copy-start.11 = (bf16[2,16,1,256]{3,1,2,0:T(8,128)(2,1)S(1)}, bf16[2,16,1,256]{3,1,2,0:T(8,128)(2,1)}, u32[]{:S(2)}) copy-start(bf16[2,16,1,256]{3,1,2,0:T(8,128)(2,1)} %param.26) | copy-start | bytes 49156
  32.0 18.9 %copy-start.12 = (f32[32]{0:T(128)S(1)}, f32[32]{0:T(128)}, u32[]{:S(2)}) copy-start(f32[32]{0:T(128)} %param.20) | copy-start | bytes 388
  47.8 18.1 %collective-permute-start.1 = (bf16[16,144,128]{2,1,0:T(8,128)(2,1)S(1)}, bf16[16,144,128]{2,1,0:T(8,128)(2,1)S(1)}, u32[]{:S(2)}, u32[]{:S(2)}) collective-permute-start(bf16[16,144,128]{2,1,0:T(8,128)(2,1)S(1)} %get-tuple-element.36), channel_id=1, source_target_pairs={{0,4},{4,0},{1,5},{5,1},{2,6},{6,2},{3,7},{7,3},{8,12},{12,8},{9,1... | collective-permute-start | bytes 1769480 | tf_op jit(solution)/shard_map/ppermute | solution.py:440
  76.7 14.6 %copy-start.25 = (bf16[2,256,512]{2,1,0:T(8,128)(2,1)S(1)}, bf16[2,256,512]{2,1,0:T(8,128)(2,1)}, u32[]{:S(2)}) copy-start(bf16[2,256,512]{2,1,0:T(8,128)(2,1)} %get-tuple-element.42) | copy-start | bytes 1572868
  86.4 28.5 %collective-permute-start.6 = (bf16[2,272,512]{2,1,0:T(8,128)(2,1)}, bf16[2,272,512]{2,1,0:T(8,128)(2,1)S(1)}, u32[]{:S(2)}, u32[]{:S(2)}) collective-permute-start(bf16[2,272,512]{2,1,0:T(8,128)(2,1)} %get-tuple-element.54), channel_id=1, source_target_pairs={{0,1},{1,0},{2,3},{3,2},{4,5},{5,4},{6,7},{7,6},{8,9},{9,8},{10,11... | collective-permute-start | bytes 1671176 | tf_op jit(solution)/shard_map/ppermute | solution.py:355
  88.3 26.6 %collective-permute-start.7 = (bf16[2,272,512]{2,1,0:T(8,128)(2,1)}, bf16[2,272,512]{2,1,0:T(8,128)(2,1)S(1)}, u32[]{:S(2)}, u32[]{:S(2)}) collective-permute-start(bf16[2,272,512]{2,1,0:T(8,128)(2,1)} %get-tuple-element.55), channel_id=1, source_target_pairs={{0,3},{1,2},{2,1},{3,0},{4,7},{5,6},{6,5},{7,4},{8,11},{9,10},{10,... | collective-permute-start | bytes 1671176 | tf_op jit(solution)/shard_map/ppermute | solution.py:355
  90.6 22.1 %collective-permute-start.2 = (bf16[2,256,512]{2,1,0:T(8,128)(2,1)S(1)}, bf16[2,256,512]{2,1,0:T(8,128)(2,1)S(1)}, u32[]{:S(2)}, u32[]{:S(2)}) collective-permute-start(bf16[2,256,512]{2,1,0:T(8,128)(2,1)S(1)} %copy-done.26), channel_id=1, source_target_pairs={{0,1},{1,0},{2,3},{3,2},{4,5},{5,4},{6,7},{7,6},{8,9},{9,8},{10,11... | collective-permute-start | bytes 1572872 | tf_op jit(solution)/shard_map/ppermute | solution.py:355
  91.3 23.6 %collective-permute-start.3 = (bf16[2,256,512]{2,1,0:T(8,128)(2,1)S(1)}, bf16[2,256,512]{2,1,0:T(8,128)(2,1)S(1)}, u32[]{:S(2)}, u32[]{:S(2)}) collective-permute-start(bf16[2,256,512]{2,1,0:T(8,128)(2,1)S(1)} %copy-done.25), channel_id=1, source_target_pairs={{0,3},{1,2},{2,1},{3,0},{4,7},{5,6},{6,5},{7,4},{8,11},{9,10},{10,... | collective-permute-start | bytes 1572872 | tf_op jit(solution)/shard_map/ppermute | solution.py:355
  99.3 15.6 %copy-start.13 = (bf16[4,272,512]{2,1,0:T(8,128)(2,1)S(1)}, bf16[4,272,512]{2,1,0:T(8,128)(2,1)}, u32[]{:S(2)}) copy-start(bf16[4,272,512]{2,1,0:T(8,128)(2,1)} %rest_two.1.refs_5_) | copy-start | bytes 3342340
  112.7 17.2 %copy-start.16 = (bf16[2,256,512]{2,1,0:T(8,128)(2,1)}, bf16[2,256,512]{2,1,0:T(8,128)(2,1)S(1)}, u32[]{:S(2)}) copy-start(bf16[2,256,512]{2,1,0:T(8,128)(2,1)S(1)} %collective-permute-done.2.refs_1_) | copy-start | bytes 1572868
  115.0 14.9 %copy-start.17 = (bf16[2,256,512]{2,1,0:T(8,128)(2,1)}, bf16[2,256,512]{2,1,0:T(8,128)(2,1)S(1)}, u32[]{:S(2)}) copy-start(bf16[2,256,512]{2,1,0:T(8,128)(2,1)S(1)} %collective-permute-done.3.refs_2_) | copy-start | bytes 1572868
  115.0 14.9 %copy-start.14 = (bf16[2,272,512]{2,1,0:T(8,128)(2,1)}, bf16[2,272,512]{2,1,0:T(8,128)(2,1)S(1)}, u32[]{:S(2)}) copy-start(bf16[2,272,512]{2,1,0:T(8,128)(2,1)S(1)} %collective-permute-done.6.refs_6_) | copy-start | bytes 1671172
  115.0 14.9 %copy-start.15 = (bf16[2,272,512]{2,1,0:T(8,128)(2,1)}, bf16[2,272,512]{2,1,0:T(8,128)(2,1)S(1)}, u32[]{:S(2)}) copy-start(bf16[2,272,512]{2,1,0:T(8,128)(2,1)S(1)} %collective-permute-done.7.refs_7_) | copy-start | bytes 1671172
  115.1 14.7 %collective-permute-start.8 = (bf16[272,512]{1,0:T(8,128)(2,1)S(1)}, bf16[272,512]{1,0:T(8,128)(2,1)S(1)}, u32[]{:S(2)}, u32[]{:S(2)}) collective-permute-start(bf16[272,512]{1,0:T(8,128)(2,1)S(1)} %get-tuple-element.58), channel_id=1, source_target_pairs={{0,3},{1,2},{2,1},{3,0},{4,7},{5,6},{6,5},{7,4},{8,11},{9,10},{10,... | collective-permute-start | bytes 835592 | tf_op jit(solution)/shard_map/ppermute | solution.py:355
  117.5 12.4 %collective-permute-start.9 = (bf16[272,512]{1,0:T(8,128)(2,1)S(1)}, bf16[272,512]{1,0:T(8,128)(2,1)S(1)}, u32[]{:S(2)}, u32[]{:S(2)}) collective-permute-start(bf16[272,512]{1,0:T(8,128)(2,1)S(1)} %get-tuple-element.59), channel_id=1, source_target_pairs={{0,1},{1,0},{2,3},{3,2},{4,5},{5,4},{6,7},{7,6},{8,9},{9,8},{10,11... | collective-permute-start | bytes 835592 | tf_op jit(solution)/shard_map/ppermute | solution.py:355
  118.6 10.5 %collective-permute-start.4 = (bf16[256,512]{1,0:T(8,128)(2,1)S(1)}, bf16[256,512]{1,0:T(8,128)(2,1)S(1)}, u32[]{:S(2)}, u32[]{:S(2)}) collective-permute-start(bf16[256,512]{1,0:T(8,128)(2,1)S(1)} %get-tuple-element.45), channel_id=1, source_target_pairs={{0,3},{1,2},{2,1},{3,0},{4,7},{5,6},{6,5},{7,4},{8,11},{9,10},{10,... | collective-permute-start | bytes 786440 | tf_op jit(solution)/shard_map/ppermute | solution.py:355
  119.2 10.7 %collective-permute-start.5 = (bf16[256,512]{1,0:T(8,128)(2,1)S(1)}, bf16[256,512]{1,0:T(8,128)(2,1)S(1)}, u32[]{:S(2)}, u32[]{:S(2)}) collective-permute-start(bf16[256,512]{1,0:T(8,128)(2,1)S(1)} %get-tuple-element.46), channel_id=1, source_target_pairs={{0,1},{1,0},{2,3},{3,2},{4,5},{5,4},{6,7},{7,6},{8,9},{9,8},{10,11... | collective-permute-start | bytes 786440 | tf_op jit(solution)/shard_map/ppermute | solution.py:355
  (13 other events, 34.9 us)

commit v2 on v1

v2 whole, which is shorter than its diff:
```python
import functools

import jax
import jax.numpy as jnp
from jax import lax
from jax.experimental import pallas as pl
from jax.experimental.pallas import tpu as pltpu
from jax.sharding import Mesh
from jax.sharding import PartitionSpec as P

HEADS = 32
HEAD_DIM = 64
STATE = 256
BLOCK = 128
SLEN = 16
TOK = 512
CH = HEADS * HEAD_DIM
PIECE = 512
ROWS = 144
CTX = ("y", "x", "core")
F32 = jnp.float32
BF16 = jnp.bfloat16
EXACT = lax.Precision.HIGHEST
CHUNKS = (256, 256)


def softplus(v):
    return jnp.maximum(v, 0.0) + jnp.log1p(jnp.exp(-jnp.abs(v)))


def iota(shape, dim):
    return lax.broadcasted_iota(jnp.int32, shape, dim)


def column(row):
    n = row.shape[1]
    square = jnp.broadcast_to(row, (n, n))
    return jnp.sum(jnp.where(iota((n, n), 0) == iota((n, n), 1), square, 0.0), axis=1, keepdims=True)


def tokens_first(x):
    pad = jnp.zeros((128 - x.shape[0], x.shape[1]), F32)
    return jnp.transpose(jnp.concatenate([x, pad], axis=0))


def per_pair(columns, pair, shape, low):
    first = jnp.broadcast_to(columns[:, 2 * pair : 2 * pair + 1], shape)
    second = jnp.broadcast_to(columns[:, 2 * pair + 1 : 2 * pair + 2], shape)
    return jnp.where(low, first, second)


def three_parts(x):
    hi = x.astype(BF16).astype(F32)
    mid = (x - hi).astype(BF16).astype(F32)
    lo = (x - hi - mid).astype(BF16).astype(F32)
    return hi, mid, lo


def decay_of(tail):
    return tail[8:9] + tail[9:10] + tail[10:11]


def with_decay(tail, decay):
    row = iota((16, 128), 0)
    hi, mid, lo = three_parts(decay)
    tail = jnp.where(row == 8, hi, tail)
    tail = jnp.where(row == 9, mid, tail)
    return jnp.where(row == 10, lo, tail)


def end_state_kernel(length, step_ref, decay_ref, values_ref, inject_ref, read_ref, keep_ref, send_ref, scaled):
    core = lax.axis_index("core")
    step = softplus(step_ref[...])
    logs = step * -jnp.exp(column(decay_ref[...]))
    later = (iota((BLOCK, BLOCK), 0) > iota((BLOCK, BLOCK), 1)).astype(F32)
    after = jnp.zeros((HEADS, 1), F32)
    parts = []
    for b in reversed(range(TOK // BLOCK)):
        here = logs[:, b * BLOCK : (b + 1) * BLOCK]
        parts.append(jnp.dot(here, later, precision=EXACT, preferred_element_type=F32) + after)
        after = after + jnp.sum(here, axis=1, keepdims=True)
    weight = tokens_first(jnp.exp(jnp.concatenate(parts[::-1], axis=1)) * step)
    total = tokens_first(jnp.broadcast_to(jnp.exp(after), (HEADS, 128)))[0:8]
    inject_t = jnp.transpose(inject_ref[...].astype(F32)).astype(BF16)
    low = iota((TOK, 128), 1) < HEAD_DIM
    low_row = iota((8, 128), 1) < HEAD_DIM
    row = iota((16, 128), 0)
    tails = []
    for half in range(2):
        lanes = slice(half * 128, (half + 1) * 128)
        tail = jnp.zeros((16, 128), F32)
        for s in range(2):
            last = iota((SLEN, 128), 0) == length[s] - 1
            picked = jnp.sum(jnp.where(last, read_ref[s, :, lanes].astype(F32), 0.0), axis=0, keepdims=True)
            tail = jnp.where(row == 2 * core + s, picked, tail)
        tails.append(tail)
    for half in range(2):
        for q in range(8):
            pair = half * 8 + q
            lanes = slice(pair * 128, (pair + 1) * 128)
            w = per_pair(weight, pair, (TOK, 128), low)
            scaled[:, q * 128 : (q + 1) * 128] = (values_ref[:, lanes].astype(F32) * w).astype(BF16)
        state = jnp.dot(inject_t, scaled[...], preferred_element_type=F32).astype(BF16)

        def put(out_ref, half=half, state=state):
            for q in range(8):
                decay = per_pair(total, half * 8 + q, (8, 128), low_row)[0:1]
                for n in range(2):
                    out_ref[2 * q + n, 0:128, :] = state[n * 128 : (n + 1) * 128, q * 128 : (q + 1) * 128]
                    out_ref[2 * q + n, 128:ROWS, :] = with_decay(tails[n], decay).astype(BF16)

        @pl.when(core == half)
        def _(put=put):
            put(keep_ref)

        @pl.when(core != half)
        def _(put=put):
            put(send_ref)


def join_cores_kernel(own_ref, sib_ref, out_ref):
    first = lax.axis_index("core") == 0
    row = iota((16, 128), 0)
    for k in range(16):
        own_tail = own_ref[k, 128:ROWS, :].astype(F32)
        sib_tail = sib_ref[k, 128:ROWS, :].astype(F32)
        own_decay, sib_decay = decay_of(own_tail), decay_of(sib_tail)
        own_weight = jnp.where(first, sib_decay, 1.0)
        sib_weight = jnp.where(first, 1.0, own_decay)
        out_ref[k, 0:128, :] = (
            own_ref[k, 0:128, :].astype(F32) * own_weight + sib_ref[k, 0:128, :].astype(F32) * sib_weight
        ).astype(BF16)
        tail = jnp.where(row < 8, own_tail + sib_tail, 0.0)
        out_ref[k, 128:ROWS, :] = with_decay(tail, own_decay * sib_decay).astype(BF16)


def prefix_kernel(in_ref, out_ref):
    state = jnp.zeros((128, 128), F32)
    for i in range(16):
        out_ref[i, 0:128, :] = state.astype(BF16)
        decay = decay_of(in_ref[i, 128:ROWS, :].astype(F32))
        state = state * decay + in_ref[i, 0:128, :].astype(F32)
    final = state.astype(BF16)
    for i in range(16):
        out_ref[i, 128:ROWS, :] = jnp.dot(
            in_ref[i, 128:ROWS, :], final, preferred_element_type=F32
        ).astype(BF16)


def split_cores_kernel(back_ref, own_ref, sib_ref, mine_ref, send_ref):
    first = lax.axis_index("core") == 0
    for k in range(16):
        q, n = k // 2, k % 2
        arrived = back_ref[k, 0:128, :].astype(F32)
        own_decay = decay_of(own_ref[k, 128:ROWS, :].astype(F32))
        sib_decay = decay_of(sib_ref[k, 128:ROWS, :].astype(F32))
        decay = jnp.where(first, own_decay, sib_decay)
        state = jnp.where(first, own_ref[k, 0:128, :].astype(F32), sib_ref[k, 0:128, :].astype(F32))
        second = arrived * decay + state
        mine_ref[n * 128 : (n + 1) * 128, q * 128 : (q + 1) * 128] = jnp.where(first, arrived, second).astype(BF16)
        send_ref[k, 0:128, :] = jnp.where(first, second, arrived).astype(BF16)
        send_ref[k, 128:ROWS, :] = back_ref[k, 128:ROWS, :]
    for q in range(8):
        mine_ref[256:272, q * 128 : (q + 1) * 128] = (
            back_ref[2 * q, 128:ROWS, :].astype(F32) + back_ref[2 * q + 1, 128:ROWS, :].astype(F32)
        ).astype(BF16)


def local_kernel(
    step_ref, decay_ref, skip_ref, values_ref, gate_ref, inject_ref, read_ref, *refs
):
    if len(refs) == 7:
        scaled_ref, gain_ref, state, before, ends, weighted, carried = refs
    else:
        start, start_before, scaled_ref, gain_ref, ends, weighted, carried, state, before = refs

    @pl.when(pl.program_id(0) == 0)
    def _():
        if len(refs) == 7:
            state[...] = jnp.zeros_like(state)
            before[...] = jnp.ones_like(before)
        else:
            state[...] = start[...]
            before[...] = start_before[...]

    step = softplus(step_ref[...])
    logs = step * -jnp.exp(column(decay_ref[...]))
    upto = (iota((BLOCK, BLOCK), 0) <= iota((BLOCK, BLOCK), 1)).astype(F32)
    running = jnp.dot(logs, upto, precision=EXACT, preferred_element_type=F32)
    running_t = tokens_first(running)
    step_t = tokens_first(step)
    read = read_ref[...]
    inject = inject_ref[...]
    inject_t = jnp.transpose(inject.astype(F32)).astype(BF16)
    scores = jnp.dot(read, inject_t, preferred_element_type=F32)
    carried[...] = jnp.dot(read, state[...].astype(BF16), preferred_element_type=F32)
    causal = iota((BLOCK, BLOCK), 0) >= iota((BLOCK, BLOCK), 1)
    low = iota((BLOCK, 128), 1) < HEAD_DIM
    for pair in range(16):
        lanes = slice(pair * 128, (pair + 1) * 128)
        mixing = []
        spread = []
        for h in (2 * pair, 2 * pair + 1):
            mine = jnp.broadcast_to(running_t[:, h : h + 1], (BLOCK, BLOCK))
            gap = jnp.where(causal, mine - running[h : h + 1, :], -1e30)
            mixing.append((scores * jnp.exp(gap)).astype(BF16))
            spread.append(mine)
        now = jnp.where(low, spread[0], spread[1])
        grown = jnp.exp(now)
        values = values_ref[:, lanes].astype(F32)
        stepped = values * per_pair(step_t, pair, (BLOCK, 128), low)
        diagonal = jnp.concatenate([jnp.where(low, stepped, 0.0), jnp.where(low, 0.0, stepped)], axis=0)
        local = jnp.dot(
            jnp.concatenate(mixing, axis=1), diagonal.astype(BF16), preferred_element_type=F32
        )
        out = local + carried[:, lanes] * grown + skip_ref[:, lanes] * values
        gate = gate_ref[:, lanes].astype(F32)
        gate = gate / (1.0 + jnp.exp(-gate))
        scaled_ref[:, lanes] = (out * gate).astype(BF16)
        gain_ref[:, lanes] = (gate * grown * before[0:1, lanes]).astype(BF16)
        end = now[BLOCK - 1 : BLOCK, :]
        weighted[:, lanes] = (stepped * jnp.exp(end - now)).astype(BF16)
        ends[0:1, lanes] = jnp.exp(end)
    state[...] = state[...] * ends[0:1, :] + jnp.dot(inject_t, weighted[...], preferred_element_type=F32)
    before[0:1, :] = before[0:1, :] * ends[0:1, :]


def sample_kernel(
    length, step_ref, decay_ref, skip_ref, values_ref, gate_ref, inject_ref, read_ref, local_ref, grown_ref, gate_out_ref
):
    rate = -jnp.exp(column(decay_ref[...]))
    row = iota((16, CH), 0)
    spread = (iota((128, CH), 1) // HEAD_DIM == iota((128, CH), 0)).astype(F32)
    local_all = jnp.zeros((16, CH), F32)
    grown_all = jnp.zeros((16, CH), F32)
    gate_all = jnp.zeros((16, CH), F32)
    for s in range(2):
        last = length[s] - 1
        step = softplus(step_ref[s])
        logs = step * rate
        pad = jnp.zeros((HEADS, 128 - SLEN), F32)
        step_t = tokens_first(jnp.concatenate([step, pad], axis=1))[0:SLEN]
        logs_t = tokens_first(jnp.concatenate([logs, pad], axis=1))[0:SLEN]
        place = iota((SLEN, 128), 0)
        logs_t = jnp.where(place <= last, logs_t, 0.0)
        gap = jnp.zeros((SLEN, 128), F32)
        for k in range(SLEN):
            gap = gap + jnp.where(place < k, logs_t[k : k + 1], 0.0)
        whole = jnp.sum(logs_t, axis=0, keepdims=True)
        place_wide = iota((SLEN, STATE), 0)
        read = jnp.sum(jnp.where(place_wide == last, read_ref[s].astype(F32), 0.0), axis=0, keepdims=True)
        scores = jnp.sum(inject_ref[s].astype(F32) * read, axis=1, keepdims=True)
        weight = jnp.where(place <= last, scores * jnp.exp(gap) * step_t, 0.0)
        both = jnp.concatenate([weight, jnp.broadcast_to(jnp.exp(whole), (8, 128))], axis=0)
        wide = jnp.dot(both, spread, precision=EXACT, preferred_element_type=F32)
        values = values_ref[s].astype(F32)
        at_last = iota((SLEN, CH), 0) == last
        picked = jnp.sum(jnp.where(at_last, values, 0.0), axis=0, keepdims=True)
        gate = jnp.sum(jnp.where(at_last, gate_ref[s].astype(F32), 0.0), axis=0, keepdims=True)
        local = jnp.sum(wide[0:SLEN] * values, axis=0, keepdims=True) + skip_ref[...] * picked
        local_all = jnp.where(row == s, local, local_all)
        grown_all = jnp.where(row == s, wide[SLEN : SLEN + 1], grown_all)
        gate_all = jnp.where(row == s, gate / (1.0 + jnp.exp(-gate)), gate_all)
    local_ref[...] = local_all
    grown_ref[...] = grown_all
    gate_out_ref[...] = gate_all


def normalize(gated, weight):
    mean = jnp.sum(gated * gated, axis=1, keepdims=True) * (1.0 / CH)
    return (gated * lax.rsqrt(mean + 1e-05) * weight).astype(BF16)


FIRST = ((1, 0), (2, 0), (3, 1), (2, 1))
REST = ((3, 0), (1, 1), (0, 0), (0, 1))


class Columns:
    def __init__(self, pieces, weight_ref, held, sems, base=0):
        z = lax.axis_index("head")
        self.held, self.base, self.copies = held, base, []
        for i, (flip, half) in enumerate(pieces):
            at = pl.multiple_of(((z ^ flip) * 2 + half) * PIECE, PIECE)
            self.copies.append(
                pltpu.make_async_copy(weight_ref.at[:, pl.ds(at, PIECE)], held.at[base + i], sems.at[base + i])
            )
        for copy in self.copies:
            copy.start()

    def project(self, normed, outs):
        for i, (copy, (ref, k)) in enumerate(zip(self.copies, outs)):
            copy.wait()
            out = jnp.dot(normed[...], self.held[self.base + i], preferred_element_type=F32)
            ref[k] = out.astype(BF16)


def gate_and_normalize(place, state_ref, read_ref, scaled_ref, gain_ref, norm_ref, normed):
    rows = CHUNKS[place]
    read = read_ref[place * rows : (place + 1) * rows, :]
    arrived = jnp.dot(read, state_ref[0:STATE, :], preferred_element_type=F32)
    gated = scaled_ref[...].astype(F32) + arrived * gain_ref[...].astype(F32)
    normed[0:rows, :] = normalize(gated, norm_ref[...])


def first_chunk_kernel(
    mine_ref, theirs_ref, read_ref, scaled_ref, gain_ref, norm_ref, weight_ref,
    first_ref, second_ref, normed_ref, state_ref, held, sems,
):
    columns = Columns(FIRST, weight_ref, held, sems)
    core = lax.axis_index("core")
    state_ref[:, pl.ds(pl.multiple_of(core * 1024, 1024), 1024)] = mine_ref[...]
    for q in range(8):
        lanes = pl.ds(pl.multiple_of((1 - core) * 1024 + q * 128, 128), 128)
        for n in range(2):
            state_ref[n * 128 : (n + 1) * 128, lanes] = theirs_ref[2 * q + n, 0:128, :]
        state_ref[256:272, lanes] = (
            theirs_ref[2 * q, 128:ROWS, :].astype(F32) + theirs_ref[2 * q + 1, 128:ROWS, :].astype(F32)
        ).astype(BF16)
    gate_and_normalize(0, state_ref, read_ref, scaled_ref, gain_ref, norm_ref, normed_ref)
    columns.project(normed_ref, ((first_ref, 0), (first_ref, 1), (second_ref, 0), (second_ref, 1)))


def next_chunk_kernel(
    place, before_ref, state_ref, read_ref, scaled_ref, gain_ref, norm_ref, weight_ref, *refs
):
    sample, (rest_ref, first_ref, second_ref, normed_ref, held, sems) = refs[:-6], refs[-6:]
    columns = Columns(FIRST, weight_ref, held, sems)
    rest = Columns(REST, weight_ref, held, sems, 4)
    gate_and_normalize(place, state_ref, read_ref, scaled_ref, gain_ref, norm_ref, normed_ref)
    if sample:
        local_ref, grown_ref, gate_ref = sample
        readings = state_ref[256:272, :].astype(F32)
        moved = jnp.concatenate([readings[2:16], readings[0:2]], axis=0)
        readings = jnp.where(lax.axis_index("core") == 0, readings, moved)
        sampled = (local_ref[...] + readings * grown_ref[...]) * gate_ref[...]
        rows = CHUNKS[place]
        normed_ref[rows : rows + 16, :] = normalize(sampled, norm_ref[...])
    columns.project(normed_ref, ((first_ref, 0), (first_ref, 1), (second_ref, 0), (second_ref, 1)))
    rest.project(before_ref, ((rest_ref, 1), (rest_ref, 3), (rest_ref, 0), (rest_ref, 2)))


def rest_kernel(normed_ref, weight_ref, rest_ref, held, sems):
    rest = Columns(REST, weight_ref, held, sems)
    rest.project(normed_ref, ((rest_ref, 1), (rest_ref, 3), (rest_ref, 0), (rest_ref, 2)))


def onward_kernel(a_ref, b_ref, rest_ref, a_out, b_out):
    a_out[...] = (rest_ref[1].astype(F32) + a_ref[1].astype(F32)).astype(BF16)
    b_out[...] = (rest_ref[3].astype(F32) + b_ref[1].astype(F32)).astype(BF16)


def finish_kernel(*refs):
    ins, out_ref, sample_ref = refs[:-2], refs[-2], refs[-1]
    start = 0
    for c, rows in enumerate(CHUNKS):
        ra, rb, rest, sa, sb = ins[5 * c : 5 * c + 5]
        for half, (own, near, far) in enumerate(((0, ra, sa), (2, rb, sb))):
            total = rest[own].astype(F32) + near[0].astype(F32) + far[...].astype(F32)
            columns = slice(half * PIECE, (half + 1) * PIECE)
            out_ref[columns, start : start + rows] = jnp.transpose(total[0:rows]).astype(BF16)
            if c == len(CHUNKS) - 1:
                sample_ref[:, columns] = total[rows : rows + 2].astype(BF16)
        start += rows


def call(kernel, name, out_shape, inputs, limit, scalars=0, streamed=None, **more):
    return pl.pallas_call(
        kernel,
        out_shape=out_shape,
        in_specs=[
            SMEM if i < scalars else pl.BlockSpec(memory_space=pl.ANY) if i == streamed else VMEM for i in range(len(inputs))
        ],
        out_specs=jax.tree.map(lambda _: VMEM, out_shape),
        compiler_params=pltpu.CompilerParams(vmem_limit_bytes=limit << 20),
        cost_estimate=pl.CostEstimate(flops=1, bytes_accessed=1, transcendentals=0),
        name=name,
        **more,
    )(*inputs)


SMEM = pl.BlockSpec(memory_space=pltpu.SMEM)
VMEM = pl.BlockSpec(memory_space=pltpu.VMEM)


def shape(dims, dtype=BF16):
    return jax.ShapeDtypeStruct(dims, dtype)


def held(pieces):
    return [pltpu.VMEM((pieces, CH, PIECE), BF16), pltpu.SemaphoreType.DMA((pieces,))]


def swap(x, step):
    return lax.ppermute(x, "head", [(i, i ^ step) for i in range(4)])


def other_core(x):
    return lax.ppermute(x, "core", [(0, 1), (1, 0)])


def local_outputs(part, step, decay, skip, values, gate, inject, read, start=()):
    blocks = TOK // BLOCK // 2
    row = lambda width: pl.BlockSpec((1, width), lambda b: (0, 0))
    tokens = lambda width: pl.BlockSpec((BLOCK, width), lambda b: (b + part * blocks, 0))
    out = pl.BlockSpec((BLOCK, CH), lambda b: (b, 0))
    whole = lambda rows: pl.BlockSpec((rows, CH), lambda b: (0, 0))
    carry = (shape((STATE, CH), F32), shape((8, CH), F32))
    results = (shape((TOK // 2, CH)), shape((TOK // 2, CH)))
    scratch = [pltpu.VMEM((8, CH), F32), pltpu.VMEM((BLOCK, CH), BF16), pltpu.VMEM((BLOCK, CH), F32)]
    if start:
        start_specs = [whole(STATE), whole(8)]
        out_specs = (out, out)
        scratch += [pltpu.VMEM((STATE, CH), F32), pltpu.VMEM((8, CH), F32)]
    else:
        start_specs = []
        results += carry
        out_specs = (out, out, whole(STATE), whole(8))
    values, gate = (pltpu.with_memory_space_constraint(x, pltpu.HBM) for x in (values, gate))
    return pl.pallas_call(
        local_kernel,
        grid=(blocks,),
        out_shape=results,
        in_specs=[
            pl.BlockSpec((HEADS, BLOCK), lambda b: (0, b + part * blocks)), row(HEADS), row(CH),
            tokens(CH), tokens(CH), tokens(STATE), tokens(STATE), *start_specs,
        ],
        out_specs=out_specs,
        scratch_shapes=scratch,
        compiler_params=pltpu.CompilerParams(vmem_limit_bytes=20 << 20),
        cost_estimate=pl.CostEstimate(flops=3 << 30, bytes_accessed=20 << 20, transcendentals=2 << 20),
        name="local_outputs",
    )(step, decay, skip, values, gate, inject, read, *start)


def per_device(
    prompt_values, prompt_gate, prompt_inject, prompt_read, prompt_step, decay_log, skip_gain, norm_weight, out_weight,
    sample_values, sample_gate, sample_inject, sample_read, sample_step, sample_length,
):
    inject = prompt_inject.reshape(TOK, STATE)
    read = prompt_read.reshape(TOK, STATE)
    decay = decay_log.reshape(1, HEADS)
    skip = jnp.repeat(skip_gain, HEAD_DIM).reshape(1, CH)
    norm = norm_weight.reshape(1, CH)
    s_read = sample_read.reshape(2, SLEN, STATE)
    s_inject = sample_inject.reshape(2, SLEN, STATE)
    slices_shape = shape((16, ROWS, 128))

    keep, send = call(
        end_state_kernel, "end_state", (slices_shape,) * 2,
        (sample_length, prompt_step, decay, prompt_values, inject, s_read), 24, 1,
        scratch_shapes=[pltpu.VMEM((TOK, 1024), BF16)],
    )
    sibling = other_core(send)
    joined = call(join_cores_kernel, "join_cores", slices_shape, (keep, sibling), 16)
    joined, step_1 = lax.optimization_barrier((joined, prompt_step))
    slices = lax.all_to_all(joined, ("y", "x"), 0, 0, tiled=True)
    scaled_1, gain_1, *carry = local_outputs(
        0, step_1, decay, skip, prompt_values, prompt_gate, inject, read
    )
    slices, scaled_1 = lax.optimization_barrier((slices, scaled_1))
    prefix = call(prefix_kernel, "prefix", slices_shape, (slices,), 16)
    prefix, step_2, s_step = lax.optimization_barrier((prefix, prompt_step, sample_step))
    back = lax.all_to_all(prefix, ("y", "x"), 0, 0, tiled=True)
    scaled_2, gain_2 = local_outputs(
        1, step_2, decay, skip, prompt_values, prompt_gate, inject, read, carry
    )
    sample = call(
        sample_kernel, "sample_outputs", (shape((16, CH), F32),) * 3,
        (sample_length, s_step.transpose(1, 0, 2), decay, skip, sample_values, sample_gate, s_inject, s_read), 16, 1,
    )
    back, scaled_2, sample = lax.optimization_barrier((back, scaled_2, sample))
    mine, send = call(
        split_cores_kernel, "split_cores", (shape((272, 1024)), slices_shape), (back, keep, sibling), 16
    )
    theirs = other_core(send)

    weight = pltpu.with_memory_space_constraint(out_weight, pltpu.HBM)
    scaled = (scaled_1, scaled_2)
    gain = (gain_1, gain_2)
    near, rests = [], []
    normed = state = None
    for c, rows in enumerate(CHUNKS):
        parts = (read, scaled[c], gain[c], norm, weight)
        last = c == len(CHUNKS) - 1
        size = rows + (16 if last else 0)
        sent = (shape((2, size, PIECE)),) * 2 + (shape((size, CH)),)
        if c == 0:
            *now, normed, state = call(
                first_chunk_kernel, "first_chunk", (*sent, shape((272, CH))), (mine, theirs, *parts), 40,
                streamed=6, scratch_shapes=held(4),
            )
        else:
            rest, *now, normed = call(
                functools.partial(next_chunk_kernel, c), "next_chunk", (shape((4, normed.shape[0], PIECE)), *sent),
                (normed, state, *parts, *(sample if last else ())), 40, streamed=6, scratch_shapes=held(8),
            )
            rests.append(rest)
        near.append(lax.optimization_barrier((swap(now[0], 1), swap(now[1], 3))))
    rests.append(
        call(
            rest_kernel, "rest", shape((4, normed.shape[0], PIECE)), (normed, weight), 40, streamed=1, scratch_shapes=held(4)
        )
    )

    ends = []
    a_on = None
    for rest, (a, b) in zip(rests, near):
        if a_on is not None:
            a, b, a_on = lax.optimization_barrier((a, b, a_on))
            ends += lax.optimization_barrier((swap(a_on, 3), swap(b_on, 1)))
        a_on, b_on = call(onward_kernel, "onward", (shape(a.shape[1:]),) * 2, (a, b, rest), 8)
        ends += [a, b, rest]
    ends += lax.optimization_barrier((swap(a_on, 3), swap(b_on, 1)))
    prompt_mixed, sample_mixed = call(
        finish_kernel, "finish", (shape((1024, TOK)), shape((2, 1024))), tuple(ends), 24
    )
    return prompt_mixed, sample_mixed.T


def solution(mesh):
    split = Mesh(mesh.devices.reshape(4, 4, 2, mesh.shape["head"]), ("y", "x", "core", "head"))
    return jax.shard_map(
        per_device,
        mesh=split,
        in_specs=(
            P(CTX, "head"), P(CTX, "head"), P(CTX, "head", None), P(CTX, "head", None), P("head", CTX),
            P("head"), P("head"), P("head"), P("head", None),
            P(CTX, None, "head"), P(CTX, None, "head"), P(CTX, None, "head", None), P(CTX, None, "head", None),
            P("head", CTX, None), P(CTX),
        ),
        out_specs=(P("head", CTX), P("head", CTX)),
        check_vma=False,
    )
```

time: 139 us -> 117 us (0.84)
  blocking collectives: 32 us -> 0 us
  Pallas kernels: 60.5 us -> 40.7 us
  waiting for transfers between devices: 19.7 us -> 33.7 us
  starting transfers between devices: 13.6 us -> 23.5 us
  local copies, waits for them, and re-layouts: 9.29 us -> 16.4 us
    all_to_all x2 -> x0, blocking collectives: 32 us -> none  [the longest x1 18.2 us: per_device(): slices = lax.all_to_all(joined, ('y', 'x'), 0, 0, tiled=True)]
    pallas_call x11 -> x13, Pallas kernels: 60.5 us -> 40.7 us  [the longest x11 28.2 us: call(): pl.pallas_call(kernel, out_shape=out_shape, in_specs=[SMEM if i < scalars...]
    all_to_all x0 -> x2, starting transfers between devices: none -> 10.9 us  [the longest x1 6.84 us: per_device(): slices = lax.all_to_all(joined, ('y', 'x'), 0, 0, tiled=True)]
    ppermute x8, waiting for transfers between devices: 17.8 us -> 27.9 us  [swap(): return lax.ppermute(x, 'head', [(i, i ^ step) for i in range(4)])]
    unnamed x55 -> x66, local copies, waits for them, and re-layouts: 6.24 us -> 16.1 us
    all_to_all x0 -> x2, waiting for transfers between devices: none -> 2.6 us  [the longest x1 2.6 us: per_device(): slices = lax.all_to_all(joined, ('y', 'x'), 0, 0, tiled=True)]
    pallas_call x1 -> x0, local copies, waits for them, and re-layouts: 1.68 us -> none  [per_device(): pl.pallas_call(finish_kernel, out_shape=(shape((1024, TOK)), shape((1024,...]
    ppermute x2, waiting for transfers between devices: 1.84 us -> 3.26 us  [other_core(): return lax.ppermute(x, 'core', [(0, 1), (1, 0)])]
  transfers between devices with their start and end apart: 10 -> 12, of which waited for: 5 -> 6; matrix products, arithmetic and copies ran while one was open for 1% -> 0% of each run, Pallas kernels for 20% -> 16%
where the time goes in v2:
time: 117 us; the launch traced here: 115 us
  Pallas kernels  40.7 us (35%)
  waiting for transfers between devices  33.7 us (29%)
  starting transfers between devices  23.5 us (20%)
  local copies, waits for them, and re-layouts  16.4 us (14%)
    pallas_call x11, Pallas kernels, call(): pl.pallas_call(kernel, out_shape=out_shape, in_specs=[SMEM if i < scalars...  28.2 us
    ppermute x8, waiting for transfers between devices, swap(): return lax.ppermute(x, 'head', [(i, i ^ step) for i in range(4)])  27.9 us
    unnamed x66, local copies, waits for them, and re-layouts  16.1 us
    pallas_call x2, Pallas kernels, local_outputs(): pl.pallas_call(local_kernel, grid=(blocks,), out_shape=results, in_specs=...  12.5 us
    ppermute x8, starting transfers between devices, swap(): return lax.ppermute(x, 'head', [(i, i ^ step) for i in range(4)])  9.51 us
    all_to_all x1, starting transfers between devices, per_device(): slices = lax.all_to_all(joined, ('y', 'x'), 0, 0, tiled=True)  6.84 us
    all_to_all x1, starting transfers between devices, per_device(): back = lax.all_to_all(prefix, ('y', 'x'), 0, 0, tiled=True)  4.07 us
    ppermute x2, waiting for transfers between devices, other_core(): return lax.ppermute(x, 'core', [(0, 1), (1, 0)])  3.26 us
  transfers between devices with their start and end apart: 12, of which 6 were waited for; matrix products, arithmetic and copies ran while one was open for 0% of the time, Pallas kernels for 16%

profile of v2, /device:TPU:1, one launch (start us, length us, event | category | flops | bytes accessed | tf_op | source)
XLA Modules:
  0.0 115.2 jit_solution(6606841736072804464)
XLA Ops:
  0.6 1.6 %copy-done = bf16[512,2048]{1,0:T(8,128)(2,1)S(1)} copy-done((bf16[512,2048]{1,0:T(8,128)(2,1)S(1)}, bf16[512,2048]{1,0:T(8,128)(2,1)}, u32[]{:S(2)}) %copy-start) | copy-done | bytes 2097176
  6.0 4.5 %end_state.1 = (bf16[16,144,128]{2,1,0:T(8,128)(2,1)S(1)}, bf16[16,144,128]{2,1,0:T(8,128)(2,1)S(1)}) custom-call(s32[2]{0:T(128)S(1)} %copy-done.23, f32[32,512]{1,0:T(8,128)S(1)} %copy-done.18, f32[1,32]{1,0:T(1,128)S(1)} %bitcast.21, bf16[512,2048]{1,0:T(8,128)(2,1)S(1)} %copy-done, bf16[512,256]{1,0:T(8,128)(2,1)S(1)} %bitcast.12, ...), custom_call_target="tpu_custom_call" | custom-call | flops 1 | bytes 1 | tf_op jit(solution)/shard_map/end_state/pallas_call | solution.py:367
  10.6 1.5 %collective-permute-start = (bf16[16,144,128]{2,1,0:T(8,128)(2,1)S(1)}, bf16[16,144,128]{2,1,0:T(8,128)(2,1)S(1)}, u32[]{:S(2)}, u32[]{:S(2)}) collective-permute-start(bf16[16,144,128]{2,1,0:T(8,128)(2,1)S(1)} %get-tuple-element.53), channel_id=1, source_target_pairs={{0,4},{4,0},{1,5},{5,1},{2,6},{6,2},{3,7},{7,3},{8,12},{12,8},{9,1... | collective-permute-start | bytes 1769480 | tf_op jit(solution)/shard_map/ppermute | solution.py:398
  12.1 1.6 %collective-permute-done.sib_ref = bf16[16,144,128]{2,1,0:T(8,128)(2,1)S(1)} collective-permute-done((bf16[16,144,128]{2,1,0:T(8,128)(2,1)S(1)}, bf16[16,144,128]{2,1,0:T(8,128)(2,1)S(1)}, u32[]{:S(2)}, u32[]{:S(2)}) %collective-permute-start) | collective-permute-done | bytes 589856 | tf_op jit(solution)/shard_map/ppermute | solution.py:398
  14.8 6.8 %all-to-all-start = ((bf16[16,144,128]{2,1,0:T(8,128)(2,1)}), bf16[16,144,128]{2,1,0:T(8,128)(2,1)S(1)}, u32[]{:S(2)}, u32[]{:S(2)}) async-start(bf16[16,144,128]{2,1,0:T(8,128)(2,1)} %join_cores.1), calls=%async_computation | async-start | bytes 1179648 | tf_op jit(solution)/shard_map/all_to_all | solution.py:456
  21.9 6.3 %local_outputs.2 = (bf16[256,2048]{1,0:T(8,128)(2,1)S(1)}, bf16[256,2048]{1,0:T(8,128)(2,1)S(1)}, f32[256,2048]{1,0:T(8,128)S(1)}, f32[8,2048]{1,0:T(8,128)S(1)}) custom-call(f32[32,512]{1,0:T(8,128)S(1)} %copy-done.19, f32[1,32]{1,0:T(1,128)S(1)} %bitcast.22, f32[1,2048]{1,0:T(1,128)S(1)} %reshape_reshape.3.skip_ref, bf16[512,2048]{1,0:T(8,128)(2,1)} %values_ref.6, ...), custom_call_target="tpu_custom_call" | custom-call | flops 3221225472 | bytes 20971520 | tf_op jit(solution)/shard_map/local_outputs/pallas_call | solution.py:419
  29.1 1.3 %copy-done.27 = f32[256,2048]{1,0:T(8,128)} copy-done((f32[256,2048]{1,0:T(8,128)}, f32[256,2048]{1,0:T(8,128)S(1)}, u32[]{:S(2)}) %copy-start.27) | copy-done | bytes 2097176
  30.5 2.6 %all-to-all-done.in_ref = bf16[16,144,128]{2,1,0:T(8,128)(2,1)S(1)} async-done(((bf16[16,144,128]{2,1,0:T(8,128)(2,1)}), bf16[16,144,128]{2,1,0:T(8,128)(2,1)S(1)}, u32[]{:S(2)}, u32[]{:S(2)}) %all-to-all-start) | async-done | bytes 589856 | tf_op jit(solution)/shard_map/all_to_all | solution.py:456
  34.3 4.1 %all-to-all-start.1 = ((bf16[16,144,128]{2,1,0:T(8,128)(2,1)}), bf16[16,144,128]{2,1,0:T(8,128)(2,1)S(1)}, u32[]{:S(2)}, u32[]{:S(2)}) async-start(bf16[16,144,128]{2,1,0:T(8,128)(2,1)} %prefix.1), calls=%async_computation.1 | async-start | bytes 1179648 | tf_op jit(solution)/shard_map/all_to_all | solution.py:463
  43.7 1.6 %copy-done.28 = f32[256,2048]{1,0:T(8,128)S(1)} copy-done((f32[256,2048]{1,0:T(8,128)S(1)}, f32[256,2048]{1,0:T(8,128)}, u32[]{:S(2)}) %copy-start.28) | copy-done | bytes 2097176
  46.2 6.2 %local_outputs.3 = (bf16[256,2048]{1,0:T(8,128)(2,1)S(1)}, bf16[256,2048]{1,0:T(8,128)(2,1)S(1)}) custom-call(f32[32,512]{1,0:T(8,128)S(1)} %copy-done.20, f32[1,32]{1,0:T(1,128)S(1)} %bitcast.24, f32[1,2048]{1,0:T(1,128)S(1)} %reshape_reshape.3.skip_ref, bf16[512,2048]{1,0:T(8,128)(2,1)} %values_ref.6, bf16[512,2048]{1,0:T(8,128)(2,1)} %gate_ref.4, ...), custom_call_target="tpu_custom_call" | custom-call | flops 3221225472 | bytes 20971520 | tf_op jit(solution)/shard_map/local_outputs/pallas_call | solution.py:419
  54.7 1.6 %collective-permute-start.1 = (bf16[16,144,128]{2,1,0:T(8,128)(2,1)S(1)}, bf16[16,144,128]{2,1,0:T(8,128)(2,1)S(1)}, u32[]{:S(2)}, u32[]{:S(2)}) collective-permute-start(bf16[16,144,128]{2,1,0:T(8,128)(2,1)S(1)} %get-tuple-element.69), channel_id=1, source_target_pairs={{0,4},{4,0},{1,5},{5,1},{2,6},{6,2},{3,7},{7,3},{8,12},{12,8},{9,1... | collective-permute-start | bytes 1769480 | tf_op jit(solution)/shard_map/ppermute | solution.py:398
  56.3 1.6 %collective-permute-done.1.theirs_ref = bf16[16,144,128]{2,1,0:T(8,128)(2,1)S(1)} collective-permute-done((bf16[16,144,128]{2,1,0:T(8,128)(2,1)S(1)}, bf16[16,144,128]{2,1,0:T(8,128)(2,1)S(1)}, u32[]{:S(2)}, u32[]{:S(2)}) %collective-permute-start.1) | collective-permute-done | bytes 589856 | tf_op jit(solution)/shard_map/ppermute | solution.py:398
  58.0 5.3 %first_chunk.1 = (bf16[2,256,512]{2,1,0:T(8,128)(2,1)S(1)}, bf16[2,256,512]{2,1,0:T(8,128)(2,1)S(1)}, bf16[256,2048]{1,0:T(8,128)(2,1)S(1)}, bf16[272,2048]{1,0:T(8,128)(2,1)S(1)}) custom-call(bf16[272,1024]{1,0:T(8,128)(2,1)S(1)} %get-tuple-element.68.mine_ref, bf16[16,144,128]{2,1,0:T(8,128)(2,1)S(1)} %collective-permute-done.1.theirs_ref, ...), custom_call_target="tpu_custom_call" | custom-call | flops 1 | bytes 1 | tf_op jit(solution)/shard_map/first_chunk/pallas_call | solution.py:367
  63.3 8.1 %next_chunk.1 = (bf16[4,256,512]{2,1,0:T(8,128)(2,1)S(1)}, bf16[2,272,512]{2,1,0:T(8,128)(2,1)S(1)}, bf16[2,272,512]{2,1,0:T(8,128)(2,1)S(1)}, bf16[272,2048]{1,0:T(8,128)(2,1)S(1)}) custom-call(bf16[256,2048]{1,0:T(8,128)(2,1)S(1)} %get-tuple-element.76.before_ref, bf16[272,2048]{1,0:T(8,128)(2,1)S(1)} %get-tuple-element.77.state_ref, ...), custom_call_target="tpu_custom_call" | custom-call | flops 1 | bytes 1 | tf_op jit(solution)/shard_map/next_chunk/pallas_call | solution.py:367
  71.4 1.7 %collective-permute-start.4 = (bf16[2,272,512]{2,1,0:T(8,128)(2,1)S(1)}, bf16[2,272,512]{2,1,0:T(8,128)(2,1)S(1)}, u32[]{:S(2)}, u32[]{:S(2)}) collective-permute-start(bf16[2,272,512]{2,1,0:T(8,128)(2,1)S(1)} %get-tuple-element.84), channel_id=1, source_target_pairs={{0,1},{1,0},{2,3},{3,2},{4,5},{5,4},{6,7},{7,6},{8,9},{9,8},{10,11... | collective-permute-start | bytes 1671176 | tf_op jit(solution)/shard_map/ppermute | solution.py:394
  73.1 2.3 %collective-permute-start.5 = (bf16[2,272,512]{2,1,0:T(8,128)(2,1)S(1)}, bf16[2,272,512]{2,1,0:T(8,128)(2,1)S(1)}, u32[]{:S(2)}, u32[]{:S(2)}) collective-permute-start(bf16[2,272,512]{2,1,0:T(8,128)(2,1)S(1)} %get-tuple-element.85), channel_id=1, source_target_pairs={{0,3},{1,2},{2,1},{3,0},{4,7},{5,6},{6,5},{7,4},{8,11},{9,10},{10,... | collective-permute-start | bytes 1671176 | tf_op jit(solution)/shard_map/ppermute | solution.py:394
  76.7 4.6 %rest.1.rest_ref.refs_7_ = bf16[4,272,512]{2,1,0:T(8,128)(2,1)S(1)} custom-call(bf16[272,2048]{1,0:T(8,128)(2,1)S(1)} %get-tuple-element.95.normed_ref, bf16[2048,4096]{1,0:T(8,128)(2,1)} %weight_ref.5), custom_call_target="tpu_custom_call" | custom-call | flops 1 | bytes 1 | tf_op jit(solution)/shard_map/rest/pallas_call | solution.py:367
  81.3 15.6 %collective-permute-done.2.a_ref.refs_0_ = bf16[2,256,512]{2,1,0:T(8,128)(2,1)S(1)} collective-permute-done((bf16[2,256,512]{2,1,0:T(8,128)(2,1)S(1)}, bf16[2,256,512]{2,1,0:T(8,128)(2,1)S(1)}, u32[]{:S(2)}, u32[]{:S(2)}) %collective-permute-start.2) | collective-permute-done | bytes 524320 | tf_op jit(solution)/shard_map/ppermute | solution.py:394
  96.9 2.1 %collective-permute-done.3.b_ref.refs_1_ = bf16[2,256,512]{2,1,0:T(8,128)(2,1)S(1)} collective-permute-done((bf16[2,256,512]{2,1,0:T(8,128)(2,1)S(1)}, bf16[2,256,512]{2,1,0:T(8,128)(2,1)S(1)}, u32[]{:S(2)}, u32[]{:S(2)}) %collective-permute-start.3) | collective-permute-done | bytes 524320 | tf_op jit(solution)/shard_map/ppermute | solution.py:394
  99.4 2.4 %collective-permute-start.8 = (bf16[272,512]{1,0:T(8,128)(2,1)S(1)}, bf16[272,512]{1,0:T(8,128)(2,1)S(1)}, u32[]{:S(2)}, u32[]{:S(2)}) collective-permute-start(bf16[272,512]{1,0:T(8,128)(2,1)S(1)} %get-tuple-element.96), channel_id=1, source_target_pairs={{0,3},{1,2},{2,1},{3,0},{4,7},{5,6},{6,5},{7,4},{8,11},{9,10},{10,... | collective-permute-start | bytes 835592 | tf_op jit(solution)/shard_map/ppermute | solution.py:394
  101.7 1.5 %collective-permute-start.7 = (bf16[256,512]{1,0:T(8,128)(2,1)S(1)}, bf16[256,512]{1,0:T(8,128)(2,1)S(1)}, u32[]{:S(2)}, u32[]{:S(2)}) collective-permute-start(bf16[256,512]{1,0:T(8,128)(2,1)S(1)} %get-tuple-element.90), channel_id=1, source_target_pairs={{0,1},{1,0},{2,3},{3,2},{4,5},{5,4},{6,7},{7,6},{8,9},{9,8},{10,11... | collective-permute-start | bytes 786440 | tf_op jit(solution)/shard_map/ppermute | solution.py:394
  103.6 10.1 %collective-permute-done.7.refs_4_ = bf16[256,512]{1,0:T(8,128)(2,1)S(1)} collective-permute-done((bf16[256,512]{1,0:T(8,128)(2,1)S(1)}, bf16[256,512]{1,0:T(8,128)(2,1)S(1)}, u32[]{:S(2)}, u32[]{:S(2)}) %collective-permute-start.7) | collective-permute-done | bytes 262176 | tf_op jit(solution)/shard_map/ppermute | solution.py:394
  113.7 1.5 %finish.1 = (bf16[1024,512]{1,0:T(8,128)(2,1)}, bf16[2,1024]{1,0:T(2,128)(2,1)}) custom-call(bf16[2,256,512]{2,1,0:T(8,128)(2,1)S(1)} %collective-permute-done.2.a_ref.refs_0_, bf16[2,256,512]{2,1,0:T(8,128)(2,1)S(1)} %collective-permute-done.3.b_ref.refs_1_, bf16[4,256,512]{2,1,0:T(8,128)(2,1)S(1)} %get-tuple-element.83.rest_ref.refs_2_, ...), custom_call_target="tpu_custom_call" | custom-call | flops 1 | bytes 1 | tf_op jit(solution)/shard_map/finish/pallas_call | solution.py:367
  (82 shorter events, 17.8 us)
Async XLA Ops:
  6.0 15.6 %copy-start.32 = (f32[32]{0:T(128)S(1)}, f32[32]{0:T(128)}, u32[]{:S(2)}) copy-start(f32[32]{0:T(128)} %param.21) | copy-start | bytes 388
  10.6 11.3 %copy-start.1 = (bf16[512,1,256]{2,0,1:T(8,128)(2,1)S(1)}, bf16[512,1,256]{2,0,1:T(8,128)(2,1)}, u32[]{:S(2)}) copy-start(bf16[512,1,256]{2,0,1:T(8,128)(2,1)} %param.18) | copy-start | bytes 786436
  10.6 11.3 %copy-start.9 = (bf16[512,1,256]{2,0,1:T(8,128)(2,1)S(1)}, bf16[512,1,256]{2,0,1:T(8,128)(2,1)}, u32[]{:S(2)}) copy-start(bf16[512,1,256]{2,0,1:T(8,128)(2,1)} %param.17) | copy-start | bytes 786436
  10.6 11.3 %copy-start.19 = (f32[32,512]{1,0:T(8,128)S(1)}, f32[32,512]{1,0:T(8,128)}, u32[]{:S(2)}) copy-start(f32[32,512]{1,0:T(8,128)} %step_ref.3) | copy-start | bytes 196612
  10.6 11.3 %copy-start.26 = (f32[32]{0:T(128)S(1)}, f32[32]{0:T(128)}, u32[]{:S(2)}) copy-start(f32[32]{0:T(128)} %param.20) | copy-start | bytes 388
  10.6 3.1 %collective-permute-start = (bf16[16,144,128]{2,1,0:T(8,128)(2,1)S(1)}, bf16[16,144,128]{2,1,0:T(8,128)(2,1)S(1)}, u32[]{:S(2)}, u32[]{:S(2)}) collective-permute-start(bf16[16,144,128]{2,1,0:T(8,128)(2,1)S(1)} %get-tuple-element.53), channel_id=1, source_target_pairs={{0,4},{4,0},{1,5},{5,1},{2,6},{6,2},{3,7},{7,3},{8,12},{12,8},{9,1... | collective-permute-start | bytes 1769480 | tf_op jit(solution)/shard_map/ppermute | solution.py:398
  14.8 18.3 %all-to-all-start = ((bf16[16,144,128]{2,1,0:T(8,128)(2,1)}), bf16[16,144,128]{2,1,0:T(8,128)(2,1)S(1)}, u32[]{:S(2)}, u32[]{:S(2)}) async-start(bf16[16,144,128]{2,1,0:T(8,128)(2,1)} %join_cores.1), calls=%async_computation | async-start | bytes 1179648 | tf_op jit(solution)/shard_map/all_to_all | solution.py:456
  30.5 8.0 %copy-start.29 = (f32[8,2048]{1,0:T(8,128)}, f32[8,2048]{1,0:T(8,128)S(1)}, u32[]{:S(2)}) copy-start(f32[8,2048]{1,0:T(8,128)S(1)} %get-tuple-element.61.refs_1_) | copy-start | bytes 196612
  30.5 7.9 %copy-start.31 = (f32[32,2,16]{0,2,1:T(8,128)S(1)}, f32[32,2,16]{0,2,1:T(8,128)}, u32[]{:S(2)}) copy-start(f32[32,2,16]{0,2,1:T(8,128)} %param.28) | copy-start | bytes 12292
  30.5 8.0 %copy-start.17 = (bf16[2,16,1,256]{3,1,2,0:T(8,128)(2,1)S(1)}, bf16[2,16,1,256]{3,1,2,0:T(8,128)(2,1)}, u32[]{:S(2)}) copy-start(bf16[2,16,1,256]{3,1,2,0:T(8,128)(2,1)} %param.27) | copy-start | bytes 49156
  30.5 8.0 %copy-start.22 = (bf16[2,16,1,256]{3,1,2,0:T(8,128)(2,1)S(1)}, bf16[2,16,1,256]{3,1,2,0:T(8,128)(2,1)}, u32[]{:S(2)}) copy-start(bf16[2,16,1,256]{3,1,2,0:T(8,128)(2,1)} %param.26) | copy-start | bytes 49156
  30.5 8.0 %copy-start.24 = (s32[2]{0:T(128)S(1)}, s32[2]{0:T(128)}, u32[]{:S(2)}) copy-start(s32[2]{0:T(128)} %length.3) | copy-start | bytes 28
  34.3 20.1 %all-to-all-start.1 = ((bf16[16,144,128]{2,1,0:T(8,128)(2,1)}), bf16[16,144,128]{2,1,0:T(8,128)(2,1)S(1)}, u32[]{:S(2)}, u32[]{:S(2)}) async-start(bf16[16,144,128]{2,1,0:T(8,128)(2,1)} %prefix.1), calls=%async_computation.1 | async-start | bytes 1179648 | tf_op jit(solution)/shard_map/all_to_all | solution.py:463
  46.2 11.8 %copy-start.21 = (f32[2048]{0:T(1024)S(1)}, f32[2048]{0:T(1024)}, u32[]{:S(2)}) copy-start(f32[2048]{0:T(1024)} %param.22) | copy-start | bytes 24580
  54.7 3.2 %collective-permute-start.1 = (bf16[16,144,128]{2,1,0:T(8,128)(2,1)S(1)}, bf16[16,144,128]{2,1,0:T(8,128)(2,1)S(1)}, u32[]{:S(2)}, u32[]{:S(2)}) collective-permute-start(bf16[16,144,128]{2,1,0:T(8,128)(2,1)S(1)} %get-tuple-element.69), channel_id=1, source_target_pairs={{0,4},{4,0},{1,5},{5,1},{2,6},{6,2},{3,7},{7,3},{8,12},{12,8},{9,1... | collective-permute-start | bytes 1769480 | tf_op jit(solution)/shard_map/ppermute | solution.py:398
  57.9 5.4 %copy-start.11 = (f32[16,2048]{1,0:T(8,128)S(1)}, f32[16,2048]{1,0:T(8,128)}, u32[]{:S(2)}) copy-start(f32[16,2048]{1,0:T(8,128)} %copy-done.10) | copy-start | bytes 393220
  71.4 27.8 %collective-permute-start.4 = (bf16[2,272,512]{2,1,0:T(8,128)(2,1)S(1)}, bf16[2,272,512]{2,1,0:T(8,128)(2,1)S(1)}, u32[]{:S(2)}, u32[]{:S(2)}) collective-permute-start(bf16[2,272,512]{2,1,0:T(8,128)(2,1)S(1)} %get-tuple-element.84), channel_id=1, source_target_pairs={{0,1},{1,0},{2,3},{3,2},{4,5},{5,4},{6,7},{7,6},{8,9},{9,8},{10,11... | collective-permute-start | bytes 1671176 | tf_op jit(solution)/shard_map/ppermute | solution.py:394
  73.1 26.1 %collective-permute-start.5 = (bf16[2,272,512]{2,1,0:T(8,128)(2,1)S(1)}, bf16[2,272,512]{2,1,0:T(8,128)(2,1)S(1)}, u32[]{:S(2)}, u32[]{:S(2)}) collective-permute-start(bf16[2,272,512]{2,1,0:T(8,128)(2,1)S(1)} %get-tuple-element.85), channel_id=1, source_target_pairs={{0,3},{1,2},{2,1},{3,0},{4,7},{5,6},{6,5},{7,4},{8,11},{9,10},{10,... | collective-permute-start | bytes 1671176 | tf_op jit(solution)/shard_map/ppermute | solution.py:394
  75.4 21.5 %collective-permute-start.2 = (bf16[2,256,512]{2,1,0:T(8,128)(2,1)S(1)}, bf16[2,256,512]{2,1,0:T(8,128)(2,1)S(1)}, u32[]{:S(2)}, u32[]{:S(2)}) collective-permute-start(bf16[2,256,512]{2,1,0:T(8,128)(2,1)S(1)} %get-tuple-element.72), channel_id=1, source_target_pairs={{0,1},{1,0},{2,3},{3,2},{4,5},{5,4},{6,7},{7,6},{8,9},{9,8},{10,11... | collective-permute-start | bytes 1572872 | tf_op jit(solution)/shard_map/ppermute | solution.py:394
  76.1 23.0 %collective-permute-start.3 = (bf16[2,256,512]{2,1,0:T(8,128)(2,1)S(1)}, bf16[2,256,512]{2,1,0:T(8,128)(2,1)S(1)}, u32[]{:S(2)}, u32[]{:S(2)}) collective-permute-start(bf16[2,256,512]{2,1,0:T(8,128)(2,1)S(1)} %get-tuple-element.73), channel_id=1, source_target_pairs={{0,3},{1,2},{2,1},{3,0},{4,7},{5,6},{6,5},{7,4},{8,11},{9,10},{10,... | collective-permute-start | bytes 1572872 | tf_op jit(solution)/shard_map/ppermute | solution.py:394
  99.4 14.3 %collective-permute-start.8 = (bf16[272,512]{1,0:T(8,128)(2,1)S(1)}, bf16[272,512]{1,0:T(8,128)(2,1)S(1)}, u32[]{:S(2)}, u32[]{:S(2)}) collective-permute-start(bf16[272,512]{1,0:T(8,128)(2,1)S(1)} %get-tuple-element.96), channel_id=1, source_target_pairs={{0,3},{1,2},{2,1},{3,0},{4,7},{5,6},{6,5},{7,4},{8,11},{9,10},{10,... | collective-permute-start | bytes 835592 | tf_op jit(solution)/shard_map/ppermute | solution.py:394
  101.7 12.0 %collective-permute-start.9 = (bf16[272,512]{1,0:T(8,128)(2,1)S(1)}, bf16[272,512]{1,0:T(8,128)(2,1)S(1)}, u32[]{:S(2)}, u32[]{:S(2)}) collective-permute-start(bf16[272,512]{1,0:T(8,128)(2,1)S(1)} %get-tuple-element.97), channel_id=1, source_target_pairs={{0,1},{1,0},{2,3},{3,2},{4,5},{5,4},{6,7},{7,6},{8,9},{9,8},{10,11... | collective-permute-start | bytes 835592 | tf_op jit(solution)/shard_map/ppermute | solution.py:394
  101.7 12.0 %collective-permute-start.7 = (bf16[256,512]{1,0:T(8,128)(2,1)S(1)}, bf16[256,512]{1,0:T(8,128)(2,1)S(1)}, u32[]{:S(2)}, u32[]{:S(2)}) collective-permute-start(bf16[256,512]{1,0:T(8,128)(2,1)S(1)} %get-tuple-element.90), channel_id=1, source_target_pairs={{0,1},{1,0},{2,3},{3,2},{4,5},{5,4},{6,7},{7,6},{8,9},{9,8},{10,11... | collective-permute-start | bytes 786440 | tf_op jit(solution)/shard_map/ppermute | solution.py:394
  103.2 10.5 %collective-permute-start.6 = (bf16[256,512]{1,0:T(8,128)(2,1)S(1)}, bf16[256,512]{1,0:T(8,128)(2,1)S(1)}, u32[]{:S(2)}, u32[]{:S(2)}) collective-permute-start(bf16[256,512]{1,0:T(8,128)(2,1)S(1)} %get-tuple-element.89), channel_id=1, source_target_pairs={{0,3},{1,2},{2,1},{3,0},{4,7},{5,6},{6,5},{7,4},{8,11},{9,10},{10,... | collective-permute-start | bytes 786440 | tf_op jit(solution)/shard_map/ppermute | solution.py:394
  (21 other events, 35.7 us)

commit v3 on v2

--- a/solution.py
+++ b/solution.py
@@ -302,11 +302,7 @@
     normed[0:rows, :] = normalize(gated, norm_ref[...])
 
 
-def first_chunk_kernel(
-    mine_ref, theirs_ref, read_ref, scaled_ref, gain_ref, norm_ref, weight_ref,
-    first_ref, second_ref, normed_ref, state_ref, held, sems,
-):
-    columns = Columns(FIRST, weight_ref, held, sems)
+def join_halves_kernel(mine_ref, theirs_ref, state_ref):
     core = lax.axis_index("core")
     state_ref[:, pl.ds(pl.multiple_of(core * 1024, 1024), 1024)] = mine_ref[...]
     for q in range(8):
@@ -316,16 +312,11 @@
         state_ref[256:272, lanes] = (
             theirs_ref[2 * q, 128:ROWS, :].astype(F32) + theirs_ref[2 * q + 1, 128:ROWS, :].astype(F32)
         ).astype(BF16)
-    gate_and_normalize(0, state_ref, read_ref, scaled_ref, gain_ref, norm_ref, normed_ref)
-    columns.project(normed_ref, ((first_ref, 0), (first_ref, 1), (second_ref, 0), (second_ref, 1)))
-
-
-def next_chunk_kernel(
-    place, before_ref, state_ref, read_ref, scaled_ref, gain_ref, norm_ref, weight_ref, *refs
-):
-    sample, (rest_ref, first_ref, second_ref, normed_ref, held, sems) = refs[:-6], refs[-6:]
+
+
+def chunk_kernel(place, state_ref, read_ref, scaled_ref, gain_ref, norm_ref, weight_ref, *refs):
+    sample, (first_ref, second_ref, normed_ref, held, sems) = refs[:-5], refs[-5:]
     columns = Columns(FIRST, weight_ref, held, sems)
-    rest = Columns(REST, weight_ref, held, sems, 4)
     gate_and_normalize(place, state_ref, read_ref, scaled_ref, gain_ref, norm_ref, normed_ref)
     if sample:
         local_ref, grown_ref, gate_ref = sample
@@ -336,7 +327,6 @@
         rows = CHUNKS[place]
         normed_ref[rows : rows + 16, :] = normalize(sampled, norm_ref[...])
     columns.project(normed_ref, ((first_ref, 0), (first_ref, 1), (second_ref, 0), (second_ref, 1)))
-    rest.project(before_ref, ((rest_ref, 1), (rest_ref, 3), (rest_ref, 0), (rest_ref, 2)))
 
 
 def rest_kernel(normed_ref, weight_ref, rest_ref, held, sems):
@@ -363,6 +353,10 @@
         start += rows
 
 
+def in_hbm(*arrays):
+    return tuple(pltpu.with_memory_space_constraint(x, pltpu.HBM) for x in arrays)
+
+
 def call(kernel, name, out_shape, inputs, limit, scalars=0, streamed=None, **more):
     return pl.pallas_call(
         kernel,
@@ -370,7 +364,7 @@
         in_specs=[
             SMEM if i < scalars else pl.BlockSpec(memory_space=pl.ANY) if i == streamed else VMEM for i in range(len(inputs))
         ],
-        out_specs=jax.tree.map(lambda _: VMEM, out_shape),
+        out_specs=jax.tree.map(lambda _: VMEM, out_shape, is_leaf=lambda x: not isinstance(x, tuple)),
         compiler_params=pltpu.CompilerParams(vmem_limit_bytes=limit << 20),
         cost_estimate=pl.CostEstimate(flops=1, bytes_accessed=1, transcendentals=0),
         name=name,
@@ -404,8 +398,8 @@
     tokens = lambda width: pl.BlockSpec((BLOCK, width), lambda b: (b + part * blocks, 0))
     out = pl.BlockSpec((BLOCK, CH), lambda b: (b, 0))
     whole = lambda rows: pl.BlockSpec((rows, CH), lambda b: (0, 0))
-    carry = (shape((STATE, CH), F32), shape((8, CH), F32))
-    results = (shape((TOK // 2, CH)), shape((TOK // 2, CH)))
+    carry = (pltpu.HBM((STATE, CH), F32), pltpu.HBM((8, CH), F32))
+    results = (pltpu.HBM((TOK // 2, CH), BF16),) * 2
     scratch = [pltpu.VMEM((8, CH), F32), pltpu.VMEM((BLOCK, CH), BF16), pltpu.VMEM((BLOCK, CH), F32)]
     if start:
         start_specs = [whole(STATE), whole(8)]
@@ -415,7 +409,7 @@
         start_specs = []
         results += carry
         out_specs = (out, out, whole(STATE), whole(8))
-    values, gate = (pltpu.with_memory_space_constraint(x, pltpu.HBM) for x in (values, gate))
+    step, values, gate, inject, read = in_hbm(step, values, gate, inject, read)
     return pl.pallas_call(
         local_kernel,
         grid=(blocks,),
@@ -447,28 +441,28 @@
 
     keep, send = call(
         end_state_kernel, "end_state", (slices_shape,) * 2,
-        (sample_length, prompt_step, decay, prompt_values, inject, s_read), 24, 1,
+        (sample_length, *in_hbm(prompt_step, decay, prompt_values, inject, s_read)), 24, 1,
         scratch_shapes=[pltpu.VMEM((TOK, 1024), BF16)],
     )
     sibling = other_core(send)
     joined = call(join_cores_kernel, "join_cores", slices_shape, (keep, sibling), 16)
-    joined, step_1 = lax.optimization_barrier((joined, prompt_step))
+    joined, step_1, s_step = lax.optimization_barrier((joined, prompt_step, sample_step.transpose(1, 0, 2)))
     slices = lax.all_to_all(joined, ("y", "x"), 0, 0, tiled=True)
     scaled_1, gain_1, *carry = local_outputs(
         0, step_1, decay, skip, prompt_values, prompt_gate, inject, read
     )
-    slices, scaled_1 = lax.optimization_barrier((slices, scaled_1))
+    sample = call(
+        sample_kernel, "sample_outputs", (pltpu.HBM((16, CH), F32),) * 3,
+        (sample_length, *in_hbm(s_step, decay, skip, sample_values, sample_gate, s_inject, s_read)), 16, 1,
+    )
+    slices, scaled_1, sample = lax.optimization_barrier((slices, scaled_1, sample))
     prefix = call(prefix_kernel, "prefix", slices_shape, (slices,), 16)
-    prefix, step_2, s_step = lax.optimization_barrier((prefix, prompt_step, sample_step))
+    prefix, step_2 = lax.optimization_barrier((prefix, prompt_step))
     back = lax.all_to_all(prefix, ("y", "x"), 0, 0, tiled=True)
     scaled_2, gain_2 = local_outputs(
         1, step_2, decay, skip, prompt_values, prompt_gate, inject, read, carry
     )
-    sample = call(
-        sample_kernel, "sample_outputs", (shape((16, CH), F32),) * 3,
-        (sample_length, s_step.transpose(1, 0, 2), decay, skip, sample_values, sample_gate, s_inject, s_read), 16, 1,
-    )
-    back, scaled_2, sample = lax.optimization_barrier((back, scaled_2, sample))
+    back, scaled_2 = lax.optimization_barrier((back, scaled_2))
     mine, send = call(
         split_cores_kernel, "split_cores", (shape((272, 1024)), slices_shape), (back, keep, sibling), 16
     )
@@ -477,40 +471,24 @@
     weight = pltpu.with_memory_space_constraint(out_weight, pltpu.HBM)
     scaled = (scaled_1, scaled_2)
     gain = (gain_1, gain_2)
+    state = call(join_halves_kernel, "join_halves", shape((272, CH)), (mine, theirs), 8)
     near, rests = [], []
-    normed = state = None
     for c, rows in enumerate(CHUNKS):
-        parts = (read, scaled[c], gain[c], norm, weight)
         last = c == len(CHUNKS) - 1
         size = rows + (16 if last else 0)
-        sent = (shape((2, size, PIECE)),) * 2 + (shape((size, CH)),)
-        if c == 0:
-            *now, normed, state = call(
-                first_chunk_kernel, "first_chunk", (*sent, shape((272, CH))), (mine, theirs, *parts), 40,
-                streamed=6, scratch_shapes=held(4),
-            )
-        else:
-            rest, *now, normed = call(
-                functools.partial(next_chunk_kernel, c), "next_chunk", (shape((4, normed.shape[0], PIECE)), *sent),
-                (normed, state, *parts, *(sample if last else ())), 40, streamed=6, scratch_shapes=held(8),
-            )
-            rests.append(rest)
+        *now, normed = call(
+            functools.partial(chunk_kernel, c), "chunk", (shape((2, size, PIECE)),) * 2 + (shape((size, CH)),),
+            (state, read, scaled[c], gain[c], norm, weight, *(sample if last else ())), 40, streamed=5, scratch_shapes=held(4),
+        )
         near.append(lax.optimization_barrier((swap(now[0], 1), swap(now[1], 3))))
-    rests.append(
-        call(
-            rest_kernel, "rest", shape((4, normed.shape[0], PIECE)), (normed, weight), 40, streamed=1, scratch_shapes=held(4)
+        rests.append(
+            call(rest_kernel, "rest", shape((4, size, PIECE)), (normed, weight), 40, streamed=1, scratch_shapes=held(4))
         )
-    )
 
     ends = []
-    a_on = None
     for rest, (a, b) in zip(rests, near):
-        if a_on is not None:
-            a, b, a_on = lax.optimization_barrier((a, b, a_on))
-            ends += lax.optimization_barrier((swap(a_on, 3), swap(b_on, 1)))
         a_on, b_on = call(onward_kernel, "onward", (shape(a.shape[1:]),) * 2, (a, b, rest), 8)
-        ends += [a, b, rest]
-    ends += lax.optimization_barrier((swap(a_on, 3), swap(b_on, 1)))
+        ends += [a, b, rest, *lax.optimization_barrier((swap(a_on, 3), swap(b_on, 1)))]
     prompt_mixed, sample_mixed = call(
         finish_kernel, "finish", (shape((1024, TOK)), shape((2, 1024))), tuple(ends), 24
     )

time: 117 us -> 100 us (0.85); the launches traced: 115 us -> 99.4 us
  waiting for transfers between devices: 33.7 us -> 19.9 us
  local copies, waits for them, and re-layouts: 16.4 us -> 4.43 us
  Pallas kernels: 40.7 us -> 46.8 us
  starting transfers between devices: 23.5 us -> 27.4 us
    ppermute x8, waiting for transfers between devices: 27.9 us -> 14.8 us  [swap(): return lax.ppermute(x, 'head', [(i, i ^ step) for i in range(4)])]
    unnamed x66 -> x37, local copies, waits for them, and re-layouts: 16.1 us -> 3.69 us
    pallas_call x11 -> x13, Pallas kernels: 28.2 us -> 32.2 us  [call(): pl.pallas_call(kernel, out_shape=out_shape, in_specs=[SMEM if i < scalars...]
    all_to_all x1, waiting for transfers between devices: 2.6 us -> 0.01 us  [per_device(): slices = lax.all_to_all(joined, ('y', 'x'), 0, 0, tiled=True)]
    all_to_all x1, starting transfers between devices: 4.07 us -> 6.65 us  [per_device(): back = lax.all_to_all(prefix, ('y', 'x'), 0, 0, tiled=True)]
    all_to_all x1, waiting for transfers between devices: 0.01 us -> 2.48 us  [per_device(): back = lax.all_to_all(prefix, ('y', 'x'), 0, 0, tiled=True)]
    pallas_call x2, Pallas kernels: 12.5 us -> 14.6 us  [local_outputs(): pl.pallas_call(local_kernel, grid=(blocks,), out_shape=results, in_specs=...]
  transfers between devices with their start and end apart: 12 -> 12, of which waited for: 6 -> 7; matrix products, arithmetic and copies ran while one was open for 0% -> 1% of each run, Pallas kernels for 16% -> 32%
where the time goes in v3:
time: 100 us; the launch traced here: 99.4 us
  Pallas kernels  46.8 us (47%)
  starting transfers between devices  27.4 us (27%)
  waiting for transfers between devices  19.9 us (20%)
  local copies, waits for them, and re-layouts  4.43 us (4%)
    pallas_call x13, Pallas kernels, call(): pl.pallas_call(kernel, out_shape=out_shape, in_specs=[SMEM if i < scalars...  32.2 us
    ppermute x8, waiting for transfers between devices, swap(): return lax.ppermute(x, 'head', [(i, i ^ step) for i in range(4)])  14.8 us
    pallas_call x2, Pallas kernels, local_outputs(): pl.pallas_call(local_kernel, grid=(blocks,), out_shape=results, in_specs=...  14.6 us
    ppermute x8, starting transfers between devices, swap(): return lax.ppermute(x, 'head', [(i, i ^ step) for i in range(4)])  10 us
    all_to_all x1, starting transfers between devices, per_device(): slices = lax.all_to_all(joined, ('y', 'x'), 0, 0, tiled=True)  6.84 us
    all_to_all x1, starting transfers between devices, per_device(): back = lax.all_to_all(prefix, ('y', 'x'), 0, 0, tiled=True)  6.65 us
    ppermute x2, starting transfers between devices, other_core(): return lax.ppermute(x, 'core', [(0, 1), (1, 0)])  3.85 us
    unnamed x37, local copies, waits for them, and re-layouts  3.69 us
  transfers between devices with their start and end apart: 12, of which 7 were waited for; matrix products, arithmetic and copies ran while one was open for 1% of the time, Pallas kernels for 32%

profile of v3, /device:TPU:1, one launch (start us, length us, event | category | flops | bytes accessed | tf_op | source)
XLA Modules:
  0.0 99.4 jit_solution(8373413832951432764)
XLA Ops:
  1.3 5.7 %end_state.1 = (bf16[16,144,128]{2,1,0:T(8,128)(2,1)S(1)}, bf16[16,144,128]{2,1,0:T(8,128)(2,1)S(1)}) custom-call(s32[2]{0:T(128)S(1)} %copy-done.11, f32[32,512]{1,0:T(8,128)} %step_ref.3, f32[1,32]{1,0:T(1,128)} %bitcast.14, bf16[512,2048]{1,0:T(8,128)(2,1)} %values_ref.7, bf16[512,256]{1,0:T(8,128)(2,1)} %bitcast.18, bf16[2,16,256]{2,1,0:T(8,128)(2,1)} %bitcast.22), custom_call_target="tpu_custom_call" | custom-call | flops 1 | bytes 1 | tf_op jit(solution)/shard_map/end_state/pallas_call | solution.py:361
  7.0 1.5 %collective-permute-start = (bf16[16,144,128]{2,1,0:T(8,128)(2,1)S(1)}, bf16[16,144,128]{2,1,0:T(8,128)(2,1)S(1)}, u32[]{:S(2)}, u32[]{:S(2)}) collective-permute-start(bf16[16,144,128]{2,1,0:T(8,128)(2,1)S(1)} %get-tuple-element.48), channel_id=1, source_target_pairs={{0,4},{4,0},{1,5},{5,1},{2,6},{6,2},{3,7},{7,3},{8,12},{12,8},{9,1... | collective-permute-start | bytes 1769480 | tf_op jit(solution)/shard_map/ppermute | solution.py:392
  11.2 6.8 %all-to-all-start = ((bf16[16,144,128]{2,1,0:T(8,128)(2,1)}), bf16[16,144,128]{2,1,0:T(8,128)(2,1)S(1)}, u32[]{:S(2)}, u32[]{:S(2)}) async-start(bf16[16,144,128]{2,1,0:T(8,128)(2,1)} %join_cores.1), calls=%async_computation | async-start | bytes 1179648 | tf_op jit(solution)/shard_map/all_to_all | solution.py:450
  18.9 2.6 %sample_outputs.1 = (f32[16,2048]{1,0:T(8,128)}, f32[16,2048]{1,0:T(8,128)}, f32[16,2048]{1,0:T(8,128)}) custom-call(s32[2]{0:T(128)S(1)} %copy-done.12, f32[2,32,16]{2,1,0:T(8,128)} %bitcast.21, f32[1,32]{1,0:T(1,128)} %bitcast.15, f32[1,2048]{1,0:T(1,128)} %reshape_reshape.3.skip_ref, bf16[2,16,2048]{2,1,0:T(8,128)(2,1)} %values_ref.6, ...), custom_call_target="tpu_custom_call" | custom-call | flops 1 | bytes 1 | tf_op jit(solution)/shard_map/sample_outputs/pallas_call | solution.py:361
  22.1 7.7 %local_outputs.2 = (bf16[256,2048]{1,0:T(8,128)(2,1)}, bf16[256,2048]{1,0:T(8,128)(2,1)}, f32[256,2048]{1,0:T(8,128)}, f32[8,2048]{1,0:T(8,128)}) custom-call(f32[32,512]{1,0:T(8,128)} %step_ref.3, f32[1,32]{1,0:T(1,128)S(1)} %bitcast.16, f32[1,2048]{1,0:T(1,128)S(1)} %copy-done.9, bf16[512,2048]{1,0:T(8,128)(2,1)} %values_ref.7, ...), custom_call_target="tpu_custom_call" | custom-call | flops 3221225472 | bytes 20971520 | tf_op jit(solution)/shard_map/local_outputs/pallas_call | solution.py:413
  31.0 6.6 %all-to-all-start.1 = ((bf16[16,144,128]{2,1,0:T(8,128)(2,1)}), bf16[16,144,128]{2,1,0:T(8,128)(2,1)S(1)}, u32[]{:S(2)}, u32[]{:S(2)}) async-start(bf16[16,144,128]{2,1,0:T(8,128)(2,1)} %prefix.1), calls=%async_computation.1 | async-start | bytes 1179648 | tf_op jit(solution)/shard_map/all_to_all | solution.py:461
  37.7 1.6 %copy-done.14 = f32[256,2048]{1,0:T(8,128)S(1)} copy-done((f32[256,2048]{1,0:T(8,128)S(1)}, f32[256,2048]{1,0:T(8,128)}, u32[]{:S(2)}) %copy-start.14) | copy-done | bytes 2097176
  39.3 7.0 %local_outputs.3 = (bf16[256,2048]{1,0:T(8,128)(2,1)}, bf16[256,2048]{1,0:T(8,128)(2,1)}) custom-call(f32[32,512]{1,0:T(8,128)} %step_ref.3, f32[1,32]{1,0:T(1,128)S(1)} %bitcast.17, f32[1,2048]{1,0:T(1,128)S(1)} %copy-done.10, bf16[512,2048]{1,0:T(8,128)(2,1)} %values_ref.7, bf16[512,2048]{1,0:T(8,128)(2,1)} %gate_ref.5, bf16[512,256]{1,0:T(8,128)(2,1)} %bitcast.20, ...), custom_call_target="tpu_custom_call" | custom-call | flops 3221225472 | bytes 20971520 | tf_op jit(solution)/shard_map/local_outputs/pallas_call | solution.py:413
  46.3 2.5 %all-to-all-done.1.back_ref = bf16[16,144,128]{2,1,0:T(8,128)(2,1)S(1)} async-done(((bf16[16,144,128]{2,1,0:T(8,128)(2,1)}), bf16[16,144,128]{2,1,0:T(8,128)(2,1)S(1)}, u32[]{:S(2)}, u32[]{:S(2)}) %all-to-all-start.1) | async-done | bytes 589856 | tf_op jit(solution)/shard_map/all_to_all | solution.py:461
  49.1 2.4 %collective-permute-start.1 = (bf16[16,144,128]{2,1,0:T(8,128)(2,1)S(1)}, bf16[16,144,128]{2,1,0:T(8,128)(2,1)S(1)}, u32[]{:S(2)}, u32[]{:S(2)}) collective-permute-start(bf16[16,144,128]{2,1,0:T(8,128)(2,1)S(1)} %get-tuple-element.64), channel_id=1, source_target_pairs={{0,4},{4,0},{1,5},{5,1},{2,6},{6,2},{3,7},{7,3},{8,12},{12,8},{9,1... | collective-permute-start | bytes 1769480 | tf_op jit(solution)/shard_map/ppermute | solution.py:392
  51.5 1.6 %collective-permute-done.1.theirs_ref = bf16[16,144,128]{2,1,0:T(8,128)(2,1)S(1)} collective-permute-done((bf16[16,144,128]{2,1,0:T(8,128)(2,1)S(1)}, bf16[16,144,128]{2,1,0:T(8,128)(2,1)S(1)}, u32[]{:S(2)}, u32[]{:S(2)}) %collective-permute-start.1) | collective-permute-done | bytes 589856 | tf_op jit(solution)/shard_map/ppermute | solution.py:392
  53.4 5.3 %chunk.3 = (bf16[2,272,512]{2,1,0:T(8,128)(2,1)S(1)}, bf16[2,272,512]{2,1,0:T(8,128)(2,1)S(1)}, bf16[272,2048]{1,0:T(8,128)(2,1)S(1)}) custom-call(bf16[272,2048]{1,0:T(8,128)(2,1)S(1)} %join_halves.1.state_ref, bf16[512,256]{1,0:T(8,128)(2,1)S(1)} %bitcast.10, bf16[256,2048]{1,0:T(8,128)(2,1)S(1)} %copy-done.3, bf16[256,2048]{1,0:T(8,128)(2,1)S(1)} %copy-done.4, ...), custom_call_target="tpu_custom_call" | custom-call | flops 1 | bytes 1 | tf_op jit(solution)/shard_map/chunk/pallas_call | solution.py:361
  58.7 1.7 %collective-permute-start.6 = (bf16[2,272,512]{2,1,0:T(8,128)(2,1)S(1)}, bf16[2,272,512]{2,1,0:T(8,128)(2,1)S(1)}, u32[]{:S(2)}, u32[]{:S(2)}) collective-permute-start(bf16[2,272,512]{2,1,0:T(8,128)(2,1)S(1)} %get-tuple-element.81), channel_id=1, source_target_pairs={{0,1},{1,0},{2,3},{3,2},{4,5},{5,4},{6,7},{7,6},{8,9},{9,8},{10,11... | collective-permute-start | bytes 1671176 | tf_op jit(solution)/shard_map/ppermute | solution.py:388
  60.4 2.2 %collective-permute-start.7 = (bf16[2,272,512]{2,1,0:T(8,128)(2,1)S(1)}, bf16[2,272,512]{2,1,0:T(8,128)(2,1)S(1)}, u32[]{:S(2)}, u32[]{:S(2)}) collective-permute-start(bf16[2,272,512]{2,1,0:T(8,128)(2,1)S(1)} %get-tuple-element.82), channel_id=1, source_target_pairs={{0,3},{1,2},{2,1},{3,0},{4,7},{5,6},{6,5},{7,4},{8,11},{9,10},{10,... | collective-permute-start | bytes 1671176 | tf_op jit(solution)/shard_map/ppermute | solution.py:388
  62.6 5.1 %chunk.2 = (bf16[2,256,512]{2,1,0:T(8,128)(2,1)S(1)}, bf16[2,256,512]{2,1,0:T(8,128)(2,1)S(1)}, bf16[256,2048]{1,0:T(8,128)(2,1)S(1)}) custom-call(bf16[272,2048]{1,0:T(8,128)(2,1)S(1)} %join_halves.1.state_ref, bf16[512,256]{1,0:T(8,128)(2,1)S(1)} %bitcast.11, bf16[256,2048]{1,0:T(8,128)(2,1)S(1)} %copy-done.1, bf16[256,2048]{1,0:T(8,128)(2,1)S(1)} %copy-done.2, ...), custom_call_target="tpu_custom_call" | custom-call | flops 1 | bytes 1 | tf_op jit(solution)/shard_map/chunk/pallas_call | solution.py:361
  69.2 4.6 %rest.3.rest_ref.refs_7_ = bf16[4,272,512]{2,1,0:T(8,128)(2,1)S(1)} custom-call(bf16[272,2048]{1,0:T(8,128)(2,1)S(1)} %get-tuple-element.85.normed_ref, bf16[2048,4096]{1,0:T(8,128)(2,1)} %weight_ref.7), custom_call_target="tpu_custom_call" | custom-call | flops 1 | bytes 1 | tf_op jit(solution)/shard_map/rest/pallas_call | solution.py:361
  73.8 1.3 %collective-permute-done.7.b_ref.refs_6_ = bf16[2,272,512]{2,1,0:T(8,128)(2,1)S(1)} collective-permute-done((bf16[2,272,512]{2,1,0:T(8,128)(2,1)S(1)}, bf16[2,272,512]{2,1,0:T(8,128)(2,1)S(1)}, u32[]{:S(2)}, u32[]{:S(2)}) %collective-permute-start.7) | collective-permute-done | bytes 557088 | tf_op jit(solution)/shard_map/ppermute | solution.py:388
  75.2 2.3 %collective-permute-start.8 = (bf16[272,512]{1,0:T(8,128)(2,1)S(1)}, bf16[272,512]{1,0:T(8,128)(2,1)S(1)}, u32[]{:S(2)}, u32[]{:S(2)}) collective-permute-start(bf16[272,512]{1,0:T(8,128)(2,1)S(1)} %get-tuple-element.86), channel_id=1, source_target_pairs={{0,3},{1,2},{2,1},{3,0},{4,7},{5,6},{6,5},{7,4},{8,11},{9,10},{10,... | collective-permute-start | bytes 835592 | tf_op jit(solution)/shard_map/ppermute | solution.py:388
  77.6 4.5 %rest.2.rest_ref.refs_2_ = bf16[4,256,512]{2,1,0:T(8,128)(2,1)S(1)} custom-call(bf16[256,2048]{1,0:T(8,128)(2,1)S(1)} %get-tuple-element.71.normed_ref, bf16[2048,4096]{1,0:T(8,128)(2,1)} %weight_ref.7), custom_call_target="tpu_custom_call" | custom-call | flops 1 | bytes 1 | tf_op jit(solution)/shard_map/rest/pallas_call | solution.py:361
  82.0 2.2 %collective-permute-done.2.a_ref.refs_0_ = bf16[2,256,512]{2,1,0:T(8,128)(2,1)S(1)} collective-permute-done((bf16[2,256,512]{2,1,0:T(8,128)(2,1)S(1)}, bf16[2,256,512]{2,1,0:T(8,128)(2,1)S(1)}, u32[]{:S(2)}, u32[]{:S(2)}) %collective-permute-start.2) | collective-permute-done | bytes 524320 | tf_op jit(solution)/shard_map/ppermute | solution.py:388
  84.2 2.1 %collective-permute-done.3.b_ref.refs_1_ = bf16[2,256,512]{2,1,0:T(8,128)(2,1)S(1)} collective-permute-done((bf16[2,256,512]{2,1,0:T(8,128)(2,1)S(1)}, bf16[2,256,512]{2,1,0:T(8,128)(2,1)S(1)}, u32[]{:S(2)}, u32[]{:S(2)}) %collective-permute-start.3) | collective-permute-done | bytes 524320 | tf_op jit(solution)/shard_map/ppermute | solution.py:388
  86.5 2.3 %collective-permute-start.4 = (bf16[256,512]{1,0:T(8,128)(2,1)S(1)}, bf16[256,512]{1,0:T(8,128)(2,1)S(1)}, u32[]{:S(2)}, u32[]{:S(2)}) collective-permute-start(bf16[256,512]{1,0:T(8,128)(2,1)S(1)} %get-tuple-element.72), channel_id=1, source_target_pairs={{0,3},{1,2},{2,1},{3,0},{4,7},{5,6},{6,5},{7,4},{8,11},{9,10},{10,... | collective-permute-start | bytes 786440 | tf_op jit(solution)/shard_map/ppermute | solution.py:388
  88.8 9.1 %collective-permute-done.4.refs_3_ = bf16[256,512]{1,0:T(8,128)(2,1)S(1)} collective-permute-done((bf16[256,512]{1,0:T(8,128)(2,1)S(1)}, bf16[256,512]{1,0:T(8,128)(2,1)S(1)}, u32[]{:S(2)}, u32[]{:S(2)}) %collective-permute-start.4) | collective-permute-done | bytes 262176 | tf_op jit(solution)/shard_map/ppermute | solution.py:388
  97.9 1.5 %finish.1 = (bf16[1024,512]{1,0:T(8,128)(2,1)}, bf16[2,1024]{1,0:T(2,128)(2,1)}) custom-call(bf16[2,256,512]{2,1,0:T(8,128)(2,1)S(1)} %collective-permute-done.2.a_ref.refs_0_, bf16[2,256,512]{2,1,0:T(8,128)(2,1)S(1)} %collective-permute-done.3.b_ref.refs_1_, bf16[4,256,512]{2,1,0:T(8,128)(2,1)S(1)} %rest.2.rest_ref.refs_2_, ...), custom_call_target="tpu_custom_call" | custom-call | flops 1 | bytes 1 | tf_op jit(solution)/shard_map/finish/pallas_call | solution.py:361
  (54 shorter events, 8.3 us)
Async XLA Ops:
  1.3 7.3 %copy-start.16 = (f32[32,2,16]{0,2,1:T(8,128)S(1)}, f32[32,2,16]{0,2,1:T(8,128)}, u32[]{:S(2)}) copy-start(f32[32,2,16]{0,2,1:T(8,128)} %param.28) | copy-start | bytes 12292
  7.0 11.1 %copy-start.17 = (f32[32]{0:T(128)S(1)}, f32[32]{0:T(128)}, u32[]{:S(2)}) copy-start(f32[32]{0:T(128)} %param.21) | copy-start | bytes 388
  7.0 11.8 %copy-start.12 = (s32[2]{0:T(128)S(1)}, s32[2]{0:T(128)}, u32[]{:S(2)}) copy-start(s32[2]{0:T(128)} %length.3) | copy-start | bytes 28
  7.0 14.4 %copy-start.13 = (f32[32]{0:T(128)S(1)}, f32[32]{0:T(128)}, u32[]{:S(2)}) copy-start(f32[32]{0:T(128)} %param.20) | copy-start | bytes 388
  7.0 3.1 %collective-permute-start = (bf16[16,144,128]{2,1,0:T(8,128)(2,1)S(1)}, bf16[16,144,128]{2,1,0:T(8,128)(2,1)S(1)}, u32[]{:S(2)}, u32[]{:S(2)}) collective-permute-start(bf16[16,144,128]{2,1,0:T(8,128)(2,1)S(1)} %get-tuple-element.48), channel_id=1, source_target_pairs={{0,4},{4,0},{1,5},{5,1},{2,6},{6,2},{3,7},{7,3},{8,12},{12,8},{9,1... | collective-permute-start | bytes 1769480 | tf_op jit(solution)/shard_map/ppermute | solution.py:392
  11.2 18.6 %all-to-all-start = ((bf16[16,144,128]{2,1,0:T(8,128)(2,1)}), bf16[16,144,128]{2,1,0:T(8,128)(2,1)S(1)}, u32[]{:S(2)}, u32[]{:S(2)}) async-start(bf16[16,144,128]{2,1,0:T(8,128)(2,1)} %join_cores.1), calls=%async_computation | async-start | bytes 1179648 | tf_op jit(solution)/shard_map/all_to_all | solution.py:450
  29.8 7.9 %copy-start.10 = (f32[1,2048]{1,0:T(1,128)S(1)}, f32[1,2048]{1,0:T(1,128)}, u32[]{:S(2)}) copy-start(f32[1,2048]{1,0:T(1,128)} %reshape_reshape.3.skip_ref) | copy-start | bytes 24580
  29.8 7.9 %copy-start.15 = (f32[8,2048]{1,0:T(8,128)S(1)}, f32[8,2048]{1,0:T(8,128)}, u32[]{:S(2)}) copy-start(f32[8,2048]{1,0:T(8,128)} %get-tuple-element.60.refs_1_) | copy-start | bytes 196612
  31.0 17.8 %all-to-all-start.1 = ((bf16[16,144,128]{2,1,0:T(8,128)(2,1)}), bf16[16,144,128]{2,1,0:T(8,128)(2,1)S(1)}, u32[]{:S(2)}, u32[]{:S(2)}) async-start(bf16[16,144,128]{2,1,0:T(8,128)(2,1)} %prefix.1), calls=%async_computation.1 | async-start | bytes 1179648 | tf_op jit(solution)/shard_map/all_to_all | solution.py:461
  46.2 7.1 %copy-start.5 = (f32[16,2048]{1,0:T(8,128)S(1)}, f32[16,2048]{1,0:T(8,128)}, u32[]{:S(2)}) copy-start(f32[16,2048]{1,0:T(8,128)} %get-tuple-element.78.refs_0_) | copy-start | bytes 393220
  46.2 7.1 %copy-start.6 = (f32[16,2048]{1,0:T(8,128)S(1)}, f32[16,2048]{1,0:T(8,128)}, u32[]{:S(2)}) copy-start(f32[16,2048]{1,0:T(8,128)} %get-tuple-element.79.refs_1_) | copy-start | bytes 393220
  46.2 7.1 %copy-start.7 = (f32[16,2048]{1,0:T(8,128)S(1)}, f32[16,2048]{1,0:T(8,128)}, u32[]{:S(2)}) copy-start(f32[16,2048]{1,0:T(8,128)} %get-tuple-element.80.refs_2_) | copy-start | bytes 393220
  46.3 7.1 %copy-start.8 = (f32[2048]{0:T(1024)S(1)}, f32[2048]{0:T(1024)}, u32[]{:S(2)}) copy-start(f32[2048]{0:T(1024)} %param.22) | copy-start | bytes 24580
  49.1 4.0 %collective-permute-start.1 = (bf16[16,144,128]{2,1,0:T(8,128)(2,1)S(1)}, bf16[16,144,128]{2,1,0:T(8,128)(2,1)S(1)}, u32[]{:S(2)}, u32[]{:S(2)}) collective-permute-start(bf16[16,144,128]{2,1,0:T(8,128)(2,1)S(1)} %get-tuple-element.64), channel_id=1, source_target_pairs={{0,4},{4,0},{1,5},{5,1},{2,6},{6,2},{3,7},{7,3},{8,12},{12,8},{9,1... | collective-permute-start | bytes 1769480 | tf_op jit(solution)/shard_map/ppermute | solution.py:392
  53.4 9.3 %copy-start.1 = (bf16[256,2048]{1,0:T(8,128)(2,1)S(1)}, bf16[256,2048]{1,0:T(8,128)(2,1)}, u32[]{:S(2)}) copy-start(bf16[256,2048]{1,0:T(8,128)(2,1)} %get-tuple-element.65.scaled_ref) | copy-start | bytes 3145732
  53.4 9.2 %copy-start.2 = (bf16[256,2048]{1,0:T(8,128)(2,1)S(1)}, bf16[256,2048]{1,0:T(8,128)(2,1)}, u32[]{:S(2)}) copy-start(bf16[256,2048]{1,0:T(8,128)(2,1)} %get-tuple-element.66.gain_ref) | copy-start | bytes 3145732
  58.7 15.1 %collective-permute-start.6 = (bf16[2,272,512]{2,1,0:T(8,128)(2,1)S(1)}, bf16[2,272,512]{2,1,0:T(8,128)(2,1)S(1)}, u32[]{:S(2)}, u32[]{:S(2)}) collective-permute-start(bf16[2,272,512]{2,1,0:T(8,128)(2,1)S(1)} %get-tuple-element.81), channel_id=1, source_target_pairs={{0,1},{1,0},{2,3},{3,2},{4,5},{5,4},{6,7},{7,6},{8,9},{9,8},{10,11... | collective-permute-start | bytes 1671176 | tf_op jit(solution)/shard_map/ppermute | solution.py:388
  60.4 14.7 %collective-permute-start.7 = (bf16[2,272,512]{2,1,0:T(8,128)(2,1)S(1)}, bf16[2,272,512]{2,1,0:T(8,128)(2,1)S(1)}, u32[]{:S(2)}, u32[]{:S(2)}) collective-permute-start(bf16[2,272,512]{2,1,0:T(8,128)(2,1)S(1)} %get-tuple-element.82), channel_id=1, source_target_pairs={{0,3},{1,2},{2,1},{3,0},{4,7},{5,6},{6,5},{7,4},{8,11},{9,10},{10,... | collective-permute-start | bytes 1671176 | tf_op jit(solution)/shard_map/ppermute | solution.py:388
  67.7 16.5 %collective-permute-start.2 = (bf16[2,256,512]{2,1,0:T(8,128)(2,1)S(1)}, bf16[2,256,512]{2,1,0:T(8,128)(2,1)S(1)}, u32[]{:S(2)}, u32[]{:S(2)}) collective-permute-start(bf16[2,256,512]{2,1,0:T(8,128)(2,1)S(1)} %get-tuple-element.67), channel_id=1, source_target_pairs={{0,1},{1,0},{2,3},{3,2},{4,5},{5,4},{6,7},{7,6},{8,9},{9,8},{10,11... | collective-permute-start | bytes 1572872 | tf_op jit(solution)/shard_map/ppermute | solution.py:388
  68.6 17.8 %collective-permute-start.3 = (bf16[2,256,512]{2,1,0:T(8,128)(2,1)S(1)}, bf16[2,256,512]{2,1,0:T(8,128)(2,1)S(1)}, u32[]{:S(2)}, u32[]{:S(2)}) collective-permute-start(bf16[2,256,512]{2,1,0:T(8,128)(2,1)S(1)} %get-tuple-element.68), channel_id=1, source_target_pairs={{0,3},{1,2},{2,1},{3,0},{4,7},{5,6},{6,5},{7,4},{8,11},{9,10},{10,... | collective-permute-start | bytes 1572872 | tf_op jit(solution)/shard_map/ppermute | solution.py:388
  75.2 22.7 %collective-permute-start.8 = (bf16[272,512]{1,0:T(8,128)(2,1)S(1)}, bf16[272,512]{1,0:T(8,128)(2,1)S(1)}, u32[]{:S(2)}, u32[]{:S(2)}) collective-permute-start(bf16[272,512]{1,0:T(8,128)(2,1)S(1)} %get-tuple-element.86), channel_id=1, source_target_pairs={{0,3},{1,2},{2,1},{3,0},{4,7},{5,6},{6,5},{7,4},{8,11},{9,10},{10,... | collective-permute-start | bytes 835592 | tf_op jit(solution)/shard_map/ppermute | solution.py:388
  77.6 20.4 %collective-permute-start.9 = (bf16[272,512]{1,0:T(8,128)(2,1)S(1)}, bf16[272,512]{1,0:T(8,128)(2,1)S(1)}, u32[]{:S(2)}, u32[]{:S(2)}) collective-permute-start(bf16[272,512]{1,0:T(8,128)(2,1)S(1)} %get-tuple-element.87), channel_id=1, source_target_pairs={{0,1},{1,0},{2,3},{3,2},{4,5},{5,4},{6,7},{7,6},{8,9},{9,8},{10,11... | collective-permute-start | bytes 835592 | tf_op jit(solution)/shard_map/ppermute | solution.py:388
  86.5 11.5 %collective-permute-start.4 = (bf16[256,512]{1,0:T(8,128)(2,1)S(1)}, bf16[256,512]{1,0:T(8,128)(2,1)S(1)}, u32[]{:S(2)}, u32[]{:S(2)}) collective-permute-start(bf16[256,512]{1,0:T(8,128)(2,1)S(1)} %get-tuple-element.72), channel_id=1, source_target_pairs={{0,3},{1,2},{2,1},{3,0},{4,7},{5,6},{6,5},{7,4},{8,11},{9,10},{10,... | collective-permute-start | bytes 786440 | tf_op jit(solution)/shard_map/ppermute | solution.py:388
  88.8 9.1 %collective-permute-start.5 = (bf16[256,512]{1,0:T(8,128)(2,1)S(1)}, bf16[256,512]{1,0:T(8,128)(2,1)S(1)}, u32[]{:S(2)}, u32[]{:S(2)}) collective-permute-start(bf16[256,512]{1,0:T(8,128)(2,1)S(1)} %get-tuple-element.73), channel_id=1, source_target_pairs={{0,1},{1,0},{2,3},{3,2},{4,5},{5,4},{6,7},{7,6},{8,9},{9,8},{10,11... | collective-permute-start | bytes 786440 | tf_op jit(solution)/shard_map/ppermute | solution.py:388
  (6 other events, 21.7 us)

commit v4 on v3

--- a/solution.py
+++ b/solution.py
@@ -16,12 +16,13 @@
 TOK = 512
 CH = HEADS * HEAD_DIM
 PIECE = 512
+HALF = TOK // 2
 ROWS = 144
 CTX = ("y", "x", "core")
 F32 = jnp.float32
 BF16 = jnp.bfloat16
 EXACT = lax.Precision.HIGHEST
-CHUNKS = (256, 256)
+CHUNKS = ((256, 256), (0, 256))
 
 
 def softplus(v):
@@ -167,20 +168,20 @@
 
 
 def local_kernel(
-    step_ref, decay_ref, skip_ref, values_ref, gate_ref, inject_ref, read_ref, *refs
+    part, step_ref, decay_ref, skip_ref, values_ref, gate_ref, inject_ref, read_ref, *refs
 ):
-    if len(refs) == 7:
-        scaled_ref, gain_ref, state, before, ends, weighted, carried = refs
+    if part == 0:
+        scaled_ref, gain_ref, carry, carry_before, ends, weighted, carried, state, before = refs
     else:
         start, start_before, scaled_ref, gain_ref, ends, weighted, carried, state, before = refs
 
     @pl.when(pl.program_id(0) == 0)
     def _():
-        if len(refs) == 7:
+        if part == 0:
             state[...] = jnp.zeros_like(state)
             before[...] = jnp.ones_like(before)
         else:
-            state[...] = start[...]
+            state[...] = start[...].astype(F32)
             before[...] = start_before[...]
 
     step = softplus(step_ref[...])
@@ -223,6 +224,12 @@
         ends[0:1, lanes] = jnp.exp(end)
     state[...] = state[...] * ends[0:1, :] + jnp.dot(inject_t, weighted[...], preferred_element_type=F32)
     before[0:1, :] = before[0:1, :] * ends[0:1, :]
+    if part == 0:
+
+        @pl.when(pl.program_id(0) == pl.num_programs(0) - 1)
+        def _():
+            carry[...] = state[...].astype(BF16)
+            carry_before[...] = before[...]
 
 
 def sample_kernel(
@@ -230,10 +237,9 @@
 ):
     rate = -jnp.exp(column(decay_ref[...]))
     row = iota((16, CH), 0)
-    spread = (iota((128, CH), 1) // HEAD_DIM == iota((128, CH), 0)).astype(F32)
-    local_all = jnp.zeros((16, CH), F32)
-    grown_all = jnp.zeros((16, CH), F32)
-    gate_all = jnp.zeros((16, CH), F32)
+    place = iota((SLEN, 128), 0)
+    place_wide = iota((SLEN, STATE), 0)
+    narrow = []
     for s in range(2):
         last = length[s] - 1
         step = softplus(step_ref[s])
@@ -241,25 +247,30 @@
         pad = jnp.zeros((HEADS, 128 - SLEN), F32)
         step_t = tokens_first(jnp.concatenate([step, pad], axis=1))[0:SLEN]
         logs_t = tokens_first(jnp.concatenate([logs, pad], axis=1))[0:SLEN]
-        place = iota((SLEN, 128), 0)
         logs_t = jnp.where(place <= last, logs_t, 0.0)
         gap = jnp.zeros((SLEN, 128), F32)
         for k in range(SLEN):
             gap = gap + jnp.where(place < k, logs_t[k : k + 1], 0.0)
         whole = jnp.sum(logs_t, axis=0, keepdims=True)
-        place_wide = iota((SLEN, STATE), 0)
         read = jnp.sum(jnp.where(place_wide == last, read_ref[s].astype(F32), 0.0), axis=0, keepdims=True)
         scores = jnp.sum(inject_ref[s].astype(F32) * read, axis=1, keepdims=True)
-        weight = jnp.where(place <= last, scores * jnp.exp(gap) * step_t, 0.0)
-        both = jnp.concatenate([weight, jnp.broadcast_to(jnp.exp(whole), (8, 128))], axis=0)
-        wide = jnp.dot(both, spread, precision=EXACT, preferred_element_type=F32)
+        narrow.append(jnp.where(place <= last, scores * jnp.exp(gap) * step_t, 0.0))
+        narrow.append(jnp.broadcast_to(jnp.exp(whole), (SLEN, 128)))
+    spread = (iota((128, CH), 1) // HEAD_DIM == iota((128, CH), 0)).astype(BF16)
+    parts = jnp.concatenate(three_parts(jnp.concatenate(narrow, axis=0)), axis=0).astype(BF16)
+    wide = jnp.dot(parts, spread, preferred_element_type=F32)
+    wide = wide[0:64] + wide[64:128] + wide[128:192]
+    local_all = jnp.zeros((16, CH), F32)
+    grown_all = jnp.zeros((16, CH), F32)
+    gate_all = jnp.zeros((16, CH), F32)
+    for s in range(2):
         values = values_ref[s].astype(F32)
-        at_last = iota((SLEN, CH), 0) == last
+        at_last = iota((SLEN, CH), 0) == length[s] - 1
         picked = jnp.sum(jnp.where(at_last, values, 0.0), axis=0, keepdims=True)
         gate = jnp.sum(jnp.where(at_last, gate_ref[s].astype(F32), 0.0), axis=0, keepdims=True)
-        local = jnp.sum(wide[0:SLEN] * values, axis=0, keepdims=True) + skip_ref[...] * picked
+        local = jnp.sum(wide[32 * s : 32 * s + SLEN] * values, axis=0, keepdims=True) + skip_ref[...] * picked
         local_all = jnp.where(row == s, local, local_all)
-        grown_all = jnp.where(row == s, wide[SLEN : SLEN + 1], grown_all)
+        grown_all = jnp.where(row == s, wide[32 * s + SLEN : 32 * s + SLEN + 1], grown_all)
         gate_all = jnp.where(row == s, gate / (1.0 + jnp.exp(-gate)), gate_all)
     local_ref[...] = local_all
     grown_ref[...] = grown_all
@@ -275,30 +286,41 @@
 REST = ((3, 0), (1, 1), (0, 0), (0, 1))
 
 
-class Columns:
-    def __init__(self, pieces, weight_ref, held, sems, base=0):
-        z = lax.axis_index("head")
-        self.held, self.base, self.copies = held, base, []
-        for i, (flip, half) in enumerate(pieces):
-            at = pl.multiple_of(((z ^ flip) * 2 + half) * PIECE, PIECE)
-            self.copies.append(
-                pltpu.make_async_copy(weight_ref.at[:, pl.ds(at, PIECE)], held.at[base + i], sems.at[base + i])
-            )
-        for copy in self.copies:
-            copy.start()
-
-    def project(self, normed, outs):
-        for i, (copy, (ref, k)) in enumerate(zip(self.copies, outs)):
-            copy.wait()
-            out = jnp.dot(normed[...], self.held[self.base + i], preferred_element_type=F32)
-            ref[k] = out.astype(BF16)
+def fetch_kernel(pieces, weight_ref, out_ref, sems):
+    z = lax.axis_index("head")
+    copies = []
+    for i, (flip, half) in enumerate(pieces):
+        at = pl.multiple_of(((z ^ flip) * 2 + half) * PIECE, PIECE)
+        copies.append(pltpu.make_async_copy(weight_ref.at[:, pl.ds(at, PIECE)], out_ref.at[i], sems.at[i]))
+    for copy in copies:
+        copy.start()
+    for copy in copies:
+        copy.wait()
+
+
+def fetch(pieces, weight):
+    out = pl.pallas_call(
+        functools.partial(fetch_kernel, pieces),
+        out_shape=pltpu.VMEM((4, CH, PIECE), BF16),
+        in_specs=[pl.BlockSpec(memory_space=pl.ANY)],
+        out_specs=VMEM,
+        scratch_shapes=[pltpu.SemaphoreType.DMA((4,))],
+        compiler_params=pltpu.CompilerParams(vmem_limit_bytes=12 << 20),
+        name="fetch_weight",
+    )(*in_hbm(weight))
+    return pltpu.with_memory_space_constraint(out, pltpu.VMEM)
+
+
+def project(normed, weight_ref, outs):
+    for i, (ref, k) in enumerate(outs):
+        ref[k] = jnp.dot(normed[...], weight_ref[i], preferred_element_type=F32).astype(BF16)
 
 
 def gate_and_normalize(place, state_ref, read_ref, scaled_ref, gain_ref, norm_ref, normed):
-    rows = CHUNKS[place]
-    read = read_ref[place * rows : (place + 1) * rows, :]
-    arrived = jnp.dot(read, state_ref[0:STATE, :], preferred_element_type=F32)
-    gated = scaled_ref[...].astype(F32) + arrived * gain_ref[...].astype(F32)
+    start, rows = CHUNKS[place]
+    arrived = jnp.dot(read_ref[start : start + rows, :], state_ref[0:STATE, :], preferred_element_type=F32)
+    here = slice(start % HALF, start % HALF + rows)
+    gated = scaled_ref[here, :].astype(F32) + arrived * gain_ref[here, :].astype(F32)
     normed[0:rows, :] = normalize(gated, norm_ref[...])
 
 
@@ -315,8 +337,7 @@
 
 
 def chunk_kernel(place, state_ref, read_ref, scaled_ref, gain_ref, norm_ref, weight_ref, *refs):
-    sample, (first_ref, second_ref, normed_ref, held, sems) = refs[:-5], refs[-5:]
-    columns = Columns(FIRST, weight_ref, held, sems)
+    sample, (first_ref, second_ref, normed_ref) = refs[:-3], refs[-3:]
     gate_and_normalize(place, state_ref, read_ref, scaled_ref, gain_ref, norm_ref, normed_ref)
     if sample:
         local_ref, grown_ref, gate_ref = sample
@@ -324,14 +345,13 @@
         moved = jnp.concatenate([readings[2:16], readings[0:2]], axis=0)
         readings = jnp.where(lax.axis_index("core") == 0, readings, moved)
         sampled = (local_ref[...] + readings * grown_ref[...]) * gate_ref[...]
-        rows = CHUNKS[place]
+        rows = CHUNKS[place][1]
         normed_ref[rows : rows + 16, :] = normalize(sampled, norm_ref[...])
-    columns.project(normed_ref, ((first_ref, 0), (first_ref, 1), (second_ref, 0), (second_ref, 1)))
-
-
-def rest_kernel(normed_ref, weight_ref, rest_ref, held, sems):
-    rest = Columns(REST, weight_ref, held, sems)
-    rest.project(normed_ref, ((rest_ref, 1), (rest_ref, 3), (rest_ref, 0), (rest_ref, 2)))
+    project(normed_ref, weight_ref, ((first_ref, 0), (first_ref, 1), (second_ref, 0), (second_ref, 1)))
+
+
+def rest_kernel(normed_ref, weight_ref, rest_ref):
+    project(normed_ref, weight_ref, ((rest_ref, 1), (rest_ref, 3), (rest_ref, 0), (rest_ref, 2)))
 
 
 def onward_kernel(a_ref, b_ref, rest_ref, a_out, b_out):
@@ -341,29 +361,25 @@
 
 def finish_kernel(*refs):
     ins, out_ref, sample_ref = refs[:-2], refs[-2], refs[-1]
-    start = 0
-    for c, rows in enumerate(CHUNKS):
-        ra, rb, rest, sa, sb = ins[5 * c : 5 * c + 5]
+    for place, (start, rows) in enumerate(CHUNKS):
+        ra, rb, rest, sa, sb = ins[5 * place : 5 * place + 5]
         for half, (own, near, far) in enumerate(((0, ra, sa), (2, rb, sb))):
             total = rest[own].astype(F32) + near[0].astype(F32) + far[...].astype(F32)
             columns = slice(half * PIECE, (half + 1) * PIECE)
             out_ref[columns, start : start + rows] = jnp.transpose(total[0:rows]).astype(BF16)
-            if c == len(CHUNKS) - 1:
+            if place == 0:
                 sample_ref[:, columns] = total[rows : rows + 2].astype(BF16)
-        start += rows
 
 
 def in_hbm(*arrays):
     return tuple(pltpu.with_memory_space_constraint(x, pltpu.HBM) for x in arrays)
 
 
-def call(kernel, name, out_shape, inputs, limit, scalars=0, streamed=None, **more):
+def call(kernel, name, out_shape, inputs, limit, scalars=0, **more):
     return pl.pallas_call(
         kernel,
         out_shape=out_shape,
-        in_specs=[
-            SMEM if i < scalars else pl.BlockSpec(memory_space=pl.ANY) if i == streamed else VMEM for i in range(len(inputs))
-        ],
+        in_specs=[SMEM] * scalars + [VMEM] * (len(inputs) - scalars),
         out_specs=jax.tree.map(lambda _: VMEM, out_shape, is_leaf=lambda x: not isinstance(x, tuple)),
         compiler_params=pltpu.CompilerParams(vmem_limit_bytes=limit << 20),
         cost_estimate=pl.CostEstimate(flops=1, bytes_accessed=1, transcendentals=0),
@@ -380,10 +396,6 @@
     return jax.ShapeDtypeStruct(dims, dtype)
 
 
-def held(pieces):
-    return [pltpu.VMEM((pieces, CH, PIECE), BF16), pltpu.SemaphoreType.DMA((pieces,))]
-
-
 def swap(x, step):
     return lax.ppermute(x, "head", [(i, i ^ step) for i in range(4)])
 
@@ -398,20 +410,22 @@
     tokens = lambda width: pl.BlockSpec((BLOCK, width), lambda b: (b + part * blocks, 0))
     out = pl.BlockSpec((BLOCK, CH), lambda b: (b, 0))
     whole = lambda rows: pl.BlockSpec((rows, CH), lambda b: (0, 0))
-    carry = (pltpu.HBM((STATE, CH), F32), pltpu.HBM((8, CH), F32))
+    carry = (pltpu.HBM((STATE, CH), BF16), pltpu.HBM((8, CH), F32))
     results = (pltpu.HBM((TOK // 2, CH), BF16),) * 2
-    scratch = [pltpu.VMEM((8, CH), F32), pltpu.VMEM((BLOCK, CH), BF16), pltpu.VMEM((BLOCK, CH), F32)]
+    scratch = [
+        pltpu.VMEM((8, CH), F32), pltpu.VMEM((BLOCK, CH), BF16), pltpu.VMEM((BLOCK, CH), F32),
+        pltpu.VMEM((STATE, CH), F32), pltpu.VMEM((8, CH), F32),
+    ]
     if start:
         start_specs = [whole(STATE), whole(8)]
         out_specs = (out, out)
-        scratch += [pltpu.VMEM((STATE, CH), F32), pltpu.VMEM((8, CH), F32)]
     else:
         start_specs = []
         results += carry
         out_specs = (out, out, whole(STATE), whole(8))
-    step, values, gate, inject, read = in_hbm(step, values, gate, inject, read)
+    step, values, gate, inject, read, *start = in_hbm(step, values, gate, inject, read, *start)
     return pl.pallas_call(
-        local_kernel,
+        functools.partial(local_kernel, part),
         grid=(blocks,),
         out_shape=results,
         in_specs=[
@@ -462,35 +476,42 @@
     scaled_2, gain_2 = local_outputs(
         1, step_2, decay, skip, prompt_values, prompt_gate, inject, read, carry
     )
-    back, scaled_2 = lax.optimization_barrier((back, scaled_2))
+    back, scaled_2, weight = lax.optimization_barrier((back, scaled_2, out_weight))
     mine, send = call(
         split_cores_kernel, "split_cores", (shape((272, 1024)), slices_shape), (back, keep, sibling), 16
     )
     theirs = other_core(send)
 
-    weight = pltpu.with_memory_space_constraint(out_weight, pltpu.HBM)
+    first_columns = fetch(FIRST, weight)
     scaled = (scaled_1, scaled_2)
     gain = (gain_1, gain_2)
     state = call(join_halves_kernel, "join_halves", shape((272, CH)), (mine, theirs), 8)
-    near, rests = [], []
-    for c, rows in enumerate(CHUNKS):
-        last = c == len(CHUNKS) - 1
-        size = rows + (16 if last else 0)
-        *now, normed = call(
-            functools.partial(chunk_kernel, c), "chunk", (shape((2, size, PIECE)),) * 2 + (shape((size, CH)),),
-            (state, read, scaled[c], gain[c], norm, weight, *(sample if last else ())), 40, streamed=5, scratch_shapes=held(4),
+
+    def chunk(place, *sample):
+        start, rows = CHUNKS[place]
+        size = rows + (16 if sample else 0)
+        *sent, normed = call(
+            functools.partial(chunk_kernel, place), "chunk", (shape((2, size, PIECE)),) * 2 + (shape((size, CH)),),
+            (state, read, scaled[start // HALF], gain[start // HALF], norm, first_columns, *sample), 24,
         )
-        near.append(lax.optimization_barrier((swap(now[0], 1), swap(now[1], 3))))
-        rests.append(
-            call(rest_kernel, "rest", shape((4, size, PIECE)), (normed, weight), 40, streamed=1, scratch_shapes=held(4))
-        )
-
-    ends = []
-    for rest, (a, b) in zip(rests, near):
+        near = lax.optimization_barrier((swap(sent[0], 1), swap(sent[1], 3)))
+        return normed, near
+
+    def exchange(normed, near, rest_columns):
+        rest = call(rest_kernel, "rest", shape((4, normed.shape[0], PIECE)), (normed, rest_columns), 24)
+        a, b = near
         a_on, b_on = call(onward_kernel, "onward", (shape(a.shape[1:]),) * 2, (a, b, rest), 8)
-        ends += [a, b, rest, *lax.optimization_barrier((swap(a_on, 3), swap(b_on, 1)))]
+        return (a, b, rest, *lax.optimization_barrier((swap(a_on, 3), swap(b_on, 1))))
+
+    normed_1, near_1 = chunk(1)
+    rest_columns = fetch(REST, weight)
+    normed_0, near_0 = chunk(0, *sample)
+    parts = [
+        exchange(normed, near, rest_columns)
+        for normed, near in ((normed_0, near_0), (normed_1, near_1))
+    ]
     prompt_mixed, sample_mixed = call(
-        finish_kernel, "finish", (shape((1024, TOK)), shape((2, 1024))), tuple(ends), 24
+        finish_kernel, "finish", (shape((1024, TOK)), shape((2, 1024))), tuple(sum(parts, ())), 16
     )
     return prompt_mixed, sample_mixed.T
 

time: 100 us -> 101 us (1.010)
  waiting for transfers between devices: 19.9 us -> 22.5 us
    ppermute x8, waiting for transfers between devices: 14.8 us -> 18 us  [swap(): return lax.ppermute(x, 'head', [(i, i ^ step) for i in range(4)])]
    ppermute x2, waiting for transfers between devices: 2.57 us -> 0.94 us  [other_core(): return lax.ppermute(x, 'core', [(0, 1), (1, 0)])]
    all_to_all x1, waiting for transfers between devices: 2.48 us -> 3.55 us  [per_device(): back = lax.all_to_all(prefix, ('y', 'x'), 0, 0, tiled=True)]
    pallas_call x15 -> x17, Pallas kernels: 46.8 us -> 46 us  [the longest x13 23.7 us: call(): pl.pallas_call(kernel, out_shape=out_shape, in_specs=[SMEM] * scalars + [...]
    unnamed x37 -> x33, local copies, waits for them, and re-layouts: 3.69 us -> 3.35 us
where the time goes in v4:
time: 101 us
  Pallas kernels  46 us (46%)
  starting transfers between devices  27.4 us (27%)
  waiting for transfers between devices  22.5 us (22%)
  local copies, waits for them, and re-layouts  4.1 us (4%)
    pallas_call x13, Pallas kernels, call(): pl.pallas_call(kernel, out_shape=out_shape, in_specs=[SMEM] * scalars + [...  23.7 us
    ppermute x8, waiting for transfers between devices, swap(): return lax.ppermute(x, 'head', [(i, i ^ step) for i in range(4)])  18 us
    pallas_call x2, Pallas kernels, local_outputs(): pl.pallas_call(functools.partial(local_kernel, part), grid=(blocks,), out...  15.2 us
    ppermute x8, starting transfers between devices, swap(): return lax.ppermute(x, 'head', [(i, i ^ step) for i in range(4)])  10 us
    pallas_call x2, Pallas kernels, fetch(): pl.pallas_call(functools.partial(fetch_kernel, pieces), out_shape=pltpu.V...  7.15 us
    all_to_all x1, starting transfers between devices, per_device(): slices = lax.all_to_all(joined, ('y', 'x'), 0, 0, tiled=True)  6.84 us
    all_to_all x1, starting transfers between devices, per_device(): back = lax.all_to_all(prefix, ('y', 'x'), 0, 0, tiled=True)  6.65 us
    ppermute x2, starting transfers between devices, other_core(): return lax.ppermute(x, 'core', [(0, 1), (1, 0)])  3.85 us
  transfers between devices with their start and end apart: 12, of which 7 were waited for; matrix products, arithmetic and copies ran while one was open for 1% of the time, Pallas kernels for 32%

profile of v4, /device:TPU:1, one launch (start us, length us, event | category | flops | bytes accessed | tf_op | source)
XLA Modules:
  0.0 100.9 jit_solution(11432225453447188970)
XLA Ops:
  1.3 5.7 %end_state.1 = (bf16[16,144,128]{2,1,0:T(8,128)(2,1)S(1)}, bf16[16,144,128]{2,1,0:T(8,128)(2,1)S(1)}) custom-call(s32[2]{0:T(128)S(1)} %copy-done.11, f32[32,512]{1,0:T(8,128)} %step_ref.3, f32[1,32]{1,0:T(1,128)} %bitcast.14, bf16[512,2048]{1,0:T(8,128)(2,1)} %values_ref.7, bf16[512,256]{1,0:T(8,128)(2,1)} %bitcast.18, bf16[2,16,256]{2,1,0:T(8,128)(2,1)} %bitcast.22), custom_call_target="tpu_custom_call" | custom-call | flops 1 | bytes 1 | tf_op jit(solution)/shard_map/end_state/pallas_call | solution.py:379
  7.0 1.5 %collective-permute-start = (bf16[16,144,128]{2,1,0:T(8,128)(2,1)S(1)}, bf16[16,144,128]{2,1,0:T(8,128)(2,1)S(1)}, u32[]{:S(2)}, u32[]{:S(2)}) collective-permute-start(bf16[16,144,128]{2,1,0:T(8,128)(2,1)S(1)} %get-tuple-element.49), channel_id=1, source_target_pairs={{0,4},{4,0},{1,5},{5,1},{2,6},{6,2},{3,7},{7,3},{8,12},{12,8},{9,1... | collective-permute-start | bytes 1769480 | tf_op jit(solution)/shard_map/ppermute | solution.py:404
  11.3 6.8 %all-to-all-start = ((bf16[16,144,128]{2,1,0:T(8,128)(2,1)}), bf16[16,144,128]{2,1,0:T(8,128)(2,1)S(1)}, u32[]{:S(2)}, u32[]{:S(2)}) async-start(bf16[16,144,128]{2,1,0:T(8,128)(2,1)} %join_cores.1), calls=%async_computation | async-start | bytes 1179648 | tf_op jit(solution)/shard_map/all_to_all | solution.py:464
  18.9 2.4 %sample_outputs.1 = (f32[16,2048]{1,0:T(8,128)}, f32[16,2048]{1,0:T(8,128)}, f32[16,2048]{1,0:T(8,128)}) custom-call(s32[2]{0:T(128)S(1)} %copy-done.12, f32[2,32,16]{2,1,0:T(8,128)} %bitcast.21, f32[1,32]{1,0:T(1,128)} %bitcast.15, f32[1,2048]{1,0:T(1,128)} %reshape_reshape.3.skip_ref, bf16[2,16,2048]{2,1,0:T(8,128)(2,1)} %values_ref.6, ...), custom_call_target="tpu_custom_call" | custom-call | flops 1 | bytes 1 | tf_op jit(solution)/shard_map/sample_outputs/pallas_call | solution.py:379
  21.9 7.7 %local_outputs.2 = (bf16[256,2048]{1,0:T(8,128)(2,1)}, bf16[256,2048]{1,0:T(8,128)(2,1)}, bf16[256,2048]{1,0:T(8,128)(2,1)}, f32[8,2048]{1,0:T(8,128)}) custom-call(f32[32,512]{1,0:T(8,128)} %step_ref.3, f32[1,32]{1,0:T(1,128)S(1)} %bitcast.16, f32[1,2048]{1,0:T(1,128)S(1)} %copy-done.8, bf16[512,2048]{1,0:T(8,128)(2,1)} %values_ref.7, ...), custom_call_target="tpu_custom_call" | custom-call | flops 3221225472 | bytes 20971520 | tf_op jit(solution)/shard_map/local_outputs/pallas_call | solution.py:427
  30.9 6.7 %all-to-all-start.1 = ((bf16[16,144,128]{2,1,0:T(8,128)(2,1)}), bf16[16,144,128]{2,1,0:T(8,128)(2,1)S(1)}, u32[]{:S(2)}, u32[]{:S(2)}) async-start(bf16[16,144,128]{2,1,0:T(8,128)(2,1)} %prefix.1), calls=%async_computation.1 | async-start | bytes 1179648 | tf_op jit(solution)/shard_map/all_to_all | solution.py:475
  37.5 7.5 %local_outputs.3 = (bf16[256,2048]{1,0:T(8,128)(2,1)}, bf16[256,2048]{1,0:T(8,128)(2,1)}) custom-call(f32[32,512]{1,0:T(8,128)} %step_ref.3, f32[1,32]{1,0:T(1,128)S(1)} %bitcast.17, f32[1,2048]{1,0:T(1,128)S(1)} %copy-done.9, bf16[512,2048]{1,0:T(8,128)(2,1)} %values_ref.7, bf16[512,2048]{1,0:T(8,128)(2,1)} %gate_ref.5, bf16[512,256]{1,0:T(8,128)(2,1)} %bitcast.20, ...), custom_call_target="tpu_custom_call" | custom-call | flops 3221225472 | bytes 20971520 | tf_op jit(solution)/shard_map/local_outputs/pallas_call | solution.py:427
  45.1 3.5 %all-to-all-done.1.back_ref = bf16[16,144,128]{2,1,0:T(8,128)(2,1)S(1)} async-done(((bf16[16,144,128]{2,1,0:T(8,128)(2,1)}), bf16[16,144,128]{2,1,0:T(8,128)(2,1)S(1)}, u32[]{:S(2)}, u32[]{:S(2)}) %all-to-all-start.1) | async-done | bytes 589856 | tf_op jit(solution)/shard_map/all_to_all | solution.py:475
  49.0 2.4 %collective-permute-start.1 = (bf16[16,144,128]{2,1,0:T(8,128)(2,1)S(1)}, bf16[16,144,128]{2,1,0:T(8,128)(2,1)S(1)}, u32[]{:S(2)}, u32[]{:S(2)}) collective-permute-start(bf16[16,144,128]{2,1,0:T(8,128)(2,1)S(1)} %get-tuple-element.65), channel_id=1, source_target_pairs={{0,4},{4,0},{1,5},{5,1},{2,6},{6,2},{3,7},{7,3},{8,12},{12,8},{9,1... | collective-permute-start | bytes 1769480 | tf_op jit(solution)/shard_map/ppermute | solution.py:404
  51.3 3.6 %fetch_weight.2.weight_ref = bf16[4,2048,512]{2,1,0:T(8,128)(2,1)S(1)} custom-call(bf16[2048,4096]{1,0:T(8,128)(2,1)} %weight_ref.1), custom_call_target="tpu_custom_call" | custom-call | tf_op jit(solution)/shard_map/fetch_weight/pallas_call | solution.py:302
  56.5 3.2 %chunk.2 = (bf16[2,272,512]{2,1,0:T(8,128)(2,1)S(1)}, bf16[2,272,512]{2,1,0:T(8,128)(2,1)S(1)}, bf16[272,2048]{1,0:T(8,128)(2,1)S(1)}) custom-call(bf16[272,2048]{1,0:T(8,128)(2,1)S(1)} %join_halves.1.state_ref, bf16[512,256]{1,0:T(8,128)(2,1)S(1)} %bitcast.10, bf16[256,2048]{1,0:T(8,128)(2,1)S(1)} %copy-done.2, bf16[256,2048]{1,0:T(8,128)(2,1)S(1)} %copy-done.3, ...), custom_call_target="tpu_custom_call" | custom-call | flops 1 | bytes 1 | tf_op jit(solution)/shard_map/chunk/pallas_call | solution.py:379
  59.7 1.7 %collective-permute-start.2 = (bf16[2,272,512]{2,1,0:T(8,128)(2,1)S(1)}, bf16[2,272,512]{2,1,0:T(8,128)(2,1)S(1)}, u32[]{:S(2)}, u32[]{:S(2)}) collective-permute-start(bf16[2,272,512]{2,1,0:T(8,128)(2,1)S(1)} %get-tuple-element.72), channel_id=1, source_target_pairs={{0,1},{1,0},{2,3},{3,2},{4,5},{5,4},{6,7},{7,6},{8,9},{9,8},{10,11... | collective-permute-start | bytes 1671176 | tf_op jit(solution)/shard_map/ppermute | solution.py:400
  61.4 2.2 %collective-permute-start.3 = (bf16[2,272,512]{2,1,0:T(8,128)(2,1)S(1)}, bf16[2,272,512]{2,1,0:T(8,128)(2,1)S(1)}, u32[]{:S(2)}, u32[]{:S(2)}) collective-permute-start(bf16[2,272,512]{2,1,0:T(8,128)(2,1)S(1)} %get-tuple-element.73), channel_id=1, source_target_pairs={{0,3},{1,2},{2,1},{3,0},{4,7},{5,6},{6,5},{7,4},{8,11},{9,10},{10,... | collective-permute-start | bytes 1671176 | tf_op jit(solution)/shard_map/ppermute | solution.py:400
  63.7 3.0 %chunk.3 = (bf16[2,256,512]{2,1,0:T(8,128)(2,1)S(1)}, bf16[2,256,512]{2,1,0:T(8,128)(2,1)S(1)}, bf16[256,2048]{1,0:T(8,128)(2,1)S(1)}) custom-call(bf16[272,2048]{1,0:T(8,128)(2,1)S(1)} %join_halves.1.state_ref, bf16[512,256]{1,0:T(8,128)(2,1)S(1)} %bitcast.11, bf16[256,2048]{1,0:T(8,128)(2,1)S(1)} %copy-done, bf16[256,2048]{1,0:T(8,128)(2,1)S(1)} %copy-done.1, ...), custom_call_target="tpu_custom_call" | custom-call | flops 1 | bytes 1 | tf_op jit(solution)/shard_map/chunk/pallas_call | solution.py:379
  68.1 3.5 %fetch_weight.3.weight_ref = bf16[4,2048,512]{2,1,0:T(8,128)(2,1)S(1)} custom-call(bf16[2048,4096]{1,0:T(8,128)(2,1)} %weight_ref.1), custom_call_target="tpu_custom_call" | custom-call | tf_op jit(solution)/shard_map/fetch_weight/pallas_call | solution.py:302
  71.7 2.5 %rest.2.rest_ref.refs_2_ = bf16[4,272,512]{2,1,0:T(8,128)(2,1)S(1)} custom-call(bf16[272,2048]{1,0:T(8,128)(2,1)S(1)} %get-tuple-element.76.normed_ref, bf16[4,2048,512]{2,1,0:T(8,128)(2,1)S(1)} %fetch_weight.3.weight_ref), custom_call_target="tpu_custom_call" | custom-call | flops 1 | bytes 1 | tf_op jit(solution)/shard_map/rest/pallas_call | solution.py:379
  74.3 2.2 %collective-permute-done.3.b_ref.refs_1_ = bf16[2,272,512]{2,1,0:T(8,128)(2,1)S(1)} collective-permute-done((bf16[2,272,512]{2,1,0:T(8,128)(2,1)S(1)}, bf16[2,272,512]{2,1,0:T(8,128)(2,1)S(1)}, u32[]{:S(2)}, u32[]{:S(2)}) %collective-permute-start.3) | collective-permute-done | bytes 557088 | tf_op jit(solution)/shard_map/ppermute | solution.py:400
  76.7 2.3 %collective-permute-start.4 = (bf16[272,512]{1,0:T(8,128)(2,1)S(1)}, bf16[272,512]{1,0:T(8,128)(2,1)S(1)}, u32[]{:S(2)}, u32[]{:S(2)}) collective-permute-start(bf16[272,512]{1,0:T(8,128)(2,1)S(1)} %get-tuple-element.77), channel_id=1, source_target_pairs={{0,3},{1,2},{2,1},{3,0},{4,7},{5,6},{6,5},{7,4},{8,11},{9,10},{10,... | collective-permute-start | bytes 835592 | tf_op jit(solution)/shard_map/ppermute | solution.py:400
  79.0 2.3 %rest.3.rest_ref.refs_7_ = bf16[4,256,512]{2,1,0:T(8,128)(2,1)S(1)} custom-call(bf16[256,2048]{1,0:T(8,128)(2,1)S(1)} %get-tuple-element.87.normed_ref, bf16[4,2048,512]{2,1,0:T(8,128)(2,1)S(1)} %fetch_weight.3.weight_ref), custom_call_target="tpu_custom_call" | custom-call | flops 1 | bytes 1 | tf_op jit(solution)/shard_map/rest/pallas_call | solution.py:379
  81.3 4.2 %collective-permute-done.6.a_ref.refs_5_ = bf16[2,256,512]{2,1,0:T(8,128)(2,1)S(1)} collective-permute-done((bf16[2,256,512]{2,1,0:T(8,128)(2,1)S(1)}, bf16[2,256,512]{2,1,0:T(8,128)(2,1)S(1)}, u32[]{:S(2)}, u32[]{:S(2)}) %collective-permute-start.6) | collective-permute-done | bytes 524320 | tf_op jit(solution)/shard_map/ppermute | solution.py:400
  85.5 2.2 %collective-permute-done.7.b_ref.refs_6_ = bf16[2,256,512]{2,1,0:T(8,128)(2,1)S(1)} collective-permute-done((bf16[2,256,512]{2,1,0:T(8,128)(2,1)S(1)}, bf16[2,256,512]{2,1,0:T(8,128)(2,1)S(1)}, u32[]{:S(2)}, u32[]{:S(2)}) %collective-permute-start.7) | collective-permute-done | bytes 524320 | tf_op jit(solution)/shard_map/ppermute | solution.py:400
  87.9 2.3 %collective-permute-start.8 = (bf16[256,512]{1,0:T(8,128)(2,1)S(1)}, bf16[256,512]{1,0:T(8,128)(2,1)S(1)}, u32[]{:S(2)}, u32[]{:S(2)}) collective-permute-start(bf16[256,512]{1,0:T(8,128)(2,1)S(1)} %get-tuple-element.88), channel_id=1, source_target_pairs={{0,3},{1,2},{2,1},{3,0},{4,7},{5,6},{6,5},{7,4},{8,11},{9,10},{10,... | collective-permute-start | bytes 786440 | tf_op jit(solution)/shard_map/ppermute | solution.py:400
  90.2 9.1 %collective-permute-done.8.refs_8_ = bf16[256,512]{1,0:T(8,128)(2,1)S(1)} collective-permute-done((bf16[256,512]{1,0:T(8,128)(2,1)S(1)}, bf16[256,512]{1,0:T(8,128)(2,1)S(1)}, u32[]{:S(2)}, u32[]{:S(2)}) %collective-permute-start.8) | collective-permute-done | bytes 262176 | tf_op jit(solution)/shard_map/ppermute | solution.py:400
  99.4 1.5 %finish.1 = (bf16[1024,512]{1,0:T(8,128)(2,1)}, bf16[2,1024]{1,0:T(2,128)(2,1)}) custom-call(bf16[2,272,512]{2,1,0:T(8,128)(2,1)S(1)} %collective-permute-done.2.a_ref.refs_0_, bf16[2,272,512]{2,1,0:T(8,128)(2,1)S(1)} %collective-permute-done.3.b_ref.refs_1_, bf16[4,272,512]{2,1,0:T(8,128)(2,1)S(1)} %rest.2.rest_ref.refs_2_, ...), custom_call_target="tpu_custom_call" | custom-call | flops 1 | bytes 1 | tf_op jit(solution)/shard_map/finish/pallas_call | solution.py:379
  (52 shorter events, 9.7 us)
Async XLA Ops:
  1.3 7.3 %copy-start.14 = (f32[32,2,16]{0,2,1:T(8,128)S(1)}, f32[32,2,16]{0,2,1:T(8,128)}, u32[]{:S(2)}) copy-start(f32[32,2,16]{0,2,1:T(8,128)} %param.28) | copy-start | bytes 12292
  7.0 11.1 %copy-start.15 = (f32[32]{0:T(128)S(1)}, f32[32]{0:T(128)}, u32[]{:S(2)}) copy-start(f32[32]{0:T(128)} %param.21) | copy-start | bytes 388
  7.0 11.9 %copy-start.12 = (s32[2]{0:T(128)S(1)}, s32[2]{0:T(128)}, u32[]{:S(2)}) copy-start(s32[2]{0:T(128)} %length.3) | copy-start | bytes 28
  7.0 14.2 %copy-start.13 = (f32[32]{0:T(128)S(1)}, f32[32]{0:T(128)}, u32[]{:S(2)}) copy-start(f32[32]{0:T(128)} %param.20) | copy-start | bytes 388
  7.0 3.1 %collective-permute-start = (bf16[16,144,128]{2,1,0:T(8,128)(2,1)S(1)}, bf16[16,144,128]{2,1,0:T(8,128)(2,1)S(1)}, u32[]{:S(2)}, u32[]{:S(2)}) collective-permute-start(bf16[16,144,128]{2,1,0:T(8,128)(2,1)S(1)} %get-tuple-element.49), channel_id=1, source_target_pairs={{0,4},{4,0},{1,5},{5,1},{2,6},{6,2},{3,7},{7,3},{8,12},{12,8},{9,1... | collective-permute-start | bytes 1769480 | tf_op jit(solution)/shard_map/ppermute | solution.py:404
  11.3 18.4 %all-to-all-start = ((bf16[16,144,128]{2,1,0:T(8,128)(2,1)}), bf16[16,144,128]{2,1,0:T(8,128)(2,1)S(1)}, u32[]{:S(2)}, u32[]{:S(2)}) async-start(bf16[16,144,128]{2,1,0:T(8,128)(2,1)} %join_cores.1), calls=%async_computation | async-start | bytes 1179648 | tf_op jit(solution)/shard_map/all_to_all | solution.py:464
  29.6 7.9 %copy-start.9 = (f32[1,2048]{1,0:T(1,128)S(1)}, f32[1,2048]{1,0:T(1,128)}, u32[]{:S(2)}) copy-start(f32[1,2048]{1,0:T(1,128)} %reshape_reshape.3.skip_ref) | copy-start | bytes 24580
  30.9 17.8 %all-to-all-start.1 = ((bf16[16,144,128]{2,1,0:T(8,128)(2,1)}), bf16[16,144,128]{2,1,0:T(8,128)(2,1)S(1)}, u32[]{:S(2)}, u32[]{:S(2)}) async-start(bf16[16,144,128]{2,1,0:T(8,128)(2,1)} %prefix.1), calls=%async_computation.1 | async-start | bytes 1179648 | tf_op jit(solution)/shard_map/all_to_all | solution.py:475
  49.0 6.0 %collective-permute-start.1 = (bf16[16,144,128]{2,1,0:T(8,128)(2,1)S(1)}, bf16[16,144,128]{2,1,0:T(8,128)(2,1)S(1)}, u32[]{:S(2)}, u32[]{:S(2)}) collective-permute-start(bf16[16,144,128]{2,1,0:T(8,128)(2,1)S(1)} %get-tuple-element.65), channel_id=1, source_target_pairs={{0,4},{4,0},{1,5},{5,1},{2,6},{6,2},{3,7},{7,3},{8,12},{12,8},{9,1... | collective-permute-start | bytes 1769480 | tf_op jit(solution)/shard_map/ppermute | solution.py:404
  51.3 3.9 %copy-start.4 = (bf16[512,1,256]{2,0,1:T(8,128)(2,1)S(1)}, bf16[512,1,256]{2,0,1:T(8,128)(2,1)}, u32[]{:S(2)}) copy-start(bf16[512,1,256]{2,0,1:T(8,128)(2,1)} %param.18) | copy-start | bytes 786436
  51.3 3.9 %copy-start.6 = (f32[16,2048]{1,0:T(8,128)S(1)}, f32[16,2048]{1,0:T(8,128)}, u32[]{:S(2)}) copy-start(f32[16,2048]{1,0:T(8,128)} %get-tuple-element.70.refs_1_) | copy-start | bytes 393220
  51.3 3.9 %copy-start.7 = (f32[16,2048]{1,0:T(8,128)S(1)}, f32[16,2048]{1,0:T(8,128)}, u32[]{:S(2)}) copy-start(f32[16,2048]{1,0:T(8,128)} %get-tuple-element.71.refs_2_) | copy-start | bytes 393220
  55.0 1.5 %copy-start.3 = (bf16[256,2048]{1,0:T(8,128)(2,1)S(1)}, bf16[256,2048]{1,0:T(8,128)(2,1)}, u32[]{:S(2)}) copy-start(bf16[256,2048]{1,0:T(8,128)(2,1)} %get-tuple-element.67.gain_ref) | copy-start | bytes 3145732
  55.0 1.5 %copy-start.5 = (f32[16,2048]{1,0:T(8,128)S(1)}, f32[16,2048]{1,0:T(8,128)}, u32[]{:S(2)}) copy-start(f32[16,2048]{1,0:T(8,128)} %get-tuple-element.69.refs_0_) | copy-start | bytes 393220
  56.5 7.2 %copy-start = (bf16[256,2048]{1,0:T(8,128)(2,1)S(1)}, bf16[256,2048]{1,0:T(8,128)(2,1)}, u32[]{:S(2)}) copy-start(bf16[256,2048]{1,0:T(8,128)(2,1)} %get-tuple-element.81.scaled_ref) | copy-start | bytes 3145732
  56.5 7.2 %copy-start.1 = (bf16[256,2048]{1,0:T(8,128)(2,1)S(1)}, bf16[256,2048]{1,0:T(8,128)(2,1)}, u32[]{:S(2)}) copy-start(bf16[256,2048]{1,0:T(8,128)(2,1)} %get-tuple-element.82.gain_ref) | copy-start | bytes 3145732
  59.7 14.6 %collective-permute-start.2 = (bf16[2,272,512]{2,1,0:T(8,128)(2,1)S(1)}, bf16[2,272,512]{2,1,0:T(8,128)(2,1)S(1)}, u32[]{:S(2)}, u32[]{:S(2)}) collective-permute-start(bf16[2,272,512]{2,1,0:T(8,128)(2,1)S(1)} %get-tuple-element.72), channel_id=1, source_target_pairs={{0,1},{1,0},{2,3},{3,2},{4,5},{5,4},{6,7},{7,6},{8,9},{9,8},{10,11... | collective-permute-start | bytes 1671176 | tf_op jit(solution)/shard_map/ppermute | solution.py:400
  61.4 15.1 %collective-permute-start.3 = (bf16[2,272,512]{2,1,0:T(8,128)(2,1)S(1)}, bf16[2,272,512]{2,1,0:T(8,128)(2,1)S(1)}, u32[]{:S(2)}, u32[]{:S(2)}) collective-permute-start(bf16[2,272,512]{2,1,0:T(8,128)(2,1)S(1)} %get-tuple-element.73), channel_id=1, source_target_pairs={{0,3},{1,2},{2,1},{3,0},{4,7},{5,6},{6,5},{7,4},{8,11},{9,10},{10,... | collective-permute-start | bytes 1671176 | tf_op jit(solution)/shard_map/ppermute | solution.py:400
  66.7 18.8 %collective-permute-start.6 = (bf16[2,256,512]{2,1,0:T(8,128)(2,1)S(1)}, bf16[2,256,512]{2,1,0:T(8,128)(2,1)S(1)}, u32[]{:S(2)}, u32[]{:S(2)}) collective-permute-start(bf16[2,256,512]{2,1,0:T(8,128)(2,1)S(1)} %get-tuple-element.83), channel_id=1, source_target_pairs={{0,1},{1,0},{2,3},{3,2},{4,5},{5,4},{6,7},{7,6},{8,9},{9,8},{10,11... | collective-permute-start | bytes 1572872 | tf_op jit(solution)/shard_map/ppermute | solution.py:400
  67.5 20.3 %collective-permute-start.7 = (bf16[2,256,512]{2,1,0:T(8,128)(2,1)S(1)}, bf16[2,256,512]{2,1,0:T(8,128)(2,1)S(1)}, u32[]{:S(2)}, u32[]{:S(2)}) collective-permute-start(bf16[2,256,512]{2,1,0:T(8,128)(2,1)S(1)} %get-tuple-element.84), channel_id=1, source_target_pairs={{0,3},{1,2},{2,1},{3,0},{4,7},{5,6},{6,5},{7,4},{8,11},{9,10},{10,... | collective-permute-start | bytes 1572872 | tf_op jit(solution)/shard_map/ppermute | solution.py:400
  76.7 22.7 %collective-permute-start.4 = (bf16[272,512]{1,0:T(8,128)(2,1)S(1)}, bf16[272,512]{1,0:T(8,128)(2,1)S(1)}, u32[]{:S(2)}, u32[]{:S(2)}) collective-permute-start(bf16[272,512]{1,0:T(8,128)(2,1)S(1)} %get-tuple-element.77), channel_id=1, source_target_pairs={{0,3},{1,2},{2,1},{3,0},{4,7},{5,6},{6,5},{7,4},{8,11},{9,10},{10,... | collective-permute-start | bytes 835592 | tf_op jit(solution)/shard_map/ppermute | solution.py:400
  79.0 20.4 %collective-permute-start.5 = (bf16[272,512]{1,0:T(8,128)(2,1)S(1)}, bf16[272,512]{1,0:T(8,128)(2,1)S(1)}, u32[]{:S(2)}, u32[]{:S(2)}) collective-permute-start(bf16[272,512]{1,0:T(8,128)(2,1)S(1)} %get-tuple-element.78), channel_id=1, source_target_pairs={{0,1},{1,0},{2,3},{3,2},{4,5},{5,4},{6,7},{7,6},{8,9},{9,8},{10,11... | collective-permute-start | bytes 835592 | tf_op jit(solution)/shard_map/ppermute | solution.py:400
  87.9 11.5 %collective-permute-start.8 = (bf16[256,512]{1,0:T(8,128)(2,1)S(1)}, bf16[256,512]{1,0:T(8,128)(2,1)S(1)}, u32[]{:S(2)}, u32[]{:S(2)}) collective-permute-start(bf16[256,512]{1,0:T(8,128)(2,1)S(1)} %get-tuple-element.88), channel_id=1, source_target_pairs={{0,3},{1,2},{2,1},{3,0},{4,7},{5,6},{6,5},{7,4},{8,11},{9,10},{10,... | collective-permute-start | bytes 786440 | tf_op jit(solution)/shard_map/ppermute | solution.py:400
  90.2 9.1 %collective-permute-start.9 = (bf16[256,512]{1,0:T(8,128)(2,1)S(1)}, bf16[256,512]{1,0:T(8,128)(2,1)S(1)}, u32[]{:S(2)}, u32[]{:S(2)}) collective-permute-start(bf16[256,512]{1,0:T(8,128)(2,1)S(1)} %get-tuple-element.89), channel_id=1, source_target_pairs={{0,1},{1,0},{2,3},{3,2},{4,5},{5,4},{6,7},{7,6},{8,9},{9,8},{10,11... | collective-permute-start | bytes 786440 | tf_op jit(solution)/shard_map/ppermute | solution.py:400
  (4 other events, 4.1 us)

commit v5 on v4

--- a/solution.py
+++ b/solution.py
@@ -22,7 +22,9 @@
 F32 = jnp.float32
 BF16 = jnp.bfloat16
 EXACT = lax.Precision.HIGHEST
+LOG2E = 1.4426950408889634
 CHUNKS = ((256, 256), (0, 256))
+LEADING = 0
 
 
 def softplus(v):
@@ -69,7 +71,20 @@
     return jnp.where(row == 10, lo, tail)
 
 
-def end_state_kernel(length, step_ref, decay_ref, values_ref, inject_ref, read_ref, keep_ref, send_ref, scaled):
+def end_state_kernel(
+    length, step_any, decay_ref, values_any, inject_any, read_ref, keep_ref, send_ref,
+    scaled, step_ref, values_ref, inject_ref, sems,
+):
+    copies = [
+        pltpu.make_async_copy(step_any, step_ref, sems.at[0]),
+        pltpu.make_async_copy(inject_any, inject_ref, sems.at[1]),
+    ]
+    for half in range(2):
+        lanes = slice(half * 1024, (half + 1) * 1024)
+        copies.append(pltpu.make_async_copy(values_any.at[:, lanes], values_ref.at[:, lanes], sems.at[2 + half]))
+    for copy in copies:
+        copy.start()
+    copies[0].wait()
     core = lax.axis_index("core")
     step = softplus(step_ref[...])
     logs = step * -jnp.exp(column(decay_ref[...]))
@@ -82,6 +97,7 @@
         after = after + jnp.sum(here, axis=1, keepdims=True)
     weight = tokens_first(jnp.exp(jnp.concatenate(parts[::-1], axis=1)) * step)
     total = tokens_first(jnp.broadcast_to(jnp.exp(after), (HEADS, 128)))[0:8]
+    copies[1].wait()
     inject_t = jnp.transpose(inject_ref[...].astype(F32)).astype(BF16)
     low = iota((TOK, 128), 1) < HEAD_DIM
     low_row = iota((8, 128), 1) < HEAD_DIM
@@ -96,6 +112,7 @@
             tail = jnp.where(row == 2 * core + s, picked, tail)
         tails.append(tail)
     for half in range(2):
+        copies[2 + half].wait()
         for q in range(8):
             pair = half * 8 + q
             lanes = slice(pair * 128, (pair + 1) * 128)
@@ -187,7 +204,7 @@
     step = softplus(step_ref[...])
     logs = step * -jnp.exp(column(decay_ref[...]))
     upto = (iota((BLOCK, BLOCK), 0) <= iota((BLOCK, BLOCK), 1)).astype(F32)
-    running = jnp.dot(logs, upto, precision=EXACT, preferred_element_type=F32)
+    running = jnp.dot(logs, upto, precision=EXACT, preferred_element_type=F32) * LOG2E
     running_t = tokens_first(running)
     step_t = tokens_first(step)
     read = read_ref[...]
@@ -204,24 +221,25 @@
         for h in (2 * pair, 2 * pair + 1):
             mine = jnp.broadcast_to(running_t[:, h : h + 1], (BLOCK, BLOCK))
             gap = jnp.where(causal, mine - running[h : h + 1, :], -1e30)
-            mixing.append((scores * jnp.exp(gap)).astype(BF16))
+            mixing.append((scores * jnp.exp2(gap)).astype(BF16))
             spread.append(mine)
         now = jnp.where(low, spread[0], spread[1])
-        grown = jnp.exp(now)
+        grown = jnp.exp2(now)
         values = values_ref[:, lanes].astype(F32)
         stepped = values * per_pair(step_t, pair, (BLOCK, 128), low)
         diagonal = jnp.concatenate([jnp.where(low, stepped, 0.0), jnp.where(low, 0.0, stepped)], axis=0)
         local = jnp.dot(
             jnp.concatenate(mixing, axis=1), diagonal.astype(BF16), preferred_element_type=F32
         )
-        out = local + carried[:, lanes] * grown + skip_ref[:, lanes] * values
+        skip = per_pair(skip_ref[...], pair, (1, 128), low[0:1])
+        out = local + carried[:, lanes] * grown + skip * values
         gate = gate_ref[:, lanes].astype(F32)
         gate = gate / (1.0 + jnp.exp(-gate))
         scaled_ref[:, lanes] = (out * gate).astype(BF16)
         gain_ref[:, lanes] = (gate * grown * before[0:1, lanes]).astype(BF16)
         end = now[BLOCK - 1 : BLOCK, :]
-        weighted[:, lanes] = (stepped * jnp.exp(end - now)).astype(BF16)
-        ends[0:1, lanes] = jnp.exp(end)
+        weighted[:, lanes] = (stepped * jnp.exp2(end - now)).astype(BF16)
+        ends[0:1, lanes] = jnp.exp2(end)
     state[...] = state[...] * ends[0:1, :] + jnp.dot(inject_t, weighted[...], preferred_element_type=F32)
     before[0:1, :] = before[0:1, :] * ends[0:1, :]
     if part == 0:
@@ -256,10 +274,12 @@
         scores = jnp.sum(inject_ref[s].astype(F32) * read, axis=1, keepdims=True)
         narrow.append(jnp.where(place <= last, scores * jnp.exp(gap) * step_t, 0.0))
         narrow.append(jnp.broadcast_to(jnp.exp(whole), (SLEN, 128)))
+    skip = jnp.concatenate([skip_ref[...], jnp.zeros((1, 128 - HEADS), F32)], axis=1)
+    narrow.append(jnp.broadcast_to(skip, (SLEN, 128)))
     spread = (iota((128, CH), 1) // HEAD_DIM == iota((128, CH), 0)).astype(BF16)
     parts = jnp.concatenate(three_parts(jnp.concatenate(narrow, axis=0)), axis=0).astype(BF16)
     wide = jnp.dot(parts, spread, preferred_element_type=F32)
-    wide = wide[0:64] + wide[64:128] + wide[128:192]
+    wide = wide[0:80] + wide[80:160] + wide[160:240]
     local_all = jnp.zeros((16, CH), F32)
     grown_all = jnp.zeros((16, CH), F32)
     gate_all = jnp.zeros((16, CH), F32)
@@ -268,7 +288,7 @@
         at_last = iota((SLEN, CH), 0) == length[s] - 1
         picked = jnp.sum(jnp.where(at_last, values, 0.0), axis=0, keepdims=True)
         gate = jnp.sum(jnp.where(at_last, gate_ref[s].astype(F32), 0.0), axis=0, keepdims=True)
-        local = jnp.sum(wide[32 * s : 32 * s + SLEN] * values, axis=0, keepdims=True) + skip_ref[...] * picked
+        local = jnp.sum(wide[32 * s : 32 * s + SLEN] * values, axis=0, keepdims=True) + wide[64:65] * picked
         local_all = jnp.where(row == s, local, local_all)
         grown_all = jnp.where(row == s, wide[32 * s + SLEN : 32 * s + SLEN + 1], grown_all)
         gate_all = jnp.where(row == s, gate / (1.0 + jnp.exp(-gate)), gate_all)
@@ -286,34 +306,42 @@
 REST = ((3, 0), (1, 1), (0, 0), (0, 1))
 
 
-def fetch_kernel(pieces, weight_ref, out_ref, sems):
+def column_copies(pieces, weight_ref, held, sems):
     z = lax.axis_index("head")
     copies = []
     for i, (flip, half) in enumerate(pieces):
         at = pl.multiple_of(((z ^ flip) * 2 + half) * PIECE, PIECE)
-        copies.append(pltpu.make_async_copy(weight_ref.at[:, pl.ds(at, PIECE)], out_ref.at[i], sems.at[i]))
+        copies.append(pltpu.make_async_copy(weight_ref.at[:, pl.ds(at, PIECE)], held.at[i], sems.at[i]))
     for copy in copies:
         copy.start()
-    for copy in copies:
+    return copies
+
+
+def fetch_kernel(pieces, weight_ref, out_ref, sems):
+    for copy in column_copies(pieces, weight_ref, out_ref, sems):
         copy.wait()
+
+
+def resident(x):
+    return pltpu.with_memory_space_constraint(x, pltpu.VMEM)
 
 
 def fetch(pieces, weight):
     out = pl.pallas_call(
         functools.partial(fetch_kernel, pieces),
-        out_shape=pltpu.VMEM((4, CH, PIECE), BF16),
+        out_shape=pltpu.VMEM((len(pieces), CH, PIECE), BF16),
         in_specs=[pl.BlockSpec(memory_space=pl.ANY)],
         out_specs=VMEM,
-        scratch_shapes=[pltpu.SemaphoreType.DMA((4,))],
+        scratch_shapes=[pltpu.SemaphoreType.DMA((len(pieces),))],
         compiler_params=pltpu.CompilerParams(vmem_limit_bytes=12 << 20),
         name="fetch_weight",
     )(*in_hbm(weight))
-    return pltpu.with_memory_space_constraint(out, pltpu.VMEM)
-
-
-def project(normed, weight_ref, outs):
-    for i, (ref, k) in enumerate(outs):
-        ref[k] = jnp.dot(normed[...], weight_ref[i], preferred_element_type=F32).astype(BF16)
+    return resident(out)
+
+
+def project(normed, columns, outs):
+    for column, (ref, k) in zip(columns, outs):
+        ref[k] = jnp.dot(normed[...], column[...], preferred_element_type=F32).astype(BF16)
 
 
 def gate_and_normalize(place, state_ref, read_ref, scaled_ref, gain_ref, norm_ref, normed):
@@ -336,10 +364,15 @@
         ).astype(BF16)
 
 
-def chunk_kernel(place, state_ref, read_ref, scaled_ref, gain_ref, norm_ref, weight_ref, *refs):
-    sample, (first_ref, second_ref, normed_ref) = refs[:-3], refs[-3:]
+def chunk_kernel(place, sampled, state_ref, read_ref, scaled_ref, gain_ref, norm_ref, near_ref, far_ref, *refs):
+    if place == LEADING:
+        *sample, first_ref, second_ref, normed_ref, held, sems = refs
+        copies = column_copies(FIRST[2:], far_ref, held, sems)
+    else:
+        *sample, first_ref, second_ref, normed_ref = refs
+        held = far_ref
     gate_and_normalize(place, state_ref, read_ref, scaled_ref, gain_ref, norm_ref, normed_ref)
-    if sample:
+    if sampled:
         local_ref, grown_ref, gate_ref = sample
         readings = state_ref[256:272, :].astype(F32)
         moved = jnp.concatenate([readings[2:16], readings[0:2]], axis=0)
@@ -347,11 +380,15 @@
         sampled = (local_ref[...] + readings * grown_ref[...]) * gate_ref[...]
         rows = CHUNKS[place][1]
         normed_ref[rows : rows + 16, :] = normalize(sampled, norm_ref[...])
-    project(normed_ref, weight_ref, ((first_ref, 0), (first_ref, 1), (second_ref, 0), (second_ref, 1)))
+    project(normed_ref, (near_ref.at[0], near_ref.at[1]), ((first_ref, 0), (first_ref, 1)))
+    for i in range(2):
+        if place == LEADING:
+            copies[i].wait()
+        project(normed_ref, (held.at[i],), ((second_ref, i),))
 
 
 def rest_kernel(normed_ref, weight_ref, rest_ref):
-    project(normed_ref, weight_ref, ((rest_ref, 1), (rest_ref, 3), (rest_ref, 0), (rest_ref, 2)))
+    project(normed_ref, [weight_ref.at[i] for i in range(4)], ((rest_ref, 1), (rest_ref, 3), (rest_ref, 0), (rest_ref, 2)))
 
 
 def onward_kernel(a_ref, b_ref, rest_ref, a_out, b_out):
@@ -360,15 +397,21 @@
 
 
 def finish_kernel(*refs):
-    ins, out_ref, sample_ref = refs[:-2], refs[-2], refs[-1]
+    ins, (out_ref, sample_ref, turned, sems) = refs[:-4], refs[-4:]
+    copies = []
     for place, (start, rows) in enumerate(CHUNKS):
         ra, rb, rest, sa, sb = ins[5 * place : 5 * place + 5]
         for half, (own, near, far) in enumerate(((0, ra, sa), (2, rb, sb))):
             total = rest[own].astype(F32) + near[0].astype(F32) + far[...].astype(F32)
             columns = slice(half * PIECE, (half + 1) * PIECE)
-            out_ref[columns, start : start + rows] = jnp.transpose(total[0:rows]).astype(BF16)
-            if place == 0:
+            here = (columns, slice(start, start + rows))
+            turned[here] = jnp.transpose(total[0:rows]).astype(BF16)
+            if place == LEADING:
                 sample_ref[:, columns] = total[rows : rows + 2].astype(BF16)
+            copies.append(pltpu.make_async_copy(turned.at[here], out_ref.at[here], sems.at[len(copies)]))
+            copies[-1].start()
+    for copy in copies:
+        copy.wait()
 
 
 def in_hbm(*arrays):
@@ -429,7 +472,7 @@
         grid=(blocks,),
         out_shape=results,
         in_specs=[
-            pl.BlockSpec((HEADS, BLOCK), lambda b: (0, b + part * blocks)), row(HEADS), row(CH),
+            pl.BlockSpec((HEADS, BLOCK), lambda b: (0, b + part * blocks)), row(HEADS), row(HEADS),
             tokens(CH), tokens(CH), tokens(STATE), tokens(STATE), *start_specs,
         ],
         out_specs=out_specs,
@@ -447,17 +490,25 @@
     inject = prompt_inject.reshape(TOK, STATE)
     read = prompt_read.reshape(TOK, STATE)
     decay = decay_log.reshape(1, HEADS)
-    skip = jnp.repeat(skip_gain, HEAD_DIM).reshape(1, CH)
+    skip = skip_gain.reshape(1, HEADS)
     norm = norm_weight.reshape(1, CH)
     s_read = sample_read.reshape(2, SLEN, STATE)
     s_inject = sample_inject.reshape(2, SLEN, STATE)
     slices_shape = shape((16, ROWS, 128))
 
-    keep, send = call(
-        end_state_kernel, "end_state", (slices_shape,) * 2,
-        (sample_length, *in_hbm(prompt_step, decay, prompt_values, inject, s_read)), 24, 1,
-        scratch_shapes=[pltpu.VMEM((TOK, 1024), BF16)],
-    )
+    anywhere = pl.BlockSpec(memory_space=pl.ANY)
+    keep, send = pl.pallas_call(
+        end_state_kernel,
+        out_shape=(slices_shape,) * 2,
+        in_specs=[SMEM, anywhere, VMEM, anywhere, anywhere, VMEM],
+        out_specs=(VMEM, VMEM),
+        scratch_shapes=[
+            pltpu.VMEM((TOK, 1024), BF16), pltpu.VMEM((HEADS, TOK), F32), pltpu.VMEM((TOK, CH), BF16),
+            pltpu.VMEM((TOK, STATE), BF16), pltpu.SemaphoreType.DMA((4,)),
+        ],
+        compiler_params=pltpu.CompilerParams(vmem_limit_bytes=24 << 20),
+        name="end_state",
+    )(*in_hbm(sample_length, prompt_step, decay, prompt_values, inject, s_read))
     sibling = other_core(send)
     joined = call(join_cores_kernel, "join_cores", slices_shape, (keep, sibling), 16)
     joined, step_1, s_step = lax.optimization_barrier((joined, prompt_step, sample_step.transpose(1, 0, 2)))
@@ -482,20 +533,28 @@
     )
     theirs = other_core(send)
 
-    first_columns = fetch(FIRST, weight)
+    near_columns = fetch(FIRST[:2], weight)
     scaled = (scaled_1, scaled_2)
     gain = (gain_1, gain_2)
     state = call(join_halves_kernel, "join_halves", shape((272, CH)), (mine, theirs), 8)
 
-    def chunk(place, *sample):
+    def chunk(place, far_columns, *sample):
         start, rows = CHUNKS[place]
         size = rows + (16 if sample else 0)
-        *sent, normed = call(
-            functools.partial(chunk_kernel, place), "chunk", (shape((2, size, PIECE)),) * 2 + (shape((size, CH)),),
-            (state, read, scaled[start // HALF], gain[start // HALF], norm, first_columns, *sample), 24,
-        )
-        near = lax.optimization_barrier((swap(sent[0], 1), swap(sent[1], 3)))
-        return normed, near
+        leading = place == LEADING
+        piece = shape((2, size, PIECE))
+        held = pltpu.VMEM((2, CH, PIECE), BF16)
+        first, second, normed, *held = pl.pallas_call(
+            functools.partial(chunk_kernel, place, bool(sample)),
+            out_shape=(piece, piece, shape((size, CH)), *([held] if leading else [])),
+            in_specs=[VMEM] * 6 + [anywhere if leading else VMEM] + [VMEM] * len(sample),
+            out_specs=(VMEM,) * (4 if leading else 3),
+            scratch_shapes=[pltpu.SemaphoreType.DMA((2,))] if leading else [],
+            compiler_params=pltpu.CompilerParams(vmem_limit_bytes=24 << 20),
+            name="chunk",
+        )(state, read, scaled[start // HALF], gain[start // HALF], norm, near_columns, far_columns, *sample)
+        near = lax.optimization_barrier((swap(first, 1), swap(second, 3)))
+        return normed, near, *held
 
     def exchange(normed, near, rest_columns):
         rest = call(rest_kernel, "rest", shape((4, normed.shape[0], PIECE)), (normed, rest_columns), 24)
@@ -503,16 +562,19 @@
         a_on, b_on = call(onward_kernel, "onward", (shape(a.shape[1:]),) * 2, (a, b, rest), 8)
         return (a, b, rest, *lax.optimization_barrier((swap(a_on, 3), swap(b_on, 1))))
 
-    normed_1, near_1 = chunk(1)
+    normed_0, near_0, far_columns = chunk(0, *in_hbm(weight), *sample)
     rest_columns = fetch(REST, weight)
-    normed_0, near_0 = chunk(0, *sample)
-    parts = [
-        exchange(normed, near, rest_columns)
-        for normed, near in ((normed_0, near_0), (normed_1, near_1))
-    ]
-    prompt_mixed, sample_mixed = call(
-        finish_kernel, "finish", (shape((1024, TOK)), shape((2, 1024))), tuple(sum(parts, ())), 16
-    )
+    normed_1, near_1 = chunk(1, resident(far_columns))
+    parts = exchange(normed_0, near_0, rest_columns) + exchange(normed_1, near_1, rest_columns)
+    prompt_mixed, sample_mixed = pl.pallas_call(
+        finish_kernel,
+        out_shape=(shape((1024, TOK)), shape((2, 1024))),
+        in_specs=[VMEM] * 10,
+        out_specs=(anywhere, VMEM),
+        scratch_shapes=[pltpu.VMEM((1024, TOK), BF16), pltpu.SemaphoreType.DMA((4,))],
+        compiler_params=pltpu.CompilerParams(vmem_limit_bytes=16 << 20),
+        name="finish",
+    )(*parts)
     return prompt_mixed, sample_mixed.T
 
 

time: 101 us -> 100 us (0.990)
  local copies, waits for them, and re-layouts: 4.1 us -> 1.86 us
  starting transfers between devices: 27.4 us -> 26.1 us
  waiting for transfers between devices: 22.5 us -> 23.7 us
  Pallas kernels: 46 us -> 47.1 us
    pallas_call x0 -> x4, Pallas kernels: none -> 15.6 us  [the longest x2 7.99 us: chunk(): pl.pallas_call(functools.partial(chunk_kernel, place, bool(sample)), out_...]
    pallas_call x13 -> x9, Pallas kernels: 23.7 us -> 10.3 us  [call(): pl.pallas_call(kernel, out_shape=out_shape, in_specs=[SMEM] * scalars + [...]
    unnamed x33 -> x27, local copies, waits for them, and re-layouts: 3.35 us -> 1.86 us
    pallas_call x2, Pallas kernels: 7.15 us -> 5.89 us  [fetch(): pl.pallas_call(functools.partial(fetch_kernel, pieces), out_shape=pltpu.V...]
    all_to_all x1, waiting for transfers between devices: 0.01 us -> 1.24 us  [per_device(): slices = lax.all_to_all(joined, ('y', 'x'), 0, 0, tiled=True)]
    all_to_all x1, starting transfers between devices: 6.65 us -> 5.43 us  [per_device(): back = lax.all_to_all(prefix, ('y', 'x'), 0, 0, tiled=True)]
  transfers between devices with their start and end apart: 12 -> 12, of which waited for: 7 -> 8; matrix products, arithmetic and copies ran while one was open for 1% -> 1% of each run, Pallas kernels for 32% -> 32%
where the time goes in v5:
time: 100 us; the launch traced here: 99.8 us
  Pallas kernels  47.1 us (47%)
  starting transfers between devices  26.1 us (26%)
  waiting for transfers between devices  23.7 us (24%)
  local copies, waits for them, and re-layouts  1.86 us (2%)
  between operations  1.01 us (1%)
    ppermute x8, waiting for transfers between devices, swap(): return lax.ppermute(x, 'head', [(i, i ^ step) for i in range(4)])  18 us
    pallas_call x2, Pallas kernels, local_outputs(): pl.pallas_call(functools.partial(local_kernel, part), grid=(blocks,), out...  15.3 us
    pallas_call x9, Pallas kernels, call(): pl.pallas_call(kernel, out_shape=out_shape, in_specs=[SMEM] * scalars + [...  10.3 us
    ppermute x8, starting transfers between devices, swap(): return lax.ppermute(x, 'head', [(i, i ^ step) for i in range(4)])  10 us
    pallas_call x2, Pallas kernels, chunk(): pl.pallas_call(functools.partial(chunk_kernel, place, bool(sample)), out_...  7.99 us
    all_to_all x1, starting transfers between devices, per_device(): slices = lax.all_to_all(joined, ('y', 'x'), 0, 0, tiled=True)  6.84 us
    pallas_call x2, Pallas kernels, fetch(): pl.pallas_call(functools.partial(fetch_kernel, pieces), out_shape=pltpu.V...  5.89 us
    pallas_call x1, Pallas kernels, per_device(): pl.pallas_call(end_state_kernel, out_shape=(slices_shape,) * 2, in_specs=...  5.75 us
  transfers between devices with their start and end apart: 12, of which 8 were waited for; matrix products, arithmetic and copies ran while one was open for 1% of the time, Pallas kernels for 32%

profile of v5, /device:TPU:1, one launch (start us, length us, event | category | flops | bytes accessed | tf_op | source)
XLA Modules:
  0.0 99.8 jit_solution(9567910921944395522)
XLA Ops:
  0.6 5.8 %end_state.1 = (bf16[16,144,128]{2,1,0:T(8,128)(2,1)S(1)}, bf16[16,144,128]{2,1,0:T(8,128)(2,1)S(1)}) custom-call(s32[2]{0:T(128)} %length.3, f32[32,512]{1,0:T(8,128)} %step_ref.1, f32[1,32]{1,0:T(1,128)} %bitcast.15, bf16[512,2048]{1,0:T(8,128)(2,1)} %values_ref.5, bf16[512,256]{1,0:T(8,128)(2,1)} %bitcast.22, bf16[2,16,256]{2,1,0:T(8,128)(2,1)} %bitcast.26), custom_call_target="tpu_custom_call" | custom-call | tf_op jit(solution)/shard_map/end_state/pallas_call | solution.py:500
  6.4 1.5 %collective-permute-start = (bf16[16,144,128]{2,1,0:T(8,128)(2,1)S(1)}, bf16[16,144,128]{2,1,0:T(8,128)(2,1)S(1)}, u32[]{:S(2)}, u32[]{:S(2)}) collective-permute-start(bf16[16,144,128]{2,1,0:T(8,128)(2,1)S(1)} %get-tuple-element.50), channel_id=1, source_target_pairs={{0,4},{4,0},{1,5},{5,1},{2,6},{6,2},{3,7},{7,3},{8,12},{12,8},{9,1... | collective-permute-start | bytes 1769480 | tf_op jit(solution)/shard_map/ppermute | solution.py:447
  10.7 6.8 %all-to-all-start = ((bf16[16,144,128]{2,1,0:T(8,128)(2,1)}), bf16[16,144,128]{2,1,0:T(8,128)(2,1)S(1)}, u32[]{:S(2)}, u32[]{:S(2)}) async-start(bf16[16,144,128]{2,1,0:T(8,128)(2,1)} %join_cores.1), calls=%async_computation | async-start | bytes 1179648 | tf_op jit(solution)/shard_map/all_to_all | solution.py:515
  17.5 2.4 %sample_outputs.1 = (f32[16,2048]{1,0:T(8,128)}, f32[16,2048]{1,0:T(8,128)}, f32[16,2048]{1,0:T(8,128)}) custom-call(s32[2]{0:T(128)S(1)} %copy-done.9, f32[2,32,16]{2,1,0:T(8,128)} %bitcast.25, f32[1,32]{1,0:T(1,128)} %bitcast.16, f32[1,32]{1,0:T(1,128)} %bitcast.19, bf16[2,16,2048]{2,1,0:T(8,128)(2,1)} %values_ref.4, bf16[2,16,2048]{2,1,0:T(8,128)(2,1)} %gate_ref.4, ...), custom_call_target="tpu_custom_call" | custom-call | flops 1 | bytes 1 | tf_op jit(solution)/shard_map/sample_outputs/pallas_call | solution.py:422
  19.9 7.7 %local_outputs.2 = (bf16[256,2048]{1,0:T(8,128)(2,1)}, bf16[256,2048]{1,0:T(8,128)(2,1)}, bf16[256,2048]{1,0:T(8,128)(2,1)}, f32[8,2048]{1,0:T(8,128)}) custom-call(f32[32,512]{1,0:T(8,128)} %step_ref.1, f32[1,32]{1,0:T(1,128)S(1)} %bitcast.17, f32[1,32]{1,0:T(1,128)S(1)} %bitcast.20, bf16[512,2048]{1,0:T(8,128)(2,1)} %values_ref.5, ...), custom_call_target="tpu_custom_call" | custom-call | flops 3221225472 | bytes 20971520 | tf_op jit(solution)/shard_map/local_outputs/pallas_call | solution.py:470
  30.1 5.4 %all-to-all-start.1 = ((bf16[16,144,128]{2,1,0:T(8,128)(2,1)}), bf16[16,144,128]{2,1,0:T(8,128)(2,1)S(1)}, u32[]{:S(2)}, u32[]{:S(2)}) async-start(bf16[16,144,128]{2,1,0:T(8,128)(2,1)} %prefix.1), calls=%async_computation.1 | async-start | bytes 1179648 | tf_op jit(solution)/shard_map/all_to_all | solution.py:526
  35.5 7.6 %local_outputs.3 = (bf16[256,2048]{1,0:T(8,128)(2,1)}, bf16[256,2048]{1,0:T(8,128)(2,1)}) custom-call(f32[32,512]{1,0:T(8,128)} %step_ref.1, f32[1,32]{1,0:T(1,128)S(1)} %bitcast.18, f32[1,32]{1,0:T(1,128)S(1)} %bitcast.21, bf16[512,2048]{1,0:T(8,128)(2,1)} %values_ref.5, bf16[512,2048]{1,0:T(8,128)(2,1)} %gate_ref.5, bf16[512,256]{1,0:T(8,128)(2,1)} %bitcast.24, ...), custom_call_target="tpu_custom_call" | custom-call | flops 3221225472 | bytes 20971520 | tf_op jit(solution)/shard_map/local_outputs/pallas_call | solution.py:470
  43.1 3.5 %all-to-all-done.1.back_ref = bf16[16,144,128]{2,1,0:T(8,128)(2,1)S(1)} async-done(((bf16[16,144,128]{2,1,0:T(8,128)(2,1)}), bf16[16,144,128]{2,1,0:T(8,128)(2,1)S(1)}, u32[]{:S(2)}, u32[]{:S(2)}) %all-to-all-start.1) | async-done | bytes 589856 | tf_op jit(solution)/shard_map/all_to_all | solution.py:526
  47.0 2.4 %collective-permute-start.1 = (bf16[16,144,128]{2,1,0:T(8,128)(2,1)S(1)}, bf16[16,144,128]{2,1,0:T(8,128)(2,1)S(1)}, u32[]{:S(2)}, u32[]{:S(2)}) collective-permute-start(bf16[16,144,128]{2,1,0:T(8,128)(2,1)S(1)} %get-tuple-element.66), channel_id=1, source_target_pairs={{0,4},{4,0},{1,5},{5,1},{2,6},{6,2},{3,7},{7,3},{8,12},{12,8},{9,1... | collective-permute-start | bytes 1769480 | tf_op jit(solution)/shard_map/ppermute | solution.py:447
  49.4 2.3 %fetch_weight.2.near_ref = bf16[2,2048,512]{2,1,0:T(8,128)(2,1)S(1)} custom-call(bf16[2048,4096]{1,0:T(8,128)(2,1)} %weight_ref.1), custom_call_target="tpu_custom_call" | custom-call | tf_op jit(solution)/shard_map/fetch_weight/pallas_call | solution.py:330
  53.1 4.9 %chunk.2 = (bf16[2,272,512]{2,1,0:T(8,128)(2,1)S(1)}, bf16[2,272,512]{2,1,0:T(8,128)(2,1)S(1)}, bf16[272,2048]{1,0:T(8,128)(2,1)S(1)}, bf16[2,2048,512]{2,1,0:T(8,128)(2,1)S(1)}) custom-call(bf16[272,2048]{1,0:T(8,128)(2,1)S(1)} %join_halves.1.state_ref, bf16[512,256]{1,0:T(8,128)(2,1)S(1)} %bitcast.11, bf16[256,2048]{1,0:T(8,128)(2,1)S(1)} %copy-done.3, ...), custom_call_target="tpu_custom_call" | custom-call | tf_op jit(solution)/shard_map/chunk/pallas_call | solution.py:547
  58.1 1.7 %collective-permute-start.2 = (bf16[2,272,512]{2,1,0:T(8,128)(2,1)S(1)}, bf16[2,272,512]{2,1,0:T(8,128)(2,1)S(1)}, u32[]{:S(2)}, u32[]{:S(2)}) collective-permute-start(bf16[2,272,512]{2,1,0:T(8,128)(2,1)S(1)} %get-tuple-element.73), channel_id=1, source_target_pairs={{0,1},{1,0},{2,3},{3,2},{4,5},{5,4},{6,7},{7,6},{8,9},{9,8},{10,11... | collective-permute-start | bytes 1671176 | tf_op jit(solution)/shard_map/ppermute | solution.py:443
  59.8 2.2 %collective-permute-start.3 = (bf16[2,272,512]{2,1,0:T(8,128)(2,1)S(1)}, bf16[2,272,512]{2,1,0:T(8,128)(2,1)S(1)}, u32[]{:S(2)}, u32[]{:S(2)}) collective-permute-start(bf16[2,272,512]{2,1,0:T(8,128)(2,1)S(1)} %get-tuple-element.74), channel_id=1, source_target_pairs={{0,3},{1,2},{2,1},{3,0},{4,7},{5,6},{6,5},{7,4},{8,11},{9,10},{10,... | collective-permute-start | bytes 1671176 | tf_op jit(solution)/shard_map/ppermute | solution.py:443
  62.0 3.1 %chunk.3 = (bf16[2,256,512]{2,1,0:T(8,128)(2,1)S(1)}, bf16[2,256,512]{2,1,0:T(8,128)(2,1)S(1)}, bf16[256,2048]{1,0:T(8,128)(2,1)S(1)}) custom-call(bf16[272,2048]{1,0:T(8,128)(2,1)S(1)} %join_halves.1.state_ref, bf16[512,256]{1,0:T(8,128)(2,1)S(1)} %bitcast.12, bf16[256,2048]{1,0:T(8,128)(2,1)S(1)} %copy-done.1, bf16[256,2048]{1,0:T(8,128)(2,1)S(1)} %copy-done.2, ...), custom_call_target="tpu_custom_call" | custom-call | tf_op jit(solution)/shard_map/chunk/pallas_call | solution.py:547
  66.5 3.5 %fetch_weight.3.weight_ref = bf16[4,2048,512]{2,1,0:T(8,128)(2,1)S(1)} custom-call(bf16[2048,4096]{1,0:T(8,128)(2,1)} %weight_ref.1), custom_call_target="tpu_custom_call" | custom-call | tf_op jit(solution)/shard_map/fetch_weight/pallas_call | solution.py:330
  70.1 2.5 %rest.2.rest_ref.refs_2_ = bf16[4,272,512]{2,1,0:T(8,128)(2,1)S(1)} custom-call(bf16[272,2048]{1,0:T(8,128)(2,1)S(1)} %get-tuple-element.77.normed_ref, bf16[4,2048,512]{2,1,0:T(8,128)(2,1)S(1)} %fetch_weight.3.weight_ref), custom_call_target="tpu_custom_call" | custom-call | flops 1 | bytes 1 | tf_op jit(solution)/shard_map/rest/pallas_call | solution.py:422
  72.7 2.3 %collective-permute-done.3.b_ref.refs_1_ = bf16[2,272,512]{2,1,0:T(8,128)(2,1)S(1)} collective-permute-done((bf16[2,272,512]{2,1,0:T(8,128)(2,1)S(1)}, bf16[2,272,512]{2,1,0:T(8,128)(2,1)S(1)}, u32[]{:S(2)}, u32[]{:S(2)}) %collective-permute-start.3) | collective-permute-done | bytes 557088 | tf_op jit(solution)/shard_map/ppermute | solution.py:443
  75.0 2.3 %collective-permute-start.4 = (bf16[272,512]{1,0:T(8,128)(2,1)S(1)}, bf16[272,512]{1,0:T(8,128)(2,1)S(1)}, u32[]{:S(2)}, u32[]{:S(2)}) collective-permute-start(bf16[272,512]{1,0:T(8,128)(2,1)S(1)} %get-tuple-element.78), channel_id=1, source_target_pairs={{0,3},{1,2},{2,1},{3,0},{4,7},{5,6},{6,5},{7,4},{8,11},{9,10},{10,... | collective-permute-start | bytes 835592 | tf_op jit(solution)/shard_map/ppermute | solution.py:443
  77.4 2.3 %rest.3.rest_ref.refs_7_ = bf16[4,256,512]{2,1,0:T(8,128)(2,1)S(1)} custom-call(bf16[256,2048]{1,0:T(8,128)(2,1)S(1)} %get-tuple-element.89.normed_ref, bf16[4,2048,512]{2,1,0:T(8,128)(2,1)S(1)} %fetch_weight.3.weight_ref), custom_call_target="tpu_custom_call" | custom-call | flops 1 | bytes 1 | tf_op jit(solution)/shard_map/rest/pallas_call | solution.py:422
  79.7 4.2 %collective-permute-done.6.a_ref.refs_5_ = bf16[2,256,512]{2,1,0:T(8,128)(2,1)S(1)} collective-permute-done((bf16[2,256,512]{2,1,0:T(8,128)(2,1)S(1)}, bf16[2,256,512]{2,1,0:T(8,128)(2,1)S(1)}, u32[]{:S(2)}, u32[]{:S(2)}) %collective-permute-start.6) | collective-permute-done | bytes 524320 | tf_op jit(solution)/shard_map/ppermute | solution.py:443
  83.9 2.3 %collective-permute-done.7.b_ref.refs_6_ = bf16[2,256,512]{2,1,0:T(8,128)(2,1)S(1)} collective-permute-done((bf16[2,256,512]{2,1,0:T(8,128)(2,1)S(1)}, bf16[2,256,512]{2,1,0:T(8,128)(2,1)S(1)}, u32[]{:S(2)}, u32[]{:S(2)}) %collective-permute-start.7) | collective-permute-done | bytes 524320 | tf_op jit(solution)/shard_map/ppermute | solution.py:443
  86.3 2.3 %collective-permute-start.8 = (bf16[256,512]{1,0:T(8,128)(2,1)S(1)}, bf16[256,512]{1,0:T(8,128)(2,1)S(1)}, u32[]{:S(2)}, u32[]{:S(2)}) collective-permute-start(bf16[256,512]{1,0:T(8,128)(2,1)S(1)} %get-tuple-element.90), channel_id=1, source_target_pairs={{0,3},{1,2},{2,1},{3,0},{4,7},{5,6},{6,5},{7,4},{8,11},{9,10},{10,... | collective-permute-start | bytes 786440 | tf_op jit(solution)/shard_map/ppermute | solution.py:443
  88.6 9.2 %collective-permute-done.8.refs_8_ = bf16[256,512]{1,0:T(8,128)(2,1)S(1)} collective-permute-done((bf16[256,512]{1,0:T(8,128)(2,1)S(1)}, bf16[256,512]{1,0:T(8,128)(2,1)S(1)}, u32[]{:S(2)}, u32[]{:S(2)}) %collective-permute-start.8) | collective-permute-done | bytes 262176 | tf_op jit(solution)/shard_map/ppermute | solution.py:443
  97.8 1.9 %finish.1 = (bf16[1024,512]{1,0:T(8,128)(2,1)}, bf16[2,1024]{1,0:T(2,128)(2,1)}) custom-call(bf16[2,272,512]{2,1,0:T(8,128)(2,1)S(1)} %collective-permute-done.2.a_ref.refs_0_, bf16[2,272,512]{2,1,0:T(8,128)(2,1)S(1)} %collective-permute-done.3.b_ref.refs_1_, bf16[4,272,512]{2,1,0:T(8,128)(2,1)S(1)} %rest.2.rest_ref.refs_2_, ...), custom_call_target="tpu_custom_call" | custom-call | tf_op jit(solution)/shard_map/finish/pallas_call | solution.py:569
  (44 shorter events, 8.7 us)
Async XLA Ops:
  0.6 7.3 %copy-start.12 = (f32[32,2,16]{0,2,1:T(8,128)S(1)}, f32[32,2,16]{0,2,1:T(8,128)}, u32[]{:S(2)}) copy-start(f32[32,2,16]{0,2,1:T(8,128)} %param.28) | copy-start | bytes 12292
  6.4 11.1 %copy-start.9 = (s32[2]{0:T(128)S(1)}, s32[2]{0:T(128)}, u32[]{:S(2)}) copy-start(s32[2]{0:T(128)} %length.3) | copy-start | bytes 28
  6.4 13.5 %copy-start.10 = (f32[32]{0:T(128)S(1)}, f32[32]{0:T(128)}, u32[]{:S(2)}) copy-start(f32[32]{0:T(128)} %param.20) | copy-start | bytes 388
  6.4 13.5 %copy-start.11 = (f32[32]{0:T(128)S(1)}, f32[32]{0:T(128)}, u32[]{:S(2)}) copy-start(f32[32]{0:T(128)} %param.21) | copy-start | bytes 388
  6.4 3.1 %collective-permute-start = (bf16[16,144,128]{2,1,0:T(8,128)(2,1)S(1)}, bf16[16,144,128]{2,1,0:T(8,128)(2,1)S(1)}, u32[]{:S(2)}, u32[]{:S(2)}) collective-permute-start(bf16[16,144,128]{2,1,0:T(8,128)(2,1)S(1)} %get-tuple-element.50), channel_id=1, source_target_pairs={{0,4},{4,0},{1,5},{5,1},{2,6},{6,2},{3,7},{7,3},{8,12},{12,8},{9,1... | collective-permute-start | bytes 1769480 | tf_op jit(solution)/shard_map/ppermute | solution.py:447
  10.7 18.3 %all-to-all-start = ((bf16[16,144,128]{2,1,0:T(8,128)(2,1)}), bf16[16,144,128]{2,1,0:T(8,128)(2,1)S(1)}, u32[]{:S(2)}, u32[]{:S(2)}) async-start(bf16[16,144,128]{2,1,0:T(8,128)(2,1)} %join_cores.1), calls=%async_computation | async-start | bytes 1179648 | tf_op jit(solution)/shard_map/all_to_all | solution.py:515
  30.1 16.5 %all-to-all-start.1 = ((bf16[16,144,128]{2,1,0:T(8,128)(2,1)}), bf16[16,144,128]{2,1,0:T(8,128)(2,1)S(1)}, u32[]{:S(2)}, u32[]{:S(2)}) async-start(bf16[16,144,128]{2,1,0:T(8,128)(2,1)} %prefix.1), calls=%async_computation.1 | async-start | bytes 1179648 | tf_op jit(solution)/shard_map/all_to_all | solution.py:526
  47.0 4.8 %collective-permute-start.1 = (bf16[16,144,128]{2,1,0:T(8,128)(2,1)S(1)}, bf16[16,144,128]{2,1,0:T(8,128)(2,1)S(1)}, u32[]{:S(2)}, u32[]{:S(2)}) collective-permute-start(bf16[16,144,128]{2,1,0:T(8,128)(2,1)S(1)} %get-tuple-element.66), channel_id=1, source_target_pairs={{0,4},{4,0},{1,5},{5,1},{2,6},{6,2},{3,7},{7,3},{8,12},{12,8},{9,1... | collective-permute-start | bytes 1769480 | tf_op jit(solution)/shard_map/ppermute | solution.py:447
  49.4 2.6 %copy-start.4 = (bf16[256,2048]{1,0:T(8,128)(2,1)S(1)}, bf16[256,2048]{1,0:T(8,128)(2,1)}, u32[]{:S(2)}) copy-start(bf16[256,2048]{1,0:T(8,128)(2,1)} %get-tuple-element.68.gain_ref) | copy-start | bytes 3145732
  51.7 1.3 %copy-start.3 = (bf16[256,2048]{1,0:T(8,128)(2,1)S(1)}, bf16[256,2048]{1,0:T(8,128)(2,1)}, u32[]{:S(2)}) copy-start(bf16[256,2048]{1,0:T(8,128)(2,1)} %get-tuple-element.67.scaled_ref) | copy-start | bytes 3145732
  51.7 1.3 %copy-start.5 = (f32[16,2048]{1,0:T(8,128)S(1)}, f32[16,2048]{1,0:T(8,128)}, u32[]{:S(2)}) copy-start(f32[16,2048]{1,0:T(8,128)} %get-tuple-element.70.refs_0_) | copy-start | bytes 393220
  51.7 1.3 %copy-start.6 = (f32[16,2048]{1,0:T(8,128)S(1)}, f32[16,2048]{1,0:T(8,128)}, u32[]{:S(2)}) copy-start(f32[16,2048]{1,0:T(8,128)} %get-tuple-element.71.refs_1_) | copy-start | bytes 393220
  51.8 1.4 %copy-start.7 = (f32[16,2048]{1,0:T(8,128)S(1)}, f32[16,2048]{1,0:T(8,128)}, u32[]{:S(2)}) copy-start(f32[16,2048]{1,0:T(8,128)} %get-tuple-element.72.refs_2_) | copy-start | bytes 393220
  51.8 1.4 %copy-start.8 = (f32[2048]{0:T(1024)S(1)}, f32[2048]{0:T(1024)}, u32[]{:S(2)}) copy-start(f32[2048]{0:T(1024)} %param.22) | copy-start | bytes 24580
  53.1 8.9 %copy-start.1 = (bf16[256,2048]{1,0:T(8,128)(2,1)S(1)}, bf16[256,2048]{1,0:T(8,128)(2,1)}, u32[]{:S(2)}) copy-start(bf16[256,2048]{1,0:T(8,128)(2,1)} %get-tuple-element.82.scaled_ref) | copy-start | bytes 3145732
  53.1 8.9 %copy-start.2 = (bf16[256,2048]{1,0:T(8,128)(2,1)S(1)}, bf16[256,2048]{1,0:T(8,128)(2,1)}, u32[]{:S(2)}) copy-start(bf16[256,2048]{1,0:T(8,128)(2,1)} %get-tuple-element.83.gain_ref) | copy-start | bytes 3145732
  58.1 14.6 %collective-permute-start.2 = (bf16[2,272,512]{2,1,0:T(8,128)(2,1)S(1)}, bf16[2,272,512]{2,1,0:T(8,128)(2,1)S(1)}, u32[]{:S(2)}, u32[]{:S(2)}) collective-permute-start(bf16[2,272,512]{2,1,0:T(8,128)(2,1)S(1)} %get-tuple-element.73), channel_id=1, source_target_pairs={{0,1},{1,0},{2,3},{3,2},{4,5},{5,4},{6,7},{7,6},{8,9},{9,8},{10,11... | collective-permute-start | bytes 1671176 | tf_op jit(solution)/shard_map/ppermute | solution.py:443
  59.8 15.1 %collective-permute-start.3 = (bf16[2,272,512]{2,1,0:T(8,128)(2,1)S(1)}, bf16[2,272,512]{2,1,0:T(8,128)(2,1)S(1)}, u32[]{:S(2)}, u32[]{:S(2)}) collective-permute-start(bf16[2,272,512]{2,1,0:T(8,128)(2,1)S(1)} %get-tuple-element.74), channel_id=1, source_target_pairs={{0,3},{1,2},{2,1},{3,0},{4,7},{5,6},{6,5},{7,4},{8,11},{9,10},{10,... | collective-permute-start | bytes 1671176 | tf_op jit(solution)/shard_map/ppermute | solution.py:443
  65.1 18.8 %collective-permute-start.6 = (bf16[2,256,512]{2,1,0:T(8,128)(2,1)S(1)}, bf16[2,256,512]{2,1,0:T(8,128)(2,1)S(1)}, u32[]{:S(2)}, u32[]{:S(2)}) collective-permute-start(bf16[2,256,512]{2,1,0:T(8,128)(2,1)S(1)} %get-tuple-element.85), channel_id=1, source_target_pairs={{0,1},{1,0},{2,3},{3,2},{4,5},{5,4},{6,7},{7,6},{8,9},{9,8},{10,11... | collective-permute-start | bytes 1572872 | tf_op jit(solution)/shard_map/ppermute | solution.py:443
  65.9 20.2 %collective-permute-start.7 = (bf16[2,256,512]{2,1,0:T(8,128)(2,1)S(1)}, bf16[2,256,512]{2,1,0:T(8,128)(2,1)S(1)}, u32[]{:S(2)}, u32[]{:S(2)}) collective-permute-start(bf16[2,256,512]{2,1,0:T(8,128)(2,1)S(1)} %get-tuple-element.86), channel_id=1, source_target_pairs={{0,3},{1,2},{2,1},{3,0},{4,7},{5,6},{6,5},{7,4},{8,11},{9,10},{10,... | collective-permute-start | bytes 1572872 | tf_op jit(solution)/shard_map/ppermute | solution.py:443
  75.0 22.7 %collective-permute-start.4 = (bf16[272,512]{1,0:T(8,128)(2,1)S(1)}, bf16[272,512]{1,0:T(8,128)(2,1)S(1)}, u32[]{:S(2)}, u32[]{:S(2)}) collective-permute-start(bf16[272,512]{1,0:T(8,128)(2,1)S(1)} %get-tuple-element.78), channel_id=1, source_target_pairs={{0,3},{1,2},{2,1},{3,0},{4,7},{5,6},{6,5},{7,4},{8,11},{9,10},{10,... | collective-permute-start | bytes 835592 | tf_op jit(solution)/shard_map/ppermute | solution.py:443
  77.4 20.4 %collective-permute-start.5 = (bf16[272,512]{1,0:T(8,128)(2,1)S(1)}, bf16[272,512]{1,0:T(8,128)(2,1)S(1)}, u32[]{:S(2)}, u32[]{:S(2)}) collective-permute-start(bf16[272,512]{1,0:T(8,128)(2,1)S(1)} %get-tuple-element.79), channel_id=1, source_target_pairs={{0,1},{1,0},{2,3},{3,2},{4,5},{5,4},{6,7},{7,6},{8,9},{9,8},{10,11... | collective-permute-start | bytes 835592 | tf_op jit(solution)/shard_map/ppermute | solution.py:443
  86.3 11.5 %collective-permute-start.8 = (bf16[256,512]{1,0:T(8,128)(2,1)S(1)}, bf16[256,512]{1,0:T(8,128)(2,1)S(1)}, u32[]{:S(2)}, u32[]{:S(2)}) collective-permute-start(bf16[256,512]{1,0:T(8,128)(2,1)S(1)} %get-tuple-element.90), channel_id=1, source_target_pairs={{0,3},{1,2},{2,1},{3,0},{4,7},{5,6},{6,5},{7,4},{8,11},{9,10},{10,... | collective-permute-start | bytes 786440 | tf_op jit(solution)/shard_map/ppermute | solution.py:443
  88.6 9.2 %collective-permute-start.9 = (bf16[256,512]{1,0:T(8,128)(2,1)S(1)}, bf16[256,512]{1,0:T(8,128)(2,1)S(1)}, u32[]{:S(2)}, u32[]{:S(2)}) collective-permute-start(bf16[256,512]{1,0:T(8,128)(2,1)S(1)} %get-tuple-element.91), channel_id=1, source_target_pairs={{0,1},{1,0},{2,3},{3,2},{4,5},{5,4},{6,7},{7,6},{8,9},{9,8},{10,11... | collective-permute-start | bytes 786440 | tf_op jit(solution)/shard_map/ppermute | solution.py:443
  (1 other events, 1.0 us)

commit v6 on v5

--- a/solution.py
+++ b/solution.py
@@ -23,7 +23,7 @@
 BF16 = jnp.bfloat16
 EXACT = lax.Precision.HIGHEST
 LOG2E = 1.4426950408889634
-CHUNKS = ((256, 256), (0, 256))
+CHUNKS = ((256, 256), (0, 128), (128, 128))
 LEADING = 0
 
 
@@ -391,18 +391,27 @@
     project(normed_ref, [weight_ref.at[i] for i in range(4)], ((rest_ref, 1), (rest_ref, 3), (rest_ref, 0), (rest_ref, 2)))
 
 
-def onward_kernel(a_ref, b_ref, rest_ref, a_out, b_out):
-    a_out[...] = (rest_ref[1].astype(F32) + a_ref[1].astype(F32)).astype(BF16)
-    b_out[...] = (rest_ref[3].astype(F32) + b_ref[1].astype(F32)).astype(BF16)
+def onward_kernel(*refs):
+    ins, (a_out, b_out) = refs[:-2], refs[-2:]
+    start = 0
+    for a_ref, b_ref, rest_ref in (ins[i : i + 3] for i in range(0, len(ins), 3)):
+        rows = slice(start, start + a_ref.shape[1])
+        a_out[rows, :] = (rest_ref[1].astype(F32) + a_ref[1].astype(F32)).astype(BF16)
+        b_out[rows, :] = (rest_ref[3].astype(F32) + b_ref[1].astype(F32)).astype(BF16)
+        start = rows.stop
 
 
 def finish_kernel(*refs):
     ins, (out_ref, sample_ref, turned, sems) = refs[:-4], refs[-4:]
     copies = []
+    skipped = 0
     for place, (start, rows) in enumerate(CHUNKS):
-        ra, rb, rest, sa, sb = ins[5 * place : 5 * place + 5]
+        ra, rb, rest = ins[3 * place : 3 * place + 3]
+        sa, sb = ins[9:11] if place == 0 else ins[11:13]
+        size = ra.shape[1]
+        skipped = skipped if place > 1 else 0
         for half, (own, near, far) in enumerate(((0, ra, sa), (2, rb, sb))):
-            total = rest[own].astype(F32) + near[0].astype(F32) + far[...].astype(F32)
+            total = rest[own].astype(F32) + near[0].astype(F32) + far[skipped : skipped + size, :].astype(F32)
             columns = slice(half * PIECE, (half + 1) * PIECE)
             here = (columns, slice(start, start + rows))
             turned[here] = jnp.transpose(total[0:rows]).astype(BF16)
@@ -410,6 +419,7 @@
                 sample_ref[:, columns] = total[rows : rows + 2].astype(BF16)
             copies.append(pltpu.make_async_copy(turned.at[here], out_ref.at[here], sems.at[len(copies)]))
             copies[-1].start()
+        skipped += size
     for copy in copies:
         copy.wait()
 
@@ -538,7 +548,7 @@
     gain = (gain_1, gain_2)
     state = call(join_halves_kernel, "join_halves", shape((272, CH)), (mine, theirs), 8)
 
-    def chunk(place, far_columns, *sample):
+    def chunk(place, norm, far_columns, *sample):
         start, rows = CHUNKS[place]
         size = rows + (16 if sample else 0)
         leading = place == LEADING
@@ -556,25 +566,39 @@
         near = lax.optimization_barrier((swap(first, 1), swap(second, 3)))
         return normed, near, *held
 
-    def exchange(normed, near, rest_columns):
-        rest = call(rest_kernel, "rest", shape((4, normed.shape[0], PIECE)), (normed, rest_columns), 24)
-        a, b = near
-        a_on, b_on = call(onward_kernel, "onward", (shape(a.shape[1:]),) * 2, (a, b, rest), 8)
-        return (a, b, rest, *lax.optimization_barrier((swap(a_on, 3), swap(b_on, 1))))
-
-    normed_0, near_0, far_columns = chunk(0, *in_hbm(weight), *sample)
+    normed_0, near_0, far_columns = chunk(0, norm, *in_hbm(weight), *sample)
     rest_columns = fetch(REST, weight)
-    normed_1, near_1 = chunk(1, resident(far_columns))
-    parts = exchange(normed_0, near_0, rest_columns) + exchange(normed_1, near_1, rest_columns)
+    far_columns = resident(far_columns)
+
+    def rest_of(normed):
+        return call(rest_kernel, "rest", shape((4, normed.shape[0], PIECE)), (normed, rest_columns), 24)
+
+    normed_1, near_1 = chunk(1, norm, far_columns)
+    rest_0 = rest_of(normed_0)
+    rest_0, norm = lax.optimization_barrier((rest_0, norm))
+    normed_2, near_2 = chunk(2, norm, far_columns)
+    near = [near_0, near_1, near_2]
+    rests = [rest_0, rest_of(normed_1), rest_of(normed_2)]
+    parts = [(*near[c], rests[c]) for c in range(3)]
+
+    def onward(*parts):
+        rows = sum(part[0].shape[1] for part in parts)
+        return call(onward_kernel, "onward", (shape((rows, PIECE)),) * 2, sum(parts, ()), 8)
+
+    def send_on(ons):
+        return lax.optimization_barrier((swap(ons[0], 3), swap(ons[1], 1)))
+
+    ons, parts[1] = lax.optimization_barrier((onward(parts[0]), parts[1]))
+    far = (*send_on(ons), *send_on(onward(*parts[1:])))
     prompt_mixed, sample_mixed = pl.pallas_call(
         finish_kernel,
         out_shape=(shape((1024, TOK)), shape((2, 1024))),
-        in_specs=[VMEM] * 10,
+        in_specs=[VMEM] * 13,
         out_specs=(anywhere, VMEM),
-        scratch_shapes=[pltpu.VMEM((1024, TOK), BF16), pltpu.SemaphoreType.DMA((4,))],
+        scratch_shapes=[pltpu.VMEM((1024, TOK), BF16), pltpu.SemaphoreType.DMA((6,))],
         compiler_params=pltpu.CompilerParams(vmem_limit_bytes=16 << 20),
         name="finish",
-    )(*parts)
+    )(*sum(parts, ()), *far)
     return prompt_mixed, sample_mixed.T
 
 

time: 100 us -> 102 us (1.020)
  starting transfers between devices: 26.1 us -> 27.8 us
  waiting for transfers between devices: 23.7 us -> 22.5 us
    ppermute x8 -> x10, starting transfers between devices: 10 us -> 11.7 us  [swap(): return lax.ppermute(x, 'head', [(i, i ^ step) for i in range(4)])]
    ppermute x8 -> x10, waiting for transfers between devices: 18 us -> 16.8 us  [swap(): return lax.ppermute(x, 'head', [(i, i ^ step) for i in range(4)])]
    pallas_call x2 -> x3, Pallas kernels: 7.99 us -> 8.3 us  [chunk(): pl.pallas_call(functools.partial(chunk_kernel, place, bool(sample)), out_...]
    pallas_call x9 -> x10, Pallas kernels: 10.3 us -> 10.5 us  [call(): pl.pallas_call(kernel, out_shape=out_shape, in_specs=[SMEM] * scalars + [...]
  transfers between devices with their start and end apart: 12 -> 14, of which waited for: 8 -> 6; matrix products, arithmetic and copies ran while one was open for 1% -> 1% of each run, Pallas kernels for 32% -> 32%
where the time goes in v6:
time: 102 us; the launch traced here: 101 us
  Pallas kernels  47.6 us (47%)
  starting transfers between devices  27.8 us (27%)
  waiting for transfers between devices  22.5 us (22%)
  local copies, waits for them, and re-layouts  1.86 us (2%)
  between operations  1.08 us (1%)
    ppermute x10, waiting for transfers between devices, swap(): return lax.ppermute(x, 'head', [(i, i ^ step) for i in range(4)])  16.8 us
    pallas_call x2, Pallas kernels, local_outputs(): pl.pallas_call(functools.partial(local_kernel, part), grid=(blocks,), out...  15.3 us
    ppermute x10, starting transfers between devices, swap(): return lax.ppermute(x, 'head', [(i, i ^ step) for i in range(4)])  11.7 us
    pallas_call x10, Pallas kernels, call(): pl.pallas_call(kernel, out_shape=out_shape, in_specs=[SMEM] * scalars + [...  10.5 us
    pallas_call x3, Pallas kernels, chunk(): pl.pallas_call(functools.partial(chunk_kernel, place, bool(sample)), out_...  8.3 us
    all_to_all x1, starting transfers between devices, per_device(): slices = lax.all_to_all(joined, ('y', 'x'), 0, 0, tiled=True)  6.84 us
    pallas_call x2, Pallas kernels, fetch(): pl.pallas_call(functools.partial(fetch_kernel, pieces), out_shape=pltpu.V...  5.89 us
    pallas_call x1, Pallas kernels, per_device(): pl.pallas_call(end_state_kernel, out_shape=(slices_shape,) * 2, in_specs=...  5.75 us
  transfers between devices with their start and end apart: 14, of which 6 were waited for; matrix products, arithmetic and copies ran while one was open for 1% of the time, Pallas kernels for 32%

profile of v6, /device:TPU:1, one launch (start us, length us, event | category | flops | bytes accessed | tf_op | source)
XLA Modules:
  0.0 100.9 jit_solution(14124322877241618076)
XLA Ops:
  0.6 5.8 %end_state.1 = (bf16[16,144,128]{2,1,0:T(8,128)(2,1)S(1)}, bf16[16,144,128]{2,1,0:T(8,128)(2,1)S(1)}) custom-call(s32[2]{0:T(128)} %length.3, f32[32,512]{1,0:T(8,128)} %step_ref.1, f32[1,32]{1,0:T(1,128)} %bitcast.17, bf16[512,2048]{1,0:T(8,128)(2,1)} %values_ref.5, bf16[512,256]{1,0:T(8,128)(2,1)} %bitcast.24, bf16[2,16,256]{2,1,0:T(8,128)(2,1)} %bitcast.28), custom_call_target="tpu_custom_call" | custom-call | tf_op jit(solution)/shard_map/end_state/pallas_call | solution.py:510
  6.4 1.5 %collective-permute-start = (bf16[16,144,128]{2,1,0:T(8,128)(2,1)S(1)}, bf16[16,144,128]{2,1,0:T(8,128)(2,1)S(1)}, u32[]{:S(2)}, u32[]{:S(2)}) collective-permute-start(bf16[16,144,128]{2,1,0:T(8,128)(2,1)S(1)} %get-tuple-element.62), channel_id=1, source_target_pairs={{0,4},{4,0},{1,5},{5,1},{2,6},{6,2},{3,7},{7,3},{8,12},{12,8},{9,1... | collective-permute-start | bytes 1769480 | tf_op jit(solution)/shard_map/ppermute | solution.py:457
  10.7 6.8 %all-to-all-start = ((bf16[16,144,128]{2,1,0:T(8,128)(2,1)}), bf16[16,144,128]{2,1,0:T(8,128)(2,1)S(1)}, u32[]{:S(2)}, u32[]{:S(2)}) async-start(bf16[16,144,128]{2,1,0:T(8,128)(2,1)} %join_cores.1), calls=%async_computation | async-start | bytes 1179648 | tf_op jit(solution)/shard_map/all_to_all | solution.py:525
  17.5 2.4 %sample_outputs.1 = (f32[16,2048]{1,0:T(8,128)}, f32[16,2048]{1,0:T(8,128)}, f32[16,2048]{1,0:T(8,128)}) custom-call(s32[2]{0:T(128)S(1)} %copy-done.9, f32[2,32,16]{2,1,0:T(8,128)} %bitcast.27, f32[1,32]{1,0:T(1,128)} %bitcast.18, f32[1,32]{1,0:T(1,128)} %bitcast.21, bf16[2,16,2048]{2,1,0:T(8,128)(2,1)} %values_ref.4, bf16[2,16,2048]{2,1,0:T(8,128)(2,1)} %gate_ref.4, ...), custom_call_target="tpu_custom_call" | custom-call | flops 1 | bytes 1 | tf_op jit(solution)/shard_map/sample_outputs/pallas_call | solution.py:432
  19.9 7.7 %local_outputs.2 = (bf16[256,2048]{1,0:T(8,128)(2,1)}, bf16[256,2048]{1,0:T(8,128)(2,1)}, bf16[256,2048]{1,0:T(8,128)(2,1)}, f32[8,2048]{1,0:T(8,128)}) custom-call(f32[32,512]{1,0:T(8,128)} %step_ref.1, f32[1,32]{1,0:T(1,128)S(1)} %bitcast.19, f32[1,32]{1,0:T(1,128)S(1)} %bitcast.22, bf16[512,2048]{1,0:T(8,128)(2,1)} %values_ref.5, ...), custom_call_target="tpu_custom_call" | custom-call | flops 3221225472 | bytes 20971520 | tf_op jit(solution)/shard_map/local_outputs/pallas_call | solution.py:480
  30.1 5.4 %all-to-all-start.1 = ((bf16[16,144,128]{2,1,0:T(8,128)(2,1)}), bf16[16,144,128]{2,1,0:T(8,128)(2,1)S(1)}, u32[]{:S(2)}, u32[]{:S(2)}) async-start(bf16[16,144,128]{2,1,0:T(8,128)(2,1)} %prefix.1), calls=%async_computation.1 | async-start | bytes 1179648 | tf_op jit(solution)/shard_map/all_to_all | solution.py:536
  35.6 7.6 %local_outputs.3 = (bf16[256,2048]{1,0:T(8,128)(2,1)}, bf16[256,2048]{1,0:T(8,128)(2,1)}) custom-call(f32[32,512]{1,0:T(8,128)} %step_ref.1, f32[1,32]{1,0:T(1,128)S(1)} %bitcast.20, f32[1,32]{1,0:T(1,128)S(1)} %bitcast.23, bf16[512,2048]{1,0:T(8,128)(2,1)} %values_ref.5, bf16[512,2048]{1,0:T(8,128)(2,1)} %gate_ref.5, bf16[512,256]{1,0:T(8,128)(2,1)} %bitcast.26, ...), custom_call_target="tpu_custom_call" | custom-call | flops 3221225472 | bytes 20971520 | tf_op jit(solution)/shard_map/local_outputs/pallas_call | solution.py:480
  43.1 3.5 %all-to-all-done.1.back_ref = bf16[16,144,128]{2,1,0:T(8,128)(2,1)S(1)} async-done(((bf16[16,144,128]{2,1,0:T(8,128)(2,1)}), bf16[16,144,128]{2,1,0:T(8,128)(2,1)S(1)}, u32[]{:S(2)}, u32[]{:S(2)}) %all-to-all-start.1) | async-done | bytes 589856 | tf_op jit(solution)/shard_map/all_to_all | solution.py:536
  47.0 2.4 %collective-permute-start.1 = (bf16[16,144,128]{2,1,0:T(8,128)(2,1)S(1)}, bf16[16,144,128]{2,1,0:T(8,128)(2,1)S(1)}, u32[]{:S(2)}, u32[]{:S(2)}) collective-permute-start(bf16[16,144,128]{2,1,0:T(8,128)(2,1)S(1)} %get-tuple-element.78), channel_id=1, source_target_pairs={{0,4},{4,0},{1,5},{5,1},{2,6},{6,2},{3,7},{7,3},{8,12},{12,8},{9,1... | collective-permute-start | bytes 1769480 | tf_op jit(solution)/shard_map/ppermute | solution.py:457
  49.4 2.3 %fetch_weight.2.near_ref = bf16[2,2048,512]{2,1,0:T(8,128)(2,1)S(1)} custom-call(bf16[2048,4096]{1,0:T(8,128)(2,1)} %weight_ref.1), custom_call_target="tpu_custom_call" | custom-call | tf_op jit(solution)/shard_map/fetch_weight/pallas_call | solution.py:330
  53.1 4.9 %chunk.3 = (bf16[2,272,512]{2,1,0:T(8,128)(2,1)S(1)}, bf16[2,272,512]{2,1,0:T(8,128)(2,1)S(1)}, bf16[272,2048]{1,0:T(8,128)(2,1)S(1)}, bf16[2,2048,512]{2,1,0:T(8,128)(2,1)S(1)}) custom-call(bf16[272,2048]{1,0:T(8,128)(2,1)S(1)} %join_halves.1.state_ref, bf16[512,256]{1,0:T(8,128)(2,1)S(1)} %bitcast.11, bf16[256,2048]{1,0:T(8,128)(2,1)S(1)} %copy-done.3, ...), custom_call_target="tpu_custom_call" | custom-call | tf_op jit(solution)/shard_map/chunk/pallas_call | solution.py:557
  58.1 1.7 %collective-permute-start.2 = (bf16[2,272,512]{2,1,0:T(8,128)(2,1)S(1)}, bf16[2,272,512]{2,1,0:T(8,128)(2,1)S(1)}, u32[]{:S(2)}, u32[]{:S(2)}) collective-permute-start(bf16[2,272,512]{2,1,0:T(8,128)(2,1)S(1)} %get-tuple-element.85), channel_id=1, source_target_pairs={{0,1},{1,0},{2,3},{3,2},{4,5},{5,4},{6,7},{7,6},{8,9},{9,8},{10,11... | collective-permute-start | bytes 1671176 | tf_op jit(solution)/shard_map/ppermute | solution.py:453
  59.8 2.2 %collective-permute-start.3 = (bf16[2,272,512]{2,1,0:T(8,128)(2,1)S(1)}, bf16[2,272,512]{2,1,0:T(8,128)(2,1)S(1)}, u32[]{:S(2)}, u32[]{:S(2)}) collective-permute-start(bf16[2,272,512]{2,1,0:T(8,128)(2,1)S(1)} %get-tuple-element.86), channel_id=1, source_target_pairs={{0,3},{1,2},{2,1},{3,0},{4,7},{5,6},{6,5},{7,4},{8,11},{9,10},{10,... | collective-permute-start | bytes 1671176 | tf_op jit(solution)/shard_map/ppermute | solution.py:453
  62.0 1.7 %chunk.4 = (bf16[2,128,512]{2,1,0:T(8,128)(2,1)S(1)}, bf16[2,128,512]{2,1,0:T(8,128)(2,1)S(1)}, bf16[128,2048]{1,0:T(8,128)(2,1)S(1)}) custom-call(bf16[272,2048]{1,0:T(8,128)(2,1)S(1)} %join_halves.1.state_ref, bf16[512,256]{1,0:T(8,128)(2,1)S(1)} %bitcast.12, bf16[256,2048]{1,0:T(8,128)(2,1)S(1)} %copy-done, bf16[256,2048]{1,0:T(8,128)(2,1)S(1)} %copy-done.1, ...), custom_call_target="tpu_custom_call" | custom-call | tf_op jit(solution)/shard_map/chunk/pallas_call | solution.py:557
  65.2 3.5 %fetch_weight.3.weight_ref = bf16[4,2048,512]{2,1,0:T(8,128)(2,1)S(1)} custom-call(bf16[2048,4096]{1,0:T(8,128)(2,1)} %weight_ref.1), custom_call_target="tpu_custom_call" | custom-call | tf_op jit(solution)/shard_map/fetch_weight/pallas_call | solution.py:330
  68.7 2.5 %rest.3.refs_2_ = bf16[4,272,512]{2,1,0:T(8,128)(2,1)S(1)} custom-call(bf16[272,2048]{1,0:T(8,128)(2,1)S(1)} %get-tuple-element.89.normed_ref, bf16[4,2048,512]{2,1,0:T(8,128)(2,1)S(1)} %fetch_weight.3.weight_ref), custom_call_target="tpu_custom_call" | custom-call | flops 1 | bytes 1 | tf_op jit(solution)/shard_map/rest/pallas_call | solution.py:432
  71.2 1.7 %chunk.5 = (bf16[2,128,512]{2,1,0:T(8,128)(2,1)S(1)}, bf16[2,128,512]{2,1,0:T(8,128)(2,1)S(1)}, bf16[128,2048]{1,0:T(8,128)(2,1)S(1)}) custom-call(bf16[272,2048]{1,0:T(8,128)(2,1)S(1)} %join_halves.1.state_ref, bf16[512,256]{1,0:T(8,128)(2,1)S(1)} %bitcast.13, bf16[256,2048]{1,0:T(8,128)(2,1)S(1)} %copy-done, bf16[256,2048]{1,0:T(8,128)(2,1)S(1)} %copy-done.1, ...), custom_call_target="tpu_custom_call" | custom-call | tf_op jit(solution)/shard_map/chunk/pallas_call | solution.py:557
  73.1 5.2 %collective-permute-done.4.refs_0_.refs_3_ = bf16[2,128,512]{2,1,0:T(8,128)(2,1)S(1)} collective-permute-done((bf16[2,128,512]{2,1,0:T(8,128)(2,1)S(1)}, bf16[2,128,512]{2,1,0:T(8,128)(2,1)S(1)}, u32[]{:S(2)}, u32[]{:S(2)}) %collective-permute-start.4) | collective-permute-done | bytes 262176 | tf_op jit(solution)/shard_map/ppermute | solution.py:453
  78.3 3.5 %collective-permute-start.7 = (bf16[2,128,512]{2,1,0:T(8,128)(2,1)S(1)}, bf16[2,128,512]{2,1,0:T(8,128)(2,1)S(1)}, u32[]{:S(2)}, u32[]{:S(2)}) collective-permute-start(bf16[2,128,512]{2,1,0:T(8,128)(2,1)S(1)} %get-tuple-element.106), channel_id=1, source_target_pairs={{0,3},{1,2},{2,1},{3,0},{4,7},{5,6},{6,5},{7,4},{8,11},{9,10},{10,... | collective-permute-start | bytes 786440 | tf_op jit(solution)/shard_map/ppermute | solution.py:453
  81.8 1.3 %rest.4.refs_2_.refs_5_ = bf16[4,128,512]{2,1,0:T(8,128)(2,1)S(1)} custom-call(bf16[128,2048]{1,0:T(8,128)(2,1)S(1)} %get-tuple-element.100.normed_ref, bf16[4,2048,512]{2,1,0:T(8,128)(2,1)S(1)} %fetch_weight.3.weight_ref), custom_call_target="tpu_custom_call" | custom-call | flops 1 | bytes 1 | tf_op jit(solution)/shard_map/rest/pallas_call | solution.py:432
  84.7 2.5 %collective-permute-done.7.refs_4_.refs_7_ = bf16[2,128,512]{2,1,0:T(8,128)(2,1)S(1)} collective-permute-done((bf16[2,128,512]{2,1,0:T(8,128)(2,1)S(1)}, bf16[2,128,512]{2,1,0:T(8,128)(2,1)S(1)}, u32[]{:S(2)}, u32[]{:S(2)}) %collective-permute-start.7) | collective-permute-done | bytes 262176 | tf_op jit(solution)/shard_map/ppermute | solution.py:453
  87.3 2.5 %collective-permute-start.10 = (bf16[256,512]{1,0:T(8,128)(2,1)S(1)}, bf16[256,512]{1,0:T(8,128)(2,1)S(1)}, u32[]{:S(2)}, u32[]{:S(2)}) collective-permute-start(bf16[256,512]{1,0:T(8,128)(2,1)S(1)} %get-tuple-element.114), channel_id=1, source_target_pairs={{0,3},{1,2},{2,1},{3,0},{4,7},{5,6},{6,5},{7,4},{8,11},{9,10},{10,... | collective-permute-start | bytes 786440 | tf_op jit(solution)/shard_map/ppermute | solution.py:453
  89.8 9.1 %collective-permute-done.10.refs_11_ = bf16[256,512]{1,0:T(8,128)(2,1)S(1)} collective-permute-done((bf16[256,512]{1,0:T(8,128)(2,1)S(1)}, bf16[256,512]{1,0:T(8,128)(2,1)S(1)}, u32[]{:S(2)}, u32[]{:S(2)}) %collective-permute-start.10) | collective-permute-done | bytes 262176 | tf_op jit(solution)/shard_map/ppermute | solution.py:453
  98.9 1.9 %finish.1 = (bf16[1024,512]{1,0:T(8,128)(2,1)}, bf16[2,1024]{1,0:T(2,128)(2,1)}) custom-call(bf16[2,272,512]{2,1,0:T(8,128)(2,1)S(1)} %collective-permute-done.2.refs_0_, bf16[2,272,512]{2,1,0:T(8,128)(2,1)S(1)} %collective-permute-done.3.refs_1_, bf16[4,272,512]{2,1,0:T(8,128)(2,1)S(1)} %rest.3.refs_2_, ...), custom_call_target="tpu_custom_call" | custom-call | tf_op jit(solution)/shard_map/finish/pallas_call | solution.py:593
  (50 shorter events, 10.2 us)
Async XLA Ops:
  0.6 7.3 %copy-start.12 = (f32[32,2,16]{0,2,1:T(8,128)S(1)}, f32[32,2,16]{0,2,1:T(8,128)}, u32[]{:S(2)}) copy-start(f32[32,2,16]{0,2,1:T(8,128)} %param.28) | copy-start | bytes 12292
  6.4 11.1 %copy-start.9 = (s32[2]{0:T(128)S(1)}, s32[2]{0:T(128)}, u32[]{:S(2)}) copy-start(s32[2]{0:T(128)} %length.3) | copy-start | bytes 28
  6.4 13.5 %copy-start.10 = (f32[32]{0:T(128)S(1)}, f32[32]{0:T(128)}, u32[]{:S(2)}) copy-start(f32[32]{0:T(128)} %param.20) | copy-start | bytes 388
  6.4 13.5 %copy-start.11 = (f32[32]{0:T(128)S(1)}, f32[32]{0:T(128)}, u32[]{:S(2)}) copy-start(f32[32]{0:T(128)} %param.21) | copy-start | bytes 388
  6.4 3.1 %collective-permute-start = (bf16[16,144,128]{2,1,0:T(8,128)(2,1)S(1)}, bf16[16,144,128]{2,1,0:T(8,128)(2,1)S(1)}, u32[]{:S(2)}, u32[]{:S(2)}) collective-permute-start(bf16[16,144,128]{2,1,0:T(8,128)(2,1)S(1)} %get-tuple-element.62), channel_id=1, source_target_pairs={{0,4},{4,0},{1,5},{5,1},{2,6},{6,2},{3,7},{7,3},{8,12},{12,8},{9,1... | collective-permute-start | bytes 1769480 | tf_op jit(solution)/shard_map/ppermute | solution.py:457
  10.7 18.3 %all-to-all-start = ((bf16[16,144,128]{2,1,0:T(8,128)(2,1)}), bf16[16,144,128]{2,1,0:T(8,128)(2,1)S(1)}, u32[]{:S(2)}, u32[]{:S(2)}) async-start(bf16[16,144,128]{2,1,0:T(8,128)(2,1)} %join_cores.1), calls=%async_computation | async-start | bytes 1179648 | tf_op jit(solution)/shard_map/all_to_all | solution.py:525
  30.1 16.5 %all-to-all-start.1 = ((bf16[16,144,128]{2,1,0:T(8,128)(2,1)}), bf16[16,144,128]{2,1,0:T(8,128)(2,1)S(1)}, u32[]{:S(2)}, u32[]{:S(2)}) async-start(bf16[16,144,128]{2,1,0:T(8,128)(2,1)} %prefix.1), calls=%async_computation.1 | async-start | bytes 1179648 | tf_op jit(solution)/shard_map/all_to_all | solution.py:536
  47.0 4.8 %collective-permute-start.1 = (bf16[16,144,128]{2,1,0:T(8,128)(2,1)S(1)}, bf16[16,144,128]{2,1,0:T(8,128)(2,1)S(1)}, u32[]{:S(2)}, u32[]{:S(2)}) collective-permute-start(bf16[16,144,128]{2,1,0:T(8,128)(2,1)S(1)} %get-tuple-element.78), channel_id=1, source_target_pairs={{0,4},{4,0},{1,5},{5,1},{2,6},{6,2},{3,7},{7,3},{8,12},{12,8},{9,1... | collective-permute-start | bytes 1769480 | tf_op jit(solution)/shard_map/ppermute | solution.py:457
  49.4 2.6 %copy-start.4 = (bf16[256,2048]{1,0:T(8,128)(2,1)S(1)}, bf16[256,2048]{1,0:T(8,128)(2,1)}, u32[]{:S(2)}) copy-start(bf16[256,2048]{1,0:T(8,128)(2,1)} %get-tuple-element.80.gain_ref) | copy-start | bytes 3145732
  51.8 1.3 %copy-start.6 = (f32[16,2048]{1,0:T(8,128)S(1)}, f32[16,2048]{1,0:T(8,128)}, u32[]{:S(2)}) copy-start(f32[16,2048]{1,0:T(8,128)} %get-tuple-element.83.refs_1_) | copy-start | bytes 393220
  51.8 1.4 %copy-start.7 = (f32[16,2048]{1,0:T(8,128)S(1)}, f32[16,2048]{1,0:T(8,128)}, u32[]{:S(2)}) copy-start(f32[16,2048]{1,0:T(8,128)} %get-tuple-element.84.refs_2_) | copy-start | bytes 393220
  51.8 1.4 %copy-start.8 = (f32[2048]{0:T(1024)S(1)}, f32[2048]{0:T(1024)}, u32[]{:S(2)}) copy-start(f32[2048]{0:T(1024)} %param.22) | copy-start | bytes 24580
  53.1 8.9 %copy-start = (bf16[256,2048]{1,0:T(8,128)(2,1)S(1)}, bf16[256,2048]{1,0:T(8,128)(2,1)}, u32[]{:S(2)}) copy-start(bf16[256,2048]{1,0:T(8,128)(2,1)} %get-tuple-element.93.scaled_ref) | copy-start | bytes 3145732
  53.1 8.9 %copy-start.1 = (bf16[256,2048]{1,0:T(8,128)(2,1)S(1)}, bf16[256,2048]{1,0:T(8,128)(2,1)}, u32[]{:S(2)}) copy-start(bf16[256,2048]{1,0:T(8,128)(2,1)} %get-tuple-element.94.gain_ref) | copy-start | bytes 3145732
  58.1 25.0 %collective-permute-start.2 = (bf16[2,272,512]{2,1,0:T(8,128)(2,1)S(1)}, bf16[2,272,512]{2,1,0:T(8,128)(2,1)S(1)}, u32[]{:S(2)}, u32[]{:S(2)}) collective-permute-start(bf16[2,272,512]{2,1,0:T(8,128)(2,1)S(1)} %get-tuple-element.85), channel_id=1, source_target_pairs={{0,1},{1,0},{2,3},{3,2},{4,5},{5,4},{6,7},{7,6},{8,9},{9,8},{10,11... | collective-permute-start | bytes 1671176 | tf_op jit(solution)/shard_map/ppermute | solution.py:453
  59.8 23.3 %collective-permute-start.3 = (bf16[2,272,512]{2,1,0:T(8,128)(2,1)S(1)}, bf16[2,272,512]{2,1,0:T(8,128)(2,1)S(1)}, u32[]{:S(2)}, u32[]{:S(2)}) collective-permute-start(bf16[2,272,512]{2,1,0:T(8,128)(2,1)S(1)} %get-tuple-element.86), channel_id=1, source_target_pairs={{0,3},{1,2},{2,1},{3,0},{4,7},{5,6},{6,5},{7,4},{8,11},{9,10},{10,... | collective-permute-start | bytes 1671176 | tf_op jit(solution)/shard_map/ppermute | solution.py:453
  63.7 14.5 %collective-permute-start.4 = (bf16[2,128,512]{2,1,0:T(8,128)(2,1)S(1)}, bf16[2,128,512]{2,1,0:T(8,128)(2,1)S(1)}, u32[]{:S(2)}, u32[]{:S(2)}) collective-permute-start(bf16[2,128,512]{2,1,0:T(8,128)(2,1)S(1)} %get-tuple-element.96), channel_id=1, source_target_pairs={{0,1},{1,0},{2,3},{3,2},{4,5},{5,4},{6,7},{7,6},{8,9},{9,8},{10,11... | collective-permute-start | bytes 786440 | tf_op jit(solution)/shard_map/ppermute | solution.py:453
  64.6 18.5 %collective-permute-start.5 = (bf16[2,128,512]{2,1,0:T(8,128)(2,1)S(1)}, bf16[2,128,512]{2,1,0:T(8,128)(2,1)S(1)}, u32[]{:S(2)}, u32[]{:S(2)}) collective-permute-start(bf16[2,128,512]{2,1,0:T(8,128)(2,1)S(1)} %get-tuple-element.97), channel_id=1, source_target_pairs={{0,3},{1,2},{2,1},{3,0},{4,7},{5,6},{6,5},{7,4},{8,11},{9,10},{10,... | collective-permute-start | bytes 786440 | tf_op jit(solution)/shard_map/ppermute | solution.py:453
  72.9 11.8 %collective-permute-start.6 = (bf16[2,128,512]{2,1,0:T(8,128)(2,1)S(1)}, bf16[2,128,512]{2,1,0:T(8,128)(2,1)S(1)}, u32[]{:S(2)}, u32[]{:S(2)}) collective-permute-start(bf16[2,128,512]{2,1,0:T(8,128)(2,1)S(1)} %get-tuple-element.105), channel_id=1, source_target_pairs={{0,1},{1,0},{2,3},{3,2},{4,5},{5,4},{6,7},{7,6},{8,9},{9,8},{10,11... | collective-permute-start | bytes 786440 | tf_op jit(solution)/shard_map/ppermute | solution.py:453
  78.3 8.9 %collective-permute-start.7 = (bf16[2,128,512]{2,1,0:T(8,128)(2,1)S(1)}, bf16[2,128,512]{2,1,0:T(8,128)(2,1)S(1)}, u32[]{:S(2)}, u32[]{:S(2)}) collective-permute-start(bf16[2,128,512]{2,1,0:T(8,128)(2,1)S(1)} %get-tuple-element.106), channel_id=1, source_target_pairs={{0,3},{1,2},{2,1},{3,0},{4,7},{5,6},{6,5},{7,4},{8,11},{9,10},{10,... | collective-permute-start | bytes 786440 | tf_op jit(solution)/shard_map/ppermute | solution.py:453
  83.2 15.7 %collective-permute-start.8 = (bf16[272,512]{1,0:T(8,128)(2,1)S(1)}, bf16[272,512]{1,0:T(8,128)(2,1)S(1)}, u32[]{:S(2)}, u32[]{:S(2)}) collective-permute-start(bf16[272,512]{1,0:T(8,128)(2,1)S(1)} %get-tuple-element.110), channel_id=1, source_target_pairs={{0,3},{1,2},{2,1},{3,0},{4,7},{5,6},{6,5},{7,4},{8,11},{9,10},{10,... | collective-permute-start | bytes 835592 | tf_op jit(solution)/shard_map/ppermute | solution.py:453
  83.3 15.6 %collective-permute-start.9 = (bf16[272,512]{1,0:T(8,128)(2,1)S(1)}, bf16[272,512]{1,0:T(8,128)(2,1)S(1)}, u32[]{:S(2)}, u32[]{:S(2)}) collective-permute-start(bf16[272,512]{1,0:T(8,128)(2,1)S(1)} %get-tuple-element.111), channel_id=1, source_target_pairs={{0,1},{1,0},{2,3},{3,2},{4,5},{5,4},{6,7},{7,6},{8,9},{9,8},{10,11... | collective-permute-start | bytes 835592 | tf_op jit(solution)/shard_map/ppermute | solution.py:453
  87.3 11.5 %collective-permute-start.10 = (bf16[256,512]{1,0:T(8,128)(2,1)S(1)}, bf16[256,512]{1,0:T(8,128)(2,1)S(1)}, u32[]{:S(2)}, u32[]{:S(2)}) collective-permute-start(bf16[256,512]{1,0:T(8,128)(2,1)S(1)} %get-tuple-element.114), channel_id=1, source_target_pairs={{0,3},{1,2},{2,1},{3,0},{4,7},{5,6},{6,5},{7,4},{8,11},{9,10},{10,... | collective-permute-start | bytes 786440 | tf_op jit(solution)/shard_map/ppermute | solution.py:453
  89.8 9.1 %collective-permute-start.11 = (bf16[256,512]{1,0:T(8,128)(2,1)S(1)}, bf16[256,512]{1,0:T(8,128)(2,1)S(1)}, u32[]{:S(2)}, u32[]{:S(2)}) collective-permute-start(bf16[256,512]{1,0:T(8,128)(2,1)S(1)} %get-tuple-element.115), channel_id=1, source_target_pairs={{0,1},{1,0},{2,3},{3,2},{4,5},{5,4},{6,7},{7,6},{8,9},{9,8},{10,11... | collective-permute-start | bytes 786440 | tf_op jit(solution)/shard_map/ppermute | solution.py:453
  (3 other events, 3.7 us)

commit v7 on v5

--- a/solution.py
+++ b/solution.py
@@ -50,6 +50,11 @@
     first = jnp.broadcast_to(columns[:, 2 * pair : 2 * pair + 1], shape)
     second = jnp.broadcast_to(columns[:, 2 * pair + 1 : 2 * pair + 2], shape)
     return jnp.where(low, first, second)
+
+
+def head_lanes(start, width):
+    row, lane = iota((128, width), 0), iota((128, width), 1) + start
+    return (((row & (HEADS - 1)) == (lane >> 6)) & (row < 3 * HEADS)).astype(BF16)
 
 
 def three_parts(x):
@@ -95,11 +100,12 @@
         here = logs[:, b * BLOCK : (b + 1) * BLOCK]
         parts.append(jnp.dot(here, later, precision=EXACT, preferred_element_type=F32) + after)
         after = after + jnp.sum(here, axis=1, keepdims=True)
-    weight = tokens_first(jnp.exp(jnp.concatenate(parts[::-1], axis=1)) * step)
+    weight = jnp.exp(jnp.concatenate(parts[::-1], axis=1)) * step
+    weight = jnp.transpose(jnp.concatenate([*three_parts(weight), jnp.zeros((128 - 3 * HEADS, TOK), F32)], axis=0))
+    weight = weight.astype(BF16)
     total = tokens_first(jnp.broadcast_to(jnp.exp(after), (HEADS, 128)))[0:8]
     copies[1].wait()
     inject_t = jnp.transpose(inject_ref[...].astype(F32)).astype(BF16)
-    low = iota((TOK, 128), 1) < HEAD_DIM
     low_row = iota((8, 128), 1) < HEAD_DIM
     row = iota((16, 128), 0)
     tails = []
@@ -112,12 +118,10 @@
             tail = jnp.where(row == 2 * core + s, picked, tail)
         tails.append(tail)
     for half in range(2):
+        lanes = slice(half * 1024, (half + 1) * 1024)
+        wide = jnp.dot(weight, head_lanes(half * 1024, 1024), preferred_element_type=F32)
         copies[2 + half].wait()
-        for q in range(8):
-            pair = half * 8 + q
-            lanes = slice(pair * 128, (pair + 1) * 128)
-            w = per_pair(weight, pair, (TOK, 128), low)
-            scaled[:, q * 128 : (q + 1) * 128] = (values_ref[:, lanes].astype(F32) * w).astype(BF16)
+        scaled[...] = (values_ref[:, lanes].astype(F32) * wide).astype(BF16)
         state = jnp.dot(inject_t, scaled[...], preferred_element_type=F32).astype(BF16)
 
         def put(out_ref, half=half, state=state):
@@ -188,9 +192,9 @@
     part, step_ref, decay_ref, skip_ref, values_ref, gate_ref, inject_ref, read_ref, *refs
 ):
     if part == 0:
-        scaled_ref, gain_ref, carry, carry_before, ends, weighted, carried, state, before = refs
+        scaled_ref, gain_ref, carry, carry_before, ends, weighted, carried, state, before, stepped_all = refs
     else:
-        start, start_before, scaled_ref, gain_ref, ends, weighted, carried, state, before = refs
+        start, start_before, scaled_ref, gain_ref, ends, weighted, carried, state, before, stepped_all = refs
 
     @pl.when(pl.program_id(0) == 0)
     def _():
@@ -206,7 +210,10 @@
     upto = (iota((BLOCK, BLOCK), 0) <= iota((BLOCK, BLOCK), 1)).astype(F32)
     running = jnp.dot(logs, upto, precision=EXACT, preferred_element_type=F32) * LOG2E
     running_t = tokens_first(running)
-    step_t = tokens_first(step)
+    parts = jnp.concatenate([*three_parts(step), jnp.zeros((128 - 3 * HEADS, BLOCK), F32)], axis=0)
+    stepped_all[...] = values_ref[...].astype(F32) * jnp.dot(
+        jnp.transpose(parts).astype(BF16), head_lanes(0, CH), preferred_element_type=F32
+    )
     read = read_ref[...]
     inject = inject_ref[...]
     inject_t = jnp.transpose(inject.astype(F32)).astype(BF16)
@@ -226,7 +233,7 @@
         now = jnp.where(low, spread[0], spread[1])
         grown = jnp.exp2(now)
         values = values_ref[:, lanes].astype(F32)
-        stepped = values * per_pair(step_t, pair, (BLOCK, 128), low)
+        stepped = stepped_all[:, lanes]
         diagonal = jnp.concatenate([jnp.where(low, stepped, 0.0), jnp.where(low, 0.0, stepped)], axis=0)
         local = jnp.dot(
             jnp.concatenate(mixing, axis=1), diagonal.astype(BF16), preferred_element_type=F32
@@ -367,7 +374,7 @@
 def chunk_kernel(place, sampled, state_ref, read_ref, scaled_ref, gain_ref, norm_ref, near_ref, far_ref, *refs):
     if place == LEADING:
         *sample, first_ref, second_ref, normed_ref, held, sems = refs
-        copies = column_copies(FIRST[2:], far_ref, held, sems)
+        copies = column_copies(FIRST[1:], far_ref, held, sems)
     else:
         *sample, first_ref, second_ref, normed_ref = refs
         held = far_ref
@@ -380,11 +387,11 @@
         sampled = (local_ref[...] + readings * grown_ref[...]) * gate_ref[...]
         rows = CHUNKS[place][1]
         normed_ref[rows : rows + 16, :] = normalize(sampled, norm_ref[...])
-    project(normed_ref, (near_ref.at[0], near_ref.at[1]), ((first_ref, 0), (first_ref, 1)))
-    for i in range(2):
+    project(normed_ref, (near_ref.at[0],), ((first_ref, 0),))
+    for i, out in enumerate(((first_ref, 1), (second_ref, 0), (second_ref, 1))):
         if place == LEADING:
             copies[i].wait()
-        project(normed_ref, (held.at[i],), ((second_ref, i),))
+        project(normed_ref, (held.at[i],), (out,))
 
 
 def rest_kernel(normed_ref, weight_ref, rest_ref):
@@ -457,7 +464,7 @@
     results = (pltpu.HBM((TOK // 2, CH), BF16),) * 2
     scratch = [
         pltpu.VMEM((8, CH), F32), pltpu.VMEM((BLOCK, CH), BF16), pltpu.VMEM((BLOCK, CH), F32),
-        pltpu.VMEM((STATE, CH), F32), pltpu.VMEM((8, CH), F32),
+        pltpu.VMEM((STATE, CH), F32), pltpu.VMEM((8, CH), F32), pltpu.VMEM((BLOCK, CH), F32),
     ]
     if start:
         start_specs = [whole(STATE), whole(8)]
@@ -533,7 +540,7 @@
     )
     theirs = other_core(send)
 
-    near_columns = fetch(FIRST[:2], weight)
+    near_columns = fetch(FIRST[:1], weight)
     scaled = (scaled_1, scaled_2)
     gain = (gain_1, gain_2)
     state = call(join_halves_kernel, "join_halves", shape((272, CH)), (mine, theirs), 8)
@@ -542,17 +549,19 @@
         start, rows = CHUNKS[place]
         size = rows + (16 if sample else 0)
         leading = place == LEADING
+        local = (scaled[start // HALF], gain[start // HALF])
+        local = local if leading else in_hbm(*local)
         piece = shape((2, size, PIECE))
-        held = pltpu.VMEM((2, CH, PIECE), BF16)
+        held = pltpu.VMEM((3, CH, PIECE), BF16)
         first, second, normed, *held = pl.pallas_call(
             functools.partial(chunk_kernel, place, bool(sample)),
             out_shape=(piece, piece, shape((size, CH)), *([held] if leading else [])),
             in_specs=[VMEM] * 6 + [anywhere if leading else VMEM] + [VMEM] * len(sample),
             out_specs=(VMEM,) * (4 if leading else 3),
-            scratch_shapes=[pltpu.SemaphoreType.DMA((2,))] if leading else [],
+            scratch_shapes=[pltpu.SemaphoreType.DMA((3,))] if leading else [],
             compiler_params=pltpu.CompilerParams(vmem_limit_bytes=24 << 20),
             name="chunk",
-        )(state, read, scaled[start // HALF], gain[start // HALF], norm, near_columns, far_columns, *sample)
+        )(state, read, *local, norm, near_columns, far_columns, *sample)
         near = lax.optimization_barrier((swap(first, 1), swap(second, 3)))
         return normed, near, *held
 

time: 100 us -> 97.9 us (0.979)
  waiting for transfers between devices: 23.7 us -> 22.4 us
  Pallas kernels: 47.1 us -> 46 us
    ppermute x8, waiting for transfers between devices: 18 us -> 16.4 us  [swap(): return lax.ppermute(x, 'head', [(i, i ^ step) for i in range(4)])]
    pallas_call x1, Pallas kernels: 5.75 us -> 4.18 us  [per_device(): pl.pallas_call(end_state_kernel, out_shape=(slices_shape,) * 2, in_specs=...]
    pallas_call x2, Pallas kernels: 7.99 us -> 9.43 us  [chunk(): pl.pallas_call(functools.partial(chunk_kernel, place, bool(sample)), out_...]
  transfers between devices with their start and end apart: 12 -> 12, of which waited for: 8 -> 7; matrix products, arithmetic and copies ran while one was open for 1% -> 1% of each run, Pallas kernels for 32% -> 33%
where the time goes in v7:
time: 97.9 us; the launch traced here: 97.4 us
  Pallas kernels  46 us (47%)
  starting transfers between devices  26 us (27%)
  waiting for transfers between devices  22.4 us (23%)
  local copies, waits for them, and re-layouts  2 us (2%)
  between operations  1.02 us (1%)
    ppermute x8, waiting for transfers between devices, swap(): return lax.ppermute(x, 'head', [(i, i ^ step) for i in range(4)])  16.4 us
    pallas_call x2, Pallas kernels, local_outputs(): pl.pallas_call(functools.partial(local_kernel, part), grid=(blocks,), out...  15 us
    pallas_call x9, Pallas kernels, call(): pl.pallas_call(kernel, out_shape=out_shape, in_specs=[SMEM] * scalars + [...  10.3 us
    ppermute x8, starting transfers between devices, swap(): return lax.ppermute(x, 'head', [(i, i ^ step) for i in range(4)])  10 us
    pallas_call x2, Pallas kernels, chunk(): pl.pallas_call(functools.partial(chunk_kernel, place, bool(sample)), out_...  9.43 us
    all_to_all x1, starting transfers between devices, per_device(): slices = lax.all_to_all(joined, ('y', 'x'), 0, 0, tiled=True)  6.84 us
    all_to_all x1, starting transfers between devices, per_device(): back = lax.all_to_all(prefix, ('y', 'x'), 0, 0, tiled=True)  5.27 us
    pallas_call x2, Pallas kernels, fetch(): pl.pallas_call(functools.partial(fetch_kernel, pieces), out_shape=pltpu.V...  5.2 us
  transfers between devices with their start and end apart: 12, of which 7 were waited for; matrix products, arithmetic and copies ran while one was open for 1% of the time, Pallas kernels for 33%

profile of v7, /device:TPU:1, one launch (start us, length us, event | category | flops | bytes accessed | tf_op | source)
XLA Modules:
  0.0 97.4 jit_solution(12507519367016459746)
XLA Ops:
  0.6 4.2 %end_state.1 = (bf16[16,144,128]{2,1,0:T(8,128)(2,1)S(1)}, bf16[16,144,128]{2,1,0:T(8,128)(2,1)S(1)}) custom-call(s32[2]{0:T(128)} %length.3, f32[32,512]{1,0:T(8,128)} %step_ref.1, f32[1,32]{1,0:T(1,128)} %bitcast.15, bf16[512,2048]{1,0:T(8,128)(2,1)} %values_ref.5, bf16[512,256]{1,0:T(8,128)(2,1)} %bitcast.22, bf16[2,16,256]{2,1,0:T(8,128)(2,1)} %bitcast.26), custom_call_target="tpu_custom_call" | custom-call | tf_op jit(solution)/shard_map/end_state/pallas_call | solution.py:507
  4.9 1.5 %collective-permute-start = (bf16[16,144,128]{2,1,0:T(8,128)(2,1)S(1)}, bf16[16,144,128]{2,1,0:T(8,128)(2,1)S(1)}, u32[]{:S(2)}, u32[]{:S(2)}) collective-permute-start(bf16[16,144,128]{2,1,0:T(8,128)(2,1)S(1)} %get-tuple-element.50), channel_id=1, source_target_pairs={{0,4},{4,0},{1,5},{5,1},{2,6},{6,2},{3,7},{7,3},{8,12},{12,8},{9,1... | collective-permute-start | bytes 1769480 | tf_op jit(solution)/shard_map/ppermute | solution.py:454
  9.1 6.8 %all-to-all-start = ((bf16[16,144,128]{2,1,0:T(8,128)(2,1)}), bf16[16,144,128]{2,1,0:T(8,128)(2,1)S(1)}, u32[]{:S(2)}, u32[]{:S(2)}) async-start(bf16[16,144,128]{2,1,0:T(8,128)(2,1)} %join_cores.1), calls=%async_computation | async-start | bytes 1179648 | tf_op jit(solution)/shard_map/all_to_all | solution.py:522
  16.0 2.4 %sample_outputs.1 = (f32[16,2048]{1,0:T(8,128)}, f32[16,2048]{1,0:T(8,128)}, f32[16,2048]{1,0:T(8,128)}) custom-call(s32[2]{0:T(128)S(1)} %copy-done.7, f32[2,32,16]{2,1,0:T(8,128)} %bitcast.25, f32[1,32]{1,0:T(1,128)} %bitcast.16, f32[1,32]{1,0:T(1,128)} %bitcast.19, bf16[2,16,2048]{2,1,0:T(8,128)(2,1)} %values_ref.4, bf16[2,16,2048]{2,1,0:T(8,128)(2,1)} %gate_ref.4, ...), custom_call_target="tpu_custom_call" | custom-call | flops 1 | bytes 1 | tf_op jit(solution)/shard_map/sample_outputs/pallas_call | solution.py:429
  18.4 7.6 %local_outputs.2 = (bf16[256,2048]{1,0:T(8,128)(2,1)}, bf16[256,2048]{1,0:T(8,128)(2,1)}, bf16[256,2048]{1,0:T(8,128)(2,1)}, f32[8,2048]{1,0:T(8,128)}) custom-call(f32[32,512]{1,0:T(8,128)} %step_ref.1, f32[1,32]{1,0:T(1,128)S(1)} %bitcast.17, f32[1,32]{1,0:T(1,128)S(1)} %bitcast.20, bf16[512,2048]{1,0:T(8,128)(2,1)} %values_ref.5, ...), custom_call_target="tpu_custom_call" | custom-call | flops 3221225472 | bytes 20971520 | tf_op jit(solution)/shard_map/local_outputs/pallas_call | solution.py:477
  26.0 1.4 %all-to-all-done.in_ref = bf16[16,144,128]{2,1,0:T(8,128)(2,1)S(1)} async-done(((bf16[16,144,128]{2,1,0:T(8,128)(2,1)}), bf16[16,144,128]{2,1,0:T(8,128)(2,1)S(1)}, u32[]{:S(2)}, u32[]{:S(2)}) %all-to-all-start) | async-done | bytes 589856 | tf_op jit(solution)/shard_map/all_to_all | solution.py:522
  28.6 5.3 %all-to-all-start.1 = ((bf16[16,144,128]{2,1,0:T(8,128)(2,1)}), bf16[16,144,128]{2,1,0:T(8,128)(2,1)S(1)}, u32[]{:S(2)}, u32[]{:S(2)}) async-start(bf16[16,144,128]{2,1,0:T(8,128)(2,1)} %prefix.1), calls=%async_computation.1 | async-start | bytes 1179648 | tf_op jit(solution)/shard_map/all_to_all | solution.py:533
  33.8 7.4 %local_outputs.3 = (bf16[256,2048]{1,0:T(8,128)(2,1)}, bf16[256,2048]{1,0:T(8,128)(2,1)}) custom-call(f32[32,512]{1,0:T(8,128)} %step_ref.1, f32[1,32]{1,0:T(1,128)S(1)} %bitcast.18, f32[1,32]{1,0:T(1,128)S(1)} %bitcast.21, bf16[512,2048]{1,0:T(8,128)(2,1)} %values_ref.5, bf16[512,2048]{1,0:T(8,128)(2,1)} %gate_ref.5, bf16[512,256]{1,0:T(8,128)(2,1)} %bitcast.24, ...), custom_call_target="tpu_custom_call" | custom-call | flops 3221225472 | bytes 20971520 | tf_op jit(solution)/shard_map/local_outputs/pallas_call | solution.py:477
  41.2 3.7 %all-to-all-done.1.back_ref = bf16[16,144,128]{2,1,0:T(8,128)(2,1)S(1)} async-done(((bf16[16,144,128]{2,1,0:T(8,128)(2,1)}), bf16[16,144,128]{2,1,0:T(8,128)(2,1)S(1)}, u32[]{:S(2)}, u32[]{:S(2)}) %all-to-all-start.1) | async-done | bytes 589856 | tf_op jit(solution)/shard_map/all_to_all | solution.py:533
  45.3 2.4 %collective-permute-start.1 = (bf16[16,144,128]{2,1,0:T(8,128)(2,1)S(1)}, bf16[16,144,128]{2,1,0:T(8,128)(2,1)S(1)}, u32[]{:S(2)}, u32[]{:S(2)}) collective-permute-start(bf16[16,144,128]{2,1,0:T(8,128)(2,1)S(1)} %get-tuple-element.66), channel_id=1, source_target_pairs={{0,4},{4,0},{1,5},{5,1},{2,6},{6,2},{3,7},{7,3},{8,12},{12,8},{9,1... | collective-permute-start | bytes 1769480 | tf_op jit(solution)/shard_map/ppermute | solution.py:454
  47.7 1.7 %fetch_weight.2.near_ref = bf16[1,2048,512]{2,1,0:T(8,128)(2,1)S(1)} custom-call(bf16[2048,4096]{1,0:T(8,128)(2,1)} %weight_ref.1), custom_call_target="tpu_custom_call" | custom-call | tf_op jit(solution)/shard_map/fetch_weight/pallas_call | solution.py:337
  50.9 4.8 %chunk.2 = (bf16[2,272,512]{2,1,0:T(8,128)(2,1)S(1)}, bf16[2,272,512]{2,1,0:T(8,128)(2,1)S(1)}, bf16[272,2048]{1,0:T(8,128)(2,1)S(1)}, bf16[3,2048,512]{2,1,0:T(8,128)(2,1)S(1)}) custom-call(bf16[272,2048]{1,0:T(8,128)(2,1)S(1)} %join_halves.1.state_ref, bf16[512,256]{1,0:T(8,128)(2,1)S(1)} %bitcast.11, bf16[256,2048]{1,0:T(8,128)(2,1)S(1)} %copy-done, ...), custom_call_target="tpu_custom_call" | custom-call | tf_op jit(solution)/shard_map/chunk/pallas_call | solution.py:556
  55.7 1.7 %collective-permute-start.2 = (bf16[2,272,512]{2,1,0:T(8,128)(2,1)S(1)}, bf16[2,272,512]{2,1,0:T(8,128)(2,1)S(1)}, u32[]{:S(2)}, u32[]{:S(2)}) collective-permute-start(bf16[2,272,512]{2,1,0:T(8,128)(2,1)S(1)} %get-tuple-element.73), channel_id=1, source_target_pairs={{0,1},{1,0},{2,3},{3,2},{4,5},{5,4},{6,7},{7,6},{8,9},{9,8},{10,11... | collective-permute-start | bytes 1671176 | tf_op jit(solution)/shard_map/ppermute | solution.py:450
  57.4 2.2 %collective-permute-start.3 = (bf16[2,272,512]{2,1,0:T(8,128)(2,1)S(1)}, bf16[2,272,512]{2,1,0:T(8,128)(2,1)S(1)}, u32[]{:S(2)}, u32[]{:S(2)}) collective-permute-start(bf16[2,272,512]{2,1,0:T(8,128)(2,1)S(1)} %get-tuple-element.74), channel_id=1, source_target_pairs={{0,3},{1,2},{2,1},{3,0},{4,7},{5,6},{6,5},{7,4},{8,11},{9,10},{10,... | collective-permute-start | bytes 1671176 | tf_op jit(solution)/shard_map/ppermute | solution.py:450
  59.7 4.6 %chunk.3 = (bf16[2,256,512]{2,1,0:T(8,128)(2,1)S(1)}, bf16[2,256,512]{2,1,0:T(8,128)(2,1)S(1)}, bf16[256,2048]{1,0:T(8,128)(2,1)S(1)}) custom-call(bf16[272,2048]{1,0:T(8,128)(2,1)S(1)} %join_halves.1.state_ref, bf16[512,256]{1,0:T(8,128)(2,1)S(1)} %bitcast.12, bf16[256,2048]{1,0:T(8,128)(2,1)} %get-tuple-element.82.scaled_ref, ...), custom_call_target="tpu_custom_call" | custom-call | tf_op jit(solution)/shard_map/chunk/pallas_call | solution.py:556
  65.7 3.5 %fetch_weight.3.weight_ref = bf16[4,2048,512]{2,1,0:T(8,128)(2,1)S(1)} custom-call(bf16[2048,4096]{1,0:T(8,128)(2,1)} %weight_ref.1), custom_call_target="tpu_custom_call" | custom-call | tf_op jit(solution)/shard_map/fetch_weight/pallas_call | solution.py:337
  69.3 2.5 %rest.2.rest_ref.refs_2_ = bf16[4,272,512]{2,1,0:T(8,128)(2,1)S(1)} custom-call(bf16[272,2048]{1,0:T(8,128)(2,1)S(1)} %get-tuple-element.77.normed_ref, bf16[4,2048,512]{2,1,0:T(8,128)(2,1)S(1)} %fetch_weight.3.weight_ref), custom_call_target="tpu_custom_call" | custom-call | flops 1 | bytes 1 | tf_op jit(solution)/shard_map/rest/pallas_call | solution.py:429
  72.7 2.3 %collective-permute-start.4 = (bf16[272,512]{1,0:T(8,128)(2,1)S(1)}, bf16[272,512]{1,0:T(8,128)(2,1)S(1)}, u32[]{:S(2)}, u32[]{:S(2)}) collective-permute-start(bf16[272,512]{1,0:T(8,128)(2,1)S(1)} %get-tuple-element.78), channel_id=1, source_target_pairs={{0,3},{1,2},{2,1},{3,0},{4,7},{5,6},{6,5},{7,4},{8,11},{9,10},{10,... | collective-permute-start | bytes 835592 | tf_op jit(solution)/shard_map/ppermute | solution.py:450
  75.0 2.3 %rest.3.rest_ref.refs_7_ = bf16[4,256,512]{2,1,0:T(8,128)(2,1)S(1)} custom-call(bf16[256,2048]{1,0:T(8,128)(2,1)S(1)} %get-tuple-element.89.normed_ref, bf16[4,2048,512]{2,1,0:T(8,128)(2,1)S(1)} %fetch_weight.3.weight_ref), custom_call_target="tpu_custom_call" | custom-call | flops 1 | bytes 1 | tf_op jit(solution)/shard_map/rest/pallas_call | solution.py:429
  77.3 4.2 %collective-permute-done.6.a_ref.refs_5_ = bf16[2,256,512]{2,1,0:T(8,128)(2,1)S(1)} collective-permute-done((bf16[2,256,512]{2,1,0:T(8,128)(2,1)S(1)}, bf16[2,256,512]{2,1,0:T(8,128)(2,1)S(1)}, u32[]{:S(2)}, u32[]{:S(2)}) %collective-permute-start.6) | collective-permute-done | bytes 524320 | tf_op jit(solution)/shard_map/ppermute | solution.py:450
  81.5 2.2 %collective-permute-done.7.b_ref.refs_6_ = bf16[2,256,512]{2,1,0:T(8,128)(2,1)S(1)} collective-permute-done((bf16[2,256,512]{2,1,0:T(8,128)(2,1)S(1)}, bf16[2,256,512]{2,1,0:T(8,128)(2,1)S(1)}, u32[]{:S(2)}, u32[]{:S(2)}) %collective-permute-start.7) | collective-permute-done | bytes 524320 | tf_op jit(solution)/shard_map/ppermute | solution.py:450
  83.9 2.3 %collective-permute-start.8 = (bf16[256,512]{1,0:T(8,128)(2,1)S(1)}, bf16[256,512]{1,0:T(8,128)(2,1)S(1)}, u32[]{:S(2)}, u32[]{:S(2)}) collective-permute-start(bf16[256,512]{1,0:T(8,128)(2,1)S(1)} %get-tuple-element.90), channel_id=1, source_target_pairs={{0,3},{1,2},{2,1},{3,0},{4,7},{5,6},{6,5},{7,4},{8,11},{9,10},{10,... | collective-permute-start | bytes 786440 | tf_op jit(solution)/shard_map/ppermute | solution.py:450
  86.2 9.1 %collective-permute-done.8.refs_8_ = bf16[256,512]{1,0:T(8,128)(2,1)S(1)} collective-permute-done((bf16[256,512]{1,0:T(8,128)(2,1)S(1)}, bf16[256,512]{1,0:T(8,128)(2,1)S(1)}, u32[]{:S(2)}, u32[]{:S(2)}) %collective-permute-start.8) | collective-permute-done | bytes 262176 | tf_op jit(solution)/shard_map/ppermute | solution.py:450
  95.4 1.9 %finish.1 = (bf16[1024,512]{1,0:T(8,128)(2,1)}, bf16[2,1024]{1,0:T(2,128)(2,1)}) custom-call(bf16[2,272,512]{2,1,0:T(8,128)(2,1)S(1)} %collective-permute-done.2.a_ref.refs_0_, bf16[2,272,512]{2,1,0:T(8,128)(2,1)S(1)} %collective-permute-done.3.b_ref.refs_1_, bf16[4,272,512]{2,1,0:T(8,128)(2,1)S(1)} %rest.2.rest_ref.refs_2_, ...), custom_call_target="tpu_custom_call" | custom-call | tf_op jit(solution)/shard_map/finish/pallas_call | solution.py:578
  (40 shorter events, 8.3 us)
Async XLA Ops:
  0.6 5.7 %copy-start.10 = (f32[32,2,16]{0,2,1:T(8,128)S(1)}, f32[32,2,16]{0,2,1:T(8,128)}, u32[]{:S(2)}) copy-start(f32[32,2,16]{0,2,1:T(8,128)} %param.28) | copy-start | bytes 12292
  4.8 11.1 %copy-start.7 = (s32[2]{0:T(128)S(1)}, s32[2]{0:T(128)}, u32[]{:S(2)}) copy-start(s32[2]{0:T(128)} %length.3) | copy-start | bytes 28
  4.8 13.5 %copy-start.8 = (f32[32]{0:T(128)S(1)}, f32[32]{0:T(128)}, u32[]{:S(2)}) copy-start(f32[32]{0:T(128)} %param.20) | copy-start | bytes 388
  4.8 13.5 %copy-start.9 = (f32[32]{0:T(128)S(1)}, f32[32]{0:T(128)}, u32[]{:S(2)}) copy-start(f32[32]{0:T(128)} %param.21) | copy-start | bytes 388
  4.9 3.1 %collective-permute-start = (bf16[16,144,128]{2,1,0:T(8,128)(2,1)S(1)}, bf16[16,144,128]{2,1,0:T(8,128)(2,1)S(1)}, u32[]{:S(2)}, u32[]{:S(2)}) collective-permute-start(bf16[16,144,128]{2,1,0:T(8,128)(2,1)S(1)} %get-tuple-element.50), channel_id=1, source_target_pairs={{0,4},{4,0},{1,5},{5,1},{2,6},{6,2},{3,7},{7,3},{8,12},{12,8},{9,1... | collective-permute-start | bytes 1769480 | tf_op jit(solution)/shard_map/ppermute | solution.py:454
  9.1 18.3 %all-to-all-start = ((bf16[16,144,128]{2,1,0:T(8,128)(2,1)}), bf16[16,144,128]{2,1,0:T(8,128)(2,1)S(1)}, u32[]{:S(2)}, u32[]{:S(2)}) async-start(bf16[16,144,128]{2,1,0:T(8,128)(2,1)} %join_cores.1), calls=%async_computation | async-start | bytes 1179648 | tf_op jit(solution)/shard_map/all_to_all | solution.py:522
  28.6 16.4 %all-to-all-start.1 = ((bf16[16,144,128]{2,1,0:T(8,128)(2,1)}), bf16[16,144,128]{2,1,0:T(8,128)(2,1)S(1)}, u32[]{:S(2)}, u32[]{:S(2)}) async-start(bf16[16,144,128]{2,1,0:T(8,128)(2,1)} %prefix.1), calls=%async_computation.1 | async-start | bytes 1179648 | tf_op jit(solution)/shard_map/all_to_all | solution.py:533
  45.3 4.1 %collective-permute-start.1 = (bf16[16,144,128]{2,1,0:T(8,128)(2,1)S(1)}, bf16[16,144,128]{2,1,0:T(8,128)(2,1)S(1)}, u32[]{:S(2)}, u32[]{:S(2)}) collective-permute-start(bf16[16,144,128]{2,1,0:T(8,128)(2,1)S(1)} %get-tuple-element.66), channel_id=1, source_target_pairs={{0,4},{4,0},{1,5},{5,1},{2,6},{6,2},{3,7},{7,3},{8,12},{12,8},{9,1... | collective-permute-start | bytes 1769480 | tf_op jit(solution)/shard_map/ppermute | solution.py:454
  47.7 1.9 %copy-start.2 = (bf16[512,1,256]{2,0,1:T(8,128)(2,1)S(1)}, bf16[512,1,256]{2,0,1:T(8,128)(2,1)}, u32[]{:S(2)}) copy-start(bf16[512,1,256]{2,0,1:T(8,128)(2,1)} %param.18) | copy-start | bytes 786436
  47.7 1.9 %copy-start.4 = (f32[16,2048]{1,0:T(8,128)S(1)}, f32[16,2048]{1,0:T(8,128)}, u32[]{:S(2)}) copy-start(f32[16,2048]{1,0:T(8,128)} %get-tuple-element.71.refs_1_) | copy-start | bytes 393220
  47.7 1.9 %copy-start.5 = (f32[16,2048]{1,0:T(8,128)S(1)}, f32[16,2048]{1,0:T(8,128)}, u32[]{:S(2)}) copy-start(f32[16,2048]{1,0:T(8,128)} %get-tuple-element.72.refs_2_) | copy-start | bytes 393220
  49.3 1.2 %copy-start = (bf16[256,2048]{1,0:T(8,128)(2,1)S(1)}, bf16[256,2048]{1,0:T(8,128)(2,1)}, u32[]{:S(2)}) copy-start(bf16[256,2048]{1,0:T(8,128)(2,1)} %get-tuple-element.67.scaled_ref) | copy-start | bytes 3145732
  49.3 1.5 %copy-start.1 = (bf16[256,2048]{1,0:T(8,128)(2,1)S(1)}, bf16[256,2048]{1,0:T(8,128)(2,1)}, u32[]{:S(2)}) copy-start(bf16[256,2048]{1,0:T(8,128)(2,1)} %get-tuple-element.68.gain_ref) | copy-start | bytes 3145732
  49.3 1.5 %copy-start.3 = (f32[16,2048]{1,0:T(8,128)S(1)}, f32[16,2048]{1,0:T(8,128)}, u32[]{:S(2)}) copy-start(f32[16,2048]{1,0:T(8,128)} %get-tuple-element.70.refs_0_) | copy-start | bytes 393220
  49.4 1.5 %copy-start.6 = (f32[2048]{0:T(1024)S(1)}, f32[2048]{0:T(1024)}, u32[]{:S(2)}) copy-start(f32[2048]{0:T(1024)} %param.22) | copy-start | bytes 24580
  55.7 16.0 %collective-permute-start.2 = (bf16[2,272,512]{2,1,0:T(8,128)(2,1)S(1)}, bf16[2,272,512]{2,1,0:T(8,128)(2,1)S(1)}, u32[]{:S(2)}, u32[]{:S(2)}) collective-permute-start(bf16[2,272,512]{2,1,0:T(8,128)(2,1)S(1)} %get-tuple-element.73), channel_id=1, source_target_pairs={{0,1},{1,0},{2,3},{3,2},{4,5},{5,4},{6,7},{7,6},{8,9},{9,8},{10,11... | collective-permute-start | bytes 1671176 | tf_op jit(solution)/shard_map/ppermute | solution.py:450
  57.4 15.1 %collective-permute-start.3 = (bf16[2,272,512]{2,1,0:T(8,128)(2,1)S(1)}, bf16[2,272,512]{2,1,0:T(8,128)(2,1)S(1)}, u32[]{:S(2)}, u32[]{:S(2)}) collective-permute-start(bf16[2,272,512]{2,1,0:T(8,128)(2,1)S(1)} %get-tuple-element.74), channel_id=1, source_target_pairs={{0,3},{1,2},{2,1},{3,0},{4,7},{5,6},{6,5},{7,4},{8,11},{9,10},{10,... | collective-permute-start | bytes 1671176 | tf_op jit(solution)/shard_map/ppermute | solution.py:450
  64.3 17.3 %collective-permute-start.6 = (bf16[2,256,512]{2,1,0:T(8,128)(2,1)S(1)}, bf16[2,256,512]{2,1,0:T(8,128)(2,1)S(1)}, u32[]{:S(2)}, u32[]{:S(2)}) collective-permute-start(bf16[2,256,512]{2,1,0:T(8,128)(2,1)S(1)} %get-tuple-element.85), channel_id=1, source_target_pairs={{0,1},{1,0},{2,3},{3,2},{4,5},{5,4},{6,7},{7,6},{8,9},{9,8},{10,11... | collective-permute-start | bytes 1572872 | tf_op jit(solution)/shard_map/ppermute | solution.py:450
  65.1 18.7 %collective-permute-start.7 = (bf16[2,256,512]{2,1,0:T(8,128)(2,1)S(1)}, bf16[2,256,512]{2,1,0:T(8,128)(2,1)S(1)}, u32[]{:S(2)}, u32[]{:S(2)}) collective-permute-start(bf16[2,256,512]{2,1,0:T(8,128)(2,1)S(1)} %get-tuple-element.86), channel_id=1, source_target_pairs={{0,3},{1,2},{2,1},{3,0},{4,7},{5,6},{6,5},{7,4},{8,11},{9,10},{10,... | collective-permute-start | bytes 1572872 | tf_op jit(solution)/shard_map/ppermute | solution.py:450
  72.7 22.7 %collective-permute-start.4 = (bf16[272,512]{1,0:T(8,128)(2,1)S(1)}, bf16[272,512]{1,0:T(8,128)(2,1)S(1)}, u32[]{:S(2)}, u32[]{:S(2)}) collective-permute-start(bf16[272,512]{1,0:T(8,128)(2,1)S(1)} %get-tuple-element.78), channel_id=1, source_target_pairs={{0,3},{1,2},{2,1},{3,0},{4,7},{5,6},{6,5},{7,4},{8,11},{9,10},{10,... | collective-permute-start | bytes 835592 | tf_op jit(solution)/shard_map/ppermute | solution.py:450
  75.0 20.4 %collective-permute-start.5 = (bf16[272,512]{1,0:T(8,128)(2,1)S(1)}, bf16[272,512]{1,0:T(8,128)(2,1)S(1)}, u32[]{:S(2)}, u32[]{:S(2)}) collective-permute-start(bf16[272,512]{1,0:T(8,128)(2,1)S(1)} %get-tuple-element.79), channel_id=1, source_target_pairs={{0,1},{1,0},{2,3},{3,2},{4,5},{5,4},{6,7},{7,6},{8,9},{9,8},{10,11... | collective-permute-start | bytes 835592 | tf_op jit(solution)/shard_map/ppermute | solution.py:450
  83.9 11.5 %collective-permute-start.8 = (bf16[256,512]{1,0:T(8,128)(2,1)S(1)}, bf16[256,512]{1,0:T(8,128)(2,1)S(1)}, u32[]{:S(2)}, u32[]{:S(2)}) collective-permute-start(bf16[256,512]{1,0:T(8,128)(2,1)S(1)} %get-tuple-element.90), channel_id=1, source_target_pairs={{0,3},{1,2},{2,1},{3,0},{4,7},{5,6},{6,5},{7,4},{8,11},{9,10},{10,... | collective-permute-start | bytes 786440 | tf_op jit(solution)/shard_map/ppermute | solution.py:450
  86.2 9.1 %collective-permute-start.9 = (bf16[256,512]{1,0:T(8,128)(2,1)S(1)}, bf16[256,512]{1,0:T(8,128)(2,1)S(1)}, u32[]{:S(2)}, u32[]{:S(2)}) collective-permute-start(bf16[256,512]{1,0:T(8,128)(2,1)S(1)} %get-tuple-element.91), channel_id=1, source_target_pairs={{0,1},{1,0},{2,3},{3,2},{4,5},{5,4},{6,7},{7,6},{8,9},{9,8},{10,11... | collective-permute-start | bytes 786440 | tf_op jit(solution)/shard_map/ppermute | solution.py:450

commit v8 on v7

--- a/solution.py
+++ b/solution.py
@@ -17,7 +17,8 @@
 CH = HEADS * HEAD_DIM
 PIECE = 512
 HALF = TOK // 2
-ROWS = 144
+TAIL = 8
+ROWS = 128 + TAIL
 CTX = ("y", "x", "core")
 F32 = jnp.float32
 BF16 = jnp.bfloat16
@@ -65,15 +66,14 @@
 
 
 def decay_of(tail):
-    return tail[8:9] + tail[9:10] + tail[10:11]
+    return tail[4:5] + tail[5:6] + tail[6:7]
 
 
 def with_decay(tail, decay):
-    row = iota((16, 128), 0)
-    hi, mid, lo = three_parts(decay)
-    tail = jnp.where(row == 8, hi, tail)
-    tail = jnp.where(row == 9, mid, tail)
-    return jnp.where(row == 10, lo, tail)
+    row = iota((TAIL, 128), 0)
+    for i, part in enumerate(three_parts(decay)):
+        tail = jnp.where(row == 4 + i, part, tail)
+    return tail
 
 
 def end_state_kernel(
@@ -107,11 +107,11 @@
     copies[1].wait()
     inject_t = jnp.transpose(inject_ref[...].astype(F32)).astype(BF16)
     low_row = iota((8, 128), 1) < HEAD_DIM
-    row = iota((16, 128), 0)
+    row = iota((TAIL, 128), 0)
     tails = []
     for half in range(2):
         lanes = slice(half * 128, (half + 1) * 128)
-        tail = jnp.zeros((16, 128), F32)
+        tail = jnp.zeros((TAIL, 128), F32)
         for s in range(2):
             last = iota((SLEN, 128), 0) == length[s] - 1
             picked = jnp.sum(jnp.where(last, read_ref[s, :, lanes].astype(F32), 0.0), axis=0, keepdims=True)
@@ -142,7 +142,7 @@
 
 def join_cores_kernel(own_ref, sib_ref, out_ref):
     first = lax.axis_index("core") == 0
-    row = iota((16, 128), 0)
+    row = iota((TAIL, 128), 0)
     for k in range(16):
         own_tail = own_ref[k, 128:ROWS, :].astype(F32)
         sib_tail = sib_ref[k, 128:ROWS, :].astype(F32)
@@ -152,7 +152,7 @@
         out_ref[k, 0:128, :] = (
             own_ref[k, 0:128, :].astype(F32) * own_weight + sib_ref[k, 0:128, :].astype(F32) * sib_weight
         ).astype(BF16)
-        tail = jnp.where(row < 8, own_tail + sib_tail, 0.0)
+        tail = jnp.where(row < 4, own_tail + sib_tail, 0.0)
         out_ref[k, 128:ROWS, :] = with_decay(tail, own_decay * sib_decay).astype(BF16)
 
 
@@ -162,11 +162,10 @@
         out_ref[i, 0:128, :] = state.astype(BF16)
         decay = decay_of(in_ref[i, 128:ROWS, :].astype(F32))
         state = state * decay + in_ref[i, 0:128, :].astype(F32)
-    final = state.astype(BF16)
+    tails = jnp.concatenate([in_ref[i, 128:ROWS, :].astype(F32) for i in range(16)], axis=0).astype(BF16)
+    readings = jnp.dot(tails, state.astype(BF16), preferred_element_type=F32)
     for i in range(16):
-        out_ref[i, 128:ROWS, :] = jnp.dot(
-            in_ref[i, 128:ROWS, :], final, preferred_element_type=F32
-        ).astype(BF16)
+        out_ref[i, 128:ROWS, :] = readings[TAIL * i : TAIL * (i + 1)].astype(BF16)
 
 
 def split_cores_kernel(back_ref, own_ref, sib_ref, mine_ref, send_ref):
@@ -183,7 +182,7 @@
         send_ref[k, 0:128, :] = jnp.where(first, second, arrived).astype(BF16)
         send_ref[k, 128:ROWS, :] = back_ref[k, 128:ROWS, :]
     for q in range(8):
-        mine_ref[256:272, q * 128 : (q + 1) * 128] = (
+        mine_ref[STATE : STATE + TAIL, q * 128 : (q + 1) * 128] = (
             back_ref[2 * q, 128:ROWS, :].astype(F32) + back_ref[2 * q + 1, 128:ROWS, :].astype(F32)
         ).astype(BF16)
 
@@ -241,7 +240,7 @@
         skip = per_pair(skip_ref[...], pair, (1, 128), low[0:1])
         out = local + carried[:, lanes] * grown + skip * values
         gate = gate_ref[:, lanes].astype(F32)
-        gate = gate / (1.0 + jnp.exp(-gate))
+        gate = gate * jax.nn.sigmoid(gate)
         scaled_ref[:, lanes] = (out * gate).astype(BF16)
         gain_ref[:, lanes] = (gate * grown * before[0:1, lanes]).astype(BF16)
         end = now[BLOCK - 1 : BLOCK, :]
@@ -319,13 +318,14 @@
     for i, (flip, half) in enumerate(pieces):
         at = pl.multiple_of(((z ^ flip) * 2 + half) * PIECE, PIECE)
         copies.append(pltpu.make_async_copy(weight_ref.at[:, pl.ds(at, PIECE)], held.at[i], sems.at[i]))
+    return copies
+
+
+def fetch_kernel(pieces, weight_ref, out_ref, sems):
+    copies = column_copies(pieces, weight_ref, out_ref, sems)
     for copy in copies:
         copy.start()
-    return copies
-
-
-def fetch_kernel(pieces, weight_ref, out_ref, sems):
-    for copy in column_copies(pieces, weight_ref, out_ref, sems):
+    for copy in copies:
         copy.wait()
 
 
@@ -351,12 +351,12 @@
         ref[k] = jnp.dot(normed[...], column[...], preferred_element_type=F32).astype(BF16)
 
 
-def gate_and_normalize(place, state_ref, read_ref, scaled_ref, gain_ref, norm_ref, normed):
+HERE = tuple(slice(start % HALF, start % HALF + rows) for start, rows in CHUNKS)
+
+
+def arriving(place, state_ref, read_ref):
     start, rows = CHUNKS[place]
-    arrived = jnp.dot(read_ref[start : start + rows, :], state_ref[0:STATE, :], preferred_element_type=F32)
-    here = slice(start % HALF, start % HALF + rows)
-    gated = scaled_ref[here, :].astype(F32) + arrived * gain_ref[here, :].astype(F32)
-    normed[0:rows, :] = normalize(gated, norm_ref[...])
+    return jnp.dot(read_ref[start : start + rows, :], state_ref[0:STATE, :], preferred_element_type=F32)
 
 
 def join_halves_kernel(mine_ref, theirs_ref, state_ref):
@@ -366,7 +366,7 @@
         lanes = pl.ds(pl.multiple_of((1 - core) * 1024 + q * 128, 128), 128)
         for n in range(2):
             state_ref[n * 128 : (n + 1) * 128, lanes] = theirs_ref[2 * q + n, 0:128, :]
-        state_ref[256:272, lanes] = (
+        state_ref[STATE : STATE + TAIL, lanes] = (
             theirs_ref[2 * q, 128:ROWS, :].astype(F32) + theirs_ref[2 * q + 1, 128:ROWS, :].astype(F32)
         ).astype(BF16)
 
@@ -375,15 +375,23 @@
     if place == LEADING:
         *sample, first_ref, second_ref, normed_ref, held, sems = refs
         copies = column_copies(FIRST[1:], far_ref, held, sems)
+        copies[0].start()
     else:
         *sample, first_ref, second_ref, normed_ref = refs
         held = far_ref
-    gate_and_normalize(place, state_ref, read_ref, scaled_ref, gain_ref, norm_ref, normed_ref)
+    arrived = arriving(place, state_ref, read_ref)
+    if place == LEADING:
+        copies[1].start()
+    gated = scaled_ref[HERE[place], :].astype(F32) + arrived * gain_ref[HERE[place], :].astype(F32)
+    normed_ref[0 : CHUNKS[place][1], :] = normalize(gated, norm_ref[...])
+    if place == LEADING:
+        copies[2].start()
     if sampled:
         local_ref, grown_ref, gate_ref = sample
-        readings = state_ref[256:272, :].astype(F32)
-        moved = jnp.concatenate([readings[2:16], readings[0:2]], axis=0)
+        readings = state_ref[STATE : STATE + TAIL, :].astype(F32)
+        moved = jnp.concatenate([readings[2:TAIL], readings[0:2]], axis=0)
         readings = jnp.where(lax.axis_index("core") == 0, readings, moved)
+        readings = jnp.concatenate([readings, jnp.zeros((16 - TAIL, CH), F32)], axis=0)
         sampled = (local_ref[...] + readings * grown_ref[...]) * gate_ref[...]
         rows = CHUNKS[place][1]
         normed_ref[rows : rows + 16, :] = normalize(sampled, norm_ref[...])
@@ -404,21 +412,15 @@
 
 
 def finish_kernel(*refs):
-    ins, (out_ref, sample_ref, turned, sems) = refs[:-4], refs[-4:]
-    copies = []
+    ins, out_ref, sample_ref = refs[:-2], refs[-2], refs[-1]
     for place, (start, rows) in enumerate(CHUNKS):
         ra, rb, rest, sa, sb = ins[5 * place : 5 * place + 5]
         for half, (own, near, far) in enumerate(((0, ra, sa), (2, rb, sb))):
             total = rest[own].astype(F32) + near[0].astype(F32) + far[...].astype(F32)
             columns = slice(half * PIECE, (half + 1) * PIECE)
-            here = (columns, slice(start, start + rows))
-            turned[here] = jnp.transpose(total[0:rows]).astype(BF16)
+            out_ref[columns, start : start + rows] = jnp.transpose(total[0:rows]).astype(BF16)
             if place == LEADING:
                 sample_ref[:, columns] = total[rows : rows + 2].astype(BF16)
-            copies.append(pltpu.make_async_copy(turned.at[here], out_ref.at[here], sems.at[len(copies)]))
-            copies[-1].start()
-    for copy in copies:
-        copy.wait()
 
 
 def in_hbm(*arrays):
@@ -536,14 +538,14 @@
     )
     back, scaled_2, weight = lax.optimization_barrier((back, scaled_2, out_weight))
     mine, send = call(
-        split_cores_kernel, "split_cores", (shape((272, 1024)), slices_shape), (back, keep, sibling), 16
+        split_cores_kernel, "split_cores", (shape((STATE + TAIL, 1024)), slices_shape), (back, keep, sibling), 16
     )
     theirs = other_core(send)
 
     near_columns = fetch(FIRST[:1], weight)
     scaled = (scaled_1, scaled_2)
     gain = (gain_1, gain_2)
-    state = call(join_halves_kernel, "join_halves", shape((272, CH)), (mine, theirs), 8)
+    state = call(join_halves_kernel, "join_halves", shape((STATE + TAIL, CH)), (mine, theirs), 8)
 
     def chunk(place, far_columns, *sample):
         start, rows = CHUNKS[place]
@@ -575,15 +577,7 @@
     rest_columns = fetch(REST, weight)
     normed_1, near_1 = chunk(1, resident(far_columns))
     parts = exchange(normed_0, near_0, rest_columns) + exchange(normed_1, near_1, rest_columns)
-    prompt_mixed, sample_mixed = pl.pallas_call(
-        finish_kernel,
-        out_shape=(shape((1024, TOK)), shape((2, 1024))),
-        in_specs=[VMEM] * 10,
-        out_specs=(anywhere, VMEM),
-        scratch_shapes=[pltpu.VMEM((1024, TOK), BF16), pltpu.SemaphoreType.DMA((4,))],
-        compiler_params=pltpu.CompilerParams(vmem_limit_bytes=16 << 20),
-        name="finish",
-    )(*parts)
+    prompt_mixed, sample_mixed = call(finish_kernel, "finish", (shape((1024, TOK)), shape((2, 1024))), parts, 16)
     return prompt_mixed, sample_mixed.T
 
 

time: 97.9 us -> 96.3 us (0.984)
  Pallas kernels: 46 us -> 44.6 us
    pallas_call x1 -> x0, Pallas kernels: 1.88 us -> none  [per_device(): pl.pallas_call(finish_kernel, out_shape=(shape((1024, TOK)), shape((2, 10...]
    pallas_call x9 -> x10, Pallas kernels: 10.3 us -> 11.6 us  [call(): pl.pallas_call(kernel, out_shape=out_shape, in_specs=[SMEM] * scalars + [...]
where the time goes in v8:
time: 96.3 us; the launch traced here: 95.7 us
  Pallas kernels  44.6 us (46%)
  starting transfers between devices  26.1 us (27%)
  waiting for transfers between devices  22.1 us (23%)
  local copies, waits for them, and re-layouts  2.01 us (2%)
    ppermute x8, waiting for transfers between devices, swap(): return lax.ppermute(x, 'head', [(i, i ^ step) for i in range(4)])  16.4 us
    pallas_call x2, Pallas kernels, local_outputs(): pl.pallas_call(functools.partial(local_kernel, part), grid=(blocks,), out...  14.5 us
    pallas_call x10, Pallas kernels, call(): pl.pallas_call(kernel, out_shape=out_shape, in_specs=[SMEM] * scalars + [...  11.6 us
    ppermute x8, starting transfers between devices, swap(): return lax.ppermute(x, 'head', [(i, i ^ step) for i in range(4)])  10 us
    pallas_call x2, Pallas kernels, chunk(): pl.pallas_call(functools.partial(chunk_kernel, place, bool(sample)), out_...  9.08 us
    all_to_all x1, starting transfers between devices, per_device(): slices = lax.all_to_all(joined, ('y', 'x'), 0, 0, tiled=True)  6.84 us
    all_to_all x1, starting transfers between devices, per_device(): back = lax.all_to_all(prefix, ('y', 'x'), 0, 0, tiled=True)  5.38 us
    pallas_call x2, Pallas kernels, fetch(): pl.pallas_call(functools.partial(fetch_kernel, pieces), out_shape=pltpu.V...  5.22 us
  transfers between devices with their start and end apart: 12, of which 7 were waited for; matrix products, arithmetic and copies ran while one was open for 1% of the time, Pallas kernels for 33%

profile of v8, /device:TPU:1, one launch (start us, length us, event | category | flops | bytes accessed | tf_op | source)
XLA Modules:
  0.0 95.7 jit_solution(7611022173503553689)
XLA Ops:
  0.6 4.2 %end_state.1 = (bf16[16,136,128]{2,1,0:T(8,128)(2,1)S(1)}, bf16[16,136,128]{2,1,0:T(8,128)(2,1)S(1)}) custom-call(s32[2]{0:T(128)} %length.3, f32[32,512]{1,0:T(8,128)} %step_ref.1, f32[1,32]{1,0:T(1,128)} %bitcast.15, bf16[512,2048]{1,0:T(8,128)(2,1)} %values_ref.5, bf16[512,256]{1,0:T(8,128)(2,1)} %bitcast.22, bf16[2,16,256]{2,1,0:T(8,128)(2,1)} %bitcast.26), custom_call_target="tpu_custom_call" | custom-call | tf_op jit(solution)/shard_map/end_state/pallas_call | solution.py:509
  4.8 1.5 %collective-permute-start = (bf16[16,136,128]{2,1,0:T(8,128)(2,1)S(1)}, bf16[16,136,128]{2,1,0:T(8,128)(2,1)S(1)}, u32[]{:S(2)}, u32[]{:S(2)}) collective-permute-start(bf16[16,136,128]{2,1,0:T(8,128)(2,1)S(1)} %get-tuple-element.50), channel_id=1, source_target_pairs={{0,4},{4,0},{1,5},{5,1},{2,6},{6,2},{3,7},{7,3},{8,12},{12,8},{9,1... | collective-permute-start | bytes 1671176 | tf_op jit(solution)/shard_map/ppermute | solution.py:456
  9.0 6.8 %all-to-all-start = ((bf16[16,136,128]{2,1,0:T(8,128)(2,1)}), bf16[16,136,128]{2,1,0:T(8,128)(2,1)S(1)}, u32[]{:S(2)}, u32[]{:S(2)}) async-start(bf16[16,136,128]{2,1,0:T(8,128)(2,1)} %join_cores.1), calls=%async_computation | async-start | bytes 1114112 | tf_op jit(solution)/shard_map/all_to_all | solution.py:524
  15.8 2.4 %sample_outputs.1 = (f32[16,2048]{1,0:T(8,128)}, f32[16,2048]{1,0:T(8,128)}, f32[16,2048]{1,0:T(8,128)}) custom-call(s32[2]{0:T(128)S(1)} %copy-done.7, f32[2,32,16]{2,1,0:T(8,128)} %bitcast.25, f32[1,32]{1,0:T(1,128)} %bitcast.16, f32[1,32]{1,0:T(1,128)} %bitcast.19, bf16[2,16,2048]{2,1,0:T(8,128)(2,1)} %values_ref.4, bf16[2,16,2048]{2,1,0:T(8,128)(2,1)} %gate_ref.4, ...), custom_call_target="tpu_custom_call" | custom-call | flops 1 | bytes 1 | tf_op jit(solution)/shard_map/sample_outputs/pallas_call | solution.py:431
  18.3 7.4 %local_outputs.2 = (bf16[256,2048]{1,0:T(8,128)(2,1)}, bf16[256,2048]{1,0:T(8,128)(2,1)}, bf16[256,2048]{1,0:T(8,128)(2,1)}, f32[8,2048]{1,0:T(8,128)}) custom-call(f32[32,512]{1,0:T(8,128)} %step_ref.1, f32[1,32]{1,0:T(1,128)S(1)} %bitcast.17, f32[1,32]{1,0:T(1,128)S(1)} %bitcast.20, bf16[512,2048]{1,0:T(8,128)(2,1)} %values_ref.5, ...), custom_call_target="tpu_custom_call" | custom-call | flops 3221225472 | bytes 20971520 | tf_op jit(solution)/shard_map/local_outputs/pallas_call | solution.py:479
  25.6 1.3 %all-to-all-done.in_ref = bf16[16,136,128]{2,1,0:T(8,128)(2,1)S(1)} async-done(((bf16[16,136,128]{2,1,0:T(8,128)(2,1)}), bf16[16,136,128]{2,1,0:T(8,128)(2,1)S(1)}, u32[]{:S(2)}, u32[]{:S(2)}) %all-to-all-start) | async-done | bytes 557088 | tf_op jit(solution)/shard_map/all_to_all | solution.py:524
  28.0 5.4 %all-to-all-start.1 = ((bf16[16,136,128]{2,1,0:T(8,128)(2,1)}), bf16[16,136,128]{2,1,0:T(8,128)(2,1)S(1)}, u32[]{:S(2)}, u32[]{:S(2)}) async-start(bf16[16,136,128]{2,1,0:T(8,128)(2,1)} %prefix.1), calls=%async_computation.1 | async-start | bytes 1114112 | tf_op jit(solution)/shard_map/all_to_all | solution.py:535
  33.4 7.2 %local_outputs.3 = (bf16[256,2048]{1,0:T(8,128)(2,1)}, bf16[256,2048]{1,0:T(8,128)(2,1)}) custom-call(f32[32,512]{1,0:T(8,128)} %step_ref.1, f32[1,32]{1,0:T(1,128)S(1)} %bitcast.18, f32[1,32]{1,0:T(1,128)S(1)} %bitcast.21, bf16[512,2048]{1,0:T(8,128)(2,1)} %values_ref.5, bf16[512,2048]{1,0:T(8,128)(2,1)} %gate_ref.5, bf16[512,256]{1,0:T(8,128)(2,1)} %bitcast.24, ...), custom_call_target="tpu_custom_call" | custom-call | flops 3221225472 | bytes 20971520 | tf_op jit(solution)/shard_map/local_outputs/pallas_call | solution.py:479
  40.6 3.6 %all-to-all-done.1.back_ref = bf16[16,136,128]{2,1,0:T(8,128)(2,1)S(1)} async-done(((bf16[16,136,128]{2,1,0:T(8,128)(2,1)}), bf16[16,136,128]{2,1,0:T(8,128)(2,1)S(1)}, u32[]{:S(2)}, u32[]{:S(2)}) %all-to-all-start.1) | async-done | bytes 557088 | tf_op jit(solution)/shard_map/all_to_all | solution.py:535
  44.5 2.4 %collective-permute-start.1 = (bf16[16,136,128]{2,1,0:T(8,128)(2,1)S(1)}, bf16[16,136,128]{2,1,0:T(8,128)(2,1)S(1)}, u32[]{:S(2)}, u32[]{:S(2)}) collective-permute-start(bf16[16,136,128]{2,1,0:T(8,128)(2,1)S(1)} %get-tuple-element.66), channel_id=1, source_target_pairs={{0,4},{4,0},{1,5},{5,1},{2,6},{6,2},{3,7},{7,3},{8,12},{12,8},{9,1... | collective-permute-start | bytes 1671176 | tf_op jit(solution)/shard_map/ppermute | solution.py:456
  46.9 1.7 %fetch_weight.2.near_ref = bf16[1,2048,512]{2,1,0:T(8,128)(2,1)S(1)} custom-call(bf16[2048,4096]{1,0:T(8,128)(2,1)} %weight_ref.1), custom_call_target="tpu_custom_call" | custom-call | tf_op jit(solution)/shard_map/fetch_weight/pallas_call | solution.py:337
  50.1 4.5 %chunk.2 = (bf16[2,272,512]{2,1,0:T(8,128)(2,1)S(1)}, bf16[2,272,512]{2,1,0:T(8,128)(2,1)S(1)}, bf16[272,2048]{1,0:T(8,128)(2,1)S(1)}, bf16[3,2048,512]{2,1,0:T(8,128)(2,1)S(1)}) custom-call(bf16[264,2048]{1,0:T(8,128)(2,1)S(1)} %join_halves.1.state_ref, bf16[512,256]{1,0:T(8,128)(2,1)S(1)} %bitcast.11, bf16[256,2048]{1,0:T(8,128)(2,1)S(1)} %copy-done, ...), custom_call_target="tpu_custom_call" | custom-call | tf_op jit(solution)/shard_map/chunk/pallas_call | solution.py:558
  54.6 1.7 %collective-permute-start.2 = (bf16[2,272,512]{2,1,0:T(8,128)(2,1)S(1)}, bf16[2,272,512]{2,1,0:T(8,128)(2,1)S(1)}, u32[]{:S(2)}, u32[]{:S(2)}) collective-permute-start(bf16[2,272,512]{2,1,0:T(8,128)(2,1)S(1)} %get-tuple-element.73), channel_id=1, source_target_pairs={{0,1},{1,0},{2,3},{3,2},{4,5},{5,4},{6,7},{7,6},{8,9},{9,8},{10,11... | collective-permute-start | bytes 1671176 | tf_op jit(solution)/shard_map/ppermute | solution.py:452
  56.3 2.2 %collective-permute-start.3 = (bf16[2,272,512]{2,1,0:T(8,128)(2,1)S(1)}, bf16[2,272,512]{2,1,0:T(8,128)(2,1)S(1)}, u32[]{:S(2)}, u32[]{:S(2)}) collective-permute-start(bf16[2,272,512]{2,1,0:T(8,128)(2,1)S(1)} %get-tuple-element.74), channel_id=1, source_target_pairs={{0,3},{1,2},{2,1},{3,0},{4,7},{5,6},{6,5},{7,4},{8,11},{9,10},{10,... | collective-permute-start | bytes 1671176 | tf_op jit(solution)/shard_map/ppermute | solution.py:452
  58.5 4.6 %chunk.3 = (bf16[2,256,512]{2,1,0:T(8,128)(2,1)S(1)}, bf16[2,256,512]{2,1,0:T(8,128)(2,1)S(1)}, bf16[256,2048]{1,0:T(8,128)(2,1)S(1)}) custom-call(bf16[264,2048]{1,0:T(8,128)(2,1)S(1)} %join_halves.1.state_ref, bf16[512,256]{1,0:T(8,128)(2,1)S(1)} %bitcast.12, bf16[256,2048]{1,0:T(8,128)(2,1)} %get-tuple-element.82.scaled_ref, ...), custom_call_target="tpu_custom_call" | custom-call | tf_op jit(solution)/shard_map/chunk/pallas_call | solution.py:558
  64.6 3.5 %fetch_weight.3.weight_ref = bf16[4,2048,512]{2,1,0:T(8,128)(2,1)S(1)} custom-call(bf16[2048,4096]{1,0:T(8,128)(2,1)} %weight_ref.1), custom_call_target="tpu_custom_call" | custom-call | tf_op jit(solution)/shard_map/fetch_weight/pallas_call | solution.py:337
  68.1 2.5 %rest.2.rest_ref.refs_2_ = bf16[4,272,512]{2,1,0:T(8,128)(2,1)S(1)} custom-call(bf16[272,2048]{1,0:T(8,128)(2,1)S(1)} %get-tuple-element.77.normed_ref, bf16[4,2048,512]{2,1,0:T(8,128)(2,1)S(1)} %fetch_weight.3.weight_ref), custom_call_target="tpu_custom_call" | custom-call | flops 1 | bytes 1 | tf_op jit(solution)/shard_map/rest/pallas_call | solution.py:431
  71.5 2.3 %collective-permute-start.4 = (bf16[272,512]{1,0:T(8,128)(2,1)S(1)}, bf16[272,512]{1,0:T(8,128)(2,1)S(1)}, u32[]{:S(2)}, u32[]{:S(2)}) collective-permute-start(bf16[272,512]{1,0:T(8,128)(2,1)S(1)} %get-tuple-element.78), channel_id=1, source_target_pairs={{0,3},{1,2},{2,1},{3,0},{4,7},{5,6},{6,5},{7,4},{8,11},{9,10},{10,... | collective-permute-start | bytes 835592 | tf_op jit(solution)/shard_map/ppermute | solution.py:452
  73.9 2.3 %rest.3.rest_ref.refs_7_ = bf16[4,256,512]{2,1,0:T(8,128)(2,1)S(1)} custom-call(bf16[256,2048]{1,0:T(8,128)(2,1)S(1)} %get-tuple-element.89.normed_ref, bf16[4,2048,512]{2,1,0:T(8,128)(2,1)S(1)} %fetch_weight.3.weight_ref), custom_call_target="tpu_custom_call" | custom-call | flops 1 | bytes 1 | tf_op jit(solution)/shard_map/rest/pallas_call | solution.py:431
  76.2 4.2 %collective-permute-done.6.a_ref.refs_5_ = bf16[2,256,512]{2,1,0:T(8,128)(2,1)S(1)} collective-permute-done((bf16[2,256,512]{2,1,0:T(8,128)(2,1)S(1)}, bf16[2,256,512]{2,1,0:T(8,128)(2,1)S(1)}, u32[]{:S(2)}, u32[]{:S(2)}) %collective-permute-start.6) | collective-permute-done | bytes 524320 | tf_op jit(solution)/shard_map/ppermute | solution.py:452
  80.4 2.2 %collective-permute-done.7.b_ref.refs_6_ = bf16[2,256,512]{2,1,0:T(8,128)(2,1)S(1)} collective-permute-done((bf16[2,256,512]{2,1,0:T(8,128)(2,1)S(1)}, bf16[2,256,512]{2,1,0:T(8,128)(2,1)S(1)}, u32[]{:S(2)}, u32[]{:S(2)}) %collective-permute-start.7) | collective-permute-done | bytes 524320 | tf_op jit(solution)/shard_map/ppermute | solution.py:452
  82.8 2.3 %collective-permute-start.8 = (bf16[256,512]{1,0:T(8,128)(2,1)S(1)}, bf16[256,512]{1,0:T(8,128)(2,1)S(1)}, u32[]{:S(2)}, u32[]{:S(2)}) collective-permute-start(bf16[256,512]{1,0:T(8,128)(2,1)S(1)} %get-tuple-element.90), channel_id=1, source_target_pairs={{0,3},{1,2},{2,1},{3,0},{4,7},{5,6},{6,5},{7,4},{8,11},{9,10},{10,... | collective-permute-start | bytes 786440 | tf_op jit(solution)/shard_map/ppermute | solution.py:452
  85.1 9.1 %collective-permute-done.8.refs_8_ = bf16[256,512]{1,0:T(8,128)(2,1)S(1)} collective-permute-done((bf16[256,512]{1,0:T(8,128)(2,1)S(1)}, bf16[256,512]{1,0:T(8,128)(2,1)S(1)}, u32[]{:S(2)}, u32[]{:S(2)}) %collective-permute-start.8) | collective-permute-done | bytes 262176 | tf_op jit(solution)/shard_map/ppermute | solution.py:452
  94.2 1.5 %finish.1 = (bf16[1024,512]{1,0:T(8,128)(2,1)}, bf16[2,1024]{1,0:T(2,128)(2,1)}) custom-call(bf16[2,272,512]{2,1,0:T(8,128)(2,1)S(1)} %collective-permute-done.2.a_ref.refs_0_, bf16[2,272,512]{2,1,0:T(8,128)(2,1)S(1)} %collective-permute-done.3.b_ref.refs_1_, bf16[4,272,512]{2,1,0:T(8,128)(2,1)S(1)} %rest.2.rest_ref.refs_2_, ...), custom_call_target="tpu_custom_call" | custom-call | flops 1 | bytes 1 | tf_op jit(solution)/shard_map/finish/pallas_call | solution.py:431
  (40 shorter events, 8.1 us)
Async XLA Ops:
  0.6 5.7 %copy-start.10 = (f32[32,2,16]{0,2,1:T(8,128)S(1)}, f32[32,2,16]{0,2,1:T(8,128)}, u32[]{:S(2)}) copy-start(f32[32,2,16]{0,2,1:T(8,128)} %param.28) | copy-start | bytes 12292
  0.6 15.2 %copy-start.7 = (s32[2]{0:T(128)S(1)}, s32[2]{0:T(128)}, u32[]{:S(2)}) copy-start(s32[2]{0:T(128)} %length.3) | copy-start | bytes 28
  4.8 13.4 %copy-start.8 = (f32[32]{0:T(128)S(1)}, f32[32]{0:T(128)}, u32[]{:S(2)}) copy-start(f32[32]{0:T(128)} %param.20) | copy-start | bytes 388
  4.8 13.4 %copy-start.9 = (f32[32]{0:T(128)S(1)}, f32[32]{0:T(128)}, u32[]{:S(2)}) copy-start(f32[32]{0:T(128)} %param.21) | copy-start | bytes 388
  4.8 3.1 %collective-permute-start = (bf16[16,136,128]{2,1,0:T(8,128)(2,1)S(1)}, bf16[16,136,128]{2,1,0:T(8,128)(2,1)S(1)}, u32[]{:S(2)}, u32[]{:S(2)}) collective-permute-start(bf16[16,136,128]{2,1,0:T(8,128)(2,1)S(1)} %get-tuple-element.50), channel_id=1, source_target_pairs={{0,4},{4,0},{1,5},{5,1},{2,6},{6,2},{3,7},{7,3},{8,12},{12,8},{9,1... | collective-permute-start | bytes 1671176 | tf_op jit(solution)/shard_map/ppermute | solution.py:456
  9.0 17.9 %all-to-all-start = ((bf16[16,136,128]{2,1,0:T(8,128)(2,1)}), bf16[16,136,128]{2,1,0:T(8,128)(2,1)S(1)}, u32[]{:S(2)}, u32[]{:S(2)}) async-start(bf16[16,136,128]{2,1,0:T(8,128)(2,1)} %join_cores.1), calls=%async_computation | async-start | bytes 1114112 | tf_op jit(solution)/shard_map/all_to_all | solution.py:524
  28.0 16.1 %all-to-all-start.1 = ((bf16[16,136,128]{2,1,0:T(8,128)(2,1)}), bf16[16,136,128]{2,1,0:T(8,128)(2,1)S(1)}, u32[]{:S(2)}, u32[]{:S(2)}) async-start(bf16[16,136,128]{2,1,0:T(8,128)(2,1)} %prefix.1), calls=%async_computation.1 | async-start | bytes 1114112 | tf_op jit(solution)/shard_map/all_to_all | solution.py:535
  44.5 4.1 %collective-permute-start.1 = (bf16[16,136,128]{2,1,0:T(8,128)(2,1)S(1)}, bf16[16,136,128]{2,1,0:T(8,128)(2,1)S(1)}, u32[]{:S(2)}, u32[]{:S(2)}) collective-permute-start(bf16[16,136,128]{2,1,0:T(8,128)(2,1)S(1)} %get-tuple-element.66), channel_id=1, source_target_pairs={{0,4},{4,0},{1,5},{5,1},{2,6},{6,2},{3,7},{7,3},{8,12},{12,8},{9,1... | collective-permute-start | bytes 1671176 | tf_op jit(solution)/shard_map/ppermute | solution.py:456
  46.8 1.9 %copy-start.2 = (bf16[512,1,256]{2,0,1:T(8,128)(2,1)S(1)}, bf16[512,1,256]{2,0,1:T(8,128)(2,1)}, u32[]{:S(2)}) copy-start(bf16[512,1,256]{2,0,1:T(8,128)(2,1)} %param.18) | copy-start | bytes 786436
  46.8 1.9 %copy-start.3 = (f32[16,2048]{1,0:T(8,128)S(1)}, f32[16,2048]{1,0:T(8,128)}, u32[]{:S(2)}) copy-start(f32[16,2048]{1,0:T(8,128)} %get-tuple-element.70.refs_0_) | copy-start | bytes 393220
  46.8 1.9 %copy-start.4 = (f32[16,2048]{1,0:T(8,128)S(1)}, f32[16,2048]{1,0:T(8,128)}, u32[]{:S(2)}) copy-start(f32[16,2048]{1,0:T(8,128)} %get-tuple-element.71.refs_1_) | copy-start | bytes 393220
  46.9 2.0 %copy-start.5 = (f32[16,2048]{1,0:T(8,128)S(1)}, f32[16,2048]{1,0:T(8,128)}, u32[]{:S(2)}) copy-start(f32[16,2048]{1,0:T(8,128)} %get-tuple-element.72.refs_2_) | copy-start | bytes 393220
  48.5 1.2 %copy-start = (bf16[256,2048]{1,0:T(8,128)(2,1)S(1)}, bf16[256,2048]{1,0:T(8,128)(2,1)}, u32[]{:S(2)}) copy-start(bf16[256,2048]{1,0:T(8,128)(2,1)} %get-tuple-element.67.scaled_ref) | copy-start | bytes 3145732
  48.5 1.5 %copy-start.1 = (bf16[256,2048]{1,0:T(8,128)(2,1)S(1)}, bf16[256,2048]{1,0:T(8,128)(2,1)}, u32[]{:S(2)}) copy-start(bf16[256,2048]{1,0:T(8,128)(2,1)} %get-tuple-element.68.gain_ref) | copy-start | bytes 3145732
  48.6 1.5 %copy-start.6 = (f32[2048]{0:T(1024)S(1)}, f32[2048]{0:T(1024)}, u32[]{:S(2)}) copy-start(f32[2048]{0:T(1024)} %param.22) | copy-start | bytes 24580
  54.6 16.0 %collective-permute-start.2 = (bf16[2,272,512]{2,1,0:T(8,128)(2,1)S(1)}, bf16[2,272,512]{2,1,0:T(8,128)(2,1)S(1)}, u32[]{:S(2)}, u32[]{:S(2)}) collective-permute-start(bf16[2,272,512]{2,1,0:T(8,128)(2,1)S(1)} %get-tuple-element.73), channel_id=1, source_target_pairs={{0,1},{1,0},{2,3},{3,2},{4,5},{5,4},{6,7},{7,6},{8,9},{9,8},{10,11... | collective-permute-start | bytes 1671176 | tf_op jit(solution)/shard_map/ppermute | solution.py:452
  56.3 15.1 %collective-permute-start.3 = (bf16[2,272,512]{2,1,0:T(8,128)(2,1)S(1)}, bf16[2,272,512]{2,1,0:T(8,128)(2,1)S(1)}, u32[]{:S(2)}, u32[]{:S(2)}) collective-permute-start(bf16[2,272,512]{2,1,0:T(8,128)(2,1)S(1)} %get-tuple-element.74), channel_id=1, source_target_pairs={{0,3},{1,2},{2,1},{3,0},{4,7},{5,6},{6,5},{7,4},{8,11},{9,10},{10,... | collective-permute-start | bytes 1671176 | tf_op jit(solution)/shard_map/ppermute | solution.py:452
  63.1 17.3 %collective-permute-start.6 = (bf16[2,256,512]{2,1,0:T(8,128)(2,1)S(1)}, bf16[2,256,512]{2,1,0:T(8,128)(2,1)S(1)}, u32[]{:S(2)}, u32[]{:S(2)}) collective-permute-start(bf16[2,256,512]{2,1,0:T(8,128)(2,1)S(1)} %get-tuple-element.85), channel_id=1, source_target_pairs={{0,1},{1,0},{2,3},{3,2},{4,5},{5,4},{6,7},{7,6},{8,9},{9,8},{10,11... | collective-permute-start | bytes 1572872 | tf_op jit(solution)/shard_map/ppermute | solution.py:452
  64.0 18.7 %collective-permute-start.7 = (bf16[2,256,512]{2,1,0:T(8,128)(2,1)S(1)}, bf16[2,256,512]{2,1,0:T(8,128)(2,1)S(1)}, u32[]{:S(2)}, u32[]{:S(2)}) collective-permute-start(bf16[2,256,512]{2,1,0:T(8,128)(2,1)S(1)} %get-tuple-element.86), channel_id=1, source_target_pairs={{0,3},{1,2},{2,1},{3,0},{4,7},{5,6},{6,5},{7,4},{8,11},{9,10},{10,... | collective-permute-start | bytes 1572872 | tf_op jit(solution)/shard_map/ppermute | solution.py:452
  71.5 22.7 %collective-permute-start.4 = (bf16[272,512]{1,0:T(8,128)(2,1)S(1)}, bf16[272,512]{1,0:T(8,128)(2,1)S(1)}, u32[]{:S(2)}, u32[]{:S(2)}) collective-permute-start(bf16[272,512]{1,0:T(8,128)(2,1)S(1)} %get-tuple-element.78), channel_id=1, source_target_pairs={{0,3},{1,2},{2,1},{3,0},{4,7},{5,6},{6,5},{7,4},{8,11},{9,10},{10,... | collective-permute-start | bytes 835592 | tf_op jit(solution)/shard_map/ppermute | solution.py:452
  73.9 20.4 %collective-permute-start.5 = (bf16[272,512]{1,0:T(8,128)(2,1)S(1)}, bf16[272,512]{1,0:T(8,128)(2,1)S(1)}, u32[]{:S(2)}, u32[]{:S(2)}) collective-permute-start(bf16[272,512]{1,0:T(8,128)(2,1)S(1)} %get-tuple-element.79), channel_id=1, source_target_pairs={{0,1},{1,0},{2,3},{3,2},{4,5},{5,4},{6,7},{7,6},{8,9},{9,8},{10,11... | collective-permute-start | bytes 835592 | tf_op jit(solution)/shard_map/ppermute | solution.py:452
  82.8 11.5 %collective-permute-start.8 = (bf16[256,512]{1,0:T(8,128)(2,1)S(1)}, bf16[256,512]{1,0:T(8,128)(2,1)S(1)}, u32[]{:S(2)}, u32[]{:S(2)}) collective-permute-start(bf16[256,512]{1,0:T(8,128)(2,1)S(1)} %get-tuple-element.90), channel_id=1, source_target_pairs={{0,3},{1,2},{2,1},{3,0},{4,7},{5,6},{6,5},{7,4},{8,11},{9,10},{10,... | collective-permute-start | bytes 786440 | tf_op jit(solution)/shard_map/ppermute | solution.py:452
  85.1 9.1 %collective-permute-start.9 = (bf16[256,512]{1,0:T(8,128)(2,1)S(1)}, bf16[256,512]{1,0:T(8,128)(2,1)S(1)}, u32[]{:S(2)}, u32[]{:S(2)}) collective-permute-start(bf16[256,512]{1,0:T(8,128)(2,1)S(1)} %get-tuple-element.91), channel_id=1, source_target_pairs={{0,1},{1,0},{2,3},{3,2},{4,5},{5,4},{6,7},{7,6},{8,9},{9,8},{10,11... | collective-permute-start | bytes 786440 | tf_op jit(solution)/shard_map/ppermute | solution.py:452

commit v9 on v8

--- a/solution.py
+++ b/solution.py
@@ -321,8 +321,12 @@
     return copies
 
 
-def fetch_kernel(pieces, weight_ref, out_ref, sems):
+def fetch_kernel(pieces, weight_ref, *refs):
+    extra = (len(refs) - 2) // 2
+    extra_refs, (out_ref, *extra_outs, sems) = refs[:extra], refs[extra:]
     copies = column_copies(pieces, weight_ref, out_ref, sems)
+    for i, (src, dst) in enumerate(zip(extra_refs, extra_outs)):
+        copies.append(pltpu.make_async_copy(src, dst, sems.at[len(pieces) + i]))
     for copy in copies:
         copy.start()
     for copy in copies:
@@ -333,17 +337,18 @@
     return pltpu.with_memory_space_constraint(x, pltpu.VMEM)
 
 
-def fetch(pieces, weight):
+def fetch(pieces, weight, *extra):
+    held = pltpu.VMEM((len(pieces), CH, PIECE), BF16)
     out = pl.pallas_call(
         functools.partial(fetch_kernel, pieces),
-        out_shape=pltpu.VMEM((len(pieces), CH, PIECE), BF16),
-        in_specs=[pl.BlockSpec(memory_space=pl.ANY)],
-        out_specs=VMEM,
-        scratch_shapes=[pltpu.SemaphoreType.DMA((len(pieces),))],
+        out_shape=(held, *(pltpu.VMEM(x.shape, x.dtype) for x in extra)),
+        in_specs=[pl.BlockSpec(memory_space=pl.ANY)] * (1 + len(extra)),
+        out_specs=(VMEM,) * (1 + len(extra)),
+        scratch_shapes=[pltpu.SemaphoreType.DMA((len(pieces) + len(extra),))],
         compiler_params=pltpu.CompilerParams(vmem_limit_bytes=12 << 20),
         name="fetch_weight",
-    )(*in_hbm(weight))
-    return resident(out)
+    )(*in_hbm(weight, *extra))
+    return tuple(resident(x) for x in out)
 
 
 def project(normed, columns, outs):
@@ -411,12 +416,17 @@
     b_out[...] = (rest_ref[3].astype(F32) + b_ref[1].astype(F32)).astype(BF16)
 
 
+def own_sum_kernel(a_ref, b_ref, rest_ref, out_ref):
+    out_ref[0] = rest_ref[0].astype(F32) + a_ref[0].astype(F32)
+    out_ref[1] = rest_ref[2].astype(F32) + b_ref[0].astype(F32)
+
+
 def finish_kernel(*refs):
     ins, out_ref, sample_ref = refs[:-2], refs[-2], refs[-1]
     for place, (start, rows) in enumerate(CHUNKS):
-        ra, rb, rest, sa, sb = ins[5 * place : 5 * place + 5]
-        for half, (own, near, far) in enumerate(((0, ra, sa), (2, rb, sb))):
-            total = rest[own].astype(F32) + near[0].astype(F32) + far[...].astype(F32)
+        own, *far = ins[3 * place : 3 * place + 3]
+        for half in range(2):
+            total = own[half] + far[half][...].astype(F32)
             columns = slice(half * PIECE, (half + 1) * PIECE)
             out_ref[columns, start : start + rows] = jnp.transpose(total[0:rows]).astype(BF16)
             if place == LEADING:
@@ -542,7 +552,7 @@
     )
     theirs = other_core(send)
 
-    near_columns = fetch(FIRST[:1], weight)
+    near_columns, scaled_2, gain_2 = fetch(FIRST[:1], weight, scaled_2, gain_2)
     scaled = (scaled_1, scaled_2)
     gain = (gain_1, gain_2)
     state = call(join_halves_kernel, "join_halves", shape((STATE + TAIL, CH)), (mine, theirs), 8)
@@ -567,16 +577,27 @@
         near = lax.optimization_barrier((swap(first, 1), swap(second, 3)))
         return normed, near, *held
 
-    def exchange(normed, near, rest_columns):
-        rest = call(rest_kernel, "rest", shape((4, normed.shape[0], PIECE)), (normed, rest_columns), 24)
-        a, b = near
-        a_on, b_on = call(onward_kernel, "onward", (shape(a.shape[1:]),) * 2, (a, b, rest), 8)
-        return (a, b, rest, *lax.optimization_barrier((swap(a_on, 3), swap(b_on, 1))))
-
     normed_0, near_0, far_columns = chunk(0, *in_hbm(weight), *sample)
-    rest_columns = fetch(REST, weight)
+    (rest_columns,) = fetch(REST, weight)
     normed_1, near_1 = chunk(1, resident(far_columns))
-    parts = exchange(normed_0, near_0, rest_columns) + exchange(normed_1, near_1, rest_columns)
+    rest_0, rest_1 = (
+        call(rest_kernel, "rest", shape((4, normed.shape[0], PIECE)), (normed, rest_columns), 24)
+        for normed in (normed_0, normed_1)
+    )
+
+    def onward(near, rest):
+        return call(onward_kernel, "onward", (shape(near[0].shape[1:]),) * 2, (*near, rest), 8)
+
+    def send_on(ons):
+        return lax.optimization_barrier((swap(ons[0], 3), swap(ons[1], 1)))
+
+    def own_sum(near, rest):
+        return call(own_sum_kernel, "own_sum", shape((2, *near[0].shape[1:]), F32), (*near, rest), 8)
+
+    ons_0, own_0, rest_1 = lax.optimization_barrier((onward(near_0, rest_0), own_sum(near_0, rest_0), rest_1))
+    far_0 = send_on(ons_0)
+    far_1 = send_on(onward(near_1, rest_1))
+    parts = (own_0, *far_0, own_sum(near_1, rest_1), *far_1)
     prompt_mixed, sample_mixed = call(finish_kernel, "finish", (shape((1024, TOK)), shape((2, 1024))), parts, 16)
     return prompt_mixed, sample_mixed.T
 

time: 96.3 us -> 96.2 us (level)
    unnamed x23 -> x19, local copies, waits for them, and re-layouts: 2.01 us -> 1.58 us
    pallas_call x10 -> x12, Pallas kernels: 11.6 us -> 11.7 us  [call(): pl.pallas_call(kernel, out_shape=out_shape, in_specs=[SMEM] * scalars + [...]
  transfers between devices with their start and end apart: 12 -> 12, of which waited for: 7 -> 6; matrix products, arithmetic and copies ran while one was open for 1% -> 1% of each run, Pallas kernels for 33% -> 34%
where the time goes in v9:
time: 96.2 us; the launch traced here: 95.7 us
  Pallas kernels  45.3 us (47%)
  starting transfers between devices  25.9 us (27%)
  waiting for transfers between devices  22.1 us (23%)
  local copies, waits for them, and re-layouts  1.58 us (2%)
    ppermute x8, waiting for transfers between devices, swap(): return lax.ppermute(x, 'head', [(i, i ^ step) for i in range(4)])  16.3 us
    pallas_call x2, Pallas kernels, local_outputs(): pl.pallas_call(functools.partial(local_kernel, part), grid=(blocks,), out...  14.5 us
    pallas_call x12, Pallas kernels, call(): pl.pallas_call(kernel, out_shape=out_shape, in_specs=[SMEM] * scalars + [...  11.7 us
    ppermute x8, starting transfers between devices, swap(): return lax.ppermute(x, 'head', [(i, i ^ step) for i in range(4)])  10 us
    pallas_call x2, Pallas kernels, chunk(): pl.pallas_call(functools.partial(chunk_kernel, place, bool(sample)), out_...  9.1 us
    all_to_all x1, starting transfers between devices, per_device(): slices = lax.all_to_all(joined, ('y', 'x'), 0, 0, tiled=True)  6.84 us
    pallas_call x2, Pallas kernels, fetch(): pl.pallas_call(functools.partial(fetch_kernel, pieces), out_shape=(held,...  5.76 us
    all_to_all x1, starting transfers between devices, per_device(): back = lax.all_to_all(prefix, ('y', 'x'), 0, 0, tiled=True)  5.37 us
  transfers between devices with their start and end apart: 12, of which 6 were waited for; matrix products, arithmetic and copies ran while one was open for 1% of the time, Pallas kernels for 34%

profile of v9, /device:TPU:1, one launch (start us, length us, event | category | flops | bytes accessed | tf_op | source)
XLA Modules:
  0.0 95.7 jit_solution(9450467600826986334)
XLA Ops:
  0.6 4.2 %end_state.1 = (bf16[16,136,128]{2,1,0:T(8,128)(2,1)S(1)}, bf16[16,136,128]{2,1,0:T(8,128)(2,1)S(1)}) custom-call(s32[2]{0:T(128)} %length.3, f32[32,512]{1,0:T(8,128)} %step_ref.1, f32[1,32]{1,0:T(1,128)} %bitcast.15, bf16[512,2048]{1,0:T(8,128)(2,1)} %values_ref.5, bf16[512,256]{1,0:T(8,128)(2,1)} %bitcast.22, bf16[2,16,256]{2,1,0:T(8,128)(2,1)} %bitcast.26), custom_call_target="tpu_custom_call" | custom-call | tf_op jit(solution)/shard_map/end_state/pallas_call | solution.py:519
  4.8 1.5 %collective-permute-start = (bf16[16,136,128]{2,1,0:T(8,128)(2,1)S(1)}, bf16[16,136,128]{2,1,0:T(8,128)(2,1)S(1)}, u32[]{:S(2)}, u32[]{:S(2)}) collective-permute-start(bf16[16,136,128]{2,1,0:T(8,128)(2,1)S(1)} %get-tuple-element.57), channel_id=1, source_target_pairs={{0,4},{4,0},{1,5},{5,1},{2,6},{6,2},{3,7},{7,3},{8,12},{12,8},{9,1... | collective-permute-start | bytes 1671176 | tf_op jit(solution)/shard_map/ppermute | solution.py:466
  9.0 6.8 %all-to-all-start = ((bf16[16,136,128]{2,1,0:T(8,128)(2,1)}), bf16[16,136,128]{2,1,0:T(8,128)(2,1)S(1)}, u32[]{:S(2)}, u32[]{:S(2)}) async-start(bf16[16,136,128]{2,1,0:T(8,128)(2,1)} %join_cores.1), calls=%async_computation | async-start | bytes 1114112 | tf_op jit(solution)/shard_map/all_to_all | solution.py:534
  15.9 2.4 %sample_outputs.1 = (f32[16,2048]{1,0:T(8,128)}, f32[16,2048]{1,0:T(8,128)}, f32[16,2048]{1,0:T(8,128)}) custom-call(s32[2]{0:T(128)S(1)} %copy-done.5, f32[2,32,16]{2,1,0:T(8,128)} %bitcast.25, f32[1,32]{1,0:T(1,128)} %bitcast.16, f32[1,32]{1,0:T(1,128)} %bitcast.19, bf16[2,16,2048]{2,1,0:T(8,128)(2,1)} %values_ref.4, bf16[2,16,2048]{2,1,0:T(8,128)(2,1)} %gate_ref.4, ...), custom_call_target="tpu_custom_call" | custom-call | flops 1 | bytes 1 | tf_op jit(solution)/shard_map/sample_outputs/pallas_call | solution.py:441
  18.3 7.3 %local_outputs.2 = (bf16[256,2048]{1,0:T(8,128)(2,1)}, bf16[256,2048]{1,0:T(8,128)(2,1)}, bf16[256,2048]{1,0:T(8,128)(2,1)}, f32[8,2048]{1,0:T(8,128)}) custom-call(f32[32,512]{1,0:T(8,128)} %step_ref.1, f32[1,32]{1,0:T(1,128)S(1)} %bitcast.17, f32[1,32]{1,0:T(1,128)S(1)} %bitcast.20, bf16[512,2048]{1,0:T(8,128)(2,1)} %values_ref.5, ...), custom_call_target="tpu_custom_call" | custom-call | flops 3221225472 | bytes 20971520 | tf_op jit(solution)/shard_map/local_outputs/pallas_call | solution.py:489
  25.6 1.3 %all-to-all-done.in_ref = bf16[16,136,128]{2,1,0:T(8,128)(2,1)S(1)} async-done(((bf16[16,136,128]{2,1,0:T(8,128)(2,1)}), bf16[16,136,128]{2,1,0:T(8,128)(2,1)S(1)}, u32[]{:S(2)}, u32[]{:S(2)}) %all-to-all-start) | async-done | bytes 557088 | tf_op jit(solution)/shard_map/all_to_all | solution.py:534
  28.0 5.4 %all-to-all-start.1 = ((bf16[16,136,128]{2,1,0:T(8,128)(2,1)}), bf16[16,136,128]{2,1,0:T(8,128)(2,1)S(1)}, u32[]{:S(2)}, u32[]{:S(2)}) async-start(bf16[16,136,128]{2,1,0:T(8,128)(2,1)} %prefix.1), calls=%async_computation.1 | async-start | bytes 1114112 | tf_op jit(solution)/shard_map/all_to_all | solution.py:545
  33.4 7.2 %local_outputs.3 = (bf16[256,2048]{1,0:T(8,128)(2,1)}, bf16[256,2048]{1,0:T(8,128)(2,1)}) custom-call(f32[32,512]{1,0:T(8,128)} %step_ref.1, f32[1,32]{1,0:T(1,128)S(1)} %bitcast.18, f32[1,32]{1,0:T(1,128)S(1)} %bitcast.21, bf16[512,2048]{1,0:T(8,128)(2,1)} %values_ref.5, bf16[512,2048]{1,0:T(8,128)(2,1)} %gate_ref.5, bf16[512,256]{1,0:T(8,128)(2,1)} %bitcast.24, ...), custom_call_target="tpu_custom_call" | custom-call | flops 3221225472 | bytes 20971520 | tf_op jit(solution)/shard_map/local_outputs/pallas_call | solution.py:489
  40.6 3.6 %all-to-all-done.1.back_ref = bf16[16,136,128]{2,1,0:T(8,128)(2,1)S(1)} async-done(((bf16[16,136,128]{2,1,0:T(8,128)(2,1)}), bf16[16,136,128]{2,1,0:T(8,128)(2,1)S(1)}, u32[]{:S(2)}, u32[]{:S(2)}) %all-to-all-start.1) | async-done | bytes 557088 | tf_op jit(solution)/shard_map/all_to_all | solution.py:545
  44.5 2.2 %collective-permute-start.1 = (bf16[16,136,128]{2,1,0:T(8,128)(2,1)S(1)}, bf16[16,136,128]{2,1,0:T(8,128)(2,1)S(1)}, u32[]{:S(2)}, u32[]{:S(2)}) collective-permute-start(bf16[16,136,128]{2,1,0:T(8,128)(2,1)S(1)} %get-tuple-element.73), channel_id=1, source_target_pairs={{0,4},{4,0},{1,5},{5,1},{2,6},{6,2},{3,7},{7,3},{8,12},{12,8},{9,1... | collective-permute-start | bytes 1671176 | tf_op jit(solution)/shard_map/ppermute | solution.py:466
  46.7 2.2 %fetch_weight.2 = (bf16[1,2048,512]{2,1,0:T(8,128)(2,1)S(1)}, bf16[256,2048]{1,0:T(8,128)(2,1)S(1)}, bf16[256,2048]{1,0:T(8,128)(2,1)S(1)}) custom-call(bf16[2048,4096]{1,0:T(8,128)(2,1)} %weight_ref.1, bf16[256,2048]{1,0:T(8,128)(2,1)} %get-tuple-element.75.refs_0_, bf16[256,2048]{1,0:T(8,128)(2,1)} %get-tuple-element.76.refs_1_), custom_call_target="tpu_custom_call" | custom-call | tf_op jit(solution)/shard_map/fetch_weight/pallas_call | solution.py:342
  50.0 4.5 %chunk.2 = (bf16[2,272,512]{2,1,0:T(8,128)(2,1)S(1)}, bf16[2,272,512]{2,1,0:T(8,128)(2,1)S(1)}, bf16[272,2048]{1,0:T(8,128)(2,1)S(1)}, bf16[3,2048,512]{2,1,0:T(8,128)(2,1)S(1)}) custom-call(bf16[264,2048]{1,0:T(8,128)(2,1)S(1)} %join_halves.1.state_ref, bf16[512,256]{1,0:T(8,128)(2,1)S(1)} %bitcast.11, bf16[256,2048]{1,0:T(8,128)(2,1)S(1)} %get-tuple-element.77.scaled_ref, ...), custom_call_target="tpu_custom_call" | custom-call | tf_op jit(solution)/shard_map/chunk/pallas_call | solution.py:568
  54.5 1.9 %collective-permute-start.2 = (bf16[2,272,512]{2,1,0:T(8,128)(2,1)S(1)}, bf16[2,272,512]{2,1,0:T(8,128)(2,1)S(1)}, u32[]{:S(2)}, u32[]{:S(2)}) collective-permute-start(bf16[2,272,512]{2,1,0:T(8,128)(2,1)S(1)} %get-tuple-element.83), channel_id=1, source_target_pairs={{0,1},{1,0},{2,3},{3,2},{4,5},{5,4},{6,7},{7,6},{8,9},{9,8},{10,11... | collective-permute-start | bytes 1671176 | tf_op jit(solution)/shard_map/ppermute | solution.py:462
  56.4 2.2 %collective-permute-start.3 = (bf16[2,272,512]{2,1,0:T(8,128)(2,1)S(1)}, bf16[2,272,512]{2,1,0:T(8,128)(2,1)S(1)}, u32[]{:S(2)}, u32[]{:S(2)}) collective-permute-start(bf16[2,272,512]{2,1,0:T(8,128)(2,1)S(1)} %get-tuple-element.84), channel_id=1, source_target_pairs={{0,3},{1,2},{2,1},{3,0},{4,7},{5,6},{6,5},{7,4},{8,11},{9,10},{10,... | collective-permute-start | bytes 1671176 | tf_op jit(solution)/shard_map/ppermute | solution.py:462
  58.7 4.6 %chunk.3 = (bf16[2,256,512]{2,1,0:T(8,128)(2,1)S(1)}, bf16[2,256,512]{2,1,0:T(8,128)(2,1)S(1)}, bf16[256,2048]{1,0:T(8,128)(2,1)S(1)}) custom-call(bf16[264,2048]{1,0:T(8,128)(2,1)S(1)} %join_halves.1.state_ref, bf16[512,256]{1,0:T(8,128)(2,1)S(1)} %bitcast.12, bf16[256,2048]{1,0:T(8,128)(2,1)} %get-tuple-element.90.scaled_ref, ...), custom_call_target="tpu_custom_call" | custom-call | tf_op jit(solution)/shard_map/chunk/pallas_call | solution.py:568
  64.7 3.5 %fetch_weight.3.weight_ref = bf16[4,2048,512]{2,1,0:T(8,128)(2,1)S(1)} custom-call(bf16[2048,4096]{1,0:T(8,128)(2,1)} %weight_ref.1), custom_call_target="tpu_custom_call" | custom-call | tf_op jit(solution)/shard_map/fetch_weight/pallas_call | solution.py:342
  68.3 2.5 %rest.2.rest_ref = bf16[4,272,512]{2,1,0:T(8,128)(2,1)S(1)} custom-call(bf16[272,2048]{1,0:T(8,128)(2,1)S(1)} %get-tuple-element.87.normed_ref, bf16[4,2048,512]{2,1,0:T(8,128)(2,1)S(1)} %fetch_weight.3.weight_ref), custom_call_target="tpu_custom_call" | custom-call | flops 1 | bytes 1 | tf_op jit(solution)/shard_map/rest/pallas_call | solution.py:441
  70.7 2.3 %rest.3.rest_ref = bf16[4,256,512]{2,1,0:T(8,128)(2,1)S(1)} custom-call(bf16[256,2048]{1,0:T(8,128)(2,1)S(1)} %get-tuple-element.93.normed_ref, bf16[4,2048,512]{2,1,0:T(8,128)(2,1)S(1)} %fetch_weight.3.weight_ref), custom_call_target="tpu_custom_call" | custom-call | flops 1 | bytes 1 | tf_op jit(solution)/shard_map/rest/pallas_call | solution.py:441
  73.3 2.1 %collective-permute-start.4 = (bf16[272,512]{1,0:T(8,128)(2,1)S(1)}, bf16[272,512]{1,0:T(8,128)(2,1)S(1)}, u32[]{:S(2)}, u32[]{:S(2)}) collective-permute-start(bf16[272,512]{1,0:T(8,128)(2,1)S(1)} %get-tuple-element.95), channel_id=1, source_target_pairs={{0,3},{1,2},{2,1},{3,0},{4,7},{5,6},{6,5},{7,4},{8,11},{9,10},{10,... | collective-permute-start | bytes 835592 | tf_op jit(solution)/shard_map/ppermute | solution.py:462
  75.5 5.0 %collective-permute-done.6.a_ref = bf16[2,256,512]{2,1,0:T(8,128)(2,1)S(1)} collective-permute-done((bf16[2,256,512]{2,1,0:T(8,128)(2,1)S(1)}, bf16[2,256,512]{2,1,0:T(8,128)(2,1)S(1)}, u32[]{:S(2)}, u32[]{:S(2)}) %collective-permute-start.6) | collective-permute-done | bytes 524320 | tf_op jit(solution)/shard_map/ppermute | solution.py:462
  80.5 2.3 %collective-permute-done.7.b_ref = bf16[2,256,512]{2,1,0:T(8,128)(2,1)S(1)} collective-permute-done((bf16[2,256,512]{2,1,0:T(8,128)(2,1)S(1)}, bf16[2,256,512]{2,1,0:T(8,128)(2,1)S(1)}, u32[]{:S(2)}, u32[]{:S(2)}) %collective-permute-start.7) | collective-permute-done | bytes 524320 | tf_op jit(solution)/shard_map/ppermute | solution.py:462
  82.9 2.3 %collective-permute-start.8 = (bf16[256,512]{1,0:T(8,128)(2,1)S(1)}, bf16[256,512]{1,0:T(8,128)(2,1)S(1)}, u32[]{:S(2)}, u32[]{:S(2)}) collective-permute-start(bf16[256,512]{1,0:T(8,128)(2,1)S(1)} %get-tuple-element.104), channel_id=1, source_target_pairs={{0,3},{1,2},{2,1},{3,0},{4,7},{5,6},{6,5},{7,4},{8,11},{9,10},{10,... | collective-permute-start | bytes 786440 | tf_op jit(solution)/shard_map/ppermute | solution.py:462
  85.3 9.0 %collective-permute-done.8.refs_4_ = bf16[256,512]{1,0:T(8,128)(2,1)S(1)} collective-permute-done((bf16[256,512]{1,0:T(8,128)(2,1)S(1)}, bf16[256,512]{1,0:T(8,128)(2,1)S(1)}, u32[]{:S(2)}, u32[]{:S(2)}) %collective-permute-start.8) | collective-permute-done | bytes 262176 | tf_op jit(solution)/shard_map/ppermute | solution.py:462
  94.4 1.3 %finish.1 = (bf16[1024,512]{1,0:T(8,128)(2,1)}, bf16[2,1024]{1,0:T(2,128)(2,1)}) custom-call(f32[2,272,512]{2,1,0:T(8,128)S(1)} %own_sum.2.refs_0_, bf16[272,512]{1,0:T(8,128)(2,1)S(1)} %collective-permute-done.4.refs_1_, bf16[272,512]{1,0:T(8,128)(2,1)S(1)} %collective-permute-done.5.refs_2_, f32[2,256,512]{2,1,0:T(8,128)S(1)} %own_sum.3.refs_3_, ...), custom_call_target="tpu_custom_call" | custom-call | flops 1 | bytes 1 | tf_op jit(solution)/shard_map/finish/pallas_call | solution.py:441
  (38 shorter events, 7.1 us)
Async XLA Ops:
  0.6 5.7 %copy-start.8 = (f32[32,2,16]{0,2,1:T(8,128)S(1)}, f32[32,2,16]{0,2,1:T(8,128)}, u32[]{:S(2)}) copy-start(f32[32,2,16]{0,2,1:T(8,128)} %param.28) | copy-start | bytes 12292
  0.6 15.2 %copy-start.5 = (s32[2]{0:T(128)S(1)}, s32[2]{0:T(128)}, u32[]{:S(2)}) copy-start(s32[2]{0:T(128)} %length.3) | copy-start | bytes 28
  4.8 13.5 %copy-start.6 = (f32[32]{0:T(128)S(1)}, f32[32]{0:T(128)}, u32[]{:S(2)}) copy-start(f32[32]{0:T(128)} %param.20) | copy-start | bytes 388
  4.8 13.5 %copy-start.7 = (f32[32]{0:T(128)S(1)}, f32[32]{0:T(128)}, u32[]{:S(2)}) copy-start(f32[32]{0:T(128)} %param.21) | copy-start | bytes 388
  4.8 3.1 %collective-permute-start = (bf16[16,136,128]{2,1,0:T(8,128)(2,1)S(1)}, bf16[16,136,128]{2,1,0:T(8,128)(2,1)S(1)}, u32[]{:S(2)}, u32[]{:S(2)}) collective-permute-start(bf16[16,136,128]{2,1,0:T(8,128)(2,1)S(1)} %get-tuple-element.57), channel_id=1, source_target_pairs={{0,4},{4,0},{1,5},{5,1},{2,6},{6,2},{3,7},{7,3},{8,12},{12,8},{9,1... | collective-permute-start | bytes 1671176 | tf_op jit(solution)/shard_map/ppermute | solution.py:466
  9.0 17.9 %all-to-all-start = ((bf16[16,136,128]{2,1,0:T(8,128)(2,1)}), bf16[16,136,128]{2,1,0:T(8,128)(2,1)S(1)}, u32[]{:S(2)}, u32[]{:S(2)}) async-start(bf16[16,136,128]{2,1,0:T(8,128)(2,1)} %join_cores.1), calls=%async_computation | async-start | bytes 1114112 | tf_op jit(solution)/shard_map/all_to_all | solution.py:534
  28.0 16.1 %all-to-all-start.1 = ((bf16[16,136,128]{2,1,0:T(8,128)(2,1)}), bf16[16,136,128]{2,1,0:T(8,128)(2,1)S(1)}, u32[]{:S(2)}, u32[]{:S(2)}) async-start(bf16[16,136,128]{2,1,0:T(8,128)(2,1)} %prefix.1), calls=%async_computation.1 | async-start | bytes 1114112 | tf_op jit(solution)/shard_map/all_to_all | solution.py:545
  44.5 4.5 %collective-permute-start.1 = (bf16[16,136,128]{2,1,0:T(8,128)(2,1)S(1)}, bf16[16,136,128]{2,1,0:T(8,128)(2,1)S(1)}, u32[]{:S(2)}, u32[]{:S(2)}) collective-permute-start(bf16[16,136,128]{2,1,0:T(8,128)(2,1)S(1)} %get-tuple-element.73), channel_id=1, source_target_pairs={{0,4},{4,0},{1,5},{5,1},{2,6},{6,2},{3,7},{7,3},{8,12},{12,8},{9,1... | collective-permute-start | bytes 1671176 | tf_op jit(solution)/shard_map/ppermute | solution.py:466
  48.9 1.0 copy-start
  48.9 1.0 %copy-start.1 = (f32[16,2048]{1,0:T(8,128)S(1)}, f32[16,2048]{1,0:T(8,128)}, u32[]{:S(2)}) copy-start(f32[16,2048]{1,0:T(8,128)} %get-tuple-element.80.refs_0_) | copy-start | bytes 393220
  48.9 1.0 %copy-start.2 = (f32[16,2048]{1,0:T(8,128)S(1)}, f32[16,2048]{1,0:T(8,128)}, u32[]{:S(2)}) copy-start(f32[16,2048]{1,0:T(8,128)} %get-tuple-element.81.refs_1_) | copy-start | bytes 393220
  48.9 1.1 %copy-start.3 = (f32[16,2048]{1,0:T(8,128)S(1)}, f32[16,2048]{1,0:T(8,128)}, u32[]{:S(2)}) copy-start(f32[16,2048]{1,0:T(8,128)} %get-tuple-element.82.refs_2_) | copy-start | bytes 393220
  48.9 1.1 %copy-start.4 = (f32[2048]{0:T(1024)S(1)}, f32[2048]{0:T(1024)}, u32[]{:S(2)}) copy-start(f32[2048]{0:T(1024)} %param.22) | copy-start | bytes 24580
  54.5 18.5 %collective-permute-start.2 = (bf16[2,272,512]{2,1,0:T(8,128)(2,1)S(1)}, bf16[2,272,512]{2,1,0:T(8,128)(2,1)S(1)}, u32[]{:S(2)}, u32[]{:S(2)}) collective-permute-start(bf16[2,272,512]{2,1,0:T(8,128)(2,1)S(1)} %get-tuple-element.83), channel_id=1, source_target_pairs={{0,1},{1,0},{2,3},{3,2},{4,5},{5,4},{6,7},{7,6},{8,9},{9,8},{10,11... | collective-permute-start | bytes 1671176 | tf_op jit(solution)/shard_map/ppermute | solution.py:462
  56.4 16.6 %collective-permute-start.3 = (bf16[2,272,512]{2,1,0:T(8,128)(2,1)S(1)}, bf16[2,272,512]{2,1,0:T(8,128)(2,1)S(1)}, u32[]{:S(2)}, u32[]{:S(2)}) collective-permute-start(bf16[2,272,512]{2,1,0:T(8,128)(2,1)S(1)} %get-tuple-element.84), channel_id=1, source_target_pairs={{0,3},{1,2},{2,1},{3,0},{4,7},{5,6},{6,5},{7,4},{8,11},{9,10},{10,... | collective-permute-start | bytes 1671176 | tf_op jit(solution)/shard_map/ppermute | solution.py:462
  63.3 17.3 %collective-permute-start.6 = (bf16[2,256,512]{2,1,0:T(8,128)(2,1)S(1)}, bf16[2,256,512]{2,1,0:T(8,128)(2,1)S(1)}, u32[]{:S(2)}, u32[]{:S(2)}) collective-permute-start(bf16[2,256,512]{2,1,0:T(8,128)(2,1)S(1)} %get-tuple-element.99), channel_id=1, source_target_pairs={{0,1},{1,0},{2,3},{3,2},{4,5},{5,4},{6,7},{7,6},{8,9},{9,8},{10,11... | collective-permute-start | bytes 1572872 | tf_op jit(solution)/shard_map/ppermute | solution.py:462
  64.1 18.7 %collective-permute-start.7 = (bf16[2,256,512]{2,1,0:T(8,128)(2,1)S(1)}, bf16[2,256,512]{2,1,0:T(8,128)(2,1)S(1)}, u32[]{:S(2)}, u32[]{:S(2)}) collective-permute-start(bf16[2,256,512]{2,1,0:T(8,128)(2,1)S(1)} %get-tuple-element.100), channel_id=1, source_target_pairs={{0,3},{1,2},{2,1},{3,0},{4,7},{5,6},{6,5},{7,4},{8,11},{9,10},{10,... | collective-permute-start | bytes 1572872 | tf_op jit(solution)/shard_map/ppermute | solution.py:462
  73.3 21.1 %collective-permute-start.4 = (bf16[272,512]{1,0:T(8,128)(2,1)S(1)}, bf16[272,512]{1,0:T(8,128)(2,1)S(1)}, u32[]{:S(2)}, u32[]{:S(2)}) collective-permute-start(bf16[272,512]{1,0:T(8,128)(2,1)S(1)} %get-tuple-element.95), channel_id=1, source_target_pairs={{0,3},{1,2},{2,1},{3,0},{4,7},{5,6},{6,5},{7,4},{8,11},{9,10},{10,... | collective-permute-start | bytes 835592 | tf_op jit(solution)/shard_map/ppermute | solution.py:462
  75.5 18.9 %collective-permute-start.5 = (bf16[272,512]{1,0:T(8,128)(2,1)S(1)}, bf16[272,512]{1,0:T(8,128)(2,1)S(1)}, u32[]{:S(2)}, u32[]{:S(2)}) collective-permute-start(bf16[272,512]{1,0:T(8,128)(2,1)S(1)} %get-tuple-element.96), channel_id=1, source_target_pairs={{0,1},{1,0},{2,3},{3,2},{4,5},{5,4},{6,7},{7,6},{8,9},{9,8},{10,11... | collective-permute-start | bytes 835592 | tf_op jit(solution)/shard_map/ppermute | solution.py:462
  82.9 11.5 %collective-permute-start.8 = (bf16[256,512]{1,0:T(8,128)(2,1)S(1)}, bf16[256,512]{1,0:T(8,128)(2,1)S(1)}, u32[]{:S(2)}, u32[]{:S(2)}) collective-permute-start(bf16[256,512]{1,0:T(8,128)(2,1)S(1)} %get-tuple-element.104), channel_id=1, source_target_pairs={{0,3},{1,2},{2,1},{3,0},{4,7},{5,6},{6,5},{7,4},{8,11},{9,10},{10,... | collective-permute-start | bytes 786440 | tf_op jit(solution)/shard_map/ppermute | solution.py:462
  85.2 9.1 %collective-permute-start.9 = (bf16[256,512]{1,0:T(8,128)(2,1)S(1)}, bf16[256,512]{1,0:T(8,128)(2,1)S(1)}, u32[]{:S(2)}, u32[]{:S(2)}) collective-permute-start(bf16[256,512]{1,0:T(8,128)(2,1)S(1)} %get-tuple-element.105), channel_id=1, source_target_pairs={{0,1},{1,0},{2,3},{3,2},{4,5},{5,4},{6,7},{7,6},{8,9},{9,8},{10,11... | collective-permute-start | bytes 786440 | tf_op jit(solution)/shard_map/ppermute | solution.py:462

commit v10 on v9

--- a/solution.py
+++ b/solution.py
@@ -535,9 +535,10 @@
     scaled_1, gain_1, *carry = local_outputs(
         0, step_1, decay, skip, prompt_values, prompt_gate, inject, read
     )
+    scaled_1, s_values = lax.optimization_barrier((scaled_1, sample_values))
     sample = call(
         sample_kernel, "sample_outputs", (pltpu.HBM((16, CH), F32),) * 3,
-        (sample_length, *in_hbm(s_step, decay, skip, sample_values, sample_gate, s_inject, s_read)), 16, 1,
+        (sample_length, s_step, decay, skip, s_values, sample_gate, s_inject, s_read), 16, 1,
     )
     slices, scaled_1, sample = lax.optimization_barrier((slices, scaled_1, sample))
     prefix = call(prefix_kernel, "prefix", slices_shape, (slices,), 16)
@@ -546,13 +547,15 @@
     scaled_2, gain_2 = local_outputs(
         1, step_2, decay, skip, prompt_values, prompt_gate, inject, read, carry
     )
-    back, scaled_2, weight = lax.optimization_barrier((back, scaled_2, out_weight))
+    back, scaled_2, weight, read_2 = lax.optimization_barrier((back, scaled_2, out_weight, read))
     mine, send = call(
         split_cores_kernel, "split_cores", (shape((STATE + TAIL, 1024)), slices_shape), (back, keep, sibling), 16
     )
     theirs = other_core(send)
 
-    near_columns, scaled_2, gain_2 = fetch(FIRST[:1], weight, scaled_2, gain_2)
+    near_columns, scaled_2, gain_2, read_2, norm, *sample = fetch(
+        FIRST[:1], weight, scaled_2, gain_2, read_2, norm, *sample
+    )
     scaled = (scaled_1, scaled_2)
     gain = (gain_1, gain_2)
     state = call(join_halves_kernel, "join_halves", shape((STATE + TAIL, CH)), (mine, theirs), 8)
@@ -573,7 +576,7 @@
             scratch_shapes=[pltpu.SemaphoreType.DMA((3,))] if leading else [],
             compiler_params=pltpu.CompilerParams(vmem_limit_bytes=24 << 20),
             name="chunk",
-        )(state, read, *local, norm, near_columns, far_columns, *sample)
+        )(state, read_2, *local, norm, near_columns, far_columns, *sample)
         near = lax.optimization_barrier((swap(first, 1), swap(second, 3)))
         return normed, near, *held
 

time: 96.2 us -> 95.2 us (0.990)
  local copies, waits for them, and re-layouts: 1.58 us -> 0.12 us
    unnamed x19 -> x17, local copies, waits for them, and re-layouts: 1.58 us -> 0.12 us
  transfers between devices with their start and end apart: 12 -> 12, of which waited for: 6 -> 6; matrix products, arithmetic and copies ran while one was open for 1% -> 0% of each run, Pallas kernels for 34% -> 34%
where the time goes in v10:
time: 95.2 us; the launch traced here: 94.7 us
  Pallas kernels  45.1 us (47%)
  starting transfers between devices  25.6 us (27%)
  waiting for transfers between devices  23 us (24%)
    ppermute x8, waiting for transfers between devices, swap(): return lax.ppermute(x, 'head', [(i, i ^ step) for i in range(4)])  16.3 us
    pallas_call x2, Pallas kernels, local_outputs(): pl.pallas_call(functools.partial(local_kernel, part), grid=(blocks,), out...  14.6 us
    pallas_call x12, Pallas kernels, call(): pl.pallas_call(kernel, out_shape=out_shape, in_specs=[SMEM] * scalars + [...  11.2 us
    ppermute x8, starting transfers between devices, swap(): return lax.ppermute(x, 'head', [(i, i ^ step) for i in range(4)])  10.1 us
    pallas_call x2, Pallas kernels, chunk(): pl.pallas_call(functools.partial(chunk_kernel, place, bool(sample)), out_...  9.1 us
    all_to_all x1, starting transfers between devices, per_device(): slices = lax.all_to_all(joined, ('y', 'x'), 0, 0, tiled=True)  6.84 us
    pallas_call x2, Pallas kernels, fetch(): pl.pallas_call(functools.partial(fetch_kernel, pieces), out_shape=(held,...  5.97 us
    all_to_all x1, starting transfers between devices, per_device(): back = lax.all_to_all(prefix, ('y', 'x'), 0, 0, tiled=True)  5.07 us
  transfers between devices with their start and end apart: 12, of which 6 were waited for; matrix products, arithmetic and copies ran while one was open for 0% of the time, Pallas kernels for 34%

profile of v10, /device:TPU:1, one launch (start us, length us, event | category | flops | bytes accessed | tf_op | source)
XLA Modules:
  0.0 94.7 jit_solution(8516372478291131489)
XLA Ops:
  0.7 4.2 %end_state.1 = (bf16[16,136,128]{2,1,0:T(8,128)(2,1)S(1)}, bf16[16,136,128]{2,1,0:T(8,128)(2,1)S(1)}) custom-call(s32[2]{0:T(128)} %length.3, f32[32,512]{1,0:T(8,128)} %step_ref.1, f32[1,32]{1,0:T(1,128)} %bitcast.13, bf16[512,2048]{1,0:T(8,128)(2,1)} %values_ref.4, bf16[512,256]{1,0:T(8,128)(2,1)} %bitcast.23, bf16[2,16,256]{2,1,0:T(8,128)(2,1)} %bitcast.10), custom_call_target="tpu_custom_call" | custom-call | tf_op jit(solution)/shard_map/end_state/pallas_call | solution.py:519
  4.8 1.5 %collective-permute-start = (bf16[16,136,128]{2,1,0:T(8,128)(2,1)S(1)}, bf16[16,136,128]{2,1,0:T(8,128)(2,1)S(1)}, u32[]{:S(2)}, u32[]{:S(2)}) collective-permute-start(bf16[16,136,128]{2,1,0:T(8,128)(2,1)S(1)} %get-tuple-element.65), channel_id=1, source_target_pairs={{0,4},{4,0},{1,5},{5,1},{2,6},{6,2},{3,7},{7,3},{8,12},{12,8},{9,1... | collective-permute-start | bytes 1671176 | tf_op jit(solution)/shard_map/ppermute | solution.py:466
  6.4 1.5 %collective-permute-done.sib_ref = bf16[16,136,128]{2,1,0:T(8,128)(2,1)S(1)} collective-permute-done((bf16[16,136,128]{2,1,0:T(8,128)(2,1)S(1)}, bf16[16,136,128]{2,1,0:T(8,128)(2,1)S(1)}, u32[]{:S(2)}, u32[]{:S(2)}) %collective-permute-start) | collective-permute-done | bytes 557088 | tf_op jit(solution)/shard_map/ppermute | solution.py:466
  9.0 6.8 %all-to-all-start = ((bf16[16,136,128]{2,1,0:T(8,128)(2,1)}), bf16[16,136,128]{2,1,0:T(8,128)(2,1)S(1)}, u32[]{:S(2)}, u32[]{:S(2)}) async-start(bf16[16,136,128]{2,1,0:T(8,128)(2,1)} %join_cores.1), calls=%async_computation | async-start | bytes 1114112 | tf_op jit(solution)/shard_map/all_to_all | solution.py:534
  15.9 7.4 %local_outputs.2 = (bf16[256,2048]{1,0:T(8,128)(2,1)}, bf16[256,2048]{1,0:T(8,128)(2,1)}, bf16[256,2048]{1,0:T(8,128)(2,1)}, f32[8,2048]{1,0:T(8,128)}) custom-call(f32[32,512]{1,0:T(8,128)} %step_ref.1, f32[1,32]{1,0:T(1,128)S(1)} %bitcast.14, f32[1,32]{1,0:T(1,128)S(1)} %bitcast.17, bf16[512,2048]{1,0:T(8,128)(2,1)} %values_ref.4, ...), custom_call_target="tpu_custom_call" | custom-call | flops 3221225472 | bytes 20971520 | tf_op jit(solution)/shard_map/local_outputs/pallas_call | solution.py:489
  23.4 1.9 %sample_outputs.1 = (f32[16,2048]{1,0:T(8,128)}, f32[16,2048]{1,0:T(8,128)}, f32[16,2048]{1,0:T(8,128)}) custom-call(s32[2]{0:T(128)S(1)} %copy-done.4, f32[2,32,16]{2,1,0:T(8,128)S(1)} %bitcast.9, f32[1,32]{1,0:T(1,128)S(1)} %bitcast.15, f32[1,32]{1,0:T(1,128)S(1)} %bitcast.18, bf16[2,16,2048]{2,1,0:T(8,128)(2,1)S(1)} %copy-done, ...), custom_call_target="tpu_custom_call" | custom-call | flops 1 | bytes 1 | tf_op jit(solution)/shard_map/sample_outputs/pallas_call | solution.py:441
  25.3 1.6 %all-to-all-done.in_ref = bf16[16,136,128]{2,1,0:T(8,128)(2,1)S(1)} async-done(((bf16[16,136,128]{2,1,0:T(8,128)(2,1)}), bf16[16,136,128]{2,1,0:T(8,128)(2,1)S(1)}, u32[]{:S(2)}, u32[]{:S(2)}) %all-to-all-start) | async-done | bytes 557088 | tf_op jit(solution)/shard_map/all_to_all | solution.py:534
  28.0 5.1 %all-to-all-start.1 = ((bf16[16,136,128]{2,1,0:T(8,128)(2,1)}), bf16[16,136,128]{2,1,0:T(8,128)(2,1)S(1)}, u32[]{:S(2)}, u32[]{:S(2)}) async-start(bf16[16,136,128]{2,1,0:T(8,128)(2,1)} %prefix.1), calls=%async_computation.1 | async-start | bytes 1114112 | tf_op jit(solution)/shard_map/all_to_all | solution.py:546
  33.1 7.2 %local_outputs.3 = (bf16[256,2048]{1,0:T(8,128)(2,1)}, bf16[256,2048]{1,0:T(8,128)(2,1)}) custom-call(f32[32,512]{1,0:T(8,128)} %step_ref.1, f32[1,32]{1,0:T(1,128)S(1)} %bitcast.16, f32[1,32]{1,0:T(1,128)S(1)} %bitcast.19, bf16[512,2048]{1,0:T(8,128)(2,1)} %values_ref.4, bf16[512,2048]{1,0:T(8,128)(2,1)} %gate_ref.5, bf16[512,256]{1,0:T(8,128)(2,1)} %bitcast.25, ...), custom_call_target="tpu_custom_call" | custom-call | flops 3221225472 | bytes 20971520 | tf_op jit(solution)/shard_map/local_outputs/pallas_call | solution.py:489
  40.3 3.6 %all-to-all-done.1.back_ref = bf16[16,136,128]{2,1,0:T(8,128)(2,1)S(1)} async-done(((bf16[16,136,128]{2,1,0:T(8,128)(2,1)}), bf16[16,136,128]{2,1,0:T(8,128)(2,1)S(1)}, u32[]{:S(2)}, u32[]{:S(2)}) %all-to-all-start.1) | async-done | bytes 557088 | tf_op jit(solution)/shard_map/all_to_all | solution.py:546
  44.2 2.2 %collective-permute-start.1 = (bf16[16,136,128]{2,1,0:T(8,128)(2,1)S(1)}, bf16[16,136,128]{2,1,0:T(8,128)(2,1)S(1)}, u32[]{:S(2)}, u32[]{:S(2)}) collective-permute-start(bf16[16,136,128]{2,1,0:T(8,128)(2,1)S(1)} %get-tuple-element.83), channel_id=1, source_target_pairs={{0,4},{4,0},{1,5},{5,1},{2,6},{6,2},{3,7},{7,3},{8,12},{12,8},{9,1... | collective-permute-start | bytes 1671176 | tf_op jit(solution)/shard_map/ppermute | solution.py:466
  46.4 2.4 %fetch_weight.2 = (bf16[1,2048,512]{2,1,0:T(8,128)(2,1)S(1)}, bf16[256,2048]{1,0:T(8,128)(2,1)S(1)}, bf16[256,2048]{1,0:T(8,128)(2,1)S(1)}, bf16[512,256]{1,0:T(...) custom-call(bf16[2048,4096]{1,0:T(8,128)(2,1)} %weight_ref.1, ...), custom_call_target="tpu_custom_call" | custom-call | tf_op jit(solution)/shard_map/fetch_weight/pallas_call | solution.py:342
  49.0 4.5 %chunk.2 = (bf16[2,272,512]{2,1,0:T(8,128)(2,1)S(1)}, bf16[2,272,512]{2,1,0:T(8,128)(2,1)S(1)}, bf16[272,2048]{1,0:T(8,128)(2,1)S(1)}, bf16[3,2048,512]{2,1,0:T(8,128)(2,1)S(1)}) custom-call(bf16[264,2048]{1,0:T(8,128)(2,1)S(1)} %join_halves.1.state_ref, bf16[512,256]{1,0:T(8,128)(2,1)S(1)} %get-tuple-element.91.read_ref, ...), custom_call_target="tpu_custom_call" | custom-call | tf_op jit(solution)/shard_map/chunk/pallas_call | solution.py:571
  53.5 1.9 %collective-permute-start.2 = (bf16[2,272,512]{2,1,0:T(8,128)(2,1)S(1)}, bf16[2,272,512]{2,1,0:T(8,128)(2,1)S(1)}, u32[]{:S(2)}, u32[]{:S(2)}) collective-permute-start(bf16[2,272,512]{2,1,0:T(8,128)(2,1)S(1)} %get-tuple-element.99), channel_id=1, source_target_pairs={{0,1},{1,0},{2,3},{3,2},{4,5},{5,4},{6,7},{7,6},{8,9},{9,8},{10,11... | collective-permute-start | bytes 1671176 | tf_op jit(solution)/shard_map/ppermute | solution.py:462
  55.4 2.2 %collective-permute-start.3 = (bf16[2,272,512]{2,1,0:T(8,128)(2,1)S(1)}, bf16[2,272,512]{2,1,0:T(8,128)(2,1)S(1)}, u32[]{:S(2)}, u32[]{:S(2)}) collective-permute-start(bf16[2,272,512]{2,1,0:T(8,128)(2,1)S(1)} %get-tuple-element.100), channel_id=1, source_target_pairs={{0,3},{1,2},{2,1},{3,0},{4,7},{5,6},{6,5},{7,4},{8,11},{9,10},{10,... | collective-permute-start | bytes 1671176 | tf_op jit(solution)/shard_map/ppermute | solution.py:462
  57.7 4.6 %chunk.3 = (bf16[2,256,512]{2,1,0:T(8,128)(2,1)S(1)}, bf16[2,256,512]{2,1,0:T(8,128)(2,1)S(1)}, bf16[256,2048]{1,0:T(8,128)(2,1)S(1)}) custom-call(bf16[264,2048]{1,0:T(8,128)(2,1)S(1)} %join_halves.1.state_ref, bf16[512,256]{1,0:T(8,128)(2,1)S(1)} %get-tuple-element.91.read_ref, bf16[256,2048]{1,0:T(8,128)(2,1)} %get-tuple-element.106.scaled_ref, ...), custom_call_target="tpu_custom_call" | custom-call | tf_op jit(solution)/shard_map/chunk/pallas_call | solution.py:571
  63.7 3.5 %fetch_weight.3.weight_ref = bf16[4,2048,512]{2,1,0:T(8,128)(2,1)S(1)} custom-call(bf16[2048,4096]{1,0:T(8,128)(2,1)} %weight_ref.1), custom_call_target="tpu_custom_call" | custom-call | tf_op jit(solution)/shard_map/fetch_weight/pallas_call | solution.py:342
  67.2 2.5 %rest.2.rest_ref = bf16[4,272,512]{2,1,0:T(8,128)(2,1)S(1)} custom-call(bf16[272,2048]{1,0:T(8,128)(2,1)S(1)} %get-tuple-element.103.normed_ref, bf16[4,2048,512]{2,1,0:T(8,128)(2,1)S(1)} %fetch_weight.3.weight_ref), custom_call_target="tpu_custom_call" | custom-call | flops 1 | bytes 1 | tf_op jit(solution)/shard_map/rest/pallas_call | solution.py:441
  69.7 2.3 %rest.3.rest_ref = bf16[4,256,512]{2,1,0:T(8,128)(2,1)S(1)} custom-call(bf16[256,2048]{1,0:T(8,128)(2,1)S(1)} %get-tuple-element.109.normed_ref, bf16[4,2048,512]{2,1,0:T(8,128)(2,1)S(1)} %fetch_weight.3.weight_ref), custom_call_target="tpu_custom_call" | custom-call | flops 1 | bytes 1 | tf_op jit(solution)/shard_map/rest/pallas_call | solution.py:441
  72.3 2.1 %collective-permute-start.4 = (bf16[272,512]{1,0:T(8,128)(2,1)S(1)}, bf16[272,512]{1,0:T(8,128)(2,1)S(1)}, u32[]{:S(2)}, u32[]{:S(2)}) collective-permute-start(bf16[272,512]{1,0:T(8,128)(2,1)S(1)} %get-tuple-element.111), channel_id=1, source_target_pairs={{0,3},{1,2},{2,1},{3,0},{4,7},{5,6},{6,5},{7,4},{8,11},{9,10},{10,... | collective-permute-start | bytes 835592 | tf_op jit(solution)/shard_map/ppermute | solution.py:462
  74.5 5.0 %collective-permute-done.6.a_ref = bf16[2,256,512]{2,1,0:T(8,128)(2,1)S(1)} collective-permute-done((bf16[2,256,512]{2,1,0:T(8,128)(2,1)S(1)}, bf16[2,256,512]{2,1,0:T(8,128)(2,1)S(1)}, u32[]{:S(2)}, u32[]{:S(2)}) %collective-permute-start.6) | collective-permute-done | bytes 524320 | tf_op jit(solution)/shard_map/ppermute | solution.py:462
  79.5 2.2 %collective-permute-done.7.b_ref = bf16[2,256,512]{2,1,0:T(8,128)(2,1)S(1)} collective-permute-done((bf16[2,256,512]{2,1,0:T(8,128)(2,1)S(1)}, bf16[2,256,512]{2,1,0:T(8,128)(2,1)S(1)}, u32[]{:S(2)}, u32[]{:S(2)}) %collective-permute-start.7) | collective-permute-done | bytes 524320 | tf_op jit(solution)/shard_map/ppermute | solution.py:462
  81.9 2.3 %collective-permute-start.8 = (bf16[256,512]{1,0:T(8,128)(2,1)S(1)}, bf16[256,512]{1,0:T(8,128)(2,1)S(1)}, u32[]{:S(2)}, u32[]{:S(2)}) collective-permute-start(bf16[256,512]{1,0:T(8,128)(2,1)S(1)} %get-tuple-element.120), channel_id=1, source_target_pairs={{0,3},{1,2},{2,1},{3,0},{4,7},{5,6},{6,5},{7,4},{8,11},{9,10},{10,... | collective-permute-start | bytes 786440 | tf_op jit(solution)/shard_map/ppermute | solution.py:462
  84.3 9.0 %collective-permute-done.8.refs_4_ = bf16[256,512]{1,0:T(8,128)(2,1)S(1)} collective-permute-done((bf16[256,512]{1,0:T(8,128)(2,1)S(1)}, bf16[256,512]{1,0:T(8,128)(2,1)S(1)}, u32[]{:S(2)}, u32[]{:S(2)}) %collective-permute-start.8) | collective-permute-done | bytes 262176 | tf_op jit(solution)/shard_map/ppermute | solution.py:462
  (36 shorter events, 6.1 us)
Async XLA Ops:
  0.6 5.7 %copy-start.7 = (f32[32,2,16]{0,2,1:T(8,128)S(1)}, f32[32,2,16]{0,2,1:T(8,128)}, u32[]{:S(2)}) copy-start(f32[32,2,16]{0,2,1:T(8,128)} %param.28) | copy-start | bytes 12292
  0.6 15.2 %copy-start.5 = (f32[32]{0:T(128)S(1)}, f32[32]{0:T(128)}, u32[]{:S(2)}) copy-start(f32[32]{0:T(128)} %param.20) | copy-start | bytes 388
  0.7 15.2 %copy-start.6 = (f32[32]{0:T(128)S(1)}, f32[32]{0:T(128)}, u32[]{:S(2)}) copy-start(f32[32]{0:T(128)} %param.21) | copy-start | bytes 388
  4.8 3.1 %collective-permute-start = (bf16[16,136,128]{2,1,0:T(8,128)(2,1)S(1)}, bf16[16,136,128]{2,1,0:T(8,128)(2,1)S(1)}, u32[]{:S(2)}, u32[]{:S(2)}) collective-permute-start(bf16[16,136,128]{2,1,0:T(8,128)(2,1)S(1)} %get-tuple-element.65), channel_id=1, source_target_pairs={{0,4},{4,0},{1,5},{5,1},{2,6},{6,2},{3,7},{7,3},{8,12},{12,8},{9,1... | collective-permute-start | bytes 1671176 | tf_op jit(solution)/shard_map/ppermute | solution.py:466
  9.0 17.9 %all-to-all-start = ((bf16[16,136,128]{2,1,0:T(8,128)(2,1)}), bf16[16,136,128]{2,1,0:T(8,128)(2,1)S(1)}, u32[]{:S(2)}, u32[]{:S(2)}) async-start(bf16[16,136,128]{2,1,0:T(8,128)(2,1)} %join_cores.1), calls=%async_computation | async-start | bytes 1114112 | tf_op jit(solution)/shard_map/all_to_all | solution.py:534
  15.8 7.5 %copy-start = (bf16[2,16,2048]{2,1,0:T(8,128)(2,1)S(1)}, bf16[2,16,2048]{2,1,0:T(8,128)(2,1)}, u32[]{:S(2)}) copy-start(bf16[2,16,2048]{2,1,0:T(8,128)(2,1)} %values_ref.3) | copy-start | bytes 393220
  15.9 7.5 %copy-start.1 = (bf16[2,16,2048]{2,1,0:T(8,128)(2,1)S(1)}, bf16[2,16,2048]{2,1,0:T(8,128)(2,1)}, u32[]{:S(2)}) copy-start(bf16[2,16,2048]{2,1,0:T(8,128)(2,1)} %gate_ref.4) | copy-start | bytes 393220
  15.9 7.5 %copy-start.2 = (bf16[2,16,1,256]{3,1,2,0:T(8,128)(2,1)S(1)}, bf16[2,16,1,256]{3,1,2,0:T(8,128)(2,1)}, u32[]{:S(2)}) copy-start(bf16[2,16,1,256]{3,1,2,0:T(8,128)(2,1)} %param.27) | copy-start | bytes 49156
  15.9 7.5 %copy-start.3 = (bf16[2,16,1,256]{3,1,2,0:T(8,128)(2,1)S(1)}, bf16[2,16,1,256]{3,1,2,0:T(8,128)(2,1)}, u32[]{:S(2)}) copy-start(bf16[2,16,1,256]{3,1,2,0:T(8,128)(2,1)} %param.26) | copy-start | bytes 49156
  15.9 7.5 %copy-start.4 = (s32[2]{0:T(128)S(1)}, s32[2]{0:T(128)}, u32[]{:S(2)}) copy-start(s32[2]{0:T(128)} %length.3) | copy-start | bytes 28
  28.0 15.8 %all-to-all-start.1 = ((bf16[16,136,128]{2,1,0:T(8,128)(2,1)}), bf16[16,136,128]{2,1,0:T(8,128)(2,1)S(1)}, u32[]{:S(2)}, u32[]{:S(2)}) async-start(bf16[16,136,128]{2,1,0:T(8,128)(2,1)} %prefix.1), calls=%async_computation.1 | async-start | bytes 1114112 | tf_op jit(solution)/shard_map/all_to_all | solution.py:546
  44.2 4.6 %collective-permute-start.1 = (bf16[16,136,128]{2,1,0:T(8,128)(2,1)S(1)}, bf16[16,136,128]{2,1,0:T(8,128)(2,1)S(1)}, u32[]{:S(2)}, u32[]{:S(2)}) collective-permute-start(bf16[16,136,128]{2,1,0:T(8,128)(2,1)S(1)} %get-tuple-element.83), channel_id=1, source_target_pairs={{0,4},{4,0},{1,5},{5,1},{2,6},{6,2},{3,7},{7,3},{8,12},{12,8},{9,1... | collective-permute-start | bytes 1671176 | tf_op jit(solution)/shard_map/ppermute | solution.py:466
  53.5 18.5 %collective-permute-start.2 = (bf16[2,272,512]{2,1,0:T(8,128)(2,1)S(1)}, bf16[2,272,512]{2,1,0:T(8,128)(2,1)S(1)}, u32[]{:S(2)}, u32[]{:S(2)}) collective-permute-start(bf16[2,272,512]{2,1,0:T(8,128)(2,1)S(1)} %get-tuple-element.99), channel_id=1, source_target_pairs={{0,1},{1,0},{2,3},{3,2},{4,5},{5,4},{6,7},{7,6},{8,9},{9,8},{10,11... | collective-permute-start | bytes 1671176 | tf_op jit(solution)/shard_map/ppermute | solution.py:462
  55.4 16.6 %collective-permute-start.3 = (bf16[2,272,512]{2,1,0:T(8,128)(2,1)S(1)}, bf16[2,272,512]{2,1,0:T(8,128)(2,1)S(1)}, u32[]{:S(2)}, u32[]{:S(2)}) collective-permute-start(bf16[2,272,512]{2,1,0:T(8,128)(2,1)S(1)} %get-tuple-element.100), channel_id=1, source_target_pairs={{0,3},{1,2},{2,1},{3,0},{4,7},{5,6},{6,5},{7,4},{8,11},{9,10},{10,... | collective-permute-start | bytes 1671176 | tf_op jit(solution)/shard_map/ppermute | solution.py:462
  62.3 17.3 %collective-permute-start.6 = (bf16[2,256,512]{2,1,0:T(8,128)(2,1)S(1)}, bf16[2,256,512]{2,1,0:T(8,128)(2,1)S(1)}, u32[]{:S(2)}, u32[]{:S(2)}) collective-permute-start(bf16[2,256,512]{2,1,0:T(8,128)(2,1)S(1)} %get-tuple-element.115), channel_id=1, source_target_pairs={{0,1},{1,0},{2,3},{3,2},{4,5},{5,4},{6,7},{7,6},{8,9},{9,8},{10,11... | collective-permute-start | bytes 1572872 | tf_op jit(solution)/shard_map/ppermute | solution.py:462
  63.1 18.7 %collective-permute-start.7 = (bf16[2,256,512]{2,1,0:T(8,128)(2,1)S(1)}, bf16[2,256,512]{2,1,0:T(8,128)(2,1)S(1)}, u32[]{:S(2)}, u32[]{:S(2)}) collective-permute-start(bf16[2,256,512]{2,1,0:T(8,128)(2,1)S(1)} %get-tuple-element.116), channel_id=1, source_target_pairs={{0,3},{1,2},{2,1},{3,0},{4,7},{5,6},{6,5},{7,4},{8,11},{9,10},{10,... | collective-permute-start | bytes 1572872 | tf_op jit(solution)/shard_map/ppermute | solution.py:462
  72.3 21.0 %collective-permute-start.4 = (bf16[272,512]{1,0:T(8,128)(2,1)S(1)}, bf16[272,512]{1,0:T(8,128)(2,1)S(1)}, u32[]{:S(2)}, u32[]{:S(2)}) collective-permute-start(bf16[272,512]{1,0:T(8,128)(2,1)S(1)} %get-tuple-element.111), channel_id=1, source_target_pairs={{0,3},{1,2},{2,1},{3,0},{4,7},{5,6},{6,5},{7,4},{8,11},{9,10},{10,... | collective-permute-start | bytes 835592 | tf_op jit(solution)/shard_map/ppermute | solution.py:462
  74.5 18.9 %collective-permute-start.5 = (bf16[272,512]{1,0:T(8,128)(2,1)S(1)}, bf16[272,512]{1,0:T(8,128)(2,1)S(1)}, u32[]{:S(2)}, u32[]{:S(2)}) collective-permute-start(bf16[272,512]{1,0:T(8,128)(2,1)S(1)} %get-tuple-element.112), channel_id=1, source_target_pairs={{0,1},{1,0},{2,3},{3,2},{4,5},{5,4},{6,7},{7,6},{8,9},{9,8},{10,11... | collective-permute-start | bytes 835592 | tf_op jit(solution)/shard_map/ppermute | solution.py:462
  81.9 11.5 %collective-permute-start.8 = (bf16[256,512]{1,0:T(8,128)(2,1)S(1)}, bf16[256,512]{1,0:T(8,128)(2,1)S(1)}, u32[]{:S(2)}, u32[]{:S(2)}) collective-permute-start(bf16[256,512]{1,0:T(8,128)(2,1)S(1)} %get-tuple-element.120), channel_id=1, source_target_pairs={{0,3},{1,2},{2,1},{3,0},{4,7},{5,6},{6,5},{7,4},{8,11},{9,10},{10,... | collective-permute-start | bytes 786440 | tf_op jit(solution)/shard_map/ppermute | solution.py:462
  84.2 9.1 %collective-permute-start.9 = (bf16[256,512]{1,0:T(8,128)(2,1)S(1)}, bf16[256,512]{1,0:T(8,128)(2,1)S(1)}, u32[]{:S(2)}, u32[]{:S(2)}) collective-permute-start(bf16[256,512]{1,0:T(8,128)(2,1)S(1)} %get-tuple-element.121), channel_id=1, source_target_pairs={{0,1},{1,0},{2,3},{3,2},{4,5},{5,4},{6,7},{7,6},{8,9},{9,8},{10,11... | collective-permute-start | bytes 786440 | tf_op jit(solution)/shard_map/ppermute | solution.py:462

commit v11 on v10

--- a/solution.py
+++ b/solution.py
@@ -411,9 +411,8 @@
     project(normed_ref, [weight_ref.at[i] for i in range(4)], ((rest_ref, 1), (rest_ref, 3), (rest_ref, 0), (rest_ref, 2)))
 
 
-def onward_kernel(a_ref, b_ref, rest_ref, a_out, b_out):
-    a_out[...] = (rest_ref[1].astype(F32) + a_ref[1].astype(F32)).astype(BF16)
-    b_out[...] = (rest_ref[3].astype(F32) + b_ref[1].astype(F32)).astype(BF16)
+def onward_kernel(piece, near_ref, rest_ref, out_ref):
+    out_ref[...] = (rest_ref[piece].astype(F32) + near_ref[1].astype(F32)).astype(BF16)
 
 
 def own_sum_kernel(a_ref, b_ref, rest_ref, out_ref):
@@ -577,7 +576,7 @@
             compiler_params=pltpu.CompilerParams(vmem_limit_bytes=24 << 20),
             name="chunk",
         )(state, read_2, *local, norm, near_columns, far_columns, *sample)
-        near = lax.optimization_barrier((swap(first, 1), swap(second, 3)))
+        near = (swap(first, 1), swap(second, 3))
         return normed, near, *held
 
     normed_0, near_0, far_columns = chunk(0, *in_hbm(weight), *sample)
@@ -589,10 +588,13 @@
     )
 
     def onward(near, rest):
-        return call(onward_kernel, "onward", (shape(near[0].shape[1:]),) * 2, (*near, rest), 8)
+        return [
+            call(functools.partial(onward_kernel, piece), "onward", shape(x.shape[1:]), (x, rest), 8)
+            for piece, x in zip((1, 3), near)
+        ]
 
     def send_on(ons):
-        return lax.optimization_barrier((swap(ons[0], 3), swap(ons[1], 1)))
+        return swap(ons[0], 3), swap(ons[1], 1)
 
     def own_sum(near, rest):
         return call(own_sum_kernel, "own_sum", shape((2, *near[0].shape[1:]), F32), (*near, rest), 8)

time: 95.2 us -> 96.1 us (level)
  waiting for transfers between devices: 23 us -> 25 us
  starting transfers between devices: 25.6 us -> 24.5 us
    ppermute x8, waiting for transfers between devices: 16.3 us -> 18.4 us  [swap(): return lax.ppermute(x, 'head', [(i, i ^ step) for i in range(4)])]
    ppermute x8, starting transfers between devices: 10.1 us -> 8.9 us  [swap(): return lax.ppermute(x, 'head', [(i, i ^ step) for i in range(4)])]
    pallas_call x12 -> x14, Pallas kernels: 11.2 us -> 11.2 us  [call(): pl.pallas_call(kernel, out_shape=out_shape, in_specs=[SMEM] * scalars + [...]
where the time goes in v11:
time: 96.1 us; the launch traced here: 95.6 us
  Pallas kernels  45.1 us (47%)
  waiting for transfers between devices  25 us (26%)
  starting transfers between devices  24.5 us (25%)
    ppermute x8, waiting for transfers between devices, swap(): return lax.ppermute(x, 'head', [(i, i ^ step) for i in range(4)])  18.4 us
    pallas_call x2, Pallas kernels, local_outputs(): pl.pallas_call(functools.partial(local_kernel, part), grid=(blocks,), out...  14.6 us
    pallas_call x14, Pallas kernels, call(): pl.pallas_call(kernel, out_shape=out_shape, in_specs=[SMEM] * scalars + [...  11.2 us
    pallas_call x2, Pallas kernels, chunk(): pl.pallas_call(functools.partial(chunk_kernel, place, bool(sample)), out_...  9.1 us
    ppermute x8, starting transfers between devices, swap(): return lax.ppermute(x, 'head', [(i, i ^ step) for i in range(4)])  8.9 us
    all_to_all x1, starting transfers between devices, per_device(): slices = lax.all_to_all(joined, ('y', 'x'), 0, 0, tiled=True)  6.84 us
    pallas_call x2, Pallas kernels, fetch(): pl.pallas_call(functools.partial(fetch_kernel, pieces), out_shape=(held,...  5.97 us
    all_to_all x1, starting transfers between devices, per_device(): back = lax.all_to_all(prefix, ('y', 'x'), 0, 0, tiled=True)  5.06 us
  transfers between devices with their start and end apart: 12, of which 6 were waited for; matrix products, arithmetic and copies ran while one was open for 0% of the time, Pallas kernels for 34%

profile of v11, /device:TPU:1, one launch (start us, length us, event | category | flops | bytes accessed | tf_op | source)
XLA Modules:
  0.0 95.6 jit_solution(16764361027555869350)
XLA Ops:
  0.7 4.2 %end_state.1 = (bf16[16,136,128]{2,1,0:T(8,128)(2,1)S(1)}, bf16[16,136,128]{2,1,0:T(8,128)(2,1)S(1)}) custom-call(s32[2]{0:T(128)} %length.3, f32[32,512]{1,0:T(8,128)} %step_ref.1, f32[1,32]{1,0:T(1,128)} %bitcast.13, bf16[512,2048]{1,0:T(8,128)(2,1)} %values_ref.4, bf16[512,256]{1,0:T(8,128)(2,1)} %bitcast.23, bf16[2,16,256]{2,1,0:T(8,128)(2,1)} %bitcast.10), custom_call_target="tpu_custom_call" | custom-call | tf_op jit(solution)/shard_map/end_state/pallas_call | solution.py:518
  4.8 1.5 %collective-permute-start = (bf16[16,136,128]{2,1,0:T(8,128)(2,1)S(1)}, bf16[16,136,128]{2,1,0:T(8,128)(2,1)S(1)}, u32[]{:S(2)}, u32[]{:S(2)}) collective-permute-start(bf16[16,136,128]{2,1,0:T(8,128)(2,1)S(1)} %get-tuple-element.53), channel_id=1, source_target_pairs={{0,4},{4,0},{1,5},{5,1},{2,6},{6,2},{3,7},{7,3},{8,12},{12,8},{9,1... | collective-permute-start | bytes 1671176 | tf_op jit(solution)/shard_map/ppermute | solution.py:465
  6.4 1.5 %collective-permute-done.sib_ref = bf16[16,136,128]{2,1,0:T(8,128)(2,1)S(1)} collective-permute-done((bf16[16,136,128]{2,1,0:T(8,128)(2,1)S(1)}, bf16[16,136,128]{2,1,0:T(8,128)(2,1)S(1)}, u32[]{:S(2)}, u32[]{:S(2)}) %collective-permute-start) | collective-permute-done | bytes 557088 | tf_op jit(solution)/shard_map/ppermute | solution.py:465
  9.0 6.8 %all-to-all-start = ((bf16[16,136,128]{2,1,0:T(8,128)(2,1)}), bf16[16,136,128]{2,1,0:T(8,128)(2,1)S(1)}, u32[]{:S(2)}, u32[]{:S(2)}) async-start(bf16[16,136,128]{2,1,0:T(8,128)(2,1)} %join_cores.1), calls=%async_computation | async-start | bytes 1114112 | tf_op jit(solution)/shard_map/all_to_all | solution.py:533
  15.9 7.4 %local_outputs.2 = (bf16[256,2048]{1,0:T(8,128)(2,1)}, bf16[256,2048]{1,0:T(8,128)(2,1)}, bf16[256,2048]{1,0:T(8,128)(2,1)}, f32[8,2048]{1,0:T(8,128)}) custom-call(f32[32,512]{1,0:T(8,128)} %step_ref.1, f32[1,32]{1,0:T(1,128)S(1)} %bitcast.14, f32[1,32]{1,0:T(1,128)S(1)} %bitcast.17, bf16[512,2048]{1,0:T(8,128)(2,1)} %values_ref.4, ...), custom_call_target="tpu_custom_call" | custom-call | flops 3221225472 | bytes 20971520 | tf_op jit(solution)/shard_map/local_outputs/pallas_call | solution.py:488
  23.4 1.9 %sample_outputs.1 = (f32[16,2048]{1,0:T(8,128)}, f32[16,2048]{1,0:T(8,128)}, f32[16,2048]{1,0:T(8,128)}) custom-call(s32[2]{0:T(128)S(1)} %copy-done.4, f32[2,32,16]{2,1,0:T(8,128)S(1)} %bitcast.9, f32[1,32]{1,0:T(1,128)S(1)} %bitcast.15, f32[1,32]{1,0:T(1,128)S(1)} %bitcast.18, bf16[2,16,2048]{2,1,0:T(8,128)(2,1)S(1)} %copy-done, ...), custom_call_target="tpu_custom_call" | custom-call | flops 1 | bytes 1 | tf_op jit(solution)/shard_map/sample_outputs/pallas_call | solution.py:440
  25.3 1.6 %all-to-all-done.in_ref = bf16[16,136,128]{2,1,0:T(8,128)(2,1)S(1)} async-done(((bf16[16,136,128]{2,1,0:T(8,128)(2,1)}), bf16[16,136,128]{2,1,0:T(8,128)(2,1)S(1)}, u32[]{:S(2)}, u32[]{:S(2)}) %all-to-all-start) | async-done | bytes 557088 | tf_op jit(solution)/shard_map/all_to_all | solution.py:533
  28.0 5.1 %all-to-all-start.1 = ((bf16[16,136,128]{2,1,0:T(8,128)(2,1)}), bf16[16,136,128]{2,1,0:T(8,128)(2,1)S(1)}, u32[]{:S(2)}, u32[]{:S(2)}) async-start(bf16[16,136,128]{2,1,0:T(8,128)(2,1)} %prefix.1), calls=%async_computation.1 | async-start | bytes 1114112 | tf_op jit(solution)/shard_map/all_to_all | solution.py:545
  33.1 7.2 %local_outputs.3 = (bf16[256,2048]{1,0:T(8,128)(2,1)}, bf16[256,2048]{1,0:T(8,128)(2,1)}) custom-call(f32[32,512]{1,0:T(8,128)} %step_ref.1, f32[1,32]{1,0:T(1,128)S(1)} %bitcast.16, f32[1,32]{1,0:T(1,128)S(1)} %bitcast.19, bf16[512,2048]{1,0:T(8,128)(2,1)} %values_ref.4, bf16[512,2048]{1,0:T(8,128)(2,1)} %gate_ref.5, bf16[512,256]{1,0:T(8,128)(2,1)} %bitcast.25, ...), custom_call_target="tpu_custom_call" | custom-call | flops 3221225472 | bytes 20971520 | tf_op jit(solution)/shard_map/local_outputs/pallas_call | solution.py:488
  40.2 3.6 %all-to-all-done.1.back_ref = bf16[16,136,128]{2,1,0:T(8,128)(2,1)S(1)} async-done(((bf16[16,136,128]{2,1,0:T(8,128)(2,1)}), bf16[16,136,128]{2,1,0:T(8,128)(2,1)S(1)}, u32[]{:S(2)}, u32[]{:S(2)}) %all-to-all-start.1) | async-done | bytes 557088 | tf_op jit(solution)/shard_map/all_to_all | solution.py:545
  44.2 2.2 %collective-permute-start.1 = (bf16[16,136,128]{2,1,0:T(8,128)(2,1)S(1)}, bf16[16,136,128]{2,1,0:T(8,128)(2,1)S(1)}, u32[]{:S(2)}, u32[]{:S(2)}) collective-permute-start(bf16[16,136,128]{2,1,0:T(8,128)(2,1)S(1)} %get-tuple-element.71), channel_id=1, source_target_pairs={{0,4},{4,0},{1,5},{5,1},{2,6},{6,2},{3,7},{7,3},{8,12},{12,8},{9,1... | collective-permute-start | bytes 1671176 | tf_op jit(solution)/shard_map/ppermute | solution.py:465
  46.3 2.4 %fetch_weight.2 = (bf16[1,2048,512]{2,1,0:T(8,128)(2,1)S(1)}, bf16[256,2048]{1,0:T(8,128)(2,1)S(1)}, bf16[256,2048]{1,0:T(8,128)(2,1)S(1)}, bf16[512,256]{1,0:T(...) custom-call(bf16[2048,4096]{1,0:T(8,128)(2,1)} %weight_ref.1, ...), custom_call_target="tpu_custom_call" | custom-call | tf_op jit(solution)/shard_map/fetch_weight/pallas_call | solution.py:342
  49.0 4.5 %chunk.2 = (bf16[2,272,512]{2,1,0:T(8,128)(2,1)S(1)}, bf16[2,272,512]{2,1,0:T(8,128)(2,1)S(1)}, bf16[272,2048]{1,0:T(8,128)(2,1)S(1)}, bf16[3,2048,512]{2,1,0:T(8,128)(2,1)S(1)}) custom-call(bf16[264,2048]{1,0:T(8,128)(2,1)S(1)} %join_halves.1.state_ref, bf16[512,256]{1,0:T(8,128)(2,1)S(1)} %get-tuple-element.79.read_ref, ...), custom_call_target="tpu_custom_call" | custom-call | tf_op jit(solution)/shard_map/chunk/pallas_call | solution.py:570
  53.5 4.0 %collective-permute-start.3 = (bf16[2,272,512]{2,1,0:T(8,128)(2,1)S(1)}, bf16[2,272,512]{2,1,0:T(8,128)(2,1)S(1)}, u32[]{:S(2)}, u32[]{:S(2)}) collective-permute-start(bf16[2,272,512]{2,1,0:T(8,128)(2,1)S(1)} %get-tuple-element.89), channel_id=1, source_target_pairs={{0,3},{1,2},{2,1},{3,0},{4,7},{5,6},{6,5},{7,4},{8,11},{9,10},{10,... | collective-permute-start | bytes 1671176 | tf_op jit(solution)/shard_map/ppermute | solution.py:461
  57.5 4.6 %chunk.3 = (bf16[2,256,512]{2,1,0:T(8,128)(2,1)S(1)}, bf16[2,256,512]{2,1,0:T(8,128)(2,1)S(1)}, bf16[256,2048]{1,0:T(8,128)(2,1)S(1)}) custom-call(bf16[264,2048]{1,0:T(8,128)(2,1)S(1)} %join_halves.1.state_ref, bf16[512,256]{1,0:T(8,128)(2,1)S(1)} %get-tuple-element.79.read_ref, bf16[256,2048]{1,0:T(8,128)(2,1)} %get-tuple-element.90.scaled_ref, ...), custom_call_target="tpu_custom_call" | custom-call | tf_op jit(solution)/shard_map/chunk/pallas_call | solution.py:570
  62.1 1.5 %collective-permute-start.6 = (bf16[2,256,512]{2,1,0:T(8,128)(2,1)S(1)}, bf16[2,256,512]{2,1,0:T(8,128)(2,1)S(1)}, u32[]{:S(2)}, u32[]{:S(2)}) collective-permute-start(bf16[2,256,512]{2,1,0:T(8,128)(2,1)S(1)} %get-tuple-element.97), channel_id=1, source_target_pairs={{0,1},{1,0},{2,3},{3,2},{4,5},{5,4},{6,7},{7,6},{8,9},{9,8},{10,11... | collective-permute-start | bytes 1572872 | tf_op jit(solution)/shard_map/ppermute | solution.py:461
  63.8 3.5 %fetch_weight.3.weight_ref = bf16[4,2048,512]{2,1,0:T(8,128)(2,1)S(1)} custom-call(bf16[2048,4096]{1,0:T(8,128)(2,1)} %weight_ref.1), custom_call_target="tpu_custom_call" | custom-call | tf_op jit(solution)/shard_map/fetch_weight/pallas_call | solution.py:342
  67.3 2.5 %rest.2.rest_ref = bf16[4,272,512]{2,1,0:T(8,128)(2,1)S(1)} custom-call(bf16[272,2048]{1,0:T(8,128)(2,1)S(1)} %get-tuple-element.88.normed_ref, bf16[4,2048,512]{2,1,0:T(8,128)(2,1)S(1)} %fetch_weight.3.weight_ref), custom_call_target="tpu_custom_call" | custom-call | flops 1 | bytes 1 | tf_op jit(solution)/shard_map/rest/pallas_call | solution.py:440
  69.8 2.3 %rest.3.rest_ref = bf16[4,256,512]{2,1,0:T(8,128)(2,1)S(1)} custom-call(bf16[256,2048]{1,0:T(8,128)(2,1)S(1)} %get-tuple-element.93.normed_ref, bf16[4,2048,512]{2,1,0:T(8,128)(2,1)S(1)} %fetch_weight.3.weight_ref), custom_call_target="tpu_custom_call" | custom-call | flops 1 | bytes 1 | tf_op jit(solution)/shard_map/rest/pallas_call | solution.py:440
  72.4 2.7 %collective-permute-start.4 = (bf16[272,512]{1,0:T(8,128)(2,1)S(1)}, bf16[272,512]{1,0:T(8,128)(2,1)S(1)}, u32[]{:S(2)}, u32[]{:S(2)}) collective-permute-start(bf16[272,512]{1,0:T(8,128)(2,1)S(1)} %onward.4), channel_id=1, source_target_pairs={{0,3},{1,2},{2,1},{3,0},{4,7},{5,6},{6,5},{7,4},{8,11},{9,10},{10,... | collective-permute-start | bytes 835592 | tf_op jit(solution)/shard_map/ppermute | solution.py:461
  75.1 7.6 %collective-permute-done.6.a_ref.near_ref = bf16[2,256,512]{2,1,0:T(8,128)(2,1)S(1)} collective-permute-done((bf16[2,256,512]{2,1,0:T(8,128)(2,1)S(1)}, bf16[2,256,512]{2,1,0:T(8,128)(2,1)S(1)}, u32[]{:S(2)}, u32[]{:S(2)}) %collective-permute-start.6) | collective-permute-done | bytes 524320 | tf_op jit(solution)/shard_map/ppermute | solution.py:461
  83.5 8.9 %collective-permute-done.8.refs_4_ = bf16[256,512]{1,0:T(8,128)(2,1)S(1)} collective-permute-done((bf16[256,512]{1,0:T(8,128)(2,1)S(1)}, bf16[256,512]{1,0:T(8,128)(2,1)S(1)}, u32[]{:S(2)}, u32[]{:S(2)}) %collective-permute-start.8) | collective-permute-done | bytes 262176 | tf_op jit(solution)/shard_map/ppermute | solution.py:461
  92.4 1.9 %collective-permute-done.9.refs_5_ = bf16[256,512]{1,0:T(8,128)(2,1)S(1)} collective-permute-done((bf16[256,512]{1,0:T(8,128)(2,1)S(1)}, bf16[256,512]{1,0:T(8,128)(2,1)S(1)}, u32[]{:S(2)}, u32[]{:S(2)}) %collective-permute-start.9) | collective-permute-done | bytes 262176 | tf_op jit(solution)/shard_map/ppermute | solution.py:461
  94.3 1.3 %finish.1 = (bf16[1024,512]{1,0:T(8,128)(2,1)}, bf16[2,1024]{1,0:T(2,128)(2,1)}) custom-call(f32[2,272,512]{2,1,0:T(8,128)S(1)} %own_sum.2.refs_0_, bf16[272,512]{1,0:T(8,128)(2,1)S(1)} %collective-permute-done.4.refs_1_, bf16[272,512]{1,0:T(8,128)(2,1)S(1)} %collective-permute-done.5.refs_2_, f32[2,256,512]{2,1,0:T(8,128)S(1)} %own_sum.3.refs_3_, ...), custom_call_target="tpu_custom_call" | custom-call | flops 1 | bytes 1 | tf_op jit(solution)/shard_map/finish/pallas_call | solution.py:440
  (38 shorter events, 4.0 us)
Async XLA Ops:
  0.6 5.7 %copy-start.7 = (f32[32,2,16]{0,2,1:T(8,128)S(1)}, f32[32,2,16]{0,2,1:T(8,128)}, u32[]{:S(2)}) copy-start(f32[32,2,16]{0,2,1:T(8,128)} %param.28) | copy-start | bytes 12292
  0.6 15.2 %copy-start.5 = (f32[32]{0:T(128)S(1)}, f32[32]{0:T(128)}, u32[]{:S(2)}) copy-start(f32[32]{0:T(128)} %param.20) | copy-start | bytes 388
  0.7 15.2 %copy-start.6 = (f32[32]{0:T(128)S(1)}, f32[32]{0:T(128)}, u32[]{:S(2)}) copy-start(f32[32]{0:T(128)} %param.21) | copy-start | bytes 388
  4.8 3.1 %collective-permute-start = (bf16[16,136,128]{2,1,0:T(8,128)(2,1)S(1)}, bf16[16,136,128]{2,1,0:T(8,128)(2,1)S(1)}, u32[]{:S(2)}, u32[]{:S(2)}) collective-permute-start(bf16[16,136,128]{2,1,0:T(8,128)(2,1)S(1)} %get-tuple-element.53), channel_id=1, source_target_pairs={{0,4},{4,0},{1,5},{5,1},{2,6},{6,2},{3,7},{7,3},{8,12},{12,8},{9,1... | collective-permute-start | bytes 1671176 | tf_op jit(solution)/shard_map/ppermute | solution.py:465
  9.0 17.9 %all-to-all-start = ((bf16[16,136,128]{2,1,0:T(8,128)(2,1)}), bf16[16,136,128]{2,1,0:T(8,128)(2,1)S(1)}, u32[]{:S(2)}, u32[]{:S(2)}) async-start(bf16[16,136,128]{2,1,0:T(8,128)(2,1)} %join_cores.1), calls=%async_computation | async-start | bytes 1114112 | tf_op jit(solution)/shard_map/all_to_all | solution.py:533
  15.9 7.5 %copy-start = (bf16[2,16,2048]{2,1,0:T(8,128)(2,1)S(1)}, bf16[2,16,2048]{2,1,0:T(8,128)(2,1)}, u32[]{:S(2)}) copy-start(bf16[2,16,2048]{2,1,0:T(8,128)(2,1)} %values_ref.3) | copy-start | bytes 393220
  15.9 7.5 %copy-start.1 = (bf16[2,16,2048]{2,1,0:T(8,128)(2,1)S(1)}, bf16[2,16,2048]{2,1,0:T(8,128)(2,1)}, u32[]{:S(2)}) copy-start(bf16[2,16,2048]{2,1,0:T(8,128)(2,1)} %gate_ref.4) | copy-start | bytes 393220
  15.9 7.5 %copy-start.2 = (bf16[2,16,1,256]{3,1,2,0:T(8,128)(2,1)S(1)}, bf16[2,16,1,256]{3,1,2,0:T(8,128)(2,1)}, u32[]{:S(2)}) copy-start(bf16[2,16,1,256]{3,1,2,0:T(8,128)(2,1)} %param.27) | copy-start | bytes 49156
  15.9 7.5 %copy-start.3 = (bf16[2,16,1,256]{3,1,2,0:T(8,128)(2,1)S(1)}, bf16[2,16,1,256]{3,1,2,0:T(8,128)(2,1)}, u32[]{:S(2)}) copy-start(bf16[2,16,1,256]{3,1,2,0:T(8,128)(2,1)} %param.26) | copy-start | bytes 49156
  15.9 7.5 %copy-start.4 = (s32[2]{0:T(128)S(1)}, s32[2]{0:T(128)}, u32[]{:S(2)}) copy-start(s32[2]{0:T(128)} %length.3) | copy-start | bytes 28
  28.0 15.8 %all-to-all-start.1 = ((bf16[16,136,128]{2,1,0:T(8,128)(2,1)}), bf16[16,136,128]{2,1,0:T(8,128)(2,1)S(1)}, u32[]{:S(2)}, u32[]{:S(2)}) async-start(bf16[16,136,128]{2,1,0:T(8,128)(2,1)} %prefix.1), calls=%async_computation.1 | async-start | bytes 1114112 | tf_op jit(solution)/shard_map/all_to_all | solution.py:545
  44.2 4.6 %collective-permute-start.1 = (bf16[16,136,128]{2,1,0:T(8,128)(2,1)S(1)}, bf16[16,136,128]{2,1,0:T(8,128)(2,1)S(1)}, u32[]{:S(2)}, u32[]{:S(2)}) collective-permute-start(bf16[16,136,128]{2,1,0:T(8,128)(2,1)S(1)} %get-tuple-element.71), channel_id=1, source_target_pairs={{0,4},{4,0},{1,5},{5,1},{2,6},{6,2},{3,7},{7,3},{8,12},{12,8},{9,1... | collective-permute-start | bytes 1671176 | tf_op jit(solution)/shard_map/ppermute | solution.py:465
  53.5 18.6 %collective-permute-start.3 = (bf16[2,272,512]{2,1,0:T(8,128)(2,1)S(1)}, bf16[2,272,512]{2,1,0:T(8,128)(2,1)S(1)}, u32[]{:S(2)}, u32[]{:S(2)}) collective-permute-start(bf16[2,272,512]{2,1,0:T(8,128)(2,1)S(1)} %get-tuple-element.89), channel_id=1, source_target_pairs={{0,3},{1,2},{2,1},{3,0},{4,7},{5,6},{6,5},{7,4},{8,11},{9,10},{10,... | collective-permute-start | bytes 1671176 | tf_op jit(solution)/shard_map/ppermute | solution.py:461
  57.5 14.7 %collective-permute-start.2 = (bf16[2,272,512]{2,1,0:T(8,128)(2,1)S(1)}, bf16[2,272,512]{2,1,0:T(8,128)(2,1)S(1)}, u32[]{:S(2)}, u32[]{:S(2)}) collective-permute-start(bf16[2,272,512]{2,1,0:T(8,128)(2,1)S(1)} %get-tuple-element.87), channel_id=1, source_target_pairs={{0,1},{1,0},{2,3},{3,2},{4,5},{5,4},{6,7},{7,6},{8,9},{9,8},{10,11... | collective-permute-start | bytes 1671176 | tf_op jit(solution)/shard_map/ppermute | solution.py:461
  62.1 20.5 %collective-permute-start.6 = (bf16[2,256,512]{2,1,0:T(8,128)(2,1)S(1)}, bf16[2,256,512]{2,1,0:T(8,128)(2,1)S(1)}, u32[]{:S(2)}, u32[]{:S(2)}) collective-permute-start(bf16[2,256,512]{2,1,0:T(8,128)(2,1)S(1)} %get-tuple-element.97), channel_id=1, source_target_pairs={{0,1},{1,0},{2,3},{3,2},{4,5},{5,4},{6,7},{7,6},{8,9},{9,8},{10,11... | collective-permute-start | bytes 1572872 | tf_op jit(solution)/shard_map/ppermute | solution.py:461
  63.7 19.6 %collective-permute-start.7 = (bf16[2,256,512]{2,1,0:T(8,128)(2,1)S(1)}, bf16[2,256,512]{2,1,0:T(8,128)(2,1)S(1)}, u32[]{:S(2)}, u32[]{:S(2)}) collective-permute-start(bf16[2,256,512]{2,1,0:T(8,128)(2,1)S(1)} %get-tuple-element.98), channel_id=1, source_target_pairs={{0,3},{1,2},{2,1},{3,0},{4,7},{5,6},{6,5},{7,4},{8,11},{9,10},{10,... | collective-permute-start | bytes 1572872 | tf_op jit(solution)/shard_map/ppermute | solution.py:461
  72.4 21.9 %collective-permute-start.4 = (bf16[272,512]{1,0:T(8,128)(2,1)S(1)}, bf16[272,512]{1,0:T(8,128)(2,1)S(1)}, u32[]{:S(2)}, u32[]{:S(2)}) collective-permute-start(bf16[272,512]{1,0:T(8,128)(2,1)S(1)} %onward.4), channel_id=1, source_target_pairs={{0,3},{1,2},{2,1},{3,0},{4,7},{5,6},{6,5},{7,4},{8,11},{9,10},{10,... | collective-permute-start | bytes 835592 | tf_op jit(solution)/shard_map/ppermute | solution.py:461
  75.1 19.2 %collective-permute-start.5 = (bf16[272,512]{1,0:T(8,128)(2,1)S(1)}, bf16[272,512]{1,0:T(8,128)(2,1)S(1)}, u32[]{:S(2)}, u32[]{:S(2)}) collective-permute-start(bf16[272,512]{1,0:T(8,128)(2,1)S(1)} %onward.5), channel_id=1, source_target_pairs={{0,1},{1,0},{2,3},{3,2},{4,5},{5,4},{6,7},{7,6},{8,9},{9,8},{10,11... | collective-permute-start | bytes 835592 | tf_op jit(solution)/shard_map/ppermute | solution.py:461
  82.7 9.6 %collective-permute-start.8 = (bf16[256,512]{1,0:T(8,128)(2,1)S(1)}, bf16[256,512]{1,0:T(8,128)(2,1)S(1)}, u32[]{:S(2)}, u32[]{:S(2)}) collective-permute-start(bf16[256,512]{1,0:T(8,128)(2,1)S(1)} %onward.6), channel_id=1, source_target_pairs={{0,3},{1,2},{2,1},{3,0},{4,7},{5,6},{6,5},{7,4},{8,11},{9,10},{10,... | collective-permute-start | bytes 786440 | tf_op jit(solution)/shard_map/ppermute | solution.py:461
  83.3 11.0 %collective-permute-start.9 = (bf16[256,512]{1,0:T(8,128)(2,1)S(1)}, bf16[256,512]{1,0:T(8,128)(2,1)S(1)}, u32[]{:S(2)}, u32[]{:S(2)}) collective-permute-start(bf16[256,512]{1,0:T(8,128)(2,1)S(1)} %onward.7), channel_id=1, source_target_pairs={{0,1},{1,0},{2,3},{3,2},{4,5},{5,4},{6,7},{7,6},{8,9},{9,8},{10,11... | collective-permute-start | bytes 786440 | tf_op jit(solution)/shard_map/ppermute | solution.py:461

commit v12 on v10

--- a/solution.py
+++ b/solution.py
@@ -282,7 +282,7 @@
         narrow.append(jnp.broadcast_to(jnp.exp(whole), (SLEN, 128)))
     skip = jnp.concatenate([skip_ref[...], jnp.zeros((1, 128 - HEADS), F32)], axis=1)
     narrow.append(jnp.broadcast_to(skip, (SLEN, 128)))
-    spread = (iota((128, CH), 1) // HEAD_DIM == iota((128, CH), 0)).astype(BF16)
+    spread = ((iota((128, CH), 1) >> 6) == iota((128, CH), 0)).astype(BF16)
     parts = jnp.concatenate(three_parts(jnp.concatenate(narrow, axis=0)), axis=0).astype(BF16)
     wide = jnp.dot(parts, spread, preferred_element_type=F32)
     wide = wide[0:80] + wide[80:160] + wide[160:240]
@@ -391,15 +391,6 @@
     normed_ref[0 : CHUNKS[place][1], :] = normalize(gated, norm_ref[...])
     if place == LEADING:
         copies[2].start()
-    if sampled:
-        local_ref, grown_ref, gate_ref = sample
-        readings = state_ref[STATE : STATE + TAIL, :].astype(F32)
-        moved = jnp.concatenate([readings[2:TAIL], readings[0:2]], axis=0)
-        readings = jnp.where(lax.axis_index("core") == 0, readings, moved)
-        readings = jnp.concatenate([readings, jnp.zeros((16 - TAIL, CH), F32)], axis=0)
-        sampled = (local_ref[...] + readings * grown_ref[...]) * gate_ref[...]
-        rows = CHUNKS[place][1]
-        normed_ref[rows : rows + 16, :] = normalize(sampled, norm_ref[...])
     project(normed_ref, (near_ref.at[0],), ((first_ref, 0),))
     for i, out in enumerate(((first_ref, 1), (second_ref, 0), (second_ref, 1))):
         if place == LEADING:
@@ -407,6 +398,20 @@
         project(normed_ref, (held.at[i],), (out,))
 
 
+def sample_rows_kernel(state_ref, norm_ref, local_ref, grown_ref, gate_ref, near_ref, far_ref, rest_ref, out_ref):
+    readings = state_ref[STATE : STATE + TAIL, :].astype(F32)
+    moved = jnp.concatenate([readings[2:TAIL], readings[0:2]], axis=0)
+    readings = jnp.where(lax.axis_index("core") == 0, readings, moved)
+    readings = jnp.concatenate([readings, jnp.zeros((16 - TAIL, CH), F32)], axis=0)
+    sampled = (local_ref[...] + readings * grown_ref[...]) * gate_ref[...]
+    normed = normalize(sampled, norm_ref[...])
+    z = lax.axis_index("head")
+    columns = [near_ref.at[0], *(far_ref.at[i] for i in range(3)), *(rest_ref.at[i] for i in range(4))]
+    for column, (flip, half) in zip(columns, FIRST + REST):
+        at = pl.multiple_of(((z ^ flip) * 2 + half) * PIECE, PIECE)
+        out_ref[:, pl.ds(at, PIECE)] = jnp.dot(normed, column[...], preferred_element_type=F32).astype(BF16)
+
+
 def rest_kernel(normed_ref, weight_ref, rest_ref):
     project(normed_ref, [weight_ref.at[i] for i in range(4)], ((rest_ref, 1), (rest_ref, 3), (rest_ref, 0), (rest_ref, 2)))
 
@@ -422,15 +427,13 @@
 
 
 def finish_kernel(*refs):
-    ins, out_ref, sample_ref = refs[:-2], refs[-2], refs[-1]
+    ins, out_ref = refs[:-1], refs[-1]
     for place, (start, rows) in enumerate(CHUNKS):
         own, *far = ins[3 * place : 3 * place + 3]
         for half in range(2):
             total = own[half] + far[half][...].astype(F32)
             columns = slice(half * PIECE, (half + 1) * PIECE)
             out_ref[columns, start : start + rows] = jnp.transpose(total[0:rows]).astype(BF16)
-            if place == LEADING:
-                sample_ref[:, columns] = total[rows : rows + 2].astype(BF16)
 
 
 def in_hbm(*arrays):
@@ -535,12 +538,7 @@
     scaled_1, gain_1, *carry = local_outputs(
         0, step_1, decay, skip, prompt_values, prompt_gate, inject, read
     )
-    scaled_1, s_values = lax.optimization_barrier((scaled_1, sample_values))
-    sample = call(
-        sample_kernel, "sample_outputs", (pltpu.HBM((16, CH), F32),) * 3,
-        (sample_length, s_step, decay, skip, s_values, sample_gate, s_inject, s_read), 16, 1,
-    )
-    slices, scaled_1, sample = lax.optimization_barrier((slices, scaled_1, sample))
+    slices, scaled_1 = lax.optimization_barrier((slices, scaled_1))
     prefix = call(prefix_kernel, "prefix", slices_shape, (slices,), 16)
     prefix, step_2 = lax.optimization_barrier((prefix, prompt_step))
     back = lax.all_to_all(prefix, ("y", "x"), 0, 0, tiled=True)
@@ -553,8 +551,8 @@
     )
     theirs = other_core(send)
 
-    near_columns, scaled_2, gain_2, read_2, norm, *sample = fetch(
-        FIRST[:1], weight, scaled_2, gain_2, read_2, norm, *sample
+    near_columns, scaled_2, gain_2, read_2, norm = fetch(
+        FIRST[:1], weight, scaled_2, gain_2, read_2, norm
     )
     scaled = (scaled_1, scaled_2)
     gain = (gain_1, gain_2)
@@ -580,8 +578,13 @@
         near = lax.optimization_barrier((swap(first, 1), swap(second, 3)))
         return normed, near, *held
 
-    normed_0, near_0, far_columns = chunk(0, *in_hbm(weight), *sample)
+    normed_0, near_0, far_columns = chunk(0, *in_hbm(weight))
     (rest_columns,) = fetch(REST, weight)
+    normed_0, s_values, s_step = lax.optimization_barrier((normed_0, sample_values, s_step))
+    sample = call(
+        sample_kernel, "sample_outputs", (shape((16, CH), F32),) * 3,
+        (sample_length, s_step, decay, skip, s_values, sample_gate, s_inject, s_read), 16, 1,
+    )
     normed_1, near_1 = chunk(1, resident(far_columns))
     rest_0, rest_1 = (
         call(rest_kernel, "rest", shape((4, normed.shape[0], PIECE)), (normed, rest_columns), 24)
@@ -597,12 +600,17 @@
     def own_sum(near, rest):
         return call(own_sum_kernel, "own_sum", shape((2, *near[0].shape[1:]), F32), (*near, rest), 8)
 
+    sample_rows = call(
+        sample_rows_kernel, "sample_rows", shape((16, 4 * 1024)),
+        (state, norm, *sample, near_columns, resident(far_columns), rest_columns), 16,
+    )
+    sample_mixed = lax.psum_scatter(sample_rows, "head", scatter_dimension=1, tiled=True)[0:2].T
     ons_0, own_0, rest_1 = lax.optimization_barrier((onward(near_0, rest_0), own_sum(near_0, rest_0), rest_1))
     far_0 = send_on(ons_0)
     far_1 = send_on(onward(near_1, rest_1))
     parts = (own_0, *far_0, own_sum(near_1, rest_1), *far_1)
-    prompt_mixed, sample_mixed = call(finish_kernel, "finish", (shape((1024, TOK)), shape((2, 1024))), parts, 16)
-    return prompt_mixed, sample_mixed.T
+    prompt_mixed = call(finish_kernel, "finish", shape((1024, TOK)), parts, 16)
+    return prompt_mixed, sample_mixed
 
 
 def solution(mesh):

time: 95.2 us -> 121 us (1.27)
  between operations: 0.9 us -> 14.3 us
  local copies, waits for them, and re-layouts: 0.12 us -> 13.1 us
  Pallas kernels: 45.1 us -> 51.6 us
  waiting for transfers between devices: 23 us -> 16.9 us
  starting transfers between devices: 25.6 us -> 23.5 us
    unnamed x17 -> x35, local copies, waits for them, and re-layouts: 0.12 us -> 11.7 us
    ppermute x8, waiting for transfers between devices: 16.3 us -> 8.52 us  [swap(): return lax.ppermute(x, 'head', [(i, i ^ step) for i in range(4)])]
    pallas_call x12 -> x13, Pallas kernels: 11.2 us -> 16 us  [call(): pl.pallas_call(kernel, out_shape=out_shape, in_specs=[SMEM] * scalars + [...]
    all_to_all x1, waiting for transfers between devices: 1.59 us -> 3.7 us  [per_device(): slices = lax.all_to_all(joined, ('y', 'x'), 0, 0, tiled=True)]
    pallas_call x2, Pallas kernels: 9.1 us -> 11.1 us  [chunk(): pl.pallas_call(functools.partial(chunk_kernel, place, bool(sample)), out_...]
    all_to_all x1, starting transfers between devices: 5.07 us -> 3.58 us  [per_device(): back = lax.all_to_all(prefix, ('y', 'x'), 0, 0, tiled=True)]
    transpose x0 -> x1, local copies, waits for them, and re-layouts: none -> 1.31 us  [per_device(): lax.psum_scatter(sample_rows, 'head', scatter_dimension=1, tiled=True)[0:2]]
  transfers between devices with their start and end apart: 12 -> 13, of which waited for: 6 -> 7; matrix products, arithmetic and copies ran while one was open for 0% -> 1% of each run, Pallas kernels for 34% -> 31%
where the time goes in v12:
time: 121 us; the launch traced here: 119 us
  Pallas kernels  51.6 us (43%)
  starting transfers between devices  23.5 us (19%)
  waiting for transfers between devices  16.9 us (14%)
  between operations  14.3 us (12%)
  local copies, waits for them, and re-layouts  13.1 us (11%)
    pallas_call x13, Pallas kernels, call(): pl.pallas_call(kernel, out_shape=out_shape, in_specs=[SMEM] * scalars + [...  16 us
    pallas_call x2, Pallas kernels, local_outputs(): pl.pallas_call(functools.partial(local_kernel, part), grid=(blocks,), out...  14.5 us
    unnamed x35, local copies, waits for them, and re-layouts  11.7 us
    pallas_call x2, Pallas kernels, chunk(): pl.pallas_call(functools.partial(chunk_kernel, place, bool(sample)), out_...  11.1 us
    ppermute x8, starting transfers between devices, swap(): return lax.ppermute(x, 'head', [(i, i ^ step) for i in range(4)])  8.99 us
    ppermute x8, waiting for transfers between devices, swap(): return lax.ppermute(x, 'head', [(i, i ^ step) for i in range(4)])  8.52 us
    all_to_all x1, starting transfers between devices, per_device(): slices = lax.all_to_all(joined, ('y', 'x'), 0, 0, tiled=True)  6.84 us
    pallas_call x2, Pallas kernels, fetch(): pl.pallas_call(functools.partial(fetch_kernel, pieces), out_shape=(held,...  5.82 us
  transfers between devices with their start and end apart: 13, of which 7 were waited for; matrix products, arithmetic and copies ran while one was open for 1% of the time, Pallas kernels for 31%

profile of v12, /device:TPU:1, one launch (start us, length us, event | category | flops | bytes accessed | tf_op | source)
XLA Modules:
  0.0 119.4 jit_solution(14554392730075452581)
XLA Ops:
  7.2 4.1 %end_state.1 = (bf16[16,136,128]{2,1,0:T(8,128)(2,1)S(1)}, bf16[16,136,128]{2,1,0:T(8,128)(2,1)S(1)}) custom-call(s32[2]{0:T(128)} %length.3, f32[32,512]{1,0:T(8,128)} %step_ref.1, f32[1,32]{1,0:T(1,128)} %bitcast.14, bf16[512,2048]{1,0:T(8,128)(2,1)} %values_ref.3, bf16[512,256]{1,0:T(8,128)(2,1)} %bitcast.24, bf16[2,16,256]{2,1,0:T(8,128)(2,1)} %bitcast.11), custom_call_target="tpu_custom_call" | custom-call | tf_op jit(solution)/shard_map/end_state/pallas_call | solution.py:522
  11.3 1.5 %collective-permute-start = (bf16[16,136,128]{2,1,0:T(8,128)(2,1)S(1)}, bf16[16,136,128]{2,1,0:T(8,128)(2,1)S(1)}, u32[]{:S(2)}, u32[]{:S(2)}) collective-permute-start(bf16[16,136,128]{2,1,0:T(8,128)(2,1)S(1)} %get-tuple-element.58), channel_id=1, source_target_pairs={{0,4},{4,0},{1,5},{5,1},{2,6},{6,2},{3,7},{7,3},{8,12},{12,8},{9,1... | collective-permute-start | bytes 1671176 | tf_op jit(solution)/shard_map/ppermute | solution.py:469
  15.5 6.8 %all-to-all-start = ((bf16[16,136,128]{2,1,0:T(8,128)(2,1)}), bf16[16,136,128]{2,1,0:T(8,128)(2,1)S(1)}, u32[]{:S(2)}, u32[]{:S(2)}) async-start(bf16[16,136,128]{2,1,0:T(8,128)(2,1)} %join_cores.1), calls=%async_computation | async-start | bytes 1114112 | tf_op jit(solution)/shard_map/all_to_all | solution.py:537
  22.4 7.3 %local_outputs.2 = (bf16[256,2048]{1,0:T(8,128)(2,1)}, bf16[256,2048]{1,0:T(8,128)(2,1)}, bf16[256,2048]{1,0:T(8,128)(2,1)}, f32[8,2048]{1,0:T(8,128)}) custom-call(f32[32,512]{1,0:T(8,128)} %step_ref.1, f32[1,32]{1,0:T(1,128)S(1)} %bitcast.15, f32[1,32]{1,0:T(1,128)S(1)} %bitcast.18, bf16[512,2048]{1,0:T(8,128)(2,1)} %values_ref.3, ...), custom_call_target="tpu_custom_call" | custom-call | flops 3221225472 | bytes 20971520 | tf_op jit(solution)/shard_map/local_outputs/pallas_call | solution.py:492
  29.7 3.7 %all-to-all-done.in_ref = bf16[16,136,128]{2,1,0:T(8,128)(2,1)S(1)} async-done(((bf16[16,136,128]{2,1,0:T(8,128)(2,1)}), bf16[16,136,128]{2,1,0:T(8,128)(2,1)S(1)}, u32[]{:S(2)}, u32[]{:S(2)}) %all-to-all-start) | async-done | bytes 557088 | tf_op jit(solution)/shard_map/all_to_all | solution.py:537
  34.5 3.6 %all-to-all-start.1 = ((bf16[16,136,128]{2,1,0:T(8,128)(2,1)}), bf16[16,136,128]{2,1,0:T(8,128)(2,1)S(1)}, u32[]{:S(2)}, u32[]{:S(2)}) async-start(bf16[16,136,128]{2,1,0:T(8,128)(2,1)} %prefix.1), calls=%async_computation.1 | async-start | bytes 1114112 | tf_op jit(solution)/shard_map/all_to_all | solution.py:544
  38.2 7.2 %local_outputs.3 = (bf16[256,2048]{1,0:T(8,128)(2,1)}, bf16[256,2048]{1,0:T(8,128)(2,1)}) custom-call(f32[32,512]{1,0:T(8,128)} %step_ref.1, f32[1,32]{1,0:T(1,128)S(1)} %bitcast.16, f32[1,32]{1,0:T(1,128)S(1)} %bitcast.19, bf16[512,2048]{1,0:T(8,128)(2,1)} %values_ref.3, bf16[512,2048]{1,0:T(8,128)(2,1)} %gate_ref.4, bf16[512,256]{1,0:T(8,128)(2,1)} %bitcast.26, ...), custom_call_target="tpu_custom_call" | custom-call | flops 3221225472 | bytes 20971520 | tf_op jit(solution)/shard_map/local_outputs/pallas_call | solution.py:492
  45.3 3.1 %all-to-all-done.1.back_ref = bf16[16,136,128]{2,1,0:T(8,128)(2,1)S(1)} async-done(((bf16[16,136,128]{2,1,0:T(8,128)(2,1)}), bf16[16,136,128]{2,1,0:T(8,128)(2,1)S(1)}, u32[]{:S(2)}, u32[]{:S(2)}) %all-to-all-start.1) | async-done | bytes 557088 | tf_op jit(solution)/shard_map/all_to_all | solution.py:544
  48.8 2.6 %collective-permute-start.1 = (bf16[16,136,128]{2,1,0:T(8,128)(2,1)S(1)}, bf16[16,136,128]{2,1,0:T(8,128)(2,1)S(1)}, u32[]{:S(2)}, u32[]{:S(2)}) collective-permute-start(bf16[16,136,128]{2,1,0:T(8,128)(2,1)S(1)} %get-tuple-element.70), channel_id=1, source_target_pairs={{0,4},{4,0},{1,5},{5,1},{2,6},{6,2},{3,7},{7,3},{8,12},{12,8},{9,1... | collective-permute-start | bytes 1671176 | tf_op jit(solution)/shard_map/ppermute | solution.py:469
  51.4 2.3 %fetch_weight.2 = (bf16[1,2048,512]{2,1,0:T(8,128)(2,1)S(1)}, bf16[256,2048]{1,0:T(8,128)(2,1)S(1)}, bf16[256,2048]{1,0:T(8,128)(2,1)S(1)}, bf16[512,256]{1,0:T(8,128)(2,1)S(1)}, f32[1,2048]{1,0:T(1,128)S(1)}) custom-call(bf16[2048,4096]{1,0:T(8,128)(2,1)} %weight_ref.1, bf16[256,2048]{1,0:T(8,128)(2,1)} %get-tuple-element.72.refs_0_, ...), custom_call_target="tpu_custom_call" | custom-call | tf_op jit(solution)/shard_map/fetch_weight/pallas_call | solution.py:342
  53.9 5.7 %chunk.2 = (bf16[2,256,512]{2,1,0:T(8,128)(2,1)}, bf16[2,256,512]{2,1,0:T(8,128)(2,1)}, bf16[256,2048]{1,0:T(8,128)(2,1)S(1)}, bf16[3,2048,512]{2,1,0:T(8,128)(2,1)S(1)}) custom-call(bf16[264,2048]{1,0:T(8,128)(2,1)S(1)} %join_halves.1.state_ref, bf16[512,256]{1,0:T(8,128)(2,1)S(1)} %get-tuple-element.75.read_ref, ...), custom_call_target="tpu_custom_call" | custom-call | tf_op jit(solution)/shard_map/chunk/pallas_call | solution.py:569
  59.6 1.7 %collective-permute-start.2 = (bf16[2,256,512]{2,1,0:T(8,128)(2,1)}, bf16[2,256,512]{2,1,0:T(8,128)(2,1)S(1)}, u32[]{:S(2)}, u32[]{:S(2)}) collective-permute-start(bf16[2,256,512]{2,1,0:T(8,128)(2,1)} %get-tuple-element.80), channel_id=1, source_target_pairs={{0,1},{1,0},{2,3},{3,2},{4,5},{5,4},{6,7},{7,6},{8,9},{9,8},{10,11... | collective-permute-start | bytes 1572872 | tf_op jit(solution)/shard_map/ppermute | solution.py:465
  61.3 2.4 %collective-permute-start.3 = (bf16[2,256,512]{2,1,0:T(8,128)(2,1)}, bf16[2,256,512]{2,1,0:T(8,128)(2,1)S(1)}, u32[]{:S(2)}, u32[]{:S(2)}) collective-permute-start(bf16[2,256,512]{2,1,0:T(8,128)(2,1)} %get-tuple-element.81), channel_id=1, source_target_pairs={{0,3},{1,2},{2,1},{3,0},{4,7},{5,6},{6,5},{7,4},{8,11},{9,10},{10,... | collective-permute-start | bytes 1572872 | tf_op jit(solution)/shard_map/ppermute | solution.py:465
  63.7 5.4 %chunk.3 = (bf16[2,256,512]{2,1,0:T(8,128)(2,1)}, bf16[2,256,512]{2,1,0:T(8,128)(2,1)}, bf16[256,2048]{1,0:T(8,128)(2,1)S(1)}) custom-call(bf16[264,2048]{1,0:T(8,128)(2,1)S(1)} %join_halves.1.state_ref, bf16[512,256]{1,0:T(8,128)(2,1)S(1)} %get-tuple-element.75.read_ref, bf16[256,2048]{1,0:T(8,128)(2,1)} %get-tuple-element.89.scaled_ref, ...), custom_call_target="tpu_custom_call" | custom-call | tf_op jit(solution)/shard_map/chunk/pallas_call | solution.py:569
  70.4 3.5 %fetch_weight.3.weight_ref.rest_ref = bf16[4,2048,512]{2,1,0:T(8,128)(2,1)S(1)} custom-call(bf16[2048,4096]{1,0:T(8,128)(2,1)} %weight_ref.1), custom_call_target="tpu_custom_call" | custom-call | tf_op jit(solution)/shard_map/fetch_weight/pallas_call | solution.py:342
  75.2 3.0 %sample_rows.1 = bf16[16,4096]{1,0:T(8,128)(2,1)} custom-call(bf16[264,2048]{1,0:T(8,128)(2,1)S(1)} %join_halves.1.state_ref, f32[1,2048]{1,0:T(1,128)S(1)} %get-tuple-element.78.norm_ref, f32[16,2048]{1,0:T(8,128)S(1)} %get-tuple-element.109.local_ref, f32[16,2048]{1,0:T(8,128)S(1)} %get-tuple-element.110.grown_ref, ...), custom_call_target="tpu_custom_call" | custom-call | flops 1 | bytes 1 | tf_op jit(solution)/shard_map/sample_rows/pallas_call | solution.py:444
  78.3 3.3 %copy-done = bf16[4,2048,512]{2,1,0:T(8,128)(2,1)} copy-done((bf16[4,2048,512]{2,1,0:T(8,128)(2,1)}, bf16[4,2048,512]{2,1,0:T(8,128)(2,1)S(1)}, u32[]{:S(2)}) %copy-start) | copy-done | bytes 8388632
  81.6 3.4 %copy-done.1 = bf16[4,2048,512]{2,1,0:T(8,128)(2,1)S(1)} copy-done((bf16[4,2048,512]{2,1,0:T(8,128)(2,1)S(1)}, bf16[4,2048,512]{2,1,0:T(8,128)(2,1)}, u32[]{:S(2)}) %copy-start.1) | copy-done | bytes 8388632
  85.0 2.3 %rest.2.rest_ref = bf16[4,256,512]{2,1,0:T(8,128)(2,1)S(1)} custom-call(bf16[256,2048]{1,0:T(8,128)(2,1)S(1)} %get-tuple-element.86.normed_ref, bf16[4,2048,512]{2,1,0:T(8,128)(2,1)S(1)} %copy-done.1), custom_call_target="tpu_custom_call" | custom-call | flops 1 | bytes 1 | tf_op jit(solution)/shard_map/rest/pallas_call | solution.py:444
  88.6 2.3 %rest.3.rest_ref = bf16[4,256,512]{2,1,0:T(8,128)(2,1)S(1)} custom-call(bf16[256,2048]{1,0:T(8,128)(2,1)S(1)} %copy-done.8, bf16[4,2048,512]{2,1,0:T(8,128)(2,1)S(1)} %copy-done.2), custom_call_target="tpu_custom_call" | custom-call | flops 1 | bytes 1 | tf_op jit(solution)/shard_map/rest/pallas_call | solution.py:444
  95.6 2.1 %collective-permute-start.4 = (bf16[256,512]{1,0:T(8,128)(2,1)}, bf16[256,512]{1,0:T(8,128)(2,1)S(1)}, u32[]{:S(2)}, u32[]{:S(2)}) collective-permute-start(bf16[256,512]{1,0:T(8,128)(2,1)} %get-tuple-element.94), channel_id=1, source_target_pairs={{0,3},{1,2},{2,1},{3,0},{4,7},{5,6},{6,5},{7,4},{8,11},{9,10},{10,... | collective-permute-start | bytes 786440 | tf_op jit(solution)/shard_map/ppermute | solution.py:465
  101.5 2.5 %collective-permute-done.4.refs_1_ = bf16[256,512]{1,0:T(8,128)(2,1)S(1)} collective-permute-done((bf16[256,512]{1,0:T(8,128)(2,1)}, bf16[256,512]{1,0:T(8,128)(2,1)S(1)}, u32[]{:S(2)}, u32[]{:S(2)}) %collective-permute-start.4) | collective-permute-done | bytes 262176 | tf_op jit(solution)/shard_map/ppermute | solution.py:465
  104.4 5.4 %collective-permute-done.8.refs_4_ = bf16[256,512]{1,0:T(8,128)(2,1)} collective-permute-done((bf16[256,512]{1,0:T(8,128)(2,1)}, bf16[256,512]{1,0:T(8,128)(2,1)}, u32[]{:S(2)}, u32[]{:S(2)}) %collective-permute-start.8) | collective-permute-done | bytes 262176 | tf_op jit(solution)/shard_map/ppermute | solution.py:465
  110.0 2.5 %finish.1 = bf16[1024,512]{1,0:T(8,128)(2,1)} custom-call(f32[2,256,512]{2,1,0:T(8,128)S(1)} %own_sum.2.refs_0_, bf16[256,512]{1,0:T(8,128)(2,1)S(1)} %collective-permute-done.4.refs_1_, bf16[256,512]{1,0:T(8,128)(2,1)} %collective-permute-done.5.refs_2_, f32[2,256,512]{2,1,0:T(8,128)S(1)} %own_sum.3.refs_3_, ...), custom_call_target="tpu_custom_call" | custom-call | flops 1 | bytes 1 | tf_op jit(solution)/shard_map/finish/pallas_call | solution.py:444
  (59 shorter events, 17.2 us)
Async XLA Ops:
  7.2 5.7 %copy-start.16 = (f32[32,2,16]{0,2,1:T(8,128)S(1)}, f32[32,2,16]{0,2,1:T(8,128)}, u32[]{:S(2)}) copy-start(f32[32,2,16]{0,2,1:T(8,128)} %param.28) | copy-start | bytes 12292
  7.2 15.2 %copy-start.14 = (f32[32]{0:T(128)S(1)}, f32[32]{0:T(128)}, u32[]{:S(2)}) copy-start(f32[32]{0:T(128)} %param.20) | copy-start | bytes 388
  7.2 15.2 %copy-start.15 = (f32[32]{0:T(128)S(1)}, f32[32]{0:T(128)}, u32[]{:S(2)}) copy-start(f32[32]{0:T(128)} %param.21) | copy-start | bytes 388
  11.3 3.1 %collective-permute-start = (bf16[16,136,128]{2,1,0:T(8,128)(2,1)S(1)}, bf16[16,136,128]{2,1,0:T(8,128)(2,1)S(1)}, u32[]{:S(2)}, u32[]{:S(2)}) collective-permute-start(bf16[16,136,128]{2,1,0:T(8,128)(2,1)S(1)} %get-tuple-element.58), channel_id=1, source_target_pairs={{0,4},{4,0},{1,5},{5,1},{2,6},{6,2},{3,7},{7,3},{8,12},{12,8},{9,1... | collective-permute-start | bytes 1671176 | tf_op jit(solution)/shard_map/ppermute | solution.py:469
  15.5 17.9 %all-to-all-start = ((bf16[16,136,128]{2,1,0:T(8,128)(2,1)}), bf16[16,136,128]{2,1,0:T(8,128)(2,1)S(1)}, u32[]{:S(2)}, u32[]{:S(2)}) async-start(bf16[16,136,128]{2,1,0:T(8,128)(2,1)} %join_cores.1), calls=%async_computation | async-start | bytes 1114112 | tf_op jit(solution)/shard_map/all_to_all | solution.py:537
  34.5 13.9 %all-to-all-start.1 = ((bf16[16,136,128]{2,1,0:T(8,128)(2,1)}), bf16[16,136,128]{2,1,0:T(8,128)(2,1)S(1)}, u32[]{:S(2)}, u32[]{:S(2)}) async-start(bf16[16,136,128]{2,1,0:T(8,128)(2,1)} %prefix.1), calls=%async_computation.1 | async-start | bytes 1114112 | tf_op jit(solution)/shard_map/all_to_all | solution.py:544
  38.1 62.0 %reduce-scatter.2.cloned.1.call-start = ((), (), s32[]{:S(2)}) async-start(), calls=%async_computation.3 | async-start | bytes 163840 | tf_op jit(solution)/shard_map/reduce_scatter | solution.py:607
  48.8 4.9 %collective-permute-start.1 = (bf16[16,136,128]{2,1,0:T(8,128)(2,1)S(1)}, bf16[16,136,128]{2,1,0:T(8,128)(2,1)S(1)}, u32[]{:S(2)}, u32[]{:S(2)}) collective-permute-start(bf16[16,136,128]{2,1,0:T(8,128)(2,1)S(1)} %get-tuple-element.70), channel_id=1, source_target_pairs={{0,4},{4,0},{1,5},{5,1},{2,6},{6,2},{3,7},{7,3},{8,12},{12,8},{9,1... | collective-permute-start | bytes 1671176 | tf_op jit(solution)/shard_map/ppermute | solution.py:469
  59.6 31.3 %collective-permute-start.2 = (bf16[2,256,512]{2,1,0:T(8,128)(2,1)}, bf16[2,256,512]{2,1,0:T(8,128)(2,1)S(1)}, u32[]{:S(2)}, u32[]{:S(2)}) collective-permute-start(bf16[2,256,512]{2,1,0:T(8,128)(2,1)} %get-tuple-element.80), channel_id=1, source_target_pairs={{0,1},{1,0},{2,3},{3,2},{4,5},{5,4},{6,7},{7,6},{8,9},{9,8},{10,11... | collective-permute-start | bytes 1572872 | tf_op jit(solution)/shard_map/ppermute | solution.py:465
  61.3 29.6 %collective-permute-start.3 = (bf16[2,256,512]{2,1,0:T(8,128)(2,1)}, bf16[2,256,512]{2,1,0:T(8,128)(2,1)S(1)}, u32[]{:S(2)}, u32[]{:S(2)}) collective-permute-start(bf16[2,256,512]{2,1,0:T(8,128)(2,1)} %get-tuple-element.81), channel_id=1, source_target_pairs={{0,3},{1,2},{2,1},{3,0},{4,7},{5,6},{6,5},{7,4},{8,11},{9,10},{10,... | collective-permute-start | bytes 1572872 | tf_op jit(solution)/shard_map/ppermute | solution.py:465
  69.1 4.9 %copy-start.7 = (bf16[256,2048]{1,0:T(8,128)(2,1)}, bf16[256,2048]{1,0:T(8,128)(2,1)S(1)}, u32[]{:S(2)}) copy-start(bf16[256,2048]{1,0:T(8,128)(2,1)S(1)} %get-tuple-element.92.normed_ref) | copy-start | bytes 3145732
  69.1 26.5 %collective-permute-start.6 = (bf16[2,256,512]{2,1,0:T(8,128)(2,1)}, bf16[2,256,512]{2,1,0:T(8,128)(2,1)S(1)}, u32[]{:S(2)}, u32[]{:S(2)}) collective-permute-start(bf16[2,256,512]{2,1,0:T(8,128)(2,1)} %get-tuple-element.98), channel_id=1, source_target_pairs={{0,1},{1,0},{2,3},{3,2},{4,5},{5,4},{6,7},{7,6},{8,9},{9,8},{10,11... | collective-permute-start | bytes 1572872 | tf_op jit(solution)/shard_map/ppermute | solution.py:465
  69.7 4.3 %copy-start.9 = (bf16[2,16,2048]{2,1,0:T(8,128)(2,1)S(1)}, bf16[2,16,2048]{2,1,0:T(8,128)(2,1)}, u32[]{:S(2)}) copy-start(bf16[2,16,2048]{2,1,0:T(8,128)(2,1)} %values_ref.4) | copy-start | bytes 393220
  69.7 4.3 %copy-start.10 = (bf16[2,16,2048]{2,1,0:T(8,128)(2,1)S(1)}, bf16[2,16,2048]{2,1,0:T(8,128)(2,1)}, u32[]{:S(2)}) copy-start(bf16[2,16,2048]{2,1,0:T(8,128)(2,1)} %gate_ref.5) | copy-start | bytes 393220
  69.7 4.3 %copy-start.11 = (bf16[2,16,1,256]{3,1,2,0:T(8,128)(2,1)S(1)}, bf16[2,16,1,256]{3,1,2,0:T(8,128)(2,1)}, u32[]{:S(2)}) copy-start(bf16[2,16,1,256]{3,1,2,0:T(8,128)(2,1)} %param.27) | copy-start | bytes 49156
  69.7 4.3 %copy-start.12 = (bf16[2,16,1,256]{3,1,2,0:T(8,128)(2,1)S(1)}, bf16[2,16,1,256]{3,1,2,0:T(8,128)(2,1)}, u32[]{:S(2)}) copy-start(bf16[2,16,1,256]{3,1,2,0:T(8,128)(2,1)} %param.26) | copy-start | bytes 49156
  69.7 4.3 %copy-start.13 = (s32[2]{0:T(128)S(1)}, s32[2]{0:T(128)}, u32[]{:S(2)}) copy-start(s32[2]{0:T(128)} %length.3) | copy-start | bytes 28
  69.7 25.9 %collective-permute-start.7 = (bf16[2,256,512]{2,1,0:T(8,128)(2,1)}, bf16[2,256,512]{2,1,0:T(8,128)(2,1)S(1)}, u32[]{:S(2)}, u32[]{:S(2)}) collective-permute-start(bf16[2,256,512]{2,1,0:T(8,128)(2,1)} %get-tuple-element.99), channel_id=1, source_target_pairs={{0,3},{1,2},{2,1},{3,0},{4,7},{5,6},{6,5},{7,4},{8,11},{9,10},{10,... | collective-permute-start | bytes 1572872 | tf_op jit(solution)/shard_map/ppermute | solution.py:465
  85.0 3.4 %copy-start.2 = (bf16[4,2048,512]{2,1,0:T(8,128)(2,1)S(1)}, bf16[4,2048,512]{2,1,0:T(8,128)(2,1)}, u32[]{:S(2)}) copy-start(bf16[4,2048,512]{2,1,0:T(8,128)(2,1)} %copy-done) | copy-start | bytes 25165828
  85.0 3.6 %copy-start.8 = (bf16[256,2048]{1,0:T(8,128)(2,1)S(1)}, bf16[256,2048]{1,0:T(8,128)(2,1)}, u32[]{:S(2)}) copy-start(bf16[256,2048]{1,0:T(8,128)(2,1)} %copy-done.7) | copy-start | bytes 3145732
  95.6 8.4 %collective-permute-start.4 = (bf16[256,512]{1,0:T(8,128)(2,1)}, bf16[256,512]{1,0:T(8,128)(2,1)S(1)}, u32[]{:S(2)}, u32[]{:S(2)}) collective-permute-start(bf16[256,512]{1,0:T(8,128)(2,1)} %get-tuple-element.94), channel_id=1, source_target_pairs={{0,3},{1,2},{2,1},{3,0},{4,7},{5,6},{6,5},{7,4},{8,11},{9,10},{10,... | collective-permute-start | bytes 786440 | tf_op jit(solution)/shard_map/ppermute | solution.py:465
  97.8 6.7 %collective-permute-start.5 = (bf16[256,512]{1,0:T(8,128)(2,1)}, bf16[256,512]{1,0:T(8,128)(2,1)}, u32[]{:S(2)}, u32[]{:S(2)}) collective-permute-start(bf16[256,512]{1,0:T(8,128)(2,1)} %get-tuple-element.95), channel_id=1, source_target_pairs={{0,1},{1,0},{2,3},{3,2},{4,5},{5,4},{6,7},{7,6},{8,9},{9,8},{10,11... | collective-permute-start | bytes 786440 | tf_op jit(solution)/shard_map/ppermute | solution.py:465
  98.6 11.2 %collective-permute-start.8 = (bf16[256,512]{1,0:T(8,128)(2,1)}, bf16[256,512]{1,0:T(8,128)(2,1)}, u32[]{:S(2)}, u32[]{:S(2)}) collective-permute-start(bf16[256,512]{1,0:T(8,128)(2,1)} %get-tuple-element.103), channel_id=1, source_target_pairs={{0,3},{1,2},{2,1},{3,0},{4,7},{5,6},{6,5},{7,4},{8,11},{9,10},{10,... | collective-permute-start | bytes 786440 | tf_op jit(solution)/shard_map/ppermute | solution.py:465
  99.2 10.8 %collective-permute-start.9 = (bf16[256,512]{1,0:T(8,128)(2,1)}, bf16[256,512]{1,0:T(8,128)(2,1)}, u32[]{:S(2)}, u32[]{:S(2)}) collective-permute-start(bf16[256,512]{1,0:T(8,128)(2,1)} %get-tuple-element.104), channel_id=1, source_target_pairs={{0,1},{1,0},{2,3},{3,2},{4,5},{5,4},{6,7},{7,6},{8,9},{9,8},{10,11... | collective-permute-start | bytes 786440 | tf_op jit(solution)/shard_map/ppermute | solution.py:465
  (6 other events, 10.3 us)
Sparse Core Ops, SparseCore 0:
  81.7 15.7 reduce-scatter.1
